TPU v7x, 32 devices: a whole 2x2x4 slice. The times are simulated.
32 devices in a mesh: grid: 4 (over z), dom: 8 (over y, x, core).
Axes of the slice: x: 2, y: 2, z: 4, core: 2. Of those that a mesh axis runs over, the one named last changes fastest.
Arguments:
- columns: bfloat16 [65536, 128], P(('grid', 'dom')), may hold values from -6 to 6
- column_live: int32 [65536], P(('grid', 'dom')), may hold values 0 or 1
- col_weight: float32 [65536], P(('grid', 'dom')), may hold values from 0.2 to 1
- col_slot: int32 [65536], P(('grid', 'dom')), may hold values from 0 to 511
- node_static: bfloat16 [16384, 256], P(('grid', 'dom')), may hold values from -6 to 6
- boundary_idx: int32 [8192], P(('grid', 'dom')), may hold values from 0 to 511
- edge_src: int32 [65536], P(('grid', 'dom')), may hold values from 0 to 1535
- edge_dst: int32 [65536], P(('grid', 'dom')), may hold values from 0 to 511
- edge_live: int32 [65536], P(('grid', 'dom')), may hold values from 0 to 1, as said below
- edge_weight: float32 [65536], P(('grid', 'dom')), may hold values from 0.2 to 1
- enc_in: bfloat16 [128, 256], replicated, may hold values from -0.5 to 0.5
- enc_out: bfloat16 [256, 256], replicated, may hold values from -0.375 to 0.375
- src_proj: bfloat16 [2, 256, 256], replicated, may hold values from -0.375 to 0.375
- dst_proj: bfloat16 [2, 256, 256], replicated, may hold values from -0.375 to 0.375
- msg_proj: bfloat16 [2, 256, 256], replicated, may hold values from -0.375 to 0.375
- node_cotangent: bfloat16 [16384, 256], P(('grid', 'dom')), may hold values from -6 to 6
Outputs:
- node_out: bfloat16 [16384, 256], P(('grid', 'dom'))
- enc_in_grad: float32 [128, 256], replicated
- enc_out_grad: float32 [256, 256], replicated
- src_grad: float32 [2, 256, 256], replicated
- dst_grad: float32 [2, 256, 256], replicated
- msg_grad: float32 [2, 256, 256], replicated
Inputs may be any that keep to these rules, and one draw needn't show every extreme that they name: `col_slot`: column slot j of a partition, with k * 64 <= j < (k + 1) * 64, is bound for partition k. `edge_live`: in each partition the live edge slots come first; some partition has all 2048 live.
All inputs are finite; a program needn't handle non-finite values. No bound on the sum of `column_live` on one device may be relied on, other than what follows from the above.
Results may differ from a plain program's by a relative error of at most 0.0095.
Values may be sent and summed in bfloat16 or wider, within the bound.
No kernel may reach another device: no remote copies, remote signals or barrier semaphores. Data moves between devices by JAX's collectives and lax.ppermute only.
A program may use at most 128 MiB of HBM per device.

v0:
```python
import jax
import jax.numpy as jnp
from jax import lax
from jax.sharding import PartitionSpec as P

AXES = ("grid", "dom")
BF = jnp.bfloat16
F32 = jnp.float32


def mm(left_side, right_side):
    return jnp.dot(left_side, right_side, preferred_element_type=F32)


def mm_t(left_side, right_side):
    return lax.dot_general(
        left_side, right_side, (((1,), (1,)), ((), ())), preferred_element_type=F32
    )


def t_mm(left_side, right_side):
    return lax.dot_general(
        left_side, right_side, (((0,), (0,)), ((), ())), preferred_element_type=F32
    )


def picks(indices, count, start=0):
    return (indices[:, None] == start + jnp.arange(count, dtype=jnp.int32)[None, :]).astype(BF)


def picks_t(indices, count, start=0):
    return (indices[None, :] == start + jnp.arange(count, dtype=jnp.int32)[:, None]).astype(BF)


def silu_grad(inputs):
    sigmoid_val = jax.nn.sigmoid(inputs)
    return sigmoid_val * (1.0 + inputs * (1.0 - sigmoid_val))


def passed_along(shard, axis, by):
    count = lax.axis_size(axis)
    pairs = [(i, i + by) for i in range(count) if 0 <= i + by < count]
    return lax.ppermute(shard, axis, pairs)


def exchange(shard, axes):
    count = shard.shape[0]
    return lax.all_to_all(shard, axes, split_axis=0, concat_axis=0, tiled=True)


def summed(rows):
    count = lax.axis_size(AXES)
    total, width = rows.shape
    share = -(-total // (16 * count)) * 16
    rows = jnp.pad(rows.astype(BF), ((0, share * count - total), (0, 0)))
    parts = exchange(rows.reshape(count, share, width), AXES)
    mine = jnp.sum(parts.astype(F32), 0).astype(BF)
    whole = exchange(jnp.broadcast_to(mine[None], (count, share, width)), AXES)
    return whole.reshape(count * share, width)[:total].astype(F32)


def per_device(
    columns,
    column_live,
    col_weight,
    col_slot,
    node_static,
    boundary_idx,
    edge_src,
    edge_dst,
    edge_live,
    edge_weight,
    enc_in,
    enc_out,
    src_proj,
    dst_proj,
    msg_proj,
    node_cotangent,
):
    peers = lax.axis_size(AXES)
    cols, fin = columns.shape
    nodes, width = node_static.shape
    rim = boundary_idx.shape[0]
    bucket = cols // peers
    layers = src_proj.shape[0]
    edge_scale = (edge_weight * edge_live.astype(F32))[:, None]

    scale = col_weight * column_live.astype(F32)
    scale_hi = lax.reduce_precision(scale, 8, 7)
    scale_lo = scale - scale_hi
    extra = jnp.stack(
        [
            (col_slot // 256).astype(BF).reshape(peers, bucket),
            (col_slot % 256).astype(BF).reshape(peers, bucket),
            scale_hi.astype(BF).reshape(peers, bucket),
            scale_lo.astype(BF).reshape(peers, bucket),
        ],
        1,
    ).reshape(peers, 4 * bucket)
    extra_rows = -(-4 * bucket // fin)
    extra = jnp.pad(extra, ((0, 0), (0, extra_rows * fin - 4 * bucket)))
    packed = jnp.concatenate(
        [columns.reshape(peers, bucket, fin), extra.reshape(peers, extra_rows, fin)], 1
    )
    packed = exchange(packed, AXES)
    got = packed[:, :bucket].reshape(cols, fin)
    extra = packed[:, bucket:].reshape(peers, extra_rows * fin)[:, : 4 * bucket]
    extra = extra.reshape(peers, 4, bucket).astype(F32).transpose(1, 0, 2).reshape(4, cols)
    slot = (extra[0] * 256.0 + extra[1]).astype(jnp.int32)
    got_scale = (extra[2] + extra[3])[:, None]

    enc_pre = mm(got, enc_in)
    pooled_act = mm(picks_t(slot, nodes), (jax.nn.silu(enc_pre) * got_scale).astype(BF)).astype(BF)
    state = (node_static.astype(F32) + mm(pooled_act, enc_out)).astype(BF)

    stored = []
    for layer in range(layers):
        from_src = mm(state, src_proj[layer]).astype(BF)
        from_dst = mm(state, dst_proj[layer]).astype(BF)
        rim_rows = mm(picks(boundary_idx, nodes), from_src).astype(BF)
        rims = jnp.concatenate(
            [
                passed_along(rim_rows, "grid", 1),
                passed_along(rim_rows, "grid", -1),
                passed_along(rim_rows, "dom", 1),
                passed_along(rim_rows, "dom", -1),
            ],
            0,
        )
        pre = (
            mm(picks(edge_src, nodes), from_src)
            + mm(picks(edge_dst, nodes), from_dst)
            + mm(picks(edge_src, 4 * rim, nodes), rims)
        )
        act = (jax.nn.silu(pre) * edge_scale).astype(BF)
        node_act = mm(picks_t(edge_dst, nodes), act).astype(BF)
        stored.append((state, pre, node_act))
        state = (state.astype(F32) + mm(node_act, msg_proj[layer])).astype(BF)

    grad = node_cotangent.astype(F32)
    terms = [None] * layers
    for layer in reversed(range(layers)):
        own, pre, node_act = stored[layer]
        grad_bf = grad.astype(BF)
        msg_term = t_mm(node_act, grad_bf)
        grad_act = mm(picks(edge_dst, nodes), mm_t(grad_bf, msg_proj[layer]).astype(BF))
        grad_pre = (grad_act * edge_scale * silu_grad(pre)).astype(BF)
        rim_sends = mm(picks_t(edge_src, 4 * rim, nodes), grad_pre).astype(BF)
        rim_sends = rim_sends.reshape(4, rim, width)
        returned = (
            passed_along(rim_sends[0], "grid", -1).astype(F32)
            + passed_along(rim_sends[1], "grid", 1).astype(F32)
            + passed_along(rim_sends[2], "dom", -1).astype(F32)
            + passed_along(rim_sends[3], "dom", 1).astype(F32)
        ).astype(BF)
        grad_src = mm(picks_t(edge_src, nodes), grad_pre) + mm(picks_t(boundary_idx, nodes), returned)
        grad_src = grad_src.astype(BF)
        grad_dst = mm(picks_t(edge_dst, nodes), grad_pre).astype(BF)
        terms[layer] = (t_mm(own, grad_src), t_mm(own, grad_dst), msg_term)
        grad = grad + mm_t(grad_src, src_proj[layer]) + mm_t(grad_dst, dst_proj[layer])

    grad_bf = grad.astype(BF)
    out_term = t_mm(pooled_act, grad_bf)
    grad_hidden = mm(picks(slot, nodes), mm_t(grad_bf, enc_out).astype(BF))
    grad_enc_pre = (grad_hidden * got_scale * silu_grad(enc_pre)).astype(BF)
    in_term = t_mm(got, grad_enc_pre)
    flat = [in_term, out_term]
    for entry in range(3):
        flat += [terms[layer][entry] for layer in range(layers)]
    whole = summed(jnp.concatenate(flat, 0))
    fin_rows = fin
    hid = enc_out.shape[0]
    rest = whole[fin_rows + hid :].reshape(3, layers, width, width)
    return (state, whole[:fin_rows], whole[fin_rows : fin_rows + hid], rest[0], rest[1], rest[2])


def solution(mesh):
    rows = P(AXES, None)
    flat = P(AXES)
    placed = (rows, flat, flat, flat, rows, flat, flat, flat, flat, flat, P(), P(), P(), P(), P(), rows)
    return jax.shard_map(
        per_device,
        mesh=mesh,
        in_specs=placed,
        out_specs=(rows, P(), P(), P(), P(), P()),
        check_vma=False,
    )
```

profile of v0, /device:TPU:0, one launch (start us, length us, event | category | flops | bytes accessed | tf_op | source)
XLA Modules:
  0.0 209.3 jit_solution(12010204212986096628)
XLA Ops:
  0.7 0.8 reduce-precision_convert_fusion
  1.6 0.7 fusion.147
  2.6 1.9 pad_maximum_fusion
  4.6 7.3 %all-to-all-start = ((bf16[32,66,128]{2,1,0:T(8,128)(2,1)}), bf16[32,66,128]{2,1,0:T(8,128)(2,1)S(1)}, u32[]{:S(2)}, u32[]{:S(2)}) async-start(bf16[32,66,128]{2,1,0:T(8,128)(2,1)} %pad_maximum_fusion), calls=%async_computation | async-start | bytes 1179648 | tf_op jit(solution)/shard_map/all_to_all | solution.py:48
  12.0 16.7 %all-to-all-done = bf16[32,66,128]{2,1,0:T(8,128)(2,1)S(1)} async-done(((bf16[32,66,128]{2,1,0:T(8,128)(2,1)}), bf16[32,66,128]{2,1,0:T(8,128)(2,1)S(1)}, u32[]{:S(2)}, u32[]{:S(2)}) %all-to-all-start) | async-done | bytes 540704 | tf_op jit(solution)/shard_map/all_to_all | solution.py:48
  29.2 0.4 fusion.160
  30.0 1.2 fusion.74
  31.5 0.5 copy-done.10
  32.5 1.3 collective-permute-start.3
  33.8 3.0 %collective-permute-start.2 = (bf16[256,256]{1,0:T(8,128)(2,1)S(1)}, bf16[256,256]{1,0:T(8,128)(2,1)S(1)}, u32[]{:S(2)}, u32[]{:S(2)}) collective-permute-start(bf16[256,256]{1,0:T(8,128)(2,1)S(1)} %convolution_convert_fusion.15), channel_id=1, source_target_pairs={{0,1},{1,2},{2,3},{3,4},{4,5},{5,6},{6,7},{8,9},{9,10},{10,11},{11... | collective-permute-start | bytes 393224 | tf_op jit(solution)/shard_map/ppermute | solution.py:43
  36.8 1.3 collective-permute-start.1
  38.1 5.2 %collective-permute-start = (bf16[256,256]{1,0:T(8,128)(2,1)S(1)}, bf16[256,256]{1,0:T(8,128)(2,1)}, u32[]{:S(2)}, u32[]{:S(2)}) collective-permute-start(bf16[256,256]{1,0:T(8,128)(2,1)S(1)} %convolution_convert_fusion.15), channel_id=1, source_target_pairs={{0,8},{8,16},{16,24},{1,9},{9,17},{17,25},{2,10},{10,18},{18,26},{... | collective-permute-start | bytes 393224 | tf_op jit(solution)/shard_map/ppermute | solution.py:43
  43.3 3.3 %fusion.17 = f32[2048,256]{1,0:T(8,128)} fusion(s32[2048]{0:T(1024)S(1)} %copy-done.34, bf16[512,256]{1,0:T(8,128)(2,1)S(1)} %fusion.70, bf16[2,256,256]{2,1,0:T(8,128)(2,1)} %param.29), kind=kOutput, calls=%fused_computation.20 | convolution fusion | flops 605159424 | bytes 2498560 | tf_op jit(solution)/shard_map/dot_general | solution.py:12
  46.6 2.3 %fusion.31 = f32[2048,256]{1,0:T(8,128)S(1)} fusion(f32[2048,256]{1,0:T(8,128)} %fusion.17, bf16[512,256]{1,0:T(8,128)(2,1)S(1)} %convolution_convert_fusion.6, s32[2048]{0:T(1024)S(1)} %copy-done.21), kind=kOutput, calls=%fused_computation.37 | convolution fusion | flops 538443776 | bytes 4464640 | tf_op jit(solution)/shard_map/dot_general | solution.py:12
  49.0 2.5 %fusion.38 = f32[2048,256]{1,0:T(8,128)S(1)} fusion(f32[2048,256]{1,0:T(8,128)S(1)} %fusion.31, s32[1024]{0:T(1024)S(1)} %iota_add_fusion, s32[2048]{0:T(1024)S(1)} %copy-done.21, bf16[256,256]{1,0:T(8,128)(2,1)S(1)} %collective-permute-done.3, bf16[256,256]{1,0:T(8,128)(2,1)S(1)} %collective-permute-done.2, bf16[256,256]{1,0:T(8,128)(2,1)} %collective-permute-done.1, ...), kind=kOutput, calls=%fused_computation.44 | convolution fusion | flops 1078460416 | bytes 4730880 | tf_op jit(solution)/shard_map/dot_general | solution.py:12
  51.5 1.2 fusion.75
  53.3 0.9 convolution_convert_fusion.14
  54.3 1.3 collective-permute-start.7
  55.6 3.8 %collective-permute-start.6 = (bf16[256,256]{1,0:T(8,128)(2,1)}, bf16[256,256]{1,0:T(8,128)(2,1)}, u32[]{:S(2)}, u32[]{:S(2)}) collective-permute-start(bf16[256,256]{1,0:T(8,128)(2,1)} %convolution_convert_fusion.14), channel_id=1, source_target_pairs={{0,1},{1,2},{2,3},{3,4},{4,5},{5,6},{6,7},{8,9},{9,10},{10,11},{11... | collective-permute-start | bytes 393224 | tf_op jit(solution)/shard_map/ppermute | solution.py:43
  59.4 1.3 collective-permute-start.5
  60.7 5.2 %collective-permute-start.4 = (bf16[256,256]{1,0:T(8,128)(2,1)}, bf16[256,256]{1,0:T(8,128)(2,1)}, u32[]{:S(2)}, u32[]{:S(2)}) collective-permute-start(bf16[256,256]{1,0:T(8,128)(2,1)} %convolution_convert_fusion.14), channel_id=1, source_target_pairs={{0,8},{8,16},{16,24},{1,9},{9,17},{17,25},{2,10},{10,18},{18,26},{... | collective-permute-start | bytes 393224 | tf_op jit(solution)/shard_map/ppermute | solution.py:43
  65.9 3.3 %fusion.16 = f32[2048,256]{1,0:T(8,128)} fusion(s32[2048]{0:T(1024)} %param.23, bf16[512,256]{1,0:T(8,128)(2,1)S(1)} %fusion.71, bf16[2,256,256]{2,1,0:T(8,128)(2,1)} %param.29), kind=kOutput, calls=%fused_computation.19 | convolution fusion | flops 605159424 | bytes 2498560 | tf_op jit(solution)/shard_map/dot_general | solution.py:12
  69.2 2.3 %fusion.32 = f32[2048,256]{1,0:T(8,128)S(1)} fusion(f32[2048,256]{1,0:T(8,128)} %fusion.16, bf16[512,256]{1,0:T(8,128)(2,1)S(1)} %convolution_convert_fusion.4, s32[2048]{0:T(1024)S(1)} %copy-done.21), kind=kOutput, calls=%fused_computation.38 | convolution fusion | flops 538443776 | bytes 4464640 | tf_op jit(solution)/shard_map/dot_general | solution.py:12
  71.7 2.6 %fusion.41 = f32[2048,256]{1,0:T(8,128)S(1)} fusion(f32[2048,256]{1,0:T(8,128)S(1)} %fusion.32, s32[1024]{0:T(1024)S(1)} %copy-done.29, s32[2048]{0:T(1024)S(1)} %copy-done.21, bf16[256,256]{1,0:T(8,128)(2,1)} %collective-permute-done.7, bf16[256,256]{1,0:T(8,128)(2,1)} %collective-permute-done.6, bf16[256,256]{1,0:T(8,128)(2,1)} %collective-permute-done.5, ...), kind=kOutput, calls=%fused_computation.45 | convolution fusion | flops 1078460416 | bytes 4730880 | tf_op jit(solution)/shard_map/dot_general | solution.py:12
  74.3 1.4 copy-done.39
  75.7 1.9 fusion.76
  77.6 4.3 %fusion.45 = bf16[2048,256]{1,0:T(8,128)(2,1)} fusion(f32[2048,256]{1,0:T(8,128)} %copy-done.39, s32[2048]{0:T(1024)} %param.23, bf16[512,256]{1,0:T(8,128)(2,1)} %param.31, f32[2048]{0:T(1024)} %copy-done.26, bf16[2,256,256]{2,1,0:T(8,128)(2,1)S(1)} %copy-done.8), kind=kOutput, calls=%fused_computation.47 | convolution fusion | flops 610402304 | bytes 3555328 | tf_op jit(solution)/shard_map/dot_general | solution.py:12
  81.9 2.7 %fusion.61 = bf16[1024,256]{1,0:T(8,128)(2,1)S(1)} fusion(bf16[2048,256]{1,0:T(8,128)(2,1)} %fusion.45, s32[2048]{0:T(1024)S(1)} %copy-done.21, s32[1024]{0:T(1024)} %copy-done.28), kind=kOutput, calls=%fused_computation.69 | convolution fusion | flops 1076101120 | bytes 1585152 | tf_op jit(solution)/shard_map/dot_general | solution.py:12
  84.6 0.8 fusion.11
  85.4 1.3 collective-permute-start.8
  86.7 2.4 %collective-permute-start.11 = (bf16[256,256]{1,0:T(8,128)(2,1)S(1)}, bf16[256,256]{1,0:T(8,128)(2,1)S(1)}, u32[]{:S(2)}, u32[]{:S(2)}) collective-permute-start(bf16[256,256]{1,0:T(8,128)(2,1)S(1)} %get-tuple-element.14), channel_id=1, source_target_pairs={{0,1},{1,2},{2,3},{3,4},{4,5},{5,6},{6,7},{8,9},{9,10},{10,11},{11... | collective-permute-start | bytes 393224 | tf_op jit(solution)/shard_map/ppermute | solution.py:43
  89.2 1.3 collective-permute-start.10
  90.5 4.6 %collective-permute-start.9 = (bf16[256,256]{1,0:T(8,128)(2,1)S(1)}, bf16[256,256]{1,0:T(8,128)(2,1)S(1)}, u32[]{:S(2)}, u32[]{:S(2)}) collective-permute-start(bf16[256,256]{1,0:T(8,128)(2,1)S(1)} %get-tuple-element.16), channel_id=1, source_target_pairs={{0,8},{8,16},{16,24},{1,9},{9,17},{17,25},{2,10},{10,18},{18,26},{... | collective-permute-start | bytes 393224 | tf_op jit(solution)/shard_map/ppermute | solution.py:43
  95.2 0.8 fusion.77
  96.0 1.6 collective-permute-done.9
  97.9 0.7 copy-done.4
  99.1 4.3 %fusion.46 = bf16[2048,256]{1,0:T(8,128)(2,1)} fusion(f32[2048,256]{1,0:T(8,128)} %copy-done.38, s32[2048]{0:T(1024)} %param.23, f32[2048]{0:T(1024)} %copy-done.26, f32[512,256]{1,0:T(8,128)S(1)} %convolution_add_fusion.4, bf16[2,256,256]{2,1,0:T(8,128)(2,1)} %param.30), kind=kOutput, calls=%fused_computation.48 | convolution fusion | flops 610533376 | bytes 3817472 | tf_op jit(solution)/shard_map/dot_general | solution.py:12
  103.4 2.7 %fusion.64 = bf16[1024,256]{1,0:T(8,128)(2,1)S(1)} fusion(bf16[2048,256]{1,0:T(8,128)(2,1)} %fusion.46, s32[2048]{0:T(1024)S(1)} %copy-done.21, s32[1024]{0:T(1024)} %copy-done.28), kind=kOutput, calls=%fused_computation.70 | convolution fusion | flops 1076101120 | bytes 1585152 | tf_op jit(solution)/shard_map/dot_general | solution.py:12
  106.1 0.8 fusion.10
  106.9 1.3 collective-permute-start.12
  108.2 3.2 %collective-permute-start.15 = (bf16[256,256]{1,0:T(8,128)(2,1)S(1)}, bf16[256,256]{1,0:T(8,128)(2,1)S(1)}, u32[]{:S(2)}, u32[]{:S(2)}) collective-permute-start(bf16[256,256]{1,0:T(8,128)(2,1)S(1)} %get-tuple-element.10), channel_id=1, source_target_pairs={{0,1},{1,2},{2,3},{3,4},{4,5},{5,6},{6,7},{8,9},{9,10},{10,11},{11... | collective-permute-start | bytes 393224 | tf_op jit(solution)/shard_map/ppermute | solution.py:43
  111.5 1.3 collective-permute-start.14
  112.8 4.9 %collective-permute-start.13 = (bf16[256,256]{1,0:T(8,128)(2,1)S(1)}, bf16[256,256]{1,0:T(8,128)(2,1)S(1)}, u32[]{:S(2)}, u32[]{:S(2)}) collective-permute-start(bf16[256,256]{1,0:T(8,128)(2,1)S(1)} %get-tuple-element.12), channel_id=1, source_target_pairs={{0,8},{8,16},{16,24},{1,9},{9,17},{17,25},{2,10},{10,18},{18,26},{... | collective-permute-start | bytes 393224 | tf_op jit(solution)/shard_map/ppermute | solution.py:43
  117.7 0.8 fusion.78
  118.5 1.7 collective-permute-done.13
  120.7 1.0 fusion.73
  121.7 1.9 convolution_convert_fusion
  123.6 3.4 %fusion.87 = bf16[1920,256]{1,0:T(8,128)(2,1)} fusion(bf16[2048,128]{1,0:T(8,128)(2,1)} %bitcast.87, bf16[512,256]{1,0:T(8,128)(2,1)} %convolution_convert_fusion, f32[2048,256]{1,0:T(8,128)S(1)} %fusion.160, s32[2048]{0:T(1024)S(1)} %copy-done.25, f32[2048]{0:T(1024)S(1)} %add.132), kind=kOutput, calls=%fused_computation.116 | convolution fusion | flops 677412864 | bytes 2965504 | tf_op jit(solution)/shard_map/dot_general | solution.py:22
  127.0 2.0 fusion.85
  129.1 1.9 fusion.84
  130.9 1.9 fusion.83
  132.8 0.9 fusion.82
  133.8 0.9 fusion.81
  134.7 0.9 fusion.80
  135.6 0.9 fusion.79
  136.5 1.3 pad.4
  137.8 37.5 %all_to_all.15 = bf16[32,64,256]{2,1,0:T(8,128)(2,1)S(1)} all-to-all(bf16[32,64,256]{2,1,0:T(8,128)(2,1)S(1)} %bitcast.85), channel_id=1, replica_groups=mesh['grid'=4,'dom'=8] {'grid','dom'}, dimensions={0} | all-to-all | bytes 2097152 | tf_op jit(solution)/shard_map/all_to_all | solution.py:48
  175.5 1.1 broadcast_in_dim.2
  176.6 3.6 %all-to-all-start.2 = ((bf16[32,64,256]{2,1,0:T(8,128)(2,1)}), bf16[32,64,256]{2,1,0:T(8,128)(2,1)S(1)}, u32[]{:S(2)}, u32[]{:S(2)}) async-start(bf16[32,64,256]{2,1,0:T(8,128)(2,1)} %broadcast_in_dim.2), calls=%async_computation.2 | async-start | bytes 2097152 | tf_op jit(solution)/shard_map/all_to_all | solution.py:48
  180.2 0.9 fusion.72
  181.2 25.3 %all-to-all-done.2 = bf16[32,64,256]{2,1,0:T(8,128)(2,1)S(1)} async-done(((bf16[32,64,256]{2,1,0:T(8,128)(2,1)}), bf16[32,64,256]{2,1,0:T(8,128)(2,1)S(1)}, u32[]{:S(2)}, u32[]{:S(2)}) %all-to-all-start.2) | async-done | bytes 1048608 | tf_op jit(solution)/shard_map/all_to_all | solution.py:48
  206.7 0.7 slice.156
  207.3 0.7 slice.157
  208.1 1.2 fusion.157
  (125 shorter events, 4.5 us)
Async XLA Ops:
  0.6 30.6 %copy-start = (bf16[256,256]{1,0:T(8,128)(2,1)S(1)}, bf16[256,256]{1,0:T(8,128)(2,1)}, u32[]{:S(2)}) copy-start(bf16[256,256]{1,0:T(8,128)(2,1)} %param.27) | copy-start | bytes 393220
  0.6 11.3 %copy-start.22 = (f32[2048]{0:T(1024)S(1)}, f32[2048]{0:T(1024)}, u32[]{:S(2)}) copy-start(f32[2048]{0:T(1024)} %param.25) | copy-start | bytes 24580
  0.7 11.3 %copy-start.23 = (s32[2048]{0:T(1024)S(1)}, s32[2048]{0:T(1024)}, u32[]{:S(2)}) copy-start(s32[2048]{0:T(1024)} %param.24) | copy-start | bytes 24580
  0.7 28.5 %copy-start.20 = (bf16[128,256]{1,0:T(8,128)(2,1)S(1)}, bf16[128,256]{1,0:T(8,128)(2,1)}, u32[]{:S(2)}) copy-start(bf16[128,256]{1,0:T(8,128)(2,1)} %param.26) | copy-start | bytes 196612
  4.6 24.1 %all-to-all-start = ((bf16[32,66,128]{2,1,0:T(8,128)(2,1)}), bf16[32,66,128]{2,1,0:T(8,128)(2,1)S(1)}, u32[]{:S(2)}, u32[]{:S(2)}) async-start(bf16[32,66,128]{2,1,0:T(8,128)(2,1)} %pad_maximum_fusion), calls=%async_computation | async-start | bytes 1179648 | tf_op jit(solution)/shard_map/all_to_all | solution.py:48
  11.9 37.1 %copy-start.28 = (s32[1024]{0:T(1024)}, s32[1024]{0:T(1024)S(1)}, u32[]{:S(2)}) copy-start(s32[1024]{0:T(1024)S(1)} %iota_add_fusion) | copy-start | bytes 12292
  11.9 39.6 %copy-start.26 = (f32[2048]{0:T(1024)}, f32[2048]{0:T(1024)S(1)}, u32[]{:S(2)}) copy-start(f32[2048]{0:T(1024)S(1)} %convert_multiply_fusion) | copy-start | bytes 24580
  29.1 2.1 %copy-start.24 = (s32[2048]{0:T(1024)}, s32[2048]{0:T(1024)S(1)}, u32[]{:S(2)}) copy-start(s32[2048]{0:T(1024)S(1)} %convert_element_type.205) | copy-start | bytes 24580
  29.2 0.8 copy-start.1
  30.0 1.3 copy-start.6
  30.0 2.0 copy-start.2
  30.0 2.2 %copy-start.30 = (s32[256]{0:T(256)S(1)}, s32[256]{0:T(256)}, u32[]{:S(2)}) copy-start(s32[256]{0:T(256)} %param.21) | copy-start | bytes 3076
  30.0 13.3 %copy-start.34 = (s32[2048]{0:T(1024)S(1)}, s32[2048]{0:T(1024)}, u32[]{:S(2)}) copy-start(s32[2048]{0:T(1024)} %param.23) | copy-start | bytes 24580
  31.2 0.7 copy-start.10
  31.9 14.7 %copy-start.21 = (s32[2048]{0:T(1024)S(1)}, s32[2048]{0:T(1024)}, u32[]{:S(2)}) copy-start(s32[2048]{0:T(1024)} %param.22) | copy-start | bytes 24580
  32.5 16.5 %collective-permute-start.3 = (bf16[256,256]{1,0:T(8,128)(2,1)S(1)}, bf16[256,256]{1,0:T(8,128)(2,1)S(1)}, u32[]{:S(2)}, u32[]{:S(2)}) collective-permute-start(bf16[256,256]{1,0:T(8,128)(2,1)S(1)} %convolution_convert_fusion.15), channel_id=1, source_target_pairs={{1,0},{2,1},{3,2},{4,3},{5,4},{6,5},{7,6},{9,8},{10,9},{11,10},{12... | collective-permute-start | bytes 393224 | tf_op jit(solution)/shard_map/ppermute | solution.py:43
  33.8 15.2 %collective-permute-start.2 = (bf16[256,256]{1,0:T(8,128)(2,1)S(1)}, bf16[256,256]{1,0:T(8,128)(2,1)S(1)}, u32[]{:S(2)}, u32[]{:S(2)}) collective-permute-start(bf16[256,256]{1,0:T(8,128)(2,1)S(1)} %convolution_convert_fusion.15), channel_id=1, source_target_pairs={{0,1},{1,2},{2,3},{3,4},{4,5},{5,6},{6,7},{8,9},{9,10},{10,11},{11... | collective-permute-start | bytes 393224 | tf_op jit(solution)/shard_map/ppermute | solution.py:43
  36.8 12.1 %collective-permute-start.1 = (bf16[256,256]{1,0:T(8,128)(2,1)S(1)}, bf16[256,256]{1,0:T(8,128)(2,1)}, u32[]{:S(2)}, u32[]{:S(2)}) collective-permute-start(bf16[256,256]{1,0:T(8,128)(2,1)S(1)} %convolution_convert_fusion.15), channel_id=1, source_target_pairs={{8,0},{16,8},{24,16},{9,1},{17,9},{25,17},{10,2},{18,10},{26,18},{... | collective-permute-start | bytes 393224 | tf_op jit(solution)/shard_map/ppermute | solution.py:43
  38.1 10.8 %collective-permute-start = (bf16[256,256]{1,0:T(8,128)(2,1)S(1)}, bf16[256,256]{1,0:T(8,128)(2,1)}, u32[]{:S(2)}, u32[]{:S(2)}) collective-permute-start(bf16[256,256]{1,0:T(8,128)(2,1)S(1)} %convolution_convert_fusion.15), channel_id=1, source_target_pairs={{0,8},{8,16},{16,24},{1,9},{9,17},{17,25},{2,10},{10,18},{18,26},{... | collective-permute-start | bytes 393224 | tf_op jit(solution)/shard_map/ppermute | solution.py:43
  51.5 1.3 copy-start.38
  51.5 1.3 copy-start.7
  51.5 1.8 copy-start.31
  54.3 17.3 %collective-permute-start.7 = (bf16[256,256]{1,0:T(8,128)(2,1)}, bf16[256,256]{1,0:T(8,128)(2,1)}, u32[]{:S(2)}, u32[]{:S(2)}) collective-permute-start(bf16[256,256]{1,0:T(8,128)(2,1)} %convolution_convert_fusion.14), channel_id=1, source_target_pairs={{1,0},{2,1},{3,2},{4,3},{5,4},{6,5},{7,6},{9,8},{10,9},{11,10},{12... | collective-permute-start | bytes 393224 | tf_op jit(solution)/shard_map/ppermute | solution.py:43
  55.6 16.1 %collective-permute-start.6 = (bf16[256,256]{1,0:T(8,128)(2,1)}, bf16[256,256]{1,0:T(8,128)(2,1)}, u32[]{:S(2)}, u32[]{:S(2)}) collective-permute-start(bf16[256,256]{1,0:T(8,128)(2,1)} %convolution_convert_fusion.14), channel_id=1, source_target_pairs={{0,1},{1,2},{2,3},{3,4},{4,5},{5,6},{6,7},{8,9},{9,10},{10,11},{11... | collective-permute-start | bytes 393224 | tf_op jit(solution)/shard_map/ppermute | solution.py:43
  59.4 12.2 %collective-permute-start.5 = (bf16[256,256]{1,0:T(8,128)(2,1)}, bf16[256,256]{1,0:T(8,128)(2,1)}, u32[]{:S(2)}, u32[]{:S(2)}) collective-permute-start(bf16[256,256]{1,0:T(8,128)(2,1)} %convolution_convert_fusion.14), channel_id=1, source_target_pairs={{8,0},{16,8},{24,16},{9,1},{17,9},{25,17},{10,2},{18,10},{26,18},{... | collective-permute-start | bytes 393224 | tf_op jit(solution)/shard_map/ppermute | solution.py:43
  60.7 10.9 %collective-permute-start.4 = (bf16[256,256]{1,0:T(8,128)(2,1)}, bf16[256,256]{1,0:T(8,128)(2,1)}, u32[]{:S(2)}, u32[]{:S(2)}) collective-permute-start(bf16[256,256]{1,0:T(8,128)(2,1)} %convolution_convert_fusion.14), channel_id=1, source_target_pairs={{0,8},{8,16},{16,24},{1,9},{9,17},{17,25},{2,10},{10,18},{18,26},{... | collective-permute-start | bytes 393224 | tf_op jit(solution)/shard_map/ppermute | solution.py:43
  69.2 2.4 %copy-start.29 = (s32[1024]{0:T(1024)S(1)}, s32[1024]{0:T(1024)}, u32[]{:S(2)}) copy-start(s32[1024]{0:T(1024)} %copy-done.28) | copy-start | bytes 12292
  71.6 4.1 %copy-start.27 = (f32[2048]{0:T(1024)S(1)}, f32[2048]{0:T(1024)}, u32[]{:S(2)}) copy-start(f32[2048]{0:T(1024)} %copy-done.26) | copy-start | bytes 24580
  71.6 4.1 %copy-start.35 = (s32[2048]{0:T(1024)S(1)}, s32[2048]{0:T(1024)}, u32[]{:S(2)}) copy-start(s32[2048]{0:T(1024)} %param.23) | copy-start | bytes 24580
  74.3 1.4 copy-start.39
  75.7 1.9 copy-start.8
  81.9 2.7 %copy-start.41 = (bf16[2048,256]{1,0:T(8,128)(2,1)S(1)}, bf16[2048,256]{1,0:T(8,128)(2,1)}, u32[]{:S(2)}) copy-start(bf16[2048,256]{1,0:T(8,128)(2,1)} %fusion.45) | copy-start | bytes 3145732
  84.6 10.5 %copy-start.36 = (s32[2048]{0:T(1024)S(1)}, s32[2048]{0:T(1024)}, u32[]{:S(2)}) copy-start(s32[2048]{0:T(1024)} %param.23) | copy-start | bytes 24580
  85.4 12.2 %copy-start.32 = (s32[256]{0:T(256)S(1)}, s32[256]{0:T(256)}, u32[]{:S(2)}) copy-start(s32[256]{0:T(256)} %param.21) | copy-start | bytes 3076
  85.4 10.5 %collective-permute-start.8 = (bf16[256,256]{1,0:T(8,128)(2,1)S(1)}, bf16[256,256]{1,0:T(8,128)(2,1)S(1)}, u32[]{:S(2)}, u32[]{:S(2)}) collective-permute-start(bf16[256,256]{1,0:T(8,128)(2,1)S(1)} %get-tuple-element.13), channel_id=1, source_target_pairs={{8,0},{16,8},{24,16},{9,1},{17,9},{25,17},{10,2},{18,10},{26,18},{... | collective-permute-start | bytes 393224 | tf_op jit(solution)/shard_map/ppermute | solution.py:43
  86.7 9.2 %collective-permute-start.11 = (bf16[256,256]{1,0:T(8,128)(2,1)S(1)}, bf16[256,256]{1,0:T(8,128)(2,1)S(1)}, u32[]{:S(2)}, u32[]{:S(2)}) collective-permute-start(bf16[256,256]{1,0:T(8,128)(2,1)S(1)} %get-tuple-element.14), channel_id=1, source_target_pairs={{0,1},{1,2},{2,3},{3,4},{4,5},{5,6},{6,7},{8,9},{9,10},{10,11},{11... | collective-permute-start | bytes 393224 | tf_op jit(solution)/shard_map/ppermute | solution.py:43
  89.2 6.8 %collective-permute-start.10 = (bf16[256,256]{1,0:T(8,128)(2,1)S(1)}, bf16[256,256]{1,0:T(8,128)(2,1)S(1)}, u32[]{:S(2)}, u32[]{:S(2)}) collective-permute-start(bf16[256,256]{1,0:T(8,128)(2,1)S(1)} %get-tuple-element.15), channel_id=1, source_target_pairs={{1,0},{2,1},{3,2},{4,3},{5,4},{6,5},{7,6},{9,8},{10,9},{11,10},{12... | collective-permute-start | bytes 393224 | tf_op jit(solution)/shard_map/ppermute | solution.py:43
  90.5 8.1 %copy-start.14 = (bf16[512,256]{1,0:T(8,128)(2,1)S(1)}, bf16[512,256]{1,0:T(8,128)(2,1)}, u32[]{:S(2)}) copy-start(bf16[512,256]{1,0:T(8,128)(2,1)} %param.31) | copy-start | bytes 786436
  90.5 7.1 %collective-permute-start.9 = (bf16[256,256]{1,0:T(8,128)(2,1)S(1)}, bf16[256,256]{1,0:T(8,128)(2,1)S(1)}, u32[]{:S(2)}, u32[]{:S(2)}) collective-permute-start(bf16[256,256]{1,0:T(8,128)(2,1)S(1)} %get-tuple-element.16), channel_id=1, source_target_pairs={{0,8},{8,16},{16,24},{1,9},{9,17},{17,25},{2,10},{10,18},{18,26},{... | collective-permute-start | bytes 393224 | tf_op jit(solution)/shard_map/ppermute | solution.py:43
  95.9 2.9 %copy-start.16 = (bf16[512,256]{1,0:T(8,128)(2,1)}, bf16[512,256]{1,0:T(8,128)(2,1)S(1)}, u32[]{:S(2)}) copy-start(bf16[512,256]{1,0:T(8,128)(2,1)S(1)} %fusion.77) | copy-start | bytes 786436
  95.9 2.9 %copy-start.12 = (bf16[2,256,256]{2,1,0:T(8,128)(2,1)S(1)}, bf16[2,256,256]{2,1,0:T(8,128)(2,1)}, u32[]{:S(2)}) copy-start(bf16[2,256,256]{2,1,0:T(8,128)(2,1)} %param.29) | copy-start | bytes 786436
  97.9 0.7 copy-start.4
  103.4 2.7 %copy-start.40 = (bf16[2048,256]{1,0:T(8,128)(2,1)S(1)}, bf16[2048,256]{1,0:T(8,128)(2,1)}, u32[]{:S(2)}) copy-start(bf16[2048,256]{1,0:T(8,128)(2,1)} %fusion.46) | copy-start | bytes 3145732
  106.1 11.5 %copy-start.37 = (s32[2048]{0:T(1024)S(1)}, s32[2048]{0:T(1024)}, u32[]{:S(2)}) copy-start(s32[2048]{0:T(1024)} %param.23) | copy-start | bytes 24580
  106.9 13.2 %copy-start.33 = (s32[256]{0:T(256)S(1)}, s32[256]{0:T(256)}, u32[]{:S(2)}) copy-start(s32[256]{0:T(256)} %param.21) | copy-start | bytes 3076
  106.9 11.5 %collective-permute-start.12 = (bf16[256,256]{1,0:T(8,128)(2,1)S(1)}, bf16[256,256]{1,0:T(8,128)(2,1)S(1)}, u32[]{:S(2)}, u32[]{:S(2)}) collective-permute-start(bf16[256,256]{1,0:T(8,128)(2,1)S(1)} %get-tuple-element.9), channel_id=1, source_target_pairs={{8,0},{16,8},{24,16},{9,1},{17,9},{25,17},{10,2},{18,10},{26,18},{... | collective-permute-start | bytes 393224 | tf_op jit(solution)/shard_map/ppermute | solution.py:43
  108.2 10.2 %collective-permute-start.15 = (bf16[256,256]{1,0:T(8,128)(2,1)S(1)}, bf16[256,256]{1,0:T(8,128)(2,1)S(1)}, u32[]{:S(2)}, u32[]{:S(2)}) collective-permute-start(bf16[256,256]{1,0:T(8,128)(2,1)S(1)} %get-tuple-element.10), channel_id=1, source_target_pairs={{0,1},{1,2},{2,3},{3,4},{4,5},{5,6},{6,7},{8,9},{9,10},{10,11},{11... | collective-permute-start | bytes 393224 | tf_op jit(solution)/shard_map/ppermute | solution.py:43
  111.5 7.0 %collective-permute-start.14 = (bf16[256,256]{1,0:T(8,128)(2,1)S(1)}, bf16[256,256]{1,0:T(8,128)(2,1)S(1)}, u32[]{:S(2)}, u32[]{:S(2)}) collective-permute-start(bf16[256,256]{1,0:T(8,128)(2,1)S(1)} %get-tuple-element.11), channel_id=1, source_target_pairs={{1,0},{2,1},{3,2},{4,3},{5,4},{6,5},{7,6},{9,8},{10,9},{11,10},{12... | collective-permute-start | bytes 393224 | tf_op jit(solution)/shard_map/ppermute | solution.py:43
  112.8 7.7 %copy-start.3 = (bf16[2,256,256]{2,1,0:T(8,128)(2,1)S(1)}, bf16[2,256,256]{2,1,0:T(8,128)(2,1)}, u32[]{:S(2)}) copy-start(bf16[2,256,256]{2,1,0:T(8,128)(2,1)} %param.28) | copy-start | bytes 786436
  112.8 7.4 %collective-permute-start.13 = (bf16[256,256]{1,0:T(8,128)(2,1)S(1)}, bf16[256,256]{1,0:T(8,128)(2,1)S(1)}, u32[]{:S(2)}, u32[]{:S(2)}) collective-permute-start(bf16[256,256]{1,0:T(8,128)(2,1)S(1)} %get-tuple-element.12), channel_id=1, source_target_pairs={{0,8},{8,16},{16,24},{1,9},{9,17},{17,25},{2,10},{10,18},{18,26},{... | collective-permute-start | bytes 393224 | tf_op jit(solution)/shard_map/ppermute | solution.py:43
  118.4 3.3 %copy-start.18 = (bf16[512,256]{1,0:T(8,128)(2,1)}, bf16[512,256]{1,0:T(8,128)(2,1)S(1)}, u32[]{:S(2)}) copy-start(bf16[512,256]{1,0:T(8,128)(2,1)S(1)} %fusion.78) | copy-start | bytes 786436
  118.4 2.3 %copy-start.13 = (bf16[2,256,256]{2,1,0:T(8,128)(2,1)S(1)}, bf16[2,256,256]{2,1,0:T(8,128)(2,1)}, u32[]{:S(2)}) copy-start(bf16[2,256,256]{2,1,0:T(8,128)(2,1)} %param.29) | copy-start | bytes 786436
  118.4 5.2 %copy-start.25 = (s32[2048]{0:T(1024)S(1)}, s32[2048]{0:T(1024)}, u32[]{:S(2)}) copy-start(s32[2048]{0:T(1024)} %copy-done.24) | copy-start | bytes 24580
  120.4 1.3 copy-start.5
  127.0 5.8 %copy-start.19 = (bf16[512,256]{1,0:T(8,128)(2,1)S(1)}, bf16[512,256]{1,0:T(8,128)(2,1)}, u32[]{:S(2)}) copy-start(bf16[512,256]{1,0:T(8,128)(2,1)} %copy-done.18) | copy-start | bytes 786436
  127.0 6.7 %copy-start.17 = (bf16[512,256]{1,0:T(8,128)(2,1)S(1)}, bf16[512,256]{1,0:T(8,128)(2,1)}, u32[]{:S(2)}) copy-start(bf16[512,256]{1,0:T(8,128)(2,1)} %copy-done.16) | copy-start | bytes 786436
  127.0 8.6 %copy-start.11 = (bf16[512,256]{1,0:T(8,128)(2,1)S(1)}, bf16[512,256]{1,0:T(8,128)(2,1)}, u32[]{:S(2)}) copy-start(bf16[512,256]{1,0:T(8,128)(2,1)} %fusion.76) | copy-start | bytes 786436
  127.0 8.6 %copy-start.15 = (bf16[512,256]{1,0:T(8,128)(2,1)S(1)}, bf16[512,256]{1,0:T(8,128)(2,1)}, u32[]{:S(2)}) copy-start(bf16[512,256]{1,0:T(8,128)(2,1)} %param.31) | copy-start | bytes 786436
  175.3 4.9 %copy-start.9 = (bf16[2,256,256]{2,1,0:T(8,128)(2,1)S(1)}, bf16[2,256,256]{2,1,0:T(8,128)(2,1)}, u32[]{:S(2)}) copy-start(bf16[2,256,256]{2,1,0:T(8,128)(2,1)} %param.30) | copy-start | bytes 786436
  176.6 29.8 %all-to-all-start.2 = ((bf16[32,64,256]{2,1,0:T(8,128)(2,1)}), bf16[32,64,256]{2,1,0:T(8,128)(2,1)S(1)}, u32[]{:S(2)}, u32[]{:S(2)}) async-start(bf16[32,64,256]{2,1,0:T(8,128)(2,1)} %broadcast_in_dim.2), calls=%async_computation.2 | async-start | bytes 2097152 | tf_op jit(solution)/shard_map/all_to_all | solution.py:48
where the time goes:
time: 211 us; the launch traced here: 209 us
  matrix products  58.3 us (28%)
  starting transfers between devices  53.7 us (25%)
  waiting for transfers between devices  45.3 us (21%)
  blocking collectives  37.5 us (18%)
  local copies, waits for them, and re-layouts  8.95 us (4%)
  other arithmetic  3.97 us (2%)
    ppermute x16, starting transfers between devices, passed_along(): return lax.ppermute(shard, axis, pairs)  42.8 us
    all_to_all x2, waiting for transfers between devices, exchange(): return lax.all_to_all(shard, axes, split_axis=0, concat_axis=0, tiled=True)  42 us
    dot_general x27, matrix products, mm(): return jnp.dot(left_side, right_side, preferred_element_type=F32)  41.8 us
    all_to_all x1, blocking collectives, exchange(): return lax.all_to_all(shard, axes, split_axis=0, concat_axis=0, tiled=True)  37.5 us
    dot_general x8, matrix products, t_mm(): lax.dot_general(left_side, right_side, (((0,), (0,)), ((), ())), preferre...  12.9 us
    all_to_all x2, starting transfers between devices, exchange(): return lax.all_to_all(shard, axes, split_axis=0, concat_axis=0, tiled=True)  10.9 us
  transfers between devices with their start and end apart: 18, of which 4 were waited for; matrix products, arithmetic and copies ran while one was open for 7% of the time, Pallas kernels for 0%

commit v1 on v0

v1 whole, which is shorter than its diff:
```python
import functools

import jax
import jax.numpy as jnp
from jax import lax
from jax.experimental import pallas as pl
from jax.experimental.pallas import tpu as pltpu
from jax.sharding import PartitionSpec as P

AXES = ("grid", "dom")
BF = jnp.bfloat16
F32 = jnp.float32
LANES = 128
TILE = 256
CHUNK = 512


def mm(left_side, right_side):
    return jnp.dot(left_side, right_side, preferred_element_type=F32)


def mm_t(left_side, right_side):
    return lax.dot_general(
        left_side, right_side, (((1,), (1,)), ((), ())), preferred_element_type=F32
    )


def t_mm(left_side, right_side):
    return lax.dot_general(
        left_side, right_side, (((0,), (0,)), ((), ())), preferred_element_type=F32
    )


def put_picks(out_ref, start, indices, count):
    rows = lax.broadcasted_iota(jnp.int32, (TILE, indices.shape[1]), 0).astype(F32).astype(BF)
    for base in range(0, count, TILE):
        shifted = (indices - float(base)).astype(BF)
        block = jnp.where(rows == shifted, jnp.ones((), BF), jnp.zeros((), BF))
        out_ref[start + base : start + base + TILE, :] = block


def sigmoid(values):
    return 0.5 * jnp.tanh(0.5 * values) + 0.5


def call(body, outs, scratch, name):
    vmem = pl.BlockSpec(memory_space=pltpu.VMEM)

    def run(*args):
        return pl.pallas_call(
            body,
            out_shape=tuple(jax.ShapeDtypeStruct(shape, dtype) for shape, dtype in outs),
            in_specs=[vmem] * len(args),
            out_specs=tuple(vmem for _ in outs),
            scratch_shapes=scratch,
            name=name,
        )(*args)

    return run


def chunks(total, size, body):
    if total == size:
        body(0)
        return

    def step(i, carry):
        body(pl.multiple_of(i * size, size))
        return carry

    lax.fori_loop(0, total // size, step, 0)


def pack_body(bucket, cols_ref, slot_ref, live_ref, weight_ref, out_ref):
    peers = out_ref.shape[0]
    per_row = LANES // bucket
    slot = slot_ref[...].astype(F32)
    high = jnp.floor(slot * (1.0 / 256.0))
    low = slot - 256.0 * high
    scale = weight_ref[...] * live_ref[...].astype(F32)
    scale_high = scale.astype(BF)
    scale_low = (scale - scale_high.astype(F32)).astype(BF)
    fields = [high.astype(BF), low.astype(BF), scale_high, scale_low]
    for peer in range(peers):
        out_ref[peer, :bucket, :] = cols_ref[peer * bucket : (peer + 1) * bucket, :]
        row = peer // per_row
        extra = jnp.concatenate([field[row : row + 1, :] for field in fields], 0)
        out_ref[peer, bucket : bucket + 4, :] = extra


def node_tables(state, state_ref, table_ref, src_t, dst_t, rim_ref, rim_picks):
    nodes, width = state.shape
    state_ref[...] = state.astype(BF)
    held = state_ref[...]
    table_ref[:, :nodes] = mm_t(src_t, held).astype(BF)
    table_ref[:, nodes:] = mm_t(dst_t, held).astype(BF)
    rim_ref[...] = t_mm(rim_picks[...], held).astype(BF)


def encode_body(
    bucket,
    packed_ref,
    rows_ref,
    enc_in_t_ref,
    enc_out_ref,
    static_ref,
    src_t_ref,
    dst_t_ref,
    bound_ref,
    pooled_ref,
    slope_ref,
    state_ref,
    table_ref,
    rim_ref,
    picks_ref,
    rim_picks,
    acc_ref,
):
    nodes = static_ref.shape[0]
    cols = rows_ref.shape[1]
    chunk = picks_ref.shape[1]
    peers_step = chunk // bucket
    acc_ref[...] = jnp.zeros_like(acc_ref)

    def step(start):
        first = start // bucket
        got = packed_ref[pl.ds(first, peers_step), :bucket, :].reshape(chunk, packed_ref.shape[2])
        pre = mm_t(enc_in_t_ref[...], got)
        slot = rows_ref[0:1, pl.ds(start, chunk)]
        scale = rows_ref[1:2, pl.ds(start, chunk)]
        sig = sigmoid(pre)
        act = (pre * sig * scale).astype(BF)
        slope_ref[:, pl.ds(start, chunk)] = (sig * (1.0 + pre * (1.0 - sig)) * scale).astype(BF)
        put_picks(picks_ref, 0, slot, nodes)
        acc_ref[...] += mm_t(picks_ref[...], act)

    chunks(cols, chunk, step)
    pooled_ref[...] = acc_ref[...].astype(BF)
    put_picks(rim_picks, 0, bound_ref[0:1, :], nodes)
    state = static_ref[...].astype(F32) + mm(pooled_ref[...], enc_out_ref[...])
    node_tables(state, state_ref, table_ref, src_t_ref[...], dst_t_ref[...], rim_ref, rim_picks)


def fill_table(full_ref, table_ref, src_t_ref, rims, flags_ref):
    width, both = table_ref.shape
    nodes = both // 2
    rim = rims[0].shape[0]
    full_ref[:, :nodes] = table_ref[:, :nodes]
    for side, rim_rows in enumerate(rims):
        start = nodes + side * rim
        part = mm_t(src_t_ref[...], rim_rows[...]) * flags_ref[side]
        full_ref[:, start : start + rim] = part.astype(BF)
    full_ref[:, nodes + 4 * rim :] = table_ref[:, nodes:]


def fill_picks(picks_ref, rows_ref, start, nodes, rim):
    chunk = picks_ref.shape[1]
    put_picks(picks_ref, 0, rows_ref[0:1, pl.ds(start, chunk)], nodes + 4 * rim)
    put_picks(picks_ref, nodes + 4 * rim, rows_ref[1:2, pl.ds(start, chunk)], nodes)


def forward_body(
    flags_ref,
    table_ref,
    up_ref,
    down_ref,
    left_ref,
    right_ref,
    rows_ref,
    state_ref,
    src_t_ref,
    msg_ref,
    next_src_t_ref,
    next_dst_t_ref,
    bound_ref,
    slope_ref,
    act_ref,
    next_state_ref,
    next_table_ref,
    rim_ref,
    full_ref,
    picks_ref,
    rim_picks,
    acc_ref,
):
    nodes = state_ref.shape[0]
    rim = up_ref.shape[0]
    ext = nodes + 4 * rim
    edges = rows_ref.shape[1]
    chunk = picks_ref.shape[1]
    fill_table(full_ref, table_ref, src_t_ref, (up_ref, down_ref, left_ref, right_ref), flags_ref)
    acc_ref[...] = jnp.zeros_like(acc_ref)

    def step(start):
        fill_picks(picks_ref, rows_ref, start, nodes, rim)
        pre = mm(full_ref[...], picks_ref[...])
        scale = rows_ref[2:3, pl.ds(start, chunk)]
        sig = sigmoid(pre)
        act = (pre * sig * scale).astype(BF)
        slope_ref[:, pl.ds(start, chunk)] = (sig * (1.0 + pre * (1.0 - sig)) * scale).astype(BF)
        acc_ref[...] += mm_t(picks_ref[ext:, :], act)

    chunks(edges, chunk, step)
    act_ref[...] = acc_ref[...].astype(BF)
    put_picks(rim_picks, 0, bound_ref[0:1, :], nodes)
    state = state_ref[...].astype(F32) + mm(act_ref[...], msg_ref[...])
    node_tables(
        state, next_state_ref, next_table_ref, next_src_t_ref[...], next_dst_t_ref[...], rim_ref, rim_picks
    )


def turn_body(
    flags_ref,
    table_ref,
    up_ref,
    down_ref,
    left_ref,
    right_ref,
    rows_ref,
    src_t_ref,
    msg_ref,
    grad_ref,
    act_ref,
    own_ref,
    rims_ref,
    full_ref,
    picks_ref,
    acc_ref,
    edge_acc_ref,
):
    nodes = grad_ref.shape[0]
    rim = up_ref.shape[0]
    ext = nodes + 4 * rim
    edges = rows_ref.shape[1]
    chunk = picks_ref.shape[1]
    fill_table(full_ref, table_ref, src_t_ref, (up_ref, down_ref, left_ref, right_ref), flags_ref)
    acc_ref[...] = jnp.zeros_like(acc_ref)
    edge_acc_ref[...] = jnp.zeros_like(edge_acc_ref)
    back = mm_t(msg_ref[...], grad_ref[...]).astype(BF)

    def step(start):
        fill_picks(picks_ref, rows_ref, start, nodes, rim)
        pre = mm(full_ref[...], picks_ref[...])
        scale = rows_ref[2:3, pl.ds(start, chunk)]
        sig = sigmoid(pre)
        act = (pre * sig * scale).astype(BF)
        acc_ref[...] += mm_t(picks_ref[ext:, :], act)
        slope = sig * (1.0 + pre * (1.0 - sig)) * scale
        grad_pre = (mm(back, picks_ref[ext:, :]) * slope).astype(BF)
        edge_acc_ref[...] += mm_t(picks_ref[...], grad_pre)

    chunks(edges, chunk, step)
    act_ref[...] = acc_ref[...].astype(BF)
    put_sums(edge_acc_ref, own_ref, rims_ref, nodes, rim)


def put_sums(edge_acc_ref, own_ref, rims_ref, nodes, rim):
    ext = nodes + 4 * rim
    own_ref[:nodes, :] = edge_acc_ref[:nodes, :].astype(BF)
    own_ref[nodes:, :] = edge_acc_ref[ext:, :].astype(BF)
    for side in range(4):
        first = nodes + side * rim
        rims_ref[side] = edge_acc_ref[first : first + rim, :].astype(BF)


def returned_sum(flags_ref, returned):
    total = returned[0][...].astype(F32) * flags_ref[4]
    for side in range(1, 4):
        total += returned[side][...].astype(F32) * flags_ref[4 + side]
    return total.astype(BF)


def merged_grad(grad, flags_ref, returned, own_ref, bound_ref, src_ref, dst_ref, rim_picks):
    nodes = grad.shape[0]
    put_picks(rim_picks, 0, bound_ref[0:1, :], nodes)
    back = mm(rim_picks[...], returned_sum(flags_ref, returned))
    grad_src = (own_ref[:nodes, :].astype(F32) + back).astype(BF)
    return grad + mm_t(grad_src, src_ref[...]) + mm_t(own_ref[nodes:, :], dst_ref[...])


def backward_body(
    flags_ref,
    up_ref,
    down_ref,
    left_ref,
    right_ref,
    own_ref,
    bound_ref,
    src_ref,
    dst_ref,
    grad_ref,
    rows_ref,
    msg_ref,
    slope_ref,
    next_grad_ref,
    next_own_ref,
    rims_ref,
    picks_ref,
    rim_picks,
    edge_acc_ref,
):
    nodes = grad_ref.shape[0]
    rim = up_ref.shape[0]
    ext = nodes + 4 * rim
    edges = rows_ref.shape[1]
    chunk = picks_ref.shape[1]
    returned = (up_ref, down_ref, left_ref, right_ref)
    grad = merged_grad(
        grad_ref[...].astype(F32), flags_ref, returned, own_ref, bound_ref, src_ref, dst_ref, rim_picks
    )
    next_grad_ref[...] = grad
    back = mm_t(msg_ref[...], grad.astype(BF)).astype(BF)
    edge_acc_ref[...] = jnp.zeros_like(edge_acc_ref)

    def step(start):
        fill_picks(picks_ref, rows_ref, start, nodes, rim)
        slope = slope_ref[:, pl.ds(start, chunk)].astype(F32)
        grad_pre = (mm(back, picks_ref[ext:, :]) * slope).astype(BF)
        edge_acc_ref[...] += mm_t(picks_ref[...], grad_pre)

    chunks(edges, chunk, step)
    put_sums(edge_acc_ref, next_own_ref, rims_ref, nodes, rim)


def terms_body(
    flags_ref, up_ref, down_ref, left_ref, right_ref, state_ref, own_ref, rims_ref, act_ref, grad_ref, out_ref
):
    nodes, width = state_ref.shape
    state = state_ref[...]
    src_term = t_mm(state, own_ref[:nodes, :])
    for side, rim_rows in enumerate((up_ref, down_ref, left_ref, right_ref)):
        src_term += t_mm(rim_rows[...], rims_ref[side]) * flags_ref[side]
    out_ref[:width, :] = src_term.astype(BF)
    out_ref[width : 2 * width, :] = t_mm(state, own_ref[nodes:, :]).astype(BF)
    out_ref[2 * width : 3 * width, :] = t_mm(act_ref[...], grad_ref[...].astype(BF)).astype(BF)
    if out_ref.shape[0] > 3 * width:
        out_ref[3 * width :, :] = jnp.zeros((out_ref.shape[0] - 3 * width, width), BF)


def last_body(
    bucket,
    flags_ref,
    up_ref,
    down_ref,
    left_ref,
    right_ref,
    own_ref,
    bound_ref,
    src_ref,
    dst_ref,
    grad_ref,
    rows_ref,
    packed_ref,
    enc_out_ref,
    pooled_ref,
    slope_ref,
    out_ref,
    picks_ref,
    rim_picks,
    acc_ref,
):
    nodes, width = grad_ref.shape
    cols = rows_ref.shape[1]
    chunk = picks_ref.shape[1]
    fin = packed_ref.shape[2]
    peers_step = chunk // bucket
    returned = (up_ref, down_ref, left_ref, right_ref)
    grad = merged_grad(
        grad_ref[...].astype(F32), flags_ref, returned, own_ref, bound_ref, src_ref, dst_ref, rim_picks
    ).astype(BF)
    back = mm_t(enc_out_ref[...], grad).astype(BF)
    acc_ref[...] = jnp.zeros_like(acc_ref)

    def step(start):
        first = start // bucket
        got = packed_ref[pl.ds(first, peers_step), :bucket, :].reshape(chunk, fin)
        put_picks(picks_ref, 0, rows_ref[0:1, pl.ds(start, chunk)], nodes)
        slope = slope_ref[:, pl.ds(start, chunk)].astype(F32)
        grad_pre = (mm(back, picks_ref[...]) * slope).astype(BF)
        acc_ref[...] += mm(grad_pre, got)

    chunks(cols, chunk, step)
    out_ref[:fin, :] = acc_ref[...].T.astype(BF)
    out_ref[fin : fin + width, :] = t_mm(pooled_ref[...], grad).astype(BF)
    if out_ref.shape[0] > fin + width:
        out_ref[fin + width :, :] = jnp.zeros((out_ref.shape[0] - fin - width, width), BF)


def state_body(state_ref, act_ref, msg_ref, out_ref):
    out_ref[...] = (state_ref[...].astype(F32) + mm(act_ref[...], msg_ref[...])).astype(BF)


def share_body(parts_ref, out_ref):
    count = parts_ref.shape[0]
    total = jnp.sum(parts_ref[...].astype(F32), 0).astype(BF)
    for peer in range(count):
        out_ref[peer] = total


def exchange(shard):
    return lax.all_to_all(shard, AXES, split_axis=0, concat_axis=0, tiled=True)


def rows_for(total, count):
    return -(-total // (8 * count)) * 8 * count


def summed(rows):
    count = lax.axis_size(AXES)
    total, width = rows.shape
    share = total // count
    parts = exchange(rows.reshape(count, share, width))
    (spread,) = call(share_body, [((count, share, width), BF)], [], "share")(parts)
    return exchange(spread).reshape(total, width)


def turned(shard, axis, by):
    count = lax.axis_size(axis)
    return lax.ppermute(shard, axis, [(i, (i + by) % count) for i in range(count)])


def from_neighbours(rim_rows):
    return (
        turned(rim_rows, "grid", 1),
        turned(rim_rows, "grid", -1),
        turned(rim_rows, "dom", 1),
        turned(rim_rows, "dom", -1),
    )


def to_neighbours(rims):
    return (
        turned(rims[0], "grid", -1),
        turned(rims[1], "grid", 1),
        turned(rims[2], "dom", -1),
        turned(rims[3], "dom", 1),
    )


def per_device(
    columns,
    column_live,
    col_weight,
    col_slot,
    node_static,
    boundary_idx,
    edge_src,
    edge_dst,
    edge_live,
    edge_weight,
    enc_in,
    enc_out,
    src_proj,
    dst_proj,
    msg_proj,
    node_cotangent,
):
    peers = lax.axis_size(AXES)
    cols, fin = columns.shape
    nodes, width = node_static.shape
    rim = boundary_idx.shape[0]
    edges = edge_src.shape[0]
    ext = nodes + 4 * rim
    bucket = cols // peers
    chunk = CHUNK

    lanes = (cols // LANES, LANES)
    (packed,) = call(
        functools.partial(pack_body, bucket), [((peers, bucket + 4, fin), BF)], [], "pack"
    )(columns, col_slot.reshape(lanes), column_live.reshape(lanes), col_weight.reshape(lanes))
    packed = exchange(packed)

    grid_at, grid_count = lax.axis_index("grid"), lax.axis_size("grid")
    dom_at, dom_count = lax.axis_index("dom"), lax.axis_size("dom")
    present = jnp.stack(
        [grid_at > 0, grid_at < grid_count - 1, dom_at > 0, dom_at < dom_count - 1]
    ).astype(F32)
    flags = jnp.concatenate([present, present[jnp.array([1, 0, 3, 2])]])
    edge_scale = edge_weight * edge_live.astype(F32)
    edge_rows = jnp.stack([edge_src.astype(F32), edge_dst.astype(F32), edge_scale])
    bound = boundary_idx.astype(F32)[None]
    enc_in_t = enc_in.T
    src_t = src_proj.transpose(0, 2, 1)
    dst_t = dst_proj.transpose(0, 2, 1)

    at = (grid_at * dom_count + dom_at) % (LANES // bucket)
    extra = lax.dynamic_slice_in_dim(packed[:, bucket : bucket + 4], at * bucket, bucket, 2)
    extra = extra.astype(F32).transpose(1, 0, 2).reshape(4, cols)
    col_rows = jnp.stack([extra[0] * 256.0 + extra[1], extra[2] + extra[3]])

    picks = pltpu.VMEM((ext + nodes, chunk), BF)
    slot_picks = pltpu.VMEM((nodes, chunk), BF)
    rim_picks = pltpu.VMEM((nodes, rim), BF)
    node_acc = pltpu.VMEM((nodes, width), F32)
    edge_acc = pltpu.VMEM((ext + nodes, width), F32)
    full = pltpu.VMEM((width, ext + nodes), BF)
    node_shape = ((nodes, width), BF)
    tables = [node_shape, ((width, 2 * nodes), BF), ((rim, width), BF)]
    slope_shape = ((width, edges), BF)
    sums = [((2 * nodes, width), BF), ((4, rim, width), BF)]
    smem = pl.BlockSpec(memory_space=pltpu.SMEM)

    def flagged(body, outs, scratch, name):
        vmem = pl.BlockSpec(memory_space=pltpu.VMEM)

        def run(*args):
            return pl.pallas_call(
                body,
                out_shape=tuple(jax.ShapeDtypeStruct(shape, dtype) for shape, dtype in outs),
                in_specs=[smem] + [vmem] * (len(args) - 1),
                out_specs=tuple(vmem for _ in outs),
                scratch_shapes=scratch,
                name=name,
            )(*args)

        return run

    pooled, col_slope, state0, table0, rim0 = call(
        functools.partial(encode_body, bucket),
        [node_shape, ((width, cols), BF)] + tables,
        [slot_picks, rim_picks, node_acc],
        "encode",
    )(packed, col_rows, enc_in_t, enc_out, node_static, src_t[0], dst_t[0], bound)

    rims0 = from_neighbours(rim0)
    slope0, act0, state1, table1, rim1 = flagged(
        forward_body, [slope_shape, node_shape] + tables, [full, picks, rim_picks, node_acc], "forward"
    )(flags, table0, *rims0, edge_rows, state0, src_t[0], msg_proj[0], src_t[1], dst_t[1], bound)

    rims1 = from_neighbours(rim1)
    act1, own1, sends1 = flagged(
        turn_body, [node_shape] + sums, [full, picks, node_acc, edge_acc], "turn"
    )(flags, table1, *rims1, edge_rows, src_t[1], msg_proj[1], node_cotangent)

    back1 = to_neighbours(sends1)
    (node_out,) = call(state_body, [node_shape], [], "state")(state1, act1, msg_proj[1])
    layer_rows = rows_for(3 * width, peers)
    (terms1,) = flagged(terms_body, [((layer_rows, width), BF)], [], "terms")(
        flags, *rims1, state1, own1, sends1, act1, node_cotangent
    )
    grad1, own0, sends0 = flagged(
        backward_body, [((nodes, width), F32)] + sums, [picks, rim_picks, edge_acc], "backward"
    )(flags, *back1, own1, bound, src_proj[1], dst_proj[1], node_cotangent, edge_rows, msg_proj[0], slope0)

    back0 = to_neighbours(sends0)
    (terms0,) = flagged(terms_body, [((layer_rows, width), BF)], [], "terms")(
        flags, *rims0, state0, own0, sends0, act0, grad1
    )
    enc_rows = rows_for(fin + enc_out.shape[0], peers)
    (terms_enc,) = flagged(
        functools.partial(last_body, bucket),
        [((enc_rows, width), BF)],
        [slot_picks, rim_picks, pltpu.VMEM((width, fin), F32)],
        "last",
    )(
        flags,
        *back0,
        own0,
        bound,
        src_proj[0],
        dst_proj[0],
        grad1,
        col_rows,
        packed,
        enc_out,
        pooled,
        col_slope,
    )

    whole1 = summed(terms1).astype(F32)
    whole0 = summed(terms0).astype(F32)
    whole_enc = summed(terms_enc).astype(F32)
    layers = [whole[: 3 * width].reshape(3, width, width) for whole in (whole0, whole1)]
    grads = [jnp.stack([layer[entry] for layer in layers], 0) for entry in range(3)]
    return (node_out, whole_enc[:fin], whole_enc[fin : fin + enc_out.shape[0]], grads[0], grads[1], grads[2])


def solution(mesh):
    rows = P(AXES, None)
    flat = P(AXES)
    placed = (rows, flat, flat, flat, rows, flat, flat, flat, flat, flat, P(), P(), P(), P(), P(), rows)
    return jax.shard_map(
        per_device,
        mesh=mesh,
        in_specs=placed,
        out_specs=(rows, P(), P(), P(), P(), P()),
        check_vma=False,
    )
```

time: 211 us -> 202 us (0.957)
  matrix products: 58.3 us -> 0 us
  Pallas kernels: 0 us -> 52.1 us
  waiting for transfers between devices: 45.3 us -> 86.2 us
  blocking collectives: 37.5 us -> 0 us
  starting transfers between devices: 53.7 us -> 44.9 us
  local copies, waits for them, and re-layouts: 8.95 us -> 11.9 us
    dot_general x40 -> x0, matrix products: 58.3 us -> none  [the longest x27 41.8 us: mm(): return jnp.dot(left_side, right_side, preferred_element_type=F32)]
    pallas_call x0 -> x12, Pallas kernels: none -> 52.1 us  [run(): pl.pallas_call(body, out_shape=tuple((jax.ShapeDtypeStruct(shape, dtype)...]
    all_to_all x1 -> x0, blocking collectives: 37.5 us -> none  [exchange(): return lax.all_to_all(shard, axes, split_axis=0, concat_axis=0, tiled=True)]
    ppermute x16, starting transfers between devices: 42.8 us -> 19.7 us  [turned(): lax.ppermute(shard, axis, [(i, (i + by) % count) for i in range(count)])]
    ppermute x16, waiting for transfers between devices: 3.32 us -> 26 us  [turned(): lax.ppermute(shard, axis, [(i, (i + by) % count) for i in range(count)])]
    all_to_all x2 -> x7, waiting for transfers between devices: 42 us -> 60.2 us  [exchange(): return lax.all_to_all(shard, AXES, split_axis=0, concat_axis=0, tiled=True)]
    all_to_all x2 -> x7, starting transfers between devices: 10.9 us -> 25.2 us  [exchange(): return lax.all_to_all(shard, AXES, split_axis=0, concat_axis=0, tiled=True)]
    another operation x1 -> x5, other arithmetic: 0.01 us -> 3.73 us  [the longest x3 2.48 us: per_device(): jnp.stack([layer[entry] for layer in layers], 0)]
  transfers between devices with their start and end apart: 18 -> 23, of which waited for: 4 -> 17; matrix products, arithmetic and copies ran while one was open for 7% -> 4% of each run, Pallas kernels for 0% -> 12%
where the time goes in v1:
time: 202 us; the launch traced here: 201 us
  waiting for transfers between devices  86.2 us (43%)
  Pallas kernels  52.1 us (26%)
  starting transfers between devices  44.9 us (22%)
  local copies, waits for them, and re-layouts  11.9 us (6%)
  other arithmetic  5.41 us (3%)
    all_to_all x7, waiting for transfers between devices, exchange(): return lax.all_to_all(shard, AXES, split_axis=0, concat_axis=0, tiled=True)  60.2 us
    pallas_call x12, Pallas kernels, run(): pl.pallas_call(body, out_shape=tuple((jax.ShapeDtypeStruct(shape, dtype)...  52.1 us
    ppermute x16, waiting for transfers between devices, turned(): lax.ppermute(shard, axis, [(i, (i + by) % count) for i in range(count)])  26 us
    all_to_all x7, starting transfers between devices, exchange(): return lax.all_to_all(shard, AXES, split_axis=0, concat_axis=0, tiled=True)  25.2 us
    ppermute x16, starting transfers between devices, turned(): lax.ppermute(shard, axis, [(i, (i + by) % count) for i in range(count)])  19.7 us
    unnamed x65, local copies, waits for them, and re-layouts  6.04 us
  transfers between devices with their start and end apart: 23, of which 17 were waited for; matrix products, arithmetic and copies ran while one was open for 4% of the time, Pallas kernels for 12%

profile of v1, /device:TPU:0, one launch (start us, length us, event | category | flops | bytes accessed | tf_op | source)
XLA Modules:
  0.0 201.4 jit_solution(5076031917810980645)
XLA Ops:
  0.6 1.9 pack.1
  2.6 7.3 %all-to-all-start = ((bf16[32,68,128]{2,1,0:T(8,128)(2,1)}), bf16[32,68,128]{2,1,0:T(8,128)(2,1)S(1)}, u32[]{:S(2)}, u32[]{:S(2)}) async-start(bf16[32,68,128]{2,1,0:T(8,128)(2,1)} %pack.1), calls=%async_computation | async-start | bytes 1179648 | tf_op jit(solution)/shard_map/all_to_all | solution.py:401
  10.8 0.7 copy.26
  11.6 0.8 copy-done.5
  12.6 0.6 copy-done.30
  13.9 0.8 slice_bitcast_fusion.22
  14.7 0.8 slice_bitcast_fusion.6
  15.5 11.3 %all-to-all-done.packed_ref = bf16[32,68,128]{2,1,0:T(8,128)(2,1)S(1)} async-done(((bf16[32,68,128]{2,1,0:T(8,128)(2,1)}), bf16[32,68,128]{2,1,0:T(8,128)(2,1)S(1)}, u32[]{:S(2)}, u32[]{:S(2)}) %all-to-all-start) | async-done | bytes 557088 | tf_op jit(solution)/shard_map/all_to_all | solution.py:401
  27.7 5.4 %encode.1 = (bf16[512,256]{1,0:T(8,128)(2,1)}, bf16[256,2048]{1,0:T(8,128)(2,1)}, bf16[512,256]{1,0:T(8,128)(2,1)}, bf16[256,1024]{1,0:T(8,128)(2,1)}, bf16[256,256]{1,0:T(8,128)(2,1)}) custom-call(bf16[32,68,128]{2,1,0:T(8,128)(2,1)} %copy-done, f32[2,2048]{1,0:T(2,128)} %pad_maximum_fusion.4.rows_ref, bf16[256,128]{1,0:T(8,128)(2,1)} %bitcast.80, ...), custom_call_target="tpu_custom_call" | custom-call | tf_op jit(solution)/shard_map/encode/pallas_call | solution.py:50
  33.1 1.2 collective-permute-start.3
  34.3 1.8 collective-permute-start.1
  36.4 0.6 gather_fusion
  37.0 0.6 pad_maximum_fusion.5.flags_ref
  37.7 0.7 collective-permute-done.3.right_ref
  38.4 1.4 collective-permute-done.2.left_ref
  39.8 0.7 collective-permute-done.1.down_ref
  40.5 3.0 %collective-permute-done.up_ref = bf16[256,256]{1,0:T(8,128)(2,1)S(1)} collective-permute-done((bf16[256,256]{1,0:T(8,128)(2,1)}, bf16[256,256]{1,0:T(8,128)(2,1)S(1)}, u32[]{:S(2)}, u32[]{:S(2)}) %collective-permute-start) | collective-permute-done | bytes 131104 | tf_op jit(solution)/shard_map/ppermute | solution.py:419
  43.5 0.6 copy-done.10
  44.1 7.8 %forward.1 = (bf16[256,2048]{1,0:T(8,128)(2,1)}, bf16[512,256]{1,0:T(8,128)(2,1)}, bf16[512,256]{1,0:T(8,128)(2,1)}, bf16[256,1024]{1,0:T(8,128)(2,1)}, bf16[256,256]{1,0:T(8,128)(2,1)}) custom-call(f32[8]{0:T(128)} %pad_maximum_fusion.5.flags_ref, bf16[256,1024]{1,0:T(8,128)(2,1)} %get-tuple-element.22.table_ref, bf16[256,256]{1,0:T(8,128)(2,1)} %copy-done.10, ...), custom_call_target="tpu_custom_call" | custom-call | tf_op jit(solution)/shard_map/forward/pallas_call | solution.py:507
  51.9 1.3 collective-permute-start.7
  53.3 1.2 collective-permute-start.5
  54.4 0.9 collective-permute-start.4
  55.3 1.1 collective-permute-done.7.right_ref
  56.4 2.4 %collective-permute-done.6.left_ref = bf16[256,256]{1,0:T(8,128)(2,1)S(1)} collective-permute-done((bf16[256,256]{1,0:T(8,128)(2,1)}, bf16[256,256]{1,0:T(8,128)(2,1)S(1)}, u32[]{:S(2)}, u32[]{:S(2)}) %collective-permute-start.6) | collective-permute-done | bytes 131104 | tf_op jit(solution)/shard_map/ppermute | solution.py:419
  58.8 4.3 %collective-permute-done.4.up_ref = bf16[256,256]{1,0:T(8,128)(2,1)S(1)} collective-permute-done((bf16[256,256]{1,0:T(8,128)(2,1)}, bf16[256,256]{1,0:T(8,128)(2,1)S(1)}, u32[]{:S(2)}, u32[]{:S(2)}) %collective-permute-start.4) | collective-permute-done | bytes 131104 | tf_op jit(solution)/shard_map/ppermute | solution.py:419
  63.1 0.6 copy-done.14
  63.7 10.1 %turn.1 = (bf16[512,256]{1,0:T(8,128)(2,1)}, bf16[1024,256]{1,0:T(8,128)(2,1)}, bf16[4,256,256]{2,1,0:T(8,128)(2,1)}) custom-call(f32[8]{0:T(128)} %pad_maximum_fusion.5.flags_ref, bf16[256,1024]{1,0:T(8,128)(2,1)} %get-tuple-element.26.table_ref, bf16[256,256]{1,0:T(8,128)(2,1)} %copy-done.14, bf16[256,256]{1,0:T(8,128)(2,1)} %copy-done.13, ...), custom_call_target="tpu_custom_call" | custom-call | tf_op jit(solution)/shard_map/turn/pallas_call | solution.py:507
  73.8 2.9 %terms.3 = bf16[768,256]{1,0:T(8,128)(2,1)} custom-call(f32[8]{0:T(128)} %pad_maximum_fusion.5.flags_ref, bf16[256,256]{1,0:T(8,128)(2,1)} %copy-done.14, bf16[256,256]{1,0:T(8,128)(2,1)} %copy-done.13, bf16[256,256]{1,0:T(8,128)(2,1)} %copy-done.12, bf16[256,256]{1,0:T(8,128)(2,1)} %copy-done.11, bf16[512,256]{1,0:T(8,128)(2,1)} %get-tuple-element.25.state_ref, ...), custom_call_target="tpu_custom_call" | custom-call | tf_op jit(solution)/shard_map/terms/pallas_call | solution.py:507
  76.8 2.7 %all-to-all-start.5 = ((bf16[32,24,256]{2,1,0:T(8,128)(2,1)}), bf16[32,24,256]{2,1,0:T(8,128)(2,1)S(1)}, u32[]{:S(2)}, u32[]{:S(2)}) async-start(bf16[32,24,256]{2,1,0:T(8,128)(2,1)} %bitcast.76), calls=%async_computation.5 | async-start | bytes 786432 | tf_op jit(solution)/shard_map/all_to_all | solution.py:401
  79.7 2.5 %collective-permute-start.10 = (bf16[256,256]{1,0:T(8,128)(2,1)S(1)}, bf16[256,256]{1,0:T(8,128)(2,1)S(1)}, u32[]{:S(2)}, u32[]{:S(2)}) collective-permute-start(bf16[256,256]{1,0:T(8,128)(2,1)S(1)} %get-tuple-element.51), channel_id=1, source_target_pairs={{0,7},{1,0},{2,1},{3,2},{4,3},{5,4},{6,5},{7,6},{8,15},{9,8},{10,9... | collective-permute-start | bytes 393224 | tf_op jit(solution)/shard_map/ppermute | solution.py:419
  82.3 1.7 collective-permute-start.9
  84.0 2.1 %collective-permute-start.8 = (bf16[256,256]{1,0:T(8,128)(2,1)S(1)}, bf16[256,256]{1,0:T(8,128)(2,1)S(1)}, u32[]{:S(2)}, u32[]{:S(2)}) collective-permute-start(bf16[256,256]{1,0:T(8,128)(2,1)S(1)} %get-tuple-element.53), channel_id=1, source_target_pairs={{0,24},{8,0},{16,8},{24,16},{1,25},{9,1},{17,9},{25,17},{2,26},{10... | collective-permute-start | bytes 393224 | tf_op jit(solution)/shard_map/ppermute | solution.py:419
  86.1 0.8 slice_bitcast_fusion.10
  86.9 1.4 collective-permute-done.11.right_ref
  88.3 5.6 %collective-permute-done.9.down_ref = bf16[256,256]{1,0:T(8,128)(2,1)S(1)} collective-permute-done((bf16[256,256]{1,0:T(8,128)(2,1)S(1)}, bf16[256,256]{1,0:T(8,128)(2,1)S(1)}, u32[]{:S(2)}, u32[]{:S(2)}) %collective-permute-start.9) | collective-permute-done | bytes 131104 | tf_op jit(solution)/shard_map/ppermute | solution.py:419
  94.6 7.7 %backward.1 = (f32[512,256]{1,0:T(8,128)}, bf16[1024,256]{1,0:T(8,128)(2,1)}, bf16[4,256,256]{2,1,0:T(8,128)(2,1)}) custom-call(f32[8]{0:T(128)} %pad_maximum_fusion.5.flags_ref, bf16[256,256]{1,0:T(8,128)(2,1)} %copy-done.22, bf16[256,256]{1,0:T(8,128)(2,1)} %copy-done.20, bf16[256,256]{1,0:T(8,128)(2,1)} %copy-done.18, bf16[256,256]{1,0:T(8,128)(2,1)} %copy-done.16, ...), custom_call_target="tpu_custom_call" | custom-call | tf_op jit(solution)/shard_map/backward/pallas_call | solution.py:507
  102.3 1.1 slice_bitcast_fusion.12
  103.5 2.6 %collective-permute-start.14 = (bf16[256,256]{1,0:T(8,128)(2,1)S(1)}, bf16[256,256]{1,0:T(8,128)(2,1)S(1)}, u32[]{:S(2)}, u32[]{:S(2)}) collective-permute-start(bf16[256,256]{1,0:T(8,128)(2,1)S(1)} %get-tuple-element.47), channel_id=1, source_target_pairs={{0,7},{1,0},{2,1},{3,2},{4,3},{5,4},{6,5},{7,6},{8,15},{9,8},{10,9... | collective-permute-start | bytes 393224 | tf_op jit(solution)/shard_map/ppermute | solution.py:419
  106.1 3.9 %collective-permute-start.13 = (bf16[256,256]{1,0:T(8,128)(2,1)S(1)}, bf16[256,256]{1,0:T(8,128)(2,1)S(1)}, u32[]{:S(2)}, u32[]{:S(2)}) collective-permute-start(bf16[256,256]{1,0:T(8,128)(2,1)S(1)} %get-tuple-element.48), channel_id=1, source_target_pairs={{0,8},{8,16},{16,24},{24,0},{1,9},{9,17},{17,25},{25,1},{2,10},{10... | collective-permute-start | bytes 393224 | tf_op jit(solution)/shard_map/ppermute | solution.py:419
  110.1 3.8 %collective-permute-done.13.down_ref = bf16[256,256]{1,0:T(8,128)(2,1)S(1)} collective-permute-done((bf16[256,256]{1,0:T(8,128)(2,1)S(1)}, bf16[256,256]{1,0:T(8,128)(2,1)S(1)}, u32[]{:S(2)}, u32[]{:S(2)}) %collective-permute-start.13) | collective-permute-done | bytes 131104 | tf_op jit(solution)/shard_map/ppermute | solution.py:419
  113.9 1.6 collective-permute-done.12.up_ref
  115.6 0.6 copy-done.23
  116.2 5.8 %last.1 = bf16[512,256]{1,0:T(8,128)(2,1)} custom-call(f32[8]{0:T(128)} %pad_maximum_fusion.5.flags_ref, bf16[256,256]{1,0:T(8,128)(2,1)} %copy-done.23, bf16[256,256]{1,0:T(8,128)(2,1)} %copy-done.21, bf16[256,256]{1,0:T(8,128)(2,1)} %copy-done.19, bf16[256,256]{1,0:T(8,128)(2,1)} %copy-done.17, bf16[1024,256]{1,0:T(8,128)(2,1)} %get-tuple-element.33.own_ref, ...), custom_call_target="tpu_custom_call" | custom-call | tf_op jit(solution)/shard_map/last/pallas_call | solution.py:507
  122.0 4.8 %all-to-all-start.1 = ((bf16[32,16,256]{2,1,0:T(8,128)(2,1)}), bf16[32,16,256]{2,1,0:T(8,128)(2,1)S(1)}, u32[]{:S(2)}, u32[]{:S(2)}) async-start(bf16[32,16,256]{2,1,0:T(8,128)(2,1)} %bitcast.77), calls=%async_computation.1 | async-start | bytes 524288 | tf_op jit(solution)/shard_map/all_to_all | solution.py:401
  126.8 3.1 %terms.2 = bf16[768,256]{1,0:T(8,128)(2,1)} custom-call(f32[8]{0:T(128)} %pad_maximum_fusion.5.flags_ref, bf16[256,256]{1,0:T(8,128)(2,1)} %copy-done.10, bf16[256,256]{1,0:T(8,128)(2,1)} %copy-done.9, bf16[256,256]{1,0:T(8,128)(2,1)} %copy-done.8, bf16[256,256]{1,0:T(8,128)(2,1)} %copy-done.7, bf16[512,256]{1,0:T(8,128)(2,1)} %get-tuple-element.24.state_ref, ...), custom_call_target="tpu_custom_call" | custom-call | tf_op jit(solution)/shard_map/terms/pallas_call | solution.py:507
  129.9 7.5 %all-to-all-done.1.parts_ref = bf16[32,16,256]{2,1,0:T(8,128)(2,1)S(1)} async-done(((bf16[32,16,256]{2,1,0:T(8,128)(2,1)}), bf16[32,16,256]{2,1,0:T(8,128)(2,1)S(1)}, u32[]{:S(2)}, u32[]{:S(2)}) %all-to-all-start.1) | async-done | bytes 262176 | tf_op jit(solution)/shard_map/all_to_all | solution.py:401
  137.4 0.7 copy-done.4
  138.1 2.6 %all-to-all-start.3 = ((bf16[32,24,256]{2,1,0:T(8,128)(2,1)}), bf16[32,24,256]{2,1,0:T(8,128)(2,1)S(1)}, u32[]{:S(2)}, u32[]{:S(2)}) async-start(bf16[32,24,256]{2,1,0:T(8,128)(2,1)} %bitcast.75), calls=%async_computation.3 | async-start | bytes 786432 | tf_op jit(solution)/shard_map/all_to_all | solution.py:401
  140.7 1.7 share.3
  142.4 11.5 %all-to-all-done.3.parts_ref = bf16[32,24,256]{2,1,0:T(8,128)(2,1)S(1)} async-done(((bf16[32,24,256]{2,1,0:T(8,128)(2,1)}), bf16[32,24,256]{2,1,0:T(8,128)(2,1)S(1)}, u32[]{:S(2)}, u32[]{:S(2)}) %all-to-all-start.3) | async-done | bytes 393248 | tf_op jit(solution)/shard_map/all_to_all | solution.py:401
  153.9 2.6 %all-to-all-start.2 = ((bf16[32,16,256]{2,1,0:T(8,128)(2,1)}), bf16[32,16,256]{2,1,0:T(8,128)(2,1)S(1)}, u32[]{:S(2)}, u32[]{:S(2)}) async-start(bf16[32,16,256]{2,1,0:T(8,128)(2,1)} %share.3), calls=%async_computation.2 | async-start | bytes 524288 | tf_op jit(solution)/shard_map/all_to_all | solution.py:401
  156.5 1.8 share.5
  158.3 8.8 %all-to-all-done.2 = bf16[32,16,256]{2,1,0:T(8,128)(2,1)S(1)} async-done(((bf16[32,16,256]{2,1,0:T(8,128)(2,1)}), bf16[32,16,256]{2,1,0:T(8,128)(2,1)S(1)}, u32[]{:S(2)}, u32[]{:S(2)}) %all-to-all-start.2) | async-done | bytes 262176 | tf_op jit(solution)/shard_map/all_to_all | solution.py:401
  167.1 2.6 %all-to-all-start.6 = ((bf16[32,24,256]{2,1,0:T(8,128)(2,1)}), bf16[32,24,256]{2,1,0:T(8,128)(2,1)S(1)}, u32[]{:S(2)}, u32[]{:S(2)}) async-start(bf16[32,24,256]{2,1,0:T(8,128)(2,1)} %share.5), calls=%async_computation.6 | async-start | bytes 786432 | tf_op jit(solution)/shard_map/all_to_all | solution.py:401
  169.7 1.8 share.4
  171.5 11.4 %all-to-all-done.6 = bf16[32,24,256]{2,1,0:T(8,128)(2,1)S(1)} async-done(((bf16[32,24,256]{2,1,0:T(8,128)(2,1)}), bf16[32,24,256]{2,1,0:T(8,128)(2,1)S(1)}, u32[]{:S(2)}, u32[]{:S(2)}) %all-to-all-start.6) | async-done | bytes 393248 | tf_op jit(solution)/shard_map/all_to_all | solution.py:401
  182.9 2.6 %all-to-all-start.4 = ((bf16[32,24,256]{2,1,0:T(8,128)(2,1)}), bf16[32,24,256]{2,1,0:T(8,128)(2,1)S(1)}, u32[]{:S(2)}, u32[]{:S(2)}) async-start(bf16[32,24,256]{2,1,0:T(8,128)(2,1)} %share.4), calls=%async_computation.4 | async-start | bytes 786432 | tf_op jit(solution)/shard_map/all_to_all | solution.py:401
  185.6 2.0 state.1
  187.5 0.7 slice.175
  188.2 0.7 slice.176
  189.1 9.7 %all-to-all-done.4 = bf16[32,24,256]{2,1,0:T(8,128)(2,1)S(1)} async-done(((bf16[32,24,256]{2,1,0:T(8,128)(2,1)}), bf16[32,24,256]{2,1,0:T(8,128)(2,1)S(1)}, u32[]{:S(2)}, u32[]{:S(2)}) %all-to-all-start.4) | async-done | bytes 393248 | tf_op jit(solution)/shard_map/all_to_all | solution.py:401
  198.9 0.8 pad_maximum_fusion.2
  199.8 0.8 pad_maximum_fusion.1
  200.6 0.8 pad_maximum_fusion
  (88 shorter events, 4.4 us)
Async XLA Ops:
  2.6 7.4 %copy-start.29 = (s32[256]{0:T(256)S(1)}, s32[256]{0:T(256)}, u32[]{:S(2)}) copy-start(s32[256]{0:T(256)} %param.22) | copy-start | bytes 3076
  2.6 8.0 %copy-start.27 = (s32[2048]{0:T(1024)S(1)}, s32[2048]{0:T(1024)}, u32[]{:S(2)}) copy-start(s32[2048]{0:T(1024)} %param.23) | copy-start | bytes 24580
  2.6 8.0 %copy-start.28 = (s32[2048]{0:T(1024)S(1)}, s32[2048]{0:T(1024)}, u32[]{:S(2)}) copy-start(s32[2048]{0:T(1024)} %param.24) | copy-start | bytes 24580
  2.6 8.9 %copy-start.6 = (bf16[2,256,256]{2,1,0:T(8,128)(2,1)S(1)}, bf16[2,256,256]{2,1,0:T(8,128)(2,1)}, u32[]{:S(2)}) copy-start(bf16[2,256,256]{2,1,0:T(8,128)(2,1)} %param.29) | copy-start | bytes 786436
  2.6 24.1 %all-to-all-start = ((bf16[32,68,128]{2,1,0:T(8,128)(2,1)}), bf16[32,68,128]{2,1,0:T(8,128)(2,1)S(1)}, u32[]{:S(2)}, u32[]{:S(2)}) async-start(bf16[32,68,128]{2,1,0:T(8,128)(2,1)} %pack.1), calls=%async_computation | async-start | bytes 1179648 | tf_op jit(solution)/shard_map/all_to_all | solution.py:401
  9.9 0.8 copy-start.24
  11.5 1.0 copy-start.5
  12.4 0.8 copy-start.25
  12.4 0.8 copy-start.26
  12.4 1.5 copy-start.15
  12.6 0.7 copy-start.30
  26.7 1.0 copy-start
  33.1 5.3 %collective-permute-start.3 = (bf16[256,256]{1,0:T(8,128)(2,1)}, bf16[256,256]{1,0:T(8,128)(2,1)S(1)}, u32[]{:S(2)}, u32[]{:S(2)}) collective-permute-start(bf16[256,256]{1,0:T(8,128)(2,1)} %get-tuple-element.23), channel_id=1, source_target_pairs={{0,7},{1,0},{2,1},{3,2},{4,3},{5,4},{6,5},{7,6},{8,15},{9,8},{10,9... | collective-permute-start | bytes 393224 | tf_op jit(solution)/shard_map/ppermute | solution.py:419
  34.3 5.5 %collective-permute-start.2 = (bf16[256,256]{1,0:T(8,128)(2,1)}, bf16[256,256]{1,0:T(8,128)(2,1)S(1)}, u32[]{:S(2)}, u32[]{:S(2)}) collective-permute-start(bf16[256,256]{1,0:T(8,128)(2,1)} %get-tuple-element.23), channel_id=1, source_target_pairs={{0,1},{1,2},{2,3},{3,4},{4,5},{5,6},{6,7},{7,0},{8,9},{9,10},{10,1... | collective-permute-start | bytes 393224 | tf_op jit(solution)/shard_map/ppermute | solution.py:419
  34.3 6.2 %collective-permute-start.1 = (bf16[256,256]{1,0:T(8,128)(2,1)}, bf16[256,256]{1,0:T(8,128)(2,1)S(1)}, u32[]{:S(2)}, u32[]{:S(2)}) collective-permute-start(bf16[256,256]{1,0:T(8,128)(2,1)} %get-tuple-element.23), channel_id=1, source_target_pairs={{0,24},{8,0},{16,8},{24,16},{1,25},{9,1},{17,9},{25,17},{2,26},{10... | collective-permute-start | bytes 393224 | tf_op jit(solution)/shard_map/ppermute | solution.py:419
  36.0 7.4 %collective-permute-start = (bf16[256,256]{1,0:T(8,128)(2,1)}, bf16[256,256]{1,0:T(8,128)(2,1)S(1)}, u32[]{:S(2)}, u32[]{:S(2)}) collective-permute-start(bf16[256,256]{1,0:T(8,128)(2,1)} %get-tuple-element.23), channel_id=1, source_target_pairs={{0,8},{8,16},{16,24},{24,0},{1,9},{9,17},{17,25},{25,1},{2,10},{10... | collective-permute-start | bytes 393224 | tf_op jit(solution)/shard_map/ppermute | solution.py:419
  38.4 5.1 %copy-start.7 = (bf16[256,256]{1,0:T(8,128)(2,1)}, bf16[256,256]{1,0:T(8,128)(2,1)S(1)}, u32[]{:S(2)}) copy-start(bf16[256,256]{1,0:T(8,128)(2,1)S(1)} %collective-permute-done.3.right_ref) | copy-start | bytes 393220
  39.8 3.7 %copy-start.8 = (bf16[256,256]{1,0:T(8,128)(2,1)}, bf16[256,256]{1,0:T(8,128)(2,1)S(1)}, u32[]{:S(2)}) copy-start(bf16[256,256]{1,0:T(8,128)(2,1)S(1)} %collective-permute-done.2.left_ref) | copy-start | bytes 393220
  40.5 3.0 %copy-start.9 = (bf16[256,256]{1,0:T(8,128)(2,1)}, bf16[256,256]{1,0:T(8,128)(2,1)S(1)}, u32[]{:S(2)}) copy-start(bf16[256,256]{1,0:T(8,128)(2,1)S(1)} %collective-permute-done.1.down_ref) | copy-start | bytes 393220
  43.5 0.7 copy-start.10
  51.9 4.5 %collective-permute-start.7 = (bf16[256,256]{1,0:T(8,128)(2,1)}, bf16[256,256]{1,0:T(8,128)(2,1)S(1)}, u32[]{:S(2)}, u32[]{:S(2)}) collective-permute-start(bf16[256,256]{1,0:T(8,128)(2,1)} %get-tuple-element.27), channel_id=1, source_target_pairs={{0,7},{1,0},{2,1},{3,2},{4,3},{5,4},{6,5},{7,6},{8,15},{9,8},{10,9... | collective-permute-start | bytes 393224 | tf_op jit(solution)/shard_map/ppermute | solution.py:419
  53.3 5.5 %collective-permute-start.6 = (bf16[256,256]{1,0:T(8,128)(2,1)}, bf16[256,256]{1,0:T(8,128)(2,1)S(1)}, u32[]{:S(2)}, u32[]{:S(2)}) collective-permute-start(bf16[256,256]{1,0:T(8,128)(2,1)} %get-tuple-element.27), channel_id=1, source_target_pairs={{0,1},{1,2},{2,3},{3,4},{4,5},{5,6},{6,7},{7,0},{8,9},{9,10},{10,1... | collective-permute-start | bytes 393224 | tf_op jit(solution)/shard_map/ppermute | solution.py:419
  53.3 5.5 %collective-permute-start.5 = (bf16[256,256]{1,0:T(8,128)(2,1)}, bf16[256,256]{1,0:T(8,128)(2,1)S(1)}, u32[]{:S(2)}, u32[]{:S(2)}) collective-permute-start(bf16[256,256]{1,0:T(8,128)(2,1)} %get-tuple-element.27), channel_id=1, source_target_pairs={{0,24},{8,0},{16,8},{24,16},{1,25},{9,1},{17,9},{25,17},{2,26},{10... | collective-permute-start | bytes 393224 | tf_op jit(solution)/shard_map/ppermute | solution.py:419
  54.4 8.6 %collective-permute-start.4 = (bf16[256,256]{1,0:T(8,128)(2,1)}, bf16[256,256]{1,0:T(8,128)(2,1)S(1)}, u32[]{:S(2)}, u32[]{:S(2)}) collective-permute-start(bf16[256,256]{1,0:T(8,128)(2,1)} %get-tuple-element.27), channel_id=1, source_target_pairs={{0,8},{8,16},{16,24},{24,0},{1,9},{9,17},{17,25},{25,1},{2,10},{10... | collective-permute-start | bytes 393224 | tf_op jit(solution)/shard_map/ppermute | solution.py:419
  56.4 6.7 %copy-start.11 = (bf16[256,256]{1,0:T(8,128)(2,1)}, bf16[256,256]{1,0:T(8,128)(2,1)S(1)}, u32[]{:S(2)}) copy-start(bf16[256,256]{1,0:T(8,128)(2,1)S(1)} %collective-permute-done.7.right_ref) | copy-start | bytes 393220
  58.8 4.3 %copy-start.12 = (bf16[256,256]{1,0:T(8,128)(2,1)}, bf16[256,256]{1,0:T(8,128)(2,1)S(1)}, u32[]{:S(2)}) copy-start(bf16[256,256]{1,0:T(8,128)(2,1)S(1)} %collective-permute-done.6.left_ref) | copy-start | bytes 393220
  58.8 4.3 %copy-start.13 = (bf16[256,256]{1,0:T(8,128)(2,1)}, bf16[256,256]{1,0:T(8,128)(2,1)S(1)}, u32[]{:S(2)}) copy-start(bf16[256,256]{1,0:T(8,128)(2,1)S(1)} %collective-permute-done.5.down_ref) | copy-start | bytes 393220
  63.1 0.7 copy-start.14
  76.8 2.7 %copy-start.1 = (bf16[4,256,256]{2,1,0:T(8,128)(2,1)S(1)}, bf16[4,256,256]{2,1,0:T(8,128)(2,1)}, u32[]{:S(2)}) copy-start(bf16[4,256,256]{2,1,0:T(8,128)(2,1)} %get-tuple-element.29.rims_ref) | copy-start | bytes 1572868
  76.8 45.2 %all-to-all-start.5 = ((bf16[32,24,256]{2,1,0:T(8,128)(2,1)}), bf16[32,24,256]{2,1,0:T(8,128)(2,1)S(1)}, u32[]{:S(2)}, u32[]{:S(2)}) async-start(bf16[32,24,256]{2,1,0:T(8,128)(2,1)} %bitcast.76), calls=%async_computation.5 | async-start | bytes 786432 | tf_op jit(solution)/shard_map/all_to_all | solution.py:401
  79.6 8.7 %collective-permute-start.11 = (bf16[256,256]{1,0:T(8,128)(2,1)S(1)}, bf16[256,256]{1,0:T(8,128)(2,1)S(1)}, u32[]{:S(2)}, u32[]{:S(2)}) collective-permute-start(bf16[256,256]{1,0:T(8,128)(2,1)S(1)} %get-tuple-element.50), channel_id=1, source_target_pairs={{0,1},{1,2},{2,3},{3,4},{4,5},{5,6},{6,7},{7,0},{8,9},{9,10},{10,1... | collective-permute-start | bytes 393224 | tf_op jit(solution)/shard_map/ppermute | solution.py:419
  79.7 8.6 %collective-permute-start.10 = (bf16[256,256]{1,0:T(8,128)(2,1)S(1)}, bf16[256,256]{1,0:T(8,128)(2,1)S(1)}, u32[]{:S(2)}, u32[]{:S(2)}) collective-permute-start(bf16[256,256]{1,0:T(8,128)(2,1)S(1)} %get-tuple-element.51), channel_id=1, source_target_pairs={{0,7},{1,0},{2,1},{3,2},{4,3},{5,4},{6,5},{7,6},{8,15},{9,8},{10,9... | collective-permute-start | bytes 393224 | tf_op jit(solution)/shard_map/ppermute | solution.py:419
  82.3 11.6 %collective-permute-start.9 = (bf16[256,256]{1,0:T(8,128)(2,1)S(1)}, bf16[256,256]{1,0:T(8,128)(2,1)S(1)}, u32[]{:S(2)}, u32[]{:S(2)}) collective-permute-start(bf16[256,256]{1,0:T(8,128)(2,1)S(1)} %get-tuple-element.52), channel_id=1, source_target_pairs={{0,8},{8,16},{16,24},{24,0},{1,9},{9,17},{17,25},{25,1},{2,10},{10... | collective-permute-start | bytes 393224 | tf_op jit(solution)/shard_map/ppermute | solution.py:419
  84.0 10.0 %collective-permute-start.8 = (bf16[256,256]{1,0:T(8,128)(2,1)S(1)}, bf16[256,256]{1,0:T(8,128)(2,1)S(1)}, u32[]{:S(2)}, u32[]{:S(2)}) collective-permute-start(bf16[256,256]{1,0:T(8,128)(2,1)S(1)} %get-tuple-element.53), channel_id=1, source_target_pairs={{0,24},{8,0},{16,8},{24,16},{1,25},{9,1},{17,9},{25,17},{2,26},{10... | collective-permute-start | bytes 393224 | tf_op jit(solution)/shard_map/ppermute | solution.py:419
  88.3 5.6 %copy-start.16 = (bf16[256,256]{1,0:T(8,128)(2,1)}, bf16[256,256]{1,0:T(8,128)(2,1)S(1)}, u32[]{:S(2)}) copy-start(bf16[256,256]{1,0:T(8,128)(2,1)S(1)} %collective-permute-done.11.right_ref) | copy-start | bytes 393220
  88.3 5.6 %copy-start.18 = (bf16[256,256]{1,0:T(8,128)(2,1)}, bf16[256,256]{1,0:T(8,128)(2,1)S(1)}, u32[]{:S(2)}) copy-start(bf16[256,256]{1,0:T(8,128)(2,1)S(1)} %collective-permute-done.10.left_ref) | copy-start | bytes 393220
  93.9 0.6 copy-start.20
  93.9 0.7 copy-start.22
  103.4 6.6 %collective-permute-start.15 = (bf16[256,256]{1,0:T(8,128)(2,1)S(1)}, bf16[256,256]{1,0:T(8,128)(2,1)S(1)}, u32[]{:S(2)}, u32[]{:S(2)}) collective-permute-start(bf16[256,256]{1,0:T(8,128)(2,1)S(1)} %get-tuple-element.46), channel_id=1, source_target_pairs={{0,1},{1,2},{2,3},{3,4},{4,5},{5,6},{6,7},{7,0},{8,9},{9,10},{10,1... | collective-permute-start | bytes 393224 | tf_op jit(solution)/shard_map/ppermute | solution.py:419
  103.5 6.6 %collective-permute-start.14 = (bf16[256,256]{1,0:T(8,128)(2,1)S(1)}, bf16[256,256]{1,0:T(8,128)(2,1)S(1)}, u32[]{:S(2)}, u32[]{:S(2)}) collective-permute-start(bf16[256,256]{1,0:T(8,128)(2,1)S(1)} %get-tuple-element.47), channel_id=1, source_target_pairs={{0,7},{1,0},{2,1},{3,2},{4,3},{5,4},{6,5},{7,6},{8,15},{9,8},{10,9... | collective-permute-start | bytes 393224 | tf_op jit(solution)/shard_map/ppermute | solution.py:419
  106.1 7.8 %collective-permute-start.13 = (bf16[256,256]{1,0:T(8,128)(2,1)S(1)}, bf16[256,256]{1,0:T(8,128)(2,1)S(1)}, u32[]{:S(2)}, u32[]{:S(2)}) collective-permute-start(bf16[256,256]{1,0:T(8,128)(2,1)S(1)} %get-tuple-element.48), channel_id=1, source_target_pairs={{0,8},{8,16},{16,24},{24,0},{1,9},{9,17},{17,25},{25,1},{2,10},{10... | collective-permute-start | bytes 393224 | tf_op jit(solution)/shard_map/ppermute | solution.py:419
  110.1 5.5 %collective-permute-start.12 = (bf16[256,256]{1,0:T(8,128)(2,1)S(1)}, bf16[256,256]{1,0:T(8,128)(2,1)S(1)}, u32[]{:S(2)}, u32[]{:S(2)}) collective-permute-start(bf16[256,256]{1,0:T(8,128)(2,1)S(1)} %get-tuple-element.49), channel_id=1, source_target_pairs={{0,24},{8,0},{16,8},{24,16},{1,25},{9,1},{17,9},{25,17},{2,26},{10... | collective-permute-start | bytes 393224 | tf_op jit(solution)/shard_map/ppermute | solution.py:419
  110.1 5.5 %copy-start.17 = (bf16[256,256]{1,0:T(8,128)(2,1)}, bf16[256,256]{1,0:T(8,128)(2,1)S(1)}, u32[]{:S(2)}) copy-start(bf16[256,256]{1,0:T(8,128)(2,1)S(1)} %collective-permute-done.15.right_ref) | copy-start | bytes 393220
  110.1 5.5 %copy-start.19 = (bf16[256,256]{1,0:T(8,128)(2,1)}, bf16[256,256]{1,0:T(8,128)(2,1)S(1)}, u32[]{:S(2)}) copy-start(bf16[256,256]{1,0:T(8,128)(2,1)S(1)} %collective-permute-done.14.left_ref) | copy-start | bytes 393220
  113.9 1.6 copy-start.21
  115.5 0.7 copy-start.23
  122.0 7.8 %copy-start.2 = (bf16[32,24,256]{2,1,0:T(8,128)(2,1)}, bf16[32,24,256]{2,1,0:T(8,128)(2,1)S(1)}, u32[]{:S(2)}) copy-start(bf16[32,24,256]{2,1,0:T(8,128)(2,1)S(1)} %all-to-all-done.5.parts_ref) | copy-start | bytes 1179652
  122.0 15.3 %all-to-all-start.1 = ((bf16[32,16,256]{2,1,0:T(8,128)(2,1)}), bf16[32,16,256]{2,1,0:T(8,128)(2,1)S(1)}, u32[]{:S(2)}, u32[]{:S(2)}) async-start(bf16[32,16,256]{2,1,0:T(8,128)(2,1)} %bitcast.77), calls=%async_computation.1 | async-start | bytes 524288 | tf_op jit(solution)/shard_map/all_to_all | solution.py:401
  137.4 0.7 copy-start.4
  138.1 15.8 %all-to-all-start.3 = ((bf16[32,24,256]{2,1,0:T(8,128)(2,1)}), bf16[32,24,256]{2,1,0:T(8,128)(2,1)S(1)}, u32[]{:S(2)}, u32[]{:S(2)}) async-start(bf16[32,24,256]{2,1,0:T(8,128)(2,1)} %bitcast.75), calls=%async_computation.3 | async-start | bytes 786432 | tf_op jit(solution)/shard_map/all_to_all | solution.py:401
  153.9 4.4 %copy-start.3 = (bf16[32,24,256]{2,1,0:T(8,128)(2,1)}, bf16[32,24,256]{2,1,0:T(8,128)(2,1)S(1)}, u32[]{:S(2)}) copy-start(bf16[32,24,256]{2,1,0:T(8,128)(2,1)S(1)} %all-to-all-done.3.parts_ref) | copy-start | bytes 1179652
  153.9 13.2 %all-to-all-start.2 = ((bf16[32,16,256]{2,1,0:T(8,128)(2,1)}), bf16[32,16,256]{2,1,0:T(8,128)(2,1)S(1)}, u32[]{:S(2)}, u32[]{:S(2)}) async-start(bf16[32,16,256]{2,1,0:T(8,128)(2,1)} %share.3), calls=%async_computation.2 | async-start | bytes 524288 | tf_op jit(solution)/shard_map/all_to_all | solution.py:401
  167.1 15.8 %all-to-all-start.6 = ((bf16[32,24,256]{2,1,0:T(8,128)(2,1)}), bf16[32,24,256]{2,1,0:T(8,128)(2,1)S(1)}, u32[]{:S(2)}, u32[]{:S(2)}) async-start(bf16[32,24,256]{2,1,0:T(8,128)(2,1)} %share.5), calls=%async_computation.6 | async-start | bytes 786432 | tf_op jit(solution)/shard_map/all_to_all | solution.py:401
  182.9 15.8 %all-to-all-start.4 = ((bf16[32,24,256]{2,1,0:T(8,128)(2,1)}), bf16[32,24,256]{2,1,0:T(8,128)(2,1)S(1)}, u32[]{:S(2)}, u32[]{:S(2)}) async-start(bf16[32,24,256]{2,1,0:T(8,128)(2,1)} %share.4), calls=%async_computation.4 | async-start | bytes 786432 | tf_op jit(solution)/shard_map/all_to_all | solution.py:401

commit v2 on v1

v2 whole, which is shorter than its diff:
```python
import functools

import jax
import jax.numpy as jnp
from jax import lax
from jax.experimental import pallas as pl
from jax.experimental.pallas import tpu as pltpu
from jax.sharding import PartitionSpec as P

AXES = ("grid", "dom")
BF = jnp.bfloat16
F32 = jnp.float32
LANES = 128
TILE = 256
CHUNK = 512
GRANT = 24 << 20


def mm(left_side, right_side):
    return jnp.dot(left_side, right_side, preferred_element_type=F32)


def mm_t(left_side, right_side):
    return lax.dot_general(
        left_side, right_side, (((1,), (1,)), ((), ())), preferred_element_type=F32
    )


def t_mm(left_side, right_side):
    return lax.dot_general(
        left_side, right_side, (((0,), (0,)), ((), ())), preferred_element_type=F32
    )


def put_picks(out_ref, start, indices, count):
    rows = lax.broadcasted_iota(jnp.int32, (TILE, indices.shape[1]), 0).astype(F32).astype(BF)
    for base in range(0, count, TILE):
        shifted = (indices - float(base)).astype(BF)
        block = jnp.where(rows == shifted, jnp.ones((), BF), jnp.zeros((), BF))
        out_ref[start + base : start + base + TILE, :] = block


def sigmoid(values):
    return 0.5 * jnp.tanh(0.5 * values) + 0.5


def call(body, outs, scratch, name, flagged=False):
    vmem = pl.BlockSpec(memory_space=pltpu.VMEM)
    first = pl.BlockSpec(memory_space=pltpu.SMEM) if flagged else vmem

    def run(*args):
        return pl.pallas_call(
            body,
            out_shape=tuple(jax.ShapeDtypeStruct(shape, dtype) for shape, dtype in outs),
            in_specs=[first] + [vmem] * (len(args) - 1),
            out_specs=tuple(vmem for _ in outs),
            scratch_shapes=scratch,
            compiler_params=pltpu.CompilerParams(vmem_limit_bytes=GRANT),
            name=name,
        )(*args)

    return run


def chunks(total, size, body):
    if total == size:
        body(0)
        return

    def step(i, carry):
        body(pl.multiple_of(i * size, size))
        return carry

    lax.fori_loop(0, total // size, step, 0)


def pack_body(bucket, cols_ref, slot_ref, live_ref, weight_ref, out_ref):
    peers = out_ref.shape[0]
    per_row = LANES // bucket
    slot = slot_ref[...].astype(F32)
    high = jnp.floor(slot * (1.0 / 256.0))
    low = slot - 256.0 * high
    scale = weight_ref[...] * live_ref[...].astype(F32)
    scale_high = scale.astype(BF)
    scale_low = (scale - scale_high.astype(F32)).astype(BF)
    fields = [high.astype(BF), low.astype(BF), scale_high, scale_low]
    for peer in range(peers):
        out_ref[peer, :bucket, :] = cols_ref[peer * bucket : (peer + 1) * bucket, :]
        row = peer // per_row
        extra = jnp.concatenate([field[row : row + 1, :] for field in fields], 0)
        out_ref[peer, bucket : bucket + 4, :] = extra


PAIR, ODD_GRID, ODD_DOM = 4, 6, 7


def put_tables(state, state_ref, table_ref, rim_ref, src_t_ref, dst_t_ref, bound_ref, rim_picks):
    nodes = state.shape[0]
    put_picks(rim_picks, 0, bound_ref[0:1, :], nodes)
    state_ref[...] = state.astype(BF)
    held = state_ref[...]
    rim_ref[...] = t_mm(rim_picks[...], held).astype(BF)
    table_ref[:, :nodes] = mm_t(src_t_ref[...], held).astype(BF)
    table_ref[:, nodes:] = mm_t(dst_t_ref[...], held).astype(BF)


def in_order(flags_ref, rims):
    first, second, left, right = (ref[...] for ref in rims)
    odd = flags_ref[ODD_GRID] > 0.5
    ordered = (jnp.where(odd, first, second), jnp.where(odd, second, first), left, right)
    return [rows * flags_ref[side].astype(BF) for side, rows in enumerate(ordered)]


def encode_body(
    bucket,
    packed_ref,
    rows_ref,
    enc_in_t_ref,
    enc_out_ref,
    static_ref,
    src_t_ref,
    dst_t_ref,
    bound_ref,
    pooled_ref,
    slope_ref,
    state_ref,
    table_ref,
    rim_ref,
    picks_ref,
    rim_picks,
    acc_ref,
):
    nodes = static_ref.shape[0]
    cols = rows_ref.shape[1]
    chunk = picks_ref.shape[1]
    peers_step = chunk // bucket
    acc_ref[...] = jnp.zeros_like(acc_ref)

    def step(start):
        first = start // bucket
        got = packed_ref[pl.ds(first, peers_step), :bucket, :].reshape(chunk, packed_ref.shape[2])
        pre = mm_t(enc_in_t_ref[...], got)
        slot = rows_ref[0:1, pl.ds(start, chunk)]
        scale = rows_ref[1:2, pl.ds(start, chunk)]
        sig = sigmoid(pre)
        act = (pre * sig * scale).astype(BF)
        slope_ref[:, pl.ds(start, chunk)] = (sig * (1.0 + pre * (1.0 - sig)) * scale).astype(BF)
        put_picks(picks_ref, 0, slot, nodes)
        acc_ref[...] += mm_t(picks_ref[...], act)

    chunks(cols, chunk, step)
    pooled_ref[...] = acc_ref[...].astype(BF)
    state = static_ref[...].astype(F32) + mm(pooled_ref[...], enc_out_ref[...])
    put_tables(state, state_ref, table_ref, rim_ref, src_t_ref, dst_t_ref, bound_ref, rim_picks)


def own_body(table_ref, rows_ref, out_ref, picks_ref):
    nodes = table_ref.shape[1] // 2
    chunk = picks_ref.shape[1]

    def step(start):
        put_picks(picks_ref, 0, rows_ref[0:1, pl.ds(start, chunk)], nodes)
        put_picks(picks_ref, nodes, rows_ref[1:2, pl.ds(start, chunk)], nodes)
        out_ref[:, pl.ds(start, chunk)] = mm(table_ref[...], picks_ref[...])

    chunks(rows_ref.shape[1], chunk, step)


def back_body(msg_ref, grad_ref, rows_ref, out_ref, picks_ref):
    nodes = grad_ref.shape[0]
    chunk = picks_ref.shape[1]
    back = mm_t(msg_ref[...], grad_ref[...]).astype(BF)

    def step(start):
        put_picks(picks_ref, 0, rows_ref[1:2, pl.ds(start, chunk)], nodes)
        out_ref[:, pl.ds(start, chunk)] = mm(back, picks_ref[...]) * rows_ref[2:3, pl.ds(start, chunk)]

    chunks(rows_ref.shape[1], chunk, step)


def fill_rims(full_ref, flags_ref, rims, src_t_ref):
    rim = rims[0].shape[0]
    for side, rim_rows in enumerate(in_order(flags_ref, rims)):
        full_ref[:, side * rim : (side + 1) * rim] = mm_t(src_t_ref[...], rim_rows).astype(BF)


def forward_body(
    flags_ref,
    first_ref,
    second_ref,
    left_ref,
    right_ref,
    own_pre_ref,
    rows_ref,
    state_ref,
    src_t_ref,
    msg_ref,
    next_src_t_ref,
    next_dst_t_ref,
    bound_ref,
    slope_ref,
    act_ref,
    next_state_ref,
    next_table_ref,
    rim_ref,
    full_ref,
    picks_ref,
    rim_picks,
    acc_ref,
):
    nodes = state_ref.shape[0]
    ext = full_ref.shape[1]
    chunk = picks_ref.shape[1]
    fill_rims(full_ref, flags_ref, (first_ref, second_ref, left_ref, right_ref), src_t_ref)
    acc_ref[...] = jnp.zeros_like(acc_ref)

    def step(start):
        put_picks(picks_ref, 0, rows_ref[0:1, pl.ds(start, chunk)] - float(nodes), ext)
        put_picks(picks_ref, ext, rows_ref[1:2, pl.ds(start, chunk)], nodes)
        pre = own_pre_ref[:, pl.ds(start, chunk)] + mm(full_ref[...], picks_ref[:ext, :])
        scale = rows_ref[2:3, pl.ds(start, chunk)]
        sig = sigmoid(pre)
        act = (pre * sig * scale).astype(BF)
        slope_ref[:, pl.ds(start, chunk)] = (sig * (1.0 + pre * (1.0 - sig)) * scale).astype(BF)
        acc_ref[...] += mm_t(picks_ref[ext:, :], act)

    chunks(rows_ref.shape[1], chunk, step)
    act_ref[...] = acc_ref[...].astype(BF)
    state = state_ref[...].astype(F32) + mm(act_ref[...], msg_ref[...])
    put_tables(
        state, next_state_ref, next_table_ref, rim_ref, next_src_t_ref, next_dst_t_ref, bound_ref, rim_picks
    )


def put_sends(flags_ref, acc_ref, sends):
    rim = acc_ref.shape[0] // 4
    up, down, left, right = (acc_ref[side * rim : (side + 1) * rim, :].astype(BF) for side in range(4))
    odd = flags_ref[ODD_GRID] > 0.5
    sends[0][...] = jnp.where(odd, up, down)
    sends[1][...] = jnp.where(odd, down, up)
    sends[2][...] = left
    sends[3][...] = right


def turn_body(
    flags_ref,
    first_ref,
    second_ref,
    left_ref,
    right_ref,
    own_pre_ref,
    back_ref,
    rows_ref,
    src_t_ref,
    act_ref,
    grad_pre_ref,
    send0_ref,
    send1_ref,
    send2_ref,
    send3_ref,
    full_ref,
    picks_ref,
    acc_ref,
    node_count=0,
):
    ext = full_ref.shape[1]
    chunk = picks_ref.shape[1]
    fill_rims(full_ref, flags_ref, (first_ref, second_ref, left_ref, right_ref), src_t_ref)
    acc_ref[...] = jnp.zeros_like(acc_ref)

    def step(start):
        at = pl.ds(start, chunk)
        put_picks(picks_ref, 0, rows_ref[0:1, at] - float(node_count), ext)
        pre = own_pre_ref[:, at] + mm(full_ref[...], picks_ref[...])
        sig = sigmoid(pre)
        act_ref[:, at] = (pre * sig * rows_ref[2:3, at]).astype(BF)
        grad_pre = (back_ref[:, at] * (sig * (1.0 + pre * (1.0 - sig)))).astype(BF)
        grad_pre_ref[:, at] = grad_pre
        acc_ref[...] += mm_t(picks_ref[...], grad_pre)

    chunks(rows_ref.shape[1], chunk, step)
    put_sends(flags_ref, acc_ref, (send0_ref, send1_ref, send2_ref, send3_ref))


def merged_grad(grad, flags_ref, returned, own_ref, bound_ref, src_ref, dst_ref, rim_picks):
    nodes = grad.shape[0]
    put_picks(rim_picks, 0, bound_ref[0:1, :], nodes)
    marks = (flags_ref[PAIR], flags_ref[PAIR + 1], flags_ref[3], flags_ref[2])
    total = returned[0][...].astype(F32) * marks[0]
    for side in range(1, 4):
        total += returned[side][...].astype(F32) * marks[side]
    back = mm(rim_picks[...], total.astype(BF))
    grad_src = (own_ref[:nodes, :].astype(F32) + back).astype(BF)
    return grad + mm_t(grad_src, src_ref[...]) + mm_t(own_ref[nodes:, :], dst_ref[...])


def backward_body(
    flags_ref,
    first_ref,
    second_ref,
    left_ref,
    right_ref,
    own_ref,
    bound_ref,
    src_ref,
    dst_ref,
    grad_ref,
    rows_ref,
    msg_ref,
    slope_ref,
    next_grad_ref,
    grad_pre_ref,
    send0_ref,
    send1_ref,
    send2_ref,
    send3_ref,
    picks_ref,
    rim_picks,
    acc_ref,
):
    nodes = grad_ref.shape[0]
    ext = acc_ref.shape[0]
    chunk = picks_ref.shape[1]
    returned = (first_ref, second_ref, left_ref, right_ref)
    grad = merged_grad(
        grad_ref[...].astype(F32), flags_ref, returned, own_ref, bound_ref, src_ref, dst_ref, rim_picks
    )
    next_grad_ref[...] = grad
    back = mm_t(msg_ref[...], grad.astype(BF)).astype(BF)
    acc_ref[...] = jnp.zeros_like(acc_ref)

    def step(start):
        at = pl.ds(start, chunk)
        put_picks(picks_ref, 0, rows_ref[0:1, at] - float(nodes), ext)
        put_picks(picks_ref, ext, rows_ref[1:2, at], nodes)
        grad_pre = (mm(back, picks_ref[ext:, :]) * slope_ref[:, at].astype(F32)).astype(BF)
        grad_pre_ref[:, at] = grad_pre
        acc_ref[...] += mm_t(picks_ref[:ext, :], grad_pre)

    chunks(rows_ref.shape[1], chunk, step)
    put_sends(flags_ref, acc_ref, (send0_ref, send1_ref, send2_ref, send3_ref))


def sums_body(rows_ref, grad_pre_ref, own_ref, picks_ref, acc_ref):
    nodes = own_ref.shape[0] // 2
    chunk = picks_ref.shape[1]
    acc_ref[...] = jnp.zeros_like(acc_ref)

    def step(start):
        at = pl.ds(start, chunk)
        put_picks(picks_ref, 0, rows_ref[0:1, at], nodes)
        put_picks(picks_ref, nodes, rows_ref[1:2, at], nodes)
        acc_ref[...] += mm_t(picks_ref[...], grad_pre_ref[:, at])

    chunks(rows_ref.shape[1], chunk, step)
    own_ref[...] = acc_ref[...].astype(BF)


def out_body(rows_ref, act_edges_ref, state_ref, msg_ref, act_ref, out_ref, picks_ref, acc_ref):
    nodes = state_ref.shape[0]
    chunk = picks_ref.shape[1]
    acc_ref[...] = jnp.zeros_like(acc_ref)

    def step(start):
        at = pl.ds(start, chunk)
        put_picks(picks_ref, 0, rows_ref[1:2, at], nodes)
        acc_ref[...] += mm_t(picks_ref[...], act_edges_ref[:, at])

    chunks(rows_ref.shape[1], chunk, step)
    act_ref[...] = acc_ref[...].astype(BF)
    out_ref[...] = (state_ref[...].astype(F32) + mm(act_ref[...], msg_ref[...])).astype(BF)


def put_halves(flags_ref, first, term, keep_ref, send_ref):
    half = term.shape[1] // 2
    odd = flags_ref[ODD_DOM] > 0.5
    low, high = term[:, :half].astype(BF), term[:, half:].astype(BF)
    keep_ref[first : first + term.shape[0], :] = jnp.where(odd, high, low)
    send_ref[first : first + term.shape[0], :] = jnp.where(odd, low, high)


def terms_body(
    flags_ref,
    first_ref,
    second_ref,
    left_ref,
    right_ref,
    send0_ref,
    send1_ref,
    send2_ref,
    send3_ref,
    state_ref,
    own_ref,
    act_ref,
    grad_ref,
    keep_ref,
    send_ref,
):
    nodes, width = state_ref.shape
    state = state_ref[...]
    src_term = t_mm(state, own_ref[:nodes, :])
    pairs = (
        (first_ref, send0_ref, flags_ref[PAIR]),
        (second_ref, send1_ref, flags_ref[PAIR + 1]),
        (left_ref, send2_ref, flags_ref[2]),
        (right_ref, send3_ref, flags_ref[3]),
    )
    for rim_ref, sums_ref, mark in pairs:
        src_term += t_mm(rim_ref[...], sums_ref[...]) * mark
    put_halves(flags_ref, 0, src_term, keep_ref, send_ref)
    put_halves(flags_ref, width, t_mm(state, own_ref[nodes:, :]), keep_ref, send_ref)
    put_halves(
        flags_ref, 2 * width, t_mm(act_ref[...], grad_ref[...].astype(BF)), keep_ref, send_ref
    )


def last_body(
    bucket,
    flags_ref,
    first_ref,
    second_ref,
    left_ref,
    right_ref,
    own_ref,
    bound_ref,
    src_ref,
    dst_ref,
    grad_ref,
    rows_ref,
    packed_ref,
    enc_out_ref,
    pooled_ref,
    slope_ref,
    keep_ref,
    send_ref,
    picks_ref,
    rim_picks,
    acc_ref,
):
    nodes = grad_ref.shape[0]
    cols = rows_ref.shape[1]
    chunk = picks_ref.shape[1]
    fin = packed_ref.shape[2]
    peers_step = chunk // bucket
    returned = (first_ref, second_ref, left_ref, right_ref)
    grad = merged_grad(
        grad_ref[...], flags_ref, returned, own_ref, bound_ref, src_ref, dst_ref, rim_picks
    ).astype(BF)
    back = mm_t(enc_out_ref[...], grad).astype(BF)
    acc_ref[...] = jnp.zeros_like(acc_ref)

    def step(start):
        first = start // bucket
        got = packed_ref[pl.ds(first, peers_step), :bucket, :].reshape(chunk, fin)
        put_picks(picks_ref, 0, rows_ref[0:1, pl.ds(start, chunk)], nodes)
        slope = slope_ref[:, pl.ds(start, chunk)].astype(F32)
        grad_pre = (mm(back, picks_ref[...]) * slope).astype(BF)
        acc_ref[...] += mm(grad_pre, got)

    chunks(cols, chunk, step)
    put_halves(flags_ref, 0, acc_ref[...].T, keep_ref, send_ref)
    put_halves(flags_ref, fin, t_mm(pooled_ref[...], grad), keep_ref, send_ref)


def merge_body(*refs):
    out_ref = refs[-1]
    first = 0
    for keep_ref, got_ref in zip(refs[:-1:2], refs[1:-1:2]):
        rows = keep_ref.shape[0]
        total = keep_ref[...].astype(F32) + got_ref[...].astype(F32)
        out_ref[first : first + rows, :] = total.astype(BF)
        first += rows
    if first < out_ref.shape[0]:
        out_ref[first:, :] = jnp.zeros((out_ref.shape[0] - first, out_ref.shape[1]), BF)


def share_body(parts_ref, out_ref):
    count = parts_ref.shape[0]
    for odd in range(2):
        total = parts_ref[odd].astype(F32)
        for peer in range(odd + 2, count, 2):
            total += parts_ref[peer].astype(F32)
        for peer in range(odd, count, 2):
            out_ref[peer] = total.astype(BF)


def unpack_body(flags_ref, mine_ref, other_ref, *outs):
    odd = flags_ref[ODD_DOM] > 0.5
    half = mine_ref.shape[1]
    first = 0

    def put(ref, rows):
        nonlocal first
        mine = mine_ref[first : first + rows, :].astype(F32)
        other = other_ref[first : first + rows, :].astype(F32)
        ref[:, :half] = jnp.where(odd, other, mine)
        ref[:, half:] = jnp.where(odd, mine, other)
        first += rows

    enc_in_ref, enc_out_ref, *layer_refs = outs
    for layer in reversed(range(layer_refs[0].shape[0])):
        for ref in layer_refs:
            put(ref.at[layer], ref.shape[1])
    put(enc_in_ref, enc_in_ref.shape[0])
    put(enc_out_ref, enc_out_ref.shape[0])


def exchange(shard):
    return lax.all_to_all(shard, AXES, split_axis=0, concat_axis=0, tiled=True)


def turned(shard, axis, by):
    count = lax.axis_size(axis)
    return lax.ppermute(shard, axis, [(i, (i + by) % count) for i in range(count)])


def swapped(shard, axis, offset):
    count = lax.axis_size(axis)
    partner = list(range(count))
    for i in range(offset, count - 1, 2):
        partner[i], partner[i + 1] = i + 1, i
    return lax.ppermute(shard, axis, list(enumerate(partner)))


def from_neighbours(rim_rows):
    return (
        swapped(rim_rows, "grid", 0),
        swapped(rim_rows, "grid", 1),
        turned(rim_rows, "dom", 1),
        turned(rim_rows, "dom", -1),
    )


def to_neighbours(sends):
    return (
        swapped(sends[0], "grid", 0),
        swapped(sends[1], "grid", 1),
        turned(sends[2], "dom", -1),
        turned(sends[3], "dom", 1),
    )


def per_device(
    columns,
    column_live,
    col_weight,
    col_slot,
    node_static,
    boundary_idx,
    edge_src,
    edge_dst,
    edge_live,
    edge_weight,
    enc_in,
    enc_out,
    src_proj,
    dst_proj,
    msg_proj,
    node_cotangent,
):
    peers = lax.axis_size(AXES)
    cols, fin = columns.shape
    nodes, width = node_static.shape
    rim = boundary_idx.shape[0]
    edges = edge_src.shape[0]
    ext = 4 * rim
    bucket = cols // peers
    chunk = CHUNK

    lanes = (cols // LANES, LANES)
    (packed,) = call(
        functools.partial(pack_body, bucket), [((peers, bucket + 4, fin), BF)], [], "pack"
    )(columns, col_slot.reshape(lanes), column_live.reshape(lanes), col_weight.reshape(lanes))
    packed = exchange(packed)

    grid_at, grid_count = lax.axis_index("grid"), lax.axis_size("grid")
    dom_at, dom_count = lax.axis_index("dom"), lax.axis_size("dom")
    odd_grid, odd_dom = grid_at % 2, dom_at % 2
    up, down = grid_at > 0, grid_at < grid_count - 1
    flags = jnp.stack(
        [
            up,
            down,
            dom_at > 0,
            dom_at < dom_count - 1,
            jnp.where(odd_grid == 1, up, down),
            jnp.where(odd_grid == 1, down, up),
            odd_grid == 1,
            odd_dom == 1,
        ]
    ).astype(F32)
    edge_scale = edge_weight * edge_live.astype(F32)
    edge_rows = jnp.stack([edge_src.astype(F32), edge_dst.astype(F32), edge_scale])
    bound = boundary_idx.astype(F32)[None]
    enc_in_t = enc_in.T
    src_t = src_proj.transpose(0, 2, 1)
    dst_t = dst_proj.transpose(0, 2, 1)

    node_picks = pltpu.VMEM((nodes, chunk), BF)
    own_picks = pltpu.VMEM((2 * nodes, chunk), BF)
    ext_picks = pltpu.VMEM((ext, chunk), BF)
    all_picks = pltpu.VMEM((ext + nodes, chunk), BF)
    rim_picks = pltpu.VMEM((nodes, rim), BF)
    node_acc = pltpu.VMEM((nodes, width), F32)
    own_acc = pltpu.VMEM((2 * nodes, width), F32)
    ext_acc = pltpu.VMEM((ext, width), F32)
    full = pltpu.VMEM((width, ext), BF)
    node_shape = ((nodes, width), BF)
    rim_shape = ((rim, width), BF)
    tables = [node_shape, ((width, 2 * nodes), BF), rim_shape]
    edge_shape = ((width, edges), BF)
    edge_wide = ((width, edges), F32)

    (back1,) = call(back_body, [edge_wide], [node_picks], "back")(
        msg_proj[1], node_cotangent, edge_rows
    )

    at = (grid_at * dom_count + dom_at) % (LANES // bucket)
    extra = lax.dynamic_slice_in_dim(packed[:, bucket : bucket + 4], at * bucket, bucket, 2)
    extra = extra.astype(F32).transpose(1, 0, 2).reshape(4, cols)
    col_rows = jnp.stack([extra[0] * 256.0 + extra[1], extra[2] + extra[3]])

    pooled, col_slope, state0, table0, rim0 = call(
        functools.partial(encode_body, bucket),
        [node_shape, ((width, cols), BF)] + tables,
        [node_picks, rim_picks, node_acc],
        "encode",
    )(packed, col_rows, enc_in_t, enc_out, node_static, src_t[0], dst_t[0], bound)

    rims0 = from_neighbours(rim0)
    (pre0,) = call(own_body, [edge_wide], [own_picks], "own")(table0, edge_rows)
    slope0, act0, state1, table1, rim1 = call(
        forward_body,
        [edge_shape, node_shape] + tables,
        [full, all_picks, rim_picks, node_acc],
        "forward",
        True,
    )(flags, *rims0, pre0, edge_rows, state0, src_t[0], msg_proj[0], src_t[1], dst_t[1], bound)

    rims1 = from_neighbours(rim1)
    (pre1,) = call(own_body, [edge_wide], [own_picks], "own")(table1, edge_rows)
    act_edges1, grad_pre1, *sends1 = call(
        functools.partial(turn_body, node_count=nodes),
        [edge_shape, edge_shape] + [rim_shape] * 4,
        [full, ext_picks, ext_acc],
        "turn",
        True,
    )(flags, *rims1, pre1, back1, edge_rows, src_t[1])

    returned1 = to_neighbours(sends1)
    own_shape = ((2 * nodes, width), BF)
    halves = [((3 * width, width // 2), BF)] * 2
    (own1,) = call(sums_body, [own_shape], [own_picks, own_acc], "sums")(edge_rows, grad_pre1)
    act1, node_out = call(out_body, [node_shape, node_shape], [node_picks, node_acc], "out")(
        edge_rows, act_edges1, state1, msg_proj[1]
    )
    keep1, send1 = call(terms_body, halves, [], "terms", True)(
        flags, *rims1, *sends1, state1, own1, act1, node_cotangent
    )
    grad1, grad_pre0, *sends0 = call(
        backward_body,
        [((nodes, width), F32), edge_shape] + [rim_shape] * 4,
        [all_picks, rim_picks, ext_acc],
        "backward",
        True,
    )(
        flags,
        *returned1,
        own1,
        bound,
        src_proj[1],
        dst_proj[1],
        node_cotangent,
        edge_rows,
        msg_proj[0],
        slope0,
    )

    returned0 = to_neighbours(sends0)
    (own0,) = call(sums_body, [own_shape], [own_picks, own_acc], "sums")(edge_rows, grad_pre0)
    keep0, send0 = call(terms_body, halves, [], "terms", True)(
        flags, *rims0, *sends0, state0, own0, act0, grad1
    )
    hidden = enc_out.shape[0]
    keep_enc, send_enc = call(
        functools.partial(last_body, bucket),
        [((fin + hidden, width // 2), BF)] * 2,
        [node_picks, rim_picks, pltpu.VMEM((width, fin), F32)],
        "last",
        True,
    )(
        flags,
        *returned0,
        own0,
        bound,
        src_proj[0],
        dst_proj[0],
        grad1,
        col_rows,
        packed,
        enc_out,
        pooled,
        col_slope,
    )

    total_rows = 2 * 3 * width + fin + hidden
    share = -(-total_rows // (16 * peers)) * 16
    rows = peers * share
    (merged,) = call(merge_body, [((rows, width // 2), BF)], [], "merge")(
        keep1,
        swapped(send1, "dom", 0),
        keep0,
        swapped(send0, "dom", 0),
        keep_enc,
        swapped(send_enc, "dom", 0),
    )
    parts = exchange(merged.reshape(peers, share, width // 2))
    (spread,) = call(share_body, [((peers, share, width // 2), BF)], [], "share")(parts)
    mine = exchange(spread).reshape(rows, width // 2)
    layer_shape = ((2, width, width), F32)
    grads = call(
        unpack_body,
        [((fin, width), F32), ((hidden, width), F32), layer_shape, layer_shape, layer_shape],
        [],
        "unpack",
        True,
    )(flags, mine, swapped(mine, "dom", 0))
    return (node_out, *grads)


def solution(mesh):
    rows = P(AXES, None)
    flat = P(AXES)
    placed = (rows, flat, flat, flat, rows, flat, flat, flat, flat, flat, P(), P(), P(), P(), P(), rows)
    return jax.shard_map(
        per_device,
        mesh=mesh,
        in_specs=placed,
        out_specs=(rows, P(), P(), P(), P(), P()),
        check_vma=False,
    )
```

time: 202 us -> 134 us (0.66)
  waiting for transfers between devices: 86.2 us -> 22.6 us
  blocking collectives: 0 us -> 39 us
  starting transfers between devices: 44.9 us -> 28.7 us
  Pallas kernels: 52.1 us -> 37.7 us
  local copies, waits for them, and re-layouts: 11.9 us -> 3.93 us
  other arithmetic: 5.41 us -> 0.28 us
    all_to_all x7 -> x1, waiting for transfers between devices: 60.2 us -> 16 us  [exchange(): return lax.all_to_all(shard, AXES, split_axis=0, concat_axis=0, tiled=True)]
    all_to_all x0 -> x2, blocking collectives: none -> 39 us  [exchange(): return lax.all_to_all(shard, AXES, split_axis=0, concat_axis=0, tiled=True)]
    ppermute x16 -> x8, waiting for transfers between devices: 26 us -> 2.04 us  [turned(): lax.ppermute(shard, axis, [(i, (i + by) % count) for i in range(count)])]
    all_to_all x7 -> x1, starting transfers between devices: 25.2 us -> 7.33 us  [exchange(): return lax.all_to_all(shard, AXES, split_axis=0, concat_axis=0, tiled=True)]
    pallas_call x12 -> x17, Pallas kernels: 52.1 us -> 37.7 us  [run(): pl.pallas_call(body, out_shape=tuple((jax.ShapeDtypeStruct(shape, dtype)...]
    ppermute x0 -> x12, starting transfers between devices: none -> 13.1 us  [swapped(): return lax.ppermute(shard, axis, list(enumerate(partner)))]
    ppermute x16 -> x8, starting transfers between devices: 19.7 us -> 8.34 us  [turned(): lax.ppermute(shard, axis, [(i, (i + by) % count) for i in range(count)])]
    ppermute x0 -> x12, waiting for transfers between devices: none -> 4.49 us  [swapped(): return lax.ppermute(shard, axis, list(enumerate(partner)))]
  transfers between devices with their start and end apart: 23 -> 21, of which waited for: 17 -> 5; matrix products, arithmetic and copies ran while one was open for 4% -> 0% of each run, Pallas kernels for 12% -> 13%
where the time goes in v2:
time: 134 us; the launch traced here: 133 us
  blocking collectives  39 us (29%)
  Pallas kernels  37.7 us (28%)
  starting transfers between devices  28.7 us (21%)
  waiting for transfers between devices  22.6 us (17%)
  local copies, waits for them, and re-layouts  3.93 us (3%)
    all_to_all x2, blocking collectives, exchange(): return lax.all_to_all(shard, AXES, split_axis=0, concat_axis=0, tiled=True)  39 us
    pallas_call x17, Pallas kernels, run(): pl.pallas_call(body, out_shape=tuple((jax.ShapeDtypeStruct(shape, dtype)...  37.7 us
    all_to_all x1, waiting for transfers between devices, exchange(): return lax.all_to_all(shard, AXES, split_axis=0, concat_axis=0, tiled=True)  16 us
    ppermute x12, starting transfers between devices, swapped(): return lax.ppermute(shard, axis, list(enumerate(partner)))  13.1 us
    ppermute x8, starting transfers between devices, turned(): lax.ppermute(shard, axis, [(i, (i + by) % count) for i in range(count)])  8.34 us
    all_to_all x1, starting transfers between devices, exchange(): return lax.all_to_all(shard, AXES, split_axis=0, concat_axis=0, tiled=True)  7.33 us
    ppermute x12, waiting for transfers between devices, swapped(): return lax.ppermute(shard, axis, list(enumerate(partner)))  4.49 us
    unnamed x35, local copies, waits for them, and re-layouts  3.56 us
  transfers between devices with their start and end apart: 21, of which 5 were waited for; matrix products, arithmetic and copies ran while one was open for 0% of the time, Pallas kernels for 13%

profile of v2, /device:TPU:0, one launch (start us, length us, event | category | flops | bytes accessed | tf_op | source)
XLA Modules:
  0.0 133.4 jit_solution(318359694622714309)
XLA Ops:
  0.7 1.0 copy-done.2
  1.7 0.7 copy-done.4
  2.4 0.7 copy-done.5
  3.1 0.7 copy-done.6
  3.8 0.9 pack.1
  4.7 7.3 %all-to-all-start = ((bf16[32,68,128]{2,1,0:T(8,128)(2,1)}), bf16[32,68,128]{2,1,0:T(8,128)(2,1)S(1)}, u32[]{:S(2)}, u32[]{:S(2)}) async-start(bf16[32,68,128]{2,1,0:T(8,128)(2,1)} %pack.1), calls=%async_computation | async-start | bytes 1179648 | tf_op jit(solution)/shard_map/all_to_all | solution.py:509
  12.1 0.1 copy.23
  12.3 0.1 copy.24
  12.4 0.1 copy.22
  12.6 0.1 stack.56
  12.8 16.0 %all-to-all-done.packed_ref = bf16[32,68,128]{2,1,0:T(8,128)(2,1)S(1)} async-done(((bf16[32,68,128]{2,1,0:T(8,128)(2,1)}), bf16[32,68,128]{2,1,0:T(8,128)(2,1)S(1)}, u32[]{:S(2)}, u32[]{:S(2)}) %all-to-all-start) | async-done | bytes 557088 | tf_op jit(solution)/shard_map/all_to_all | solution.py:509
  28.9 0.1 convert_bitcast_fusion
  29.0 0.1 fusion.1
  29.1 0.1 add.48
  29.2 0.1 add.50
  29.3 3.2 %encode.1 = (bf16[512,256]{1,0:T(8,128)(2,1)S(1)}, bf16[256,2048]{1,0:T(8,128)(2,1)S(1)}, bf16[512,256]{1,0:T(8,128)(2,1)S(1)}, bf16[256,1024]{1,0:T(8,128)(2,1)S(1)}, bf16[256,256]{1,0:T(8,128)(2,1)S(1)}) custom-call(bf16[32,68,128]{2,1,0:T(8,128)(2,1)S(1)} %all-to-all-done.packed_ref, f32[2,2048]{1,0:T(2,128)S(1)} %pad_maximum_fusion.1.rows_ref, ...), custom_call_target="tpu_custom_call" | custom-call | tf_op jit(solution)/shard_map/encode/pallas_call | solution.py:52
  32.5 1.4 %collective-permute-start = (bf16[256,256]{1,0:T(8,128)(2,1)S(1)}, bf16[256,256]{1,0:T(8,128)(2,1)S(1)}, u32[]{:S(2)}, u32[]{:S(2)}) collective-permute-start(bf16[256,256]{1,0:T(8,128)(2,1)S(1)} %get-tuple-element.41), channel_id=1, source_target_pairs={{0,8},{8,0},{16,24},{24,16},{1,9},{9,1},{17,25},{25,17},{2,10},{10... | collective-permute-start | bytes 393224 | tf_op jit(solution)/shard_map/ppermute | solution.py:522
  34.0 0.7 collective-permute-start.1
  34.6 0.1 collective-permute-start.2
  34.7 2.6 %collective-permute-start.3 = (bf16[256,256]{1,0:T(8,128)(2,1)S(1)}, bf16[256,256]{1,0:T(8,128)(2,1)S(1)}, u32[]{:S(2)}, u32[]{:S(2)}) collective-permute-start(bf16[256,256]{1,0:T(8,128)(2,1)S(1)} %get-tuple-element.41), channel_id=1, source_target_pairs={{0,7},{1,0},{2,1},{3,2},{4,3},{5,4},{6,5},{7,6},{8,15},{9,8},{10,9... | collective-permute-start | bytes 393224 | tf_op jit(solution)/shard_map/ppermute | solution.py:514
  37.3 1.8 %own.2.own_pre_ref = f32[256,2048]{1,0:T(8,128)S(1)} custom-call(bf16[256,1024]{1,0:T(8,128)(2,1)S(1)} %get-tuple-element.42.table_ref, f32[3,2048]{1,0:T(4,128)S(1)} %pad_maximum_fusion.rows_ref), custom_call_target="tpu_custom_call" | custom-call | tf_op jit(solution)/shard_map/own/pallas_call | solution.py:52
  39.1 0.0 copy-start
  39.1 0.0 collective-permute-done.first_ref
  39.2 2.0 %collective-permute-done.2.left_ref = bf16[256,256]{1,0:T(8,128)(2,1)S(1)} collective-permute-done((bf16[256,256]{1,0:T(8,128)(2,1)S(1)}, bf16[256,256]{1,0:T(8,128)(2,1)S(1)}, u32[]{:S(2)}, u32[]{:S(2)}) %collective-permute-start.2) | collective-permute-done | bytes 131104 | tf_op jit(solution)/shard_map/ppermute | solution.py:514
  41.2 5.0 %forward.1 = (bf16[256,2048]{1,0:T(8,128)(2,1)S(1)}, bf16[512,256]{1,0:T(8,128)(2,1)S(1)}, bf16[512,256]{1,0:T(8,128)(2,1)S(1)}, bf16[256,1024]{1,0:T(8,128)(2,1)S(1)}, bf16[256,256]{1,0:T(8,128)(2,1)S(1)}) custom-call(f32[8]{0:T(128)S(1)} %convert_element_type.19.flags_ref, bf16[256,256]{1,0:T(8,128)(2,1)S(1)} %collective-permute-done.first_ref, ...), custom_call_target="tpu_custom_call" | custom-call | tf_op jit(solution)/shard_map/forward/pallas_call | solution.py:52
  46.2 0.9 collective-permute-start.4
  47.1 0.7 collective-permute-start.5
  47.8 1.0 collective-permute-start.6
  48.8 1.7 %collective-permute-start.7 = (bf16[256,256]{1,0:T(8,128)(2,1)S(1)}, bf16[256,256]{1,0:T(8,128)(2,1)S(1)}, u32[]{:S(2)}, u32[]{:S(2)}) collective-permute-start(bf16[256,256]{1,0:T(8,128)(2,1)S(1)} %get-tuple-element.44), channel_id=1, source_target_pairs={{0,7},{1,0},{2,1},{3,2},{4,3},{5,4},{6,5},{7,6},{8,15},{9,8},{10,9... | collective-permute-start | bytes 393224 | tf_op jit(solution)/shard_map/ppermute | solution.py:514
  50.5 1.5 %back.1.back_ref = f32[256,2048]{1,0:T(8,128)S(1)} custom-call(bf16[256,256]{1,0:T(8,128)(2,1)S(1)} %get-tuple-element.82.msg_ref, bf16[512,256]{1,0:T(8,128)(2,1)S(1)} %copy-done, f32[3,2048]{1,0:T(4,128)S(1)} %pad_maximum_fusion.rows_ref), custom_call_target="tpu_custom_call" | custom-call | tf_op jit(solution)/shard_map/back/pallas_call | solution.py:52
  52.0 1.8 %own.3.own_pre_ref = f32[256,2048]{1,0:T(8,128)S(1)} custom-call(bf16[256,1024]{1,0:T(8,128)(2,1)S(1)} %get-tuple-element.45.table_ref, f32[3,2048]{1,0:T(4,128)S(1)} %pad_maximum_fusion.rows_ref), custom_call_target="tpu_custom_call" | custom-call | tf_op jit(solution)/shard_map/own/pallas_call | solution.py:52
  53.8 0.0 collective-permute-done.4.first_ref
  53.8 0.0 collective-permute-done.5.second_ref
  53.8 0.0 collective-permute-done.7.right_ref
  53.8 5.2 %turn.1 = (bf16[256,2048]{1,0:T(8,128)(2,1)S(1)}, bf16[256,2048]{1,0:T(8,128)(2,1)S(1)}, bf16[256,256]{1,0:T(8,128)(2,1)S(1)}, bf16[256,256]{1,0:T(8,128)(2,1)S(...) custom-call(f32[8]{0:T(128)S(1)} %convert_element_type.19.flags_ref, ...), custom_call_target="tpu_custom_call" | custom-call | tf_op jit(solution)/shard_map/turn/pallas_call | solution.py:52
  59.0 0.7 collective-permute-start.10
  59.7 2.0 %collective-permute-start.11 = (bf16[256,256]{1,0:T(8,128)(2,1)S(1)}, bf16[256,256]{1,0:T(8,128)(2,1)S(1)}, u32[]{:S(2)}, u32[]{:S(2)}) collective-permute-start(bf16[256,256]{1,0:T(8,128)(2,1)S(1)} %get-tuple-element.51.send2_ref), channel_id=1, source_target_pairs={{0,7},{1,0},{2,1},{3,2},{4,3},{5,4},{6,5},{7,6},{8,15},{9,8},{10,9... | collective-permute-start | bytes 393224 | tf_op jit(solution)/shard_map/ppermute | solution.py:514
  61.7 0.0 collective-permute-start.12
  61.7 5.4 %collective-permute-start.9 = (bf16[256,256]{1,0:T(8,128)(2,1)S(1)}, bf16[256,256]{1,0:T(8,128)(2,1)S(1)}, u32[]{:S(2)}, u32[]{:S(2)}) collective-permute-start(bf16[256,256]{1,0:T(8,128)(2,1)S(1)} %get-tuple-element.49.send0_ref), channel_id=1, source_target_pairs={{0,8},{8,0},{16,24},{24,16},{1,9},{9,1},{17,25},{25,17},{2,10},{10... | collective-permute-start | bytes 393224 | tf_op jit(solution)/shard_map/ppermute | solution.py:522
  67.1 2.0 %sums.2.own_ref = bf16[1024,256]{1,0:T(8,128)(2,1)S(1)} custom-call(f32[3,2048]{1,0:T(4,128)S(1)} %pad_maximum_fusion.rows_ref, bf16[256,2048]{1,0:T(8,128)(2,1)S(1)} %get-tuple-element.53.grad_pre_ref), custom_call_target="tpu_custom_call" | custom-call | tf_op jit(solution)/shard_map/sums/pallas_call | solution.py:52
  69.2 0.0 collective-permute-done.11.left_ref
  69.2 0.0 collective-permute-done.12.right_ref
  69.2 1.3 collective-permute-done.9.first_ref
  70.5 4.3 %backward.1 = (f32[512,256]{1,0:T(8,128)S(1)}, bf16[256,2048]{1,0:T(8,128)(2,1)S(1)}, bf16[256,256]{1,0:T(8,128)(2,1)S(1)}, bf16[256,256]{1,0:T(8,128)(2,1)S(1)}...) custom-call(f32[8]{0:T(128)S(1)} %convert_element_type.19.flags_ref, ...), custom_call_target="tpu_custom_call" | custom-call | tf_op jit(solution)/shard_map/backward/pallas_call | solution.py:52
  74.8 2.0 %collective-permute-start.14 = (bf16[256,256]{1,0:T(8,128)(2,1)S(1)}, bf16[256,256]{1,0:T(8,128)(2,1)S(1)}, u32[]{:S(2)}, u32[]{:S(2)}) collective-permute-start(bf16[256,256]{1,0:T(8,128)(2,1)S(1)} %get-tuple-element.58.send0_ref), channel_id=1, source_target_pairs={{0,8},{8,0},{16,24},{24,16},{1,9},{9,1},{17,25},{25,17},{2,10},{10... | collective-permute-start | bytes 393224 | tf_op jit(solution)/shard_map/ppermute | solution.py:522
  76.7 0.7 collective-permute-start.15
  77.4 0.9 collective-permute-start.16
  78.3 0.0 collective-permute-start.17
  78.3 2.3 %out.1 = (bf16[512,256]{1,0:T(8,128)(2,1)S(1)}, bf16[512,256]{1,0:T(8,128)(2,1)}) custom-call(f32[3,2048]{1,0:T(4,128)S(1)} %pad_maximum_fusion.rows_ref, bf16[256,2048]{1,0:T(8,128)(2,1)S(1)} %get-tuple-element.46.act_edges_ref, bf16[512,256]{1,0:T(8,128)(2,1)S(1)} %get-tuple-element.47.state_ref, bf16[256,256]{1,0:T(8,128)(2,1)S(1)} %get-tuple-element.82.msg_ref), custom_call_target="tpu_custom_call" | custom-call | tf_op jit(solution)/shard_map/out/pallas_call | solution.py:52
  80.7 1.1 terms.2
  81.8 0.1 collective-permute-start.8
  81.9 2.0 %sums.3.own_ref = bf16[1024,256]{1,0:T(8,128)(2,1)S(1)} custom-call(f32[3,2048]{1,0:T(4,128)S(1)} %pad_maximum_fusion.rows_ref, bf16[256,2048]{1,0:T(8,128)(2,1)S(1)} %get-tuple-element.62.grad_pre_ref), custom_call_target="tpu_custom_call" | custom-call | tf_op jit(solution)/shard_map/sums/pallas_call | solution.py:52
  83.9 1.1 terms.3
  85.0 0.6 collective-permute-start.13
  85.6 0.0 collective-permute-done.15.second_ref
  85.6 3.4 %last.1 = (bf16[384,128]{1,0:T(8,128)(2,1)S(1)}, bf16[384,128]{1,0:T(8,128)(2,1)S(1)}) custom-call(f32[8]{0:T(128)S(1)} %convert_element_type.19.flags_ref, bf16[256,256]{1,0:T(8,128)(2,1)S(1)} %collective-permute-done.14.first_ref, bf16[256,256]{1,0:T(8,128)(2,1)S(1)} %collective-permute-done.15.second_ref, ...), custom_call_target="tpu_custom_call" | custom-call | tf_op jit(solution)/shard_map/last/pallas_call | solution.py:52
  89.0 0.1 collective-permute-start.18
  89.2 1.3 collective-permute-done.18.refs_5_
  90.4 0.1 merge.1
  90.5 20.6 %all_to_all.15.parts_ref = bf16[32,64,128]{2,1,0:T(8,128)(2,1)S(1)} all-to-all(bf16[32,64,128]{2,1,0:T(8,128)(2,1)S(1)} %bitcast.42), channel_id=1, replica_groups=mesh['grid'=4,'dom'=8] {'grid','dom'}, dimensions={0} | all-to-all | bytes 1048576 | tf_op jit(solution)/shard_map/all_to_all | solution.py:509
  111.2 0.1 share.1
  111.3 18.4 %all_to_all.16 = bf16[32,64,128]{2,1,0:T(8,128)(2,1)S(1)} all-to-all(bf16[32,64,128]{2,1,0:T(8,128)(2,1)S(1)} %share.1), channel_id=1, replica_groups=mesh['grid'=4,'dom'=8] {'grid','dom'}, dimensions={0} | all-to-all | bytes 1048576 | tf_op jit(solution)/shard_map/all_to_all | solution.py:509
  129.7 1.9 %collective-permute-done.19.other_ref = bf16[2048,128]{1,0:T(8,128)(2,1)S(1)} collective-permute-done((bf16[2048,128]{1,0:T(8,128)(2,1)S(1)}, bf16[2048,128]{1,0:T(8,128)(2,1)S(1)}, u32[]{:S(2)}, u32[]{:S(2)}) %collective-permute-start.19) | collective-permute-done | bytes 524320 | tf_op jit(solution)/shard_map/ppermute | solution.py:522
  131.6 1.8 %unpack.1 = (f32[128,256]{1,0:T(8,128)}, f32[256,256]{1,0:T(8,128)}, f32[2,256,256]{2,1,0:T(8,128)}, f32[2,256,256]{2,1,0:T(8,128)}, f32[2,256,256]{2,1,0:T(8,128)}) custom-call(f32[8]{0:T(128)S(1)} %convert_element_type.19.flags_ref, bf16[2048,128]{1,0:T(8,128)(2,1)S(1)} %bitcast.44, bf16[2048,128]{1,0:T(8,128)(2,1)S(1)} %collective-permute-done.19.other_ref), custom_call_target="tpu_custom_call" | custom-call | tf_op jit(solution)/shard_map/unpack/pallas_call | solution.py:52
  (48 shorter events, 0.2 us)
Async XLA Ops:
  0.6 11.8 %copy-start.15 = (s32[256]{0:T(256)S(1)}, s32[256]{0:T(256)}, u32[]{:S(2)}) copy-start(s32[256]{0:T(256)} %param.21) | copy-start | bytes 3076
  0.6 1.0 copy-start.2
  1.7 0.7 copy-start.4
  2.4 0.7 copy-start.5
  3.1 0.7 copy-start.6
  3.8 8.3 %copy-start.8 = (bf16[2,256,256]{2,1,0:T(8,128)(2,1)S(1)}, bf16[2,256,256]{2,1,0:T(8,128)(2,1)}, u32[]{:S(2)}) copy-start(bf16[2,256,256]{2,1,0:T(8,128)(2,1)} %param.28) | copy-start | bytes 786436
  3.8 8.5 %copy-start.7 = (bf16[2,256,256]{2,1,0:T(8,128)(2,1)S(1)}, bf16[2,256,256]{2,1,0:T(8,128)(2,1)}, u32[]{:S(2)}) copy-start(bf16[2,256,256]{2,1,0:T(8,128)(2,1)} %param.29) | copy-start | bytes 786436
  3.8 8.6 %copy-start.10 = (bf16[128,256]{1,0:T(8,128)(2,1)S(1)}, bf16[128,256]{1,0:T(8,128)(2,1)}, u32[]{:S(2)}) copy-start(bf16[128,256]{1,0:T(8,128)(2,1)} %param.26) | copy-start | bytes 196612
  3.8 8.7 %copy-start.13 = (s32[2048]{0:T(1024)S(1)}, s32[2048]{0:T(1024)}, u32[]{:S(2)}) copy-start(s32[2048]{0:T(1024)} %param.22) | copy-start | bytes 24580
  3.8 8.8 %copy-start.14 = (s32[2048]{0:T(1024)S(1)}, s32[2048]{0:T(1024)}, u32[]{:S(2)}) copy-start(s32[2048]{0:T(1024)} %param.23) | copy-start | bytes 24580
  3.8 8.9 %copy-start.11 = (f32[2048]{0:T(1024)S(1)}, f32[2048]{0:T(1024)}, u32[]{:S(2)}) copy-start(f32[2048]{0:T(1024)} %param.25) | copy-start | bytes 24580
  3.8 8.9 %copy-start.12 = (s32[2048]{0:T(1024)S(1)}, s32[2048]{0:T(1024)}, u32[]{:S(2)}) copy-start(s32[2048]{0:T(1024)} %param.24) | copy-start | bytes 24580
  3.8 8.9 %copy-start.9 = (bf16[2,256,256]{2,1,0:T(8,128)(2,1)S(1)}, bf16[2,256,256]{2,1,0:T(8,128)(2,1)}, u32[]{:S(2)}) copy-start(bf16[2,256,256]{2,1,0:T(8,128)(2,1)} %param.30) | copy-start | bytes 786436
  4.7 24.6 %copy-start.1 = (bf16[256,256]{1,0:T(8,128)(2,1)S(1)}, bf16[256,256]{1,0:T(8,128)(2,1)}, u32[]{:S(2)}) copy-start(bf16[256,256]{1,0:T(8,128)(2,1)} %enc_out_ref.3) | copy-start | bytes 393220
  4.7 24.6 %copy-start.3 = (bf16[512,256]{1,0:T(8,128)(2,1)S(1)}, bf16[512,256]{1,0:T(8,128)(2,1)}, u32[]{:S(2)}) copy-start(bf16[512,256]{1,0:T(8,128)(2,1)} %static_ref.1) | copy-start | bytes 786436
  4.7 24.1 %all-to-all-start = ((bf16[32,68,128]{2,1,0:T(8,128)(2,1)}), bf16[32,68,128]{2,1,0:T(8,128)(2,1)S(1)}, u32[]{:S(2)}, u32[]{:S(2)}) async-start(bf16[32,68,128]{2,1,0:T(8,128)(2,1)} %pack.1), calls=%async_computation | async-start | bytes 1179648 | tf_op jit(solution)/shard_map/all_to_all | solution.py:509
  32.5 6.6 %collective-permute-start = (bf16[256,256]{1,0:T(8,128)(2,1)S(1)}, bf16[256,256]{1,0:T(8,128)(2,1)S(1)}, u32[]{:S(2)}, u32[]{:S(2)}) collective-permute-start(bf16[256,256]{1,0:T(8,128)(2,1)S(1)} %get-tuple-element.41), channel_id=1, source_target_pairs={{0,8},{8,0},{16,24},{24,16},{1,9},{9,1},{17,25},{25,17},{2,10},{10... | collective-permute-start | bytes 393224 | tf_op jit(solution)/shard_map/ppermute | solution.py:522
  34.0 5.2 %collective-permute-start.1 = (bf16[256,256]{1,0:T(8,128)(2,1)S(1)}, bf16[256,256]{1,0:T(8,128)(2,1)S(1)}, u32[]{:S(2)}, u32[]{:S(2)}) collective-permute-start(bf16[256,256]{1,0:T(8,128)(2,1)S(1)} %get-tuple-element.41), channel_id=1, source_target_pairs={{0,0},{8,16},{16,8},{24,24},{1,1},{9,17},{17,9},{25,25},{2,2},{10,... | collective-permute-start | bytes 393224 | tf_op jit(solution)/shard_map/ppermute | solution.py:522
  34.6 6.6 %collective-permute-start.2 = (bf16[256,256]{1,0:T(8,128)(2,1)S(1)}, bf16[256,256]{1,0:T(8,128)(2,1)S(1)}, u32[]{:S(2)}, u32[]{:S(2)}) collective-permute-start(bf16[256,256]{1,0:T(8,128)(2,1)S(1)} %get-tuple-element.41), channel_id=1, source_target_pairs={{0,1},{1,2},{2,3},{3,4},{4,5},{5,6},{6,7},{7,0},{8,9},{9,10},{10,1... | collective-permute-start | bytes 393224 | tf_op jit(solution)/shard_map/ppermute | solution.py:514
  34.7 6.5 %collective-permute-start.3 = (bf16[256,256]{1,0:T(8,128)(2,1)S(1)}, bf16[256,256]{1,0:T(8,128)(2,1)S(1)}, u32[]{:S(2)}, u32[]{:S(2)}) collective-permute-start(bf16[256,256]{1,0:T(8,128)(2,1)S(1)} %get-tuple-element.41), channel_id=1, source_target_pairs={{0,7},{1,0},{2,1},{3,2},{4,3},{5,4},{6,5},{7,6},{8,15},{9,8},{10,9... | collective-permute-start | bytes 393224 | tf_op jit(solution)/shard_map/ppermute | solution.py:514
  39.1 11.4 %copy-start = (bf16[512,256]{1,0:T(8,128)(2,1)S(1)}, bf16[512,256]{1,0:T(8,128)(2,1)}, u32[]{:S(2)}) copy-start(bf16[512,256]{1,0:T(8,128)(2,1)} %grad_ref.5) | copy-start | bytes 786436
  46.2 7.6 %collective-permute-start.4 = (bf16[256,256]{1,0:T(8,128)(2,1)S(1)}, bf16[256,256]{1,0:T(8,128)(2,1)S(1)}, u32[]{:S(2)}, u32[]{:S(2)}) collective-permute-start(bf16[256,256]{1,0:T(8,128)(2,1)S(1)} %get-tuple-element.44), channel_id=1, source_target_pairs={{0,8},{8,0},{16,24},{24,16},{1,9},{9,1},{17,25},{25,17},{2,10},{10... | collective-permute-start | bytes 393224 | tf_op jit(solution)/shard_map/ppermute | solution.py:522
  47.1 6.7 %collective-permute-start.5 = (bf16[256,256]{1,0:T(8,128)(2,1)S(1)}, bf16[256,256]{1,0:T(8,128)(2,1)S(1)}, u32[]{:S(2)}, u32[]{:S(2)}) collective-permute-start(bf16[256,256]{1,0:T(8,128)(2,1)S(1)} %get-tuple-element.44), channel_id=1, source_target_pairs={{0,0},{8,16},{16,8},{24,24},{1,1},{9,17},{17,9},{25,25},{2,2},{10,... | collective-permute-start | bytes 393224 | tf_op jit(solution)/shard_map/ppermute | solution.py:522
  47.8 6.0 %collective-permute-start.6 = (bf16[256,256]{1,0:T(8,128)(2,1)S(1)}, bf16[256,256]{1,0:T(8,128)(2,1)S(1)}, u32[]{:S(2)}, u32[]{:S(2)}) collective-permute-start(bf16[256,256]{1,0:T(8,128)(2,1)S(1)} %get-tuple-element.44), channel_id=1, source_target_pairs={{0,1},{1,2},{2,3},{3,4},{4,5},{5,6},{6,7},{7,0},{8,9},{9,10},{10,1... | collective-permute-start | bytes 393224 | tf_op jit(solution)/shard_map/ppermute | solution.py:514
  48.8 5.1 %collective-permute-start.7 = (bf16[256,256]{1,0:T(8,128)(2,1)S(1)}, bf16[256,256]{1,0:T(8,128)(2,1)S(1)}, u32[]{:S(2)}, u32[]{:S(2)}) collective-permute-start(bf16[256,256]{1,0:T(8,128)(2,1)S(1)} %get-tuple-element.44), channel_id=1, source_target_pairs={{0,7},{1,0},{2,1},{3,2},{4,3},{5,4},{6,5},{7,6},{8,15},{9,8},{10,9... | collective-permute-start | bytes 393224 | tf_op jit(solution)/shard_map/ppermute | solution.py:514
  59.0 10.2 %collective-permute-start.10 = (bf16[256,256]{1,0:T(8,128)(2,1)S(1)}, bf16[256,256]{1,0:T(8,128)(2,1)S(1)}, u32[]{:S(2)}, u32[]{:S(2)}) collective-permute-start(bf16[256,256]{1,0:T(8,128)(2,1)S(1)} %get-tuple-element.50.send1_ref), channel_id=1, source_target_pairs={{0,0},{8,16},{16,8},{24,24},{1,1},{9,17},{17,9},{25,25},{2,2},{10,... | collective-permute-start | bytes 393224 | tf_op jit(solution)/shard_map/ppermute | solution.py:522
  59.7 9.5 %collective-permute-start.11 = (bf16[256,256]{1,0:T(8,128)(2,1)S(1)}, bf16[256,256]{1,0:T(8,128)(2,1)S(1)}, u32[]{:S(2)}, u32[]{:S(2)}) collective-permute-start(bf16[256,256]{1,0:T(8,128)(2,1)S(1)} %get-tuple-element.51.send2_ref), channel_id=1, source_target_pairs={{0,7},{1,0},{2,1},{3,2},{4,3},{5,4},{6,5},{7,6},{8,15},{9,8},{10,9... | collective-permute-start | bytes 393224 | tf_op jit(solution)/shard_map/ppermute | solution.py:514
  61.7 7.5 %collective-permute-start.12 = (bf16[256,256]{1,0:T(8,128)(2,1)S(1)}, bf16[256,256]{1,0:T(8,128)(2,1)S(1)}, u32[]{:S(2)}, u32[]{:S(2)}) collective-permute-start(bf16[256,256]{1,0:T(8,128)(2,1)S(1)} %get-tuple-element.52.send3_ref), channel_id=1, source_target_pairs={{0,1},{1,2},{2,3},{3,4},{4,5},{5,6},{6,7},{7,0},{8,9},{9,10},{10,1... | collective-permute-start | bytes 393224 | tf_op jit(solution)/shard_map/ppermute | solution.py:514
  61.7 8.8 %collective-permute-start.9 = (bf16[256,256]{1,0:T(8,128)(2,1)S(1)}, bf16[256,256]{1,0:T(8,128)(2,1)S(1)}, u32[]{:S(2)}, u32[]{:S(2)}) collective-permute-start(bf16[256,256]{1,0:T(8,128)(2,1)S(1)} %get-tuple-element.49.send0_ref), channel_id=1, source_target_pairs={{0,8},{8,0},{16,24},{24,16},{1,9},{9,1},{17,25},{25,17},{2,10},{10... | collective-permute-start | bytes 393224 | tf_op jit(solution)/shard_map/ppermute | solution.py:522
  74.8 10.2 %collective-permute-start.14 = (bf16[256,256]{1,0:T(8,128)(2,1)S(1)}, bf16[256,256]{1,0:T(8,128)(2,1)S(1)}, u32[]{:S(2)}, u32[]{:S(2)}) collective-permute-start(bf16[256,256]{1,0:T(8,128)(2,1)S(1)} %get-tuple-element.58.send0_ref), channel_id=1, source_target_pairs={{0,8},{8,0},{16,24},{24,16},{1,9},{9,1},{17,25},{25,17},{2,10},{10... | collective-permute-start | bytes 393224 | tf_op jit(solution)/shard_map/ppermute | solution.py:522
  76.7 8.8 %collective-permute-start.15 = (bf16[256,256]{1,0:T(8,128)(2,1)S(1)}, bf16[256,256]{1,0:T(8,128)(2,1)S(1)}, u32[]{:S(2)}, u32[]{:S(2)}) collective-permute-start(bf16[256,256]{1,0:T(8,128)(2,1)S(1)} %get-tuple-element.59.send1_ref), channel_id=1, source_target_pairs={{0,0},{8,16},{16,8},{24,24},{1,1},{9,17},{17,9},{25,25},{2,2},{10,... | collective-permute-start | bytes 393224 | tf_op jit(solution)/shard_map/ppermute | solution.py:522
  77.4 8.2 %collective-permute-start.16 = (bf16[256,256]{1,0:T(8,128)(2,1)S(1)}, bf16[256,256]{1,0:T(8,128)(2,1)S(1)}, u32[]{:S(2)}, u32[]{:S(2)}) collective-permute-start(bf16[256,256]{1,0:T(8,128)(2,1)S(1)} %get-tuple-element.60.send2_ref), channel_id=1, source_target_pairs={{0,7},{1,0},{2,1},{3,2},{4,3},{5,4},{6,5},{7,6},{8,15},{9,8},{10,9... | collective-permute-start | bytes 393224 | tf_op jit(solution)/shard_map/ppermute | solution.py:514
  78.3 7.2 %collective-permute-start.17 = (bf16[256,256]{1,0:T(8,128)(2,1)S(1)}, bf16[256,256]{1,0:T(8,128)(2,1)S(1)}, u32[]{:S(2)}, u32[]{:S(2)}) collective-permute-start(bf16[256,256]{1,0:T(8,128)(2,1)S(1)} %get-tuple-element.61.send3_ref), channel_id=1, source_target_pairs={{0,1},{1,2},{2,3},{3,4},{4,5},{5,6},{6,7},{7,0},{8,9},{9,10},{10,1... | collective-permute-start | bytes 393224 | tf_op jit(solution)/shard_map/ppermute | solution.py:514
  81.8 7.4 %collective-permute-start.8 = (bf16[768,128]{1,0:T(8,128)(2,1)S(1)}, bf16[768,128]{1,0:T(8,128)(2,1)S(1)}, u32[]{:S(2)}, u32[]{:S(2)}) collective-permute-start(bf16[768,128]{1,0:T(8,128)(2,1)S(1)} %get-tuple-element.56), channel_id=1, source_target_pairs={{0,1},{1,0},{2,3},{3,2},{4,5},{5,4},{6,7},{7,6},{8,9},{9,8},{10,11... | collective-permute-start | bytes 589832 | tf_op jit(solution)/shard_map/ppermute | solution.py:522
  85.0 4.1 %collective-permute-start.13 = (bf16[768,128]{1,0:T(8,128)(2,1)S(1)}, bf16[768,128]{1,0:T(8,128)(2,1)S(1)}, u32[]{:S(2)}, u32[]{:S(2)}) collective-permute-start(bf16[768,128]{1,0:T(8,128)(2,1)S(1)} %get-tuple-element.66), channel_id=1, source_target_pairs={{0,1},{1,0},{2,3},{3,2},{4,5},{5,4},{6,7},{7,6},{8,9},{9,8},{10,11... | collective-permute-start | bytes 589832 | tf_op jit(solution)/shard_map/ppermute | solution.py:522
  89.0 1.4 %collective-permute-start.18 = (bf16[384,128]{1,0:T(8,128)(2,1)S(1)}, bf16[384,128]{1,0:T(8,128)(2,1)S(1)}, u32[]{:S(2)}, u32[]{:S(2)}) collective-permute-start(bf16[384,128]{1,0:T(8,128)(2,1)S(1)} %get-tuple-element.70), channel_id=1, source_target_pairs={{0,1},{1,0},{2,3},{3,2},{4,5},{5,4},{6,7},{7,6},{8,9},{9,8},{10,11... | collective-permute-start | bytes 294920 | tf_op jit(solution)/shard_map/ppermute | solution.py:522
  129.7 1.9 %collective-permute-start.19 = (bf16[2048,128]{1,0:T(8,128)(2,1)S(1)}, bf16[2048,128]{1,0:T(8,128)(2,1)S(1)}, u32[]{:S(2)}, u32[]{:S(2)}) collective-permute-start(bf16[2048,128]{1,0:T(8,128)(2,1)S(1)} %bitcast.43), channel_id=1, source_target_pairs={{0,1},{1,0},{2,3},{3,2},{4,5},{5,4},{6,7},{7,6},{8,9},{9,8},{10,11... | collective-permute-start | bytes 1572872 | tf_op jit(solution)/shard_map/ppermute | solution.py:522

commit v3 on v2

v3 whole, which is shorter than its diff:
```python
import functools

import jax
import jax.numpy as jnp
from jax import lax
from jax.experimental import pallas as pl
from jax.experimental.pallas import tpu as pltpu
from jax.sharding import PartitionSpec as P

AXES = ("grid", "dom")
BF = jnp.bfloat16
F32 = jnp.float32
LANES = 128
TILE = 256
CHUNK = 512
GRANT = 20 << 20


def mm(left_side, right_side):
    return jnp.dot(left_side, right_side, preferred_element_type=F32)


def mm_t(left_side, right_side):
    return lax.dot_general(
        left_side, right_side, (((1,), (1,)), ((), ())), preferred_element_type=F32
    )


def t_mm(left_side, right_side):
    return lax.dot_general(
        left_side, right_side, (((0,), (0,)), ((), ())), preferred_element_type=F32
    )


def put_picks(out_ref, start, indices, count):
    rows = lax.broadcasted_iota(jnp.int32, (TILE, indices.shape[1]), 0).astype(F32).astype(BF)
    for base in range(0, count, TILE):
        shifted = (indices - float(base)).astype(BF)
        block = jnp.where(rows == shifted, jnp.ones((), BF), jnp.zeros((), BF))
        out_ref[start + base : start + base + TILE, :] = block


def sigmoid(values):
    return 0.5 * jnp.tanh(0.5 * values) + 0.5


def call(body, outs, scratch, name, flagged=False, space=pltpu.VMEM):
    vmem = pl.BlockSpec(memory_space=pltpu.VMEM)
    operand = pl.BlockSpec(memory_space=space)
    first = pl.BlockSpec(memory_space=pltpu.SMEM) if flagged else operand

    def run(*args):
        return pl.pallas_call(
            body,
            out_shape=tuple(jax.ShapeDtypeStruct(shape, dtype) for shape, dtype in outs),
            in_specs=[first] + [operand] * (len(args) - 1),
            out_specs=tuple(vmem for _ in outs),
            scratch_shapes=scratch,
            compiler_params=pltpu.CompilerParams(vmem_limit_bytes=GRANT),
            name=name,
        )(*args)

    return run


def chunks(total, body):
    for start in range(0, total, CHUNK):
        body(start, pl.ds(start, CHUNK))


def pack_body(cols_ref, slot_ref, live_ref, weight_ref, out_ref, slot_buf, live_buf, weight_buf, sems):
    peers, bucket, _ = cols_ref.shape
    per_row = LANES // bucket
    copies = [
        pltpu.make_async_copy(cols_ref, out_ref.at[:, :bucket, :], sems.at[0]),
        pltpu.make_async_copy(slot_ref, slot_buf, sems.at[1]),
        pltpu.make_async_copy(live_ref, live_buf, sems.at[2]),
        pltpu.make_async_copy(weight_ref, weight_buf, sems.at[3]),
    ]
    for copy in copies:
        copy.start()
    for copy in copies[1:]:
        copy.wait()
    slot = slot_buf[...].astype(F32)
    high = jnp.floor(slot * (1.0 / 256.0))
    low = slot - 256.0 * high
    scale = weight_buf[...] * live_buf[...].astype(F32)
    scale_high = scale.astype(BF)
    scale_low = (scale - scale_high.astype(F32)).astype(BF)
    fields = [high.astype(BF), low.astype(BF), scale_high, scale_low]
    for peer in range(peers):
        row = peer // per_row
        extra = jnp.concatenate([field[row : row + 1, :] for field in fields], 0)
        out_ref[peer, bucket : bucket + 4, :] = extra
    copies[0].wait()


PAIR, ODD_GRID, ODD_DOM = 4, 6, 7


def picks_body(rows_ref, bound_ref, picks_ref, rim_picks, rim_picks_t):
    nodes = rim_picks.shape[0]
    ext = picks_ref.shape[0] - 2 * nodes
    for start in range(0, rows_ref.shape[1], CHUNK):
        at = pl.ds(start, CHUNK)
        block = picks_ref.at[:, at]
        put_picks(block, 0, rows_ref[1:2, at], nodes)
        put_picks(block, nodes, rows_ref[0:1, at], nodes + ext)
    put_picks(rim_picks, 0, bound_ref[0:1, :], nodes)
    rim_picks_t[...] = rim_picks[...].astype(F32).T.astype(BF)


def put_state(state, state_ref, rim_ref, rim_picks_t):
    state_ref[...] = state.astype(BF)
    rim_ref[...] = mm(rim_picks_t[...], state_ref[...]).astype(BF)


def in_order(flags_ref, rims):
    first, second, left, right = (ref[...] for ref in rims)
    odd = flags_ref[ODD_GRID] > 0.5
    ordered = (jnp.where(odd, first, second), jnp.where(odd, second, first), left, right)
    return [rows * flags_ref[side].astype(BF) for side, rows in enumerate(ordered)]


def encode_body(
    bucket,
    packed_ref,
    rows_ref,
    enc_in_t_ref,
    enc_out_ref,
    static_ref,
    rim_picks_t,
    pooled_ref,
    slope_ref,
    picks_ref,
    state_ref,
    rim_ref,
    act_ref,
):
    nodes = static_ref.shape[0]
    peers_step = CHUNK // bucket

    def step(start, at):
        first = start // bucket
        got = packed_ref[first : first + peers_step, :bucket, :].reshape(CHUNK, packed_ref.shape[2])
        pre = mm_t(enc_in_t_ref[...], got)
        scale = rows_ref[1:2, at]
        sig = sigmoid(pre)
        act_ref[:, at] = (pre * sig * scale).astype(BF)
        slope_ref[:, at] = (sig * (1.0 + pre * (1.0 - sig)) * scale).astype(BF)
        put_picks(picks_ref.at[:, at], 0, rows_ref[0:1, at], nodes)

    chunks(rows_ref.shape[1], step)
    pooled_ref[...] = mm_t(picks_ref[...], act_ref[...]).astype(BF)
    state = static_ref[...].astype(F32) + mm(pooled_ref[...], enc_out_ref[...])
    put_state(state, state_ref, rim_ref, rim_picks_t)


def own_body(state_ref, src_t_ref, dst_t_ref, picks_ref, out_ref, table_ref):
    nodes = state_ref.shape[0]
    held = state_ref[...]
    table_ref[:, :nodes] = mm_t(dst_t_ref[...], held).astype(BF)
    table_ref[:, nodes:] = mm_t(src_t_ref[...], held).astype(BF)
    out_ref[...] = mm(table_ref[...], picks_ref[: 2 * nodes, :])


def back_body(msg_ref, grad_ref, rows_ref, picks_ref, out_ref):
    nodes = grad_ref.shape[0]
    back = mm_t(msg_ref[...], grad_ref[...]).astype(BF)
    out_ref[...] = mm(back, picks_ref[:nodes, :]) * rows_ref[2:3, :]


def fill_rims(full_ref, flags_ref, rims, src_t_ref):
    rim = rims[0].shape[0]
    for side, rim_rows in enumerate(in_order(flags_ref, rims)):
        full_ref[:, side * rim : (side + 1) * rim] = mm_t(src_t_ref[...], rim_rows).astype(BF)


def forward_body(
    flags_ref,
    first_ref,
    second_ref,
    left_ref,
    right_ref,
    own_pre_ref,
    rows_ref,
    picks_ref,
    state_ref,
    src_t_ref,
    msg_ref,
    rim_picks_t,
    slope_ref,
    node_act_ref,
    next_state_ref,
    rim_ref,
    full_ref,
    act_ref,
):
    nodes = state_ref.shape[0]
    fill_rims(full_ref, flags_ref, (first_ref, second_ref, left_ref, right_ref), src_t_ref)

    def step(start, at):
        pre = own_pre_ref[:, at] + mm(full_ref[...], picks_ref[2 * nodes :, at])
        scale = rows_ref[2:3, at]
        sig = sigmoid(pre)
        act_ref[:, at] = (pre * sig * scale).astype(BF)
        slope_ref[:, at] = (sig * (1.0 + pre * (1.0 - sig)) * scale).astype(BF)

    chunks(rows_ref.shape[1], step)
    node_act_ref[...] = mm_t(picks_ref[:nodes, :], act_ref[...]).astype(BF)
    state = state_ref[...].astype(F32) + mm(node_act_ref[...], msg_ref[...])
    put_state(state, next_state_ref, rim_ref, rim_picks_t)


def put_sends(flags_ref, sums, sends):
    rim = sums.shape[0] // 4
    up, down, left, right = (sums[side * rim : (side + 1) * rim, :].astype(BF) for side in range(4))
    odd = flags_ref[ODD_GRID] > 0.5
    sends[0][...] = jnp.where(odd, up, down)
    sends[1][...] = jnp.where(odd, down, up)
    sends[2][...] = left
    sends[3][...] = right


def turn_body(
    flags_ref,
    first_ref,
    second_ref,
    left_ref,
    right_ref,
    own_pre_ref,
    back_ref,
    rows_ref,
    picks_ref,
    src_t_ref,
    act_ref,
    grad_pre_ref,
    send0_ref,
    send1_ref,
    send2_ref,
    send3_ref,
    full_ref,
):
    first = picks_ref.shape[0] - full_ref.shape[1]
    fill_rims(full_ref, flags_ref, (first_ref, second_ref, left_ref, right_ref), src_t_ref)

    def step(start, at):
        pre = own_pre_ref[:, at] + mm(full_ref[...], picks_ref[first:, at])
        sig = sigmoid(pre)
        act_ref[:, at] = (pre * sig * rows_ref[2:3, at]).astype(BF)
        grad_pre_ref[:, at] = (back_ref[:, at] * (sig * (1.0 + pre * (1.0 - sig)))).astype(BF)

    chunks(rows_ref.shape[1], step)
    sums = mm_t(picks_ref[first:, :], grad_pre_ref[...])
    put_sends(flags_ref, sums, (send0_ref, send1_ref, send2_ref, send3_ref))


def merged_grad(partial_ref, flags_ref, returned, src_ref, rim_picks):
    marks = (flags_ref[PAIR], flags_ref[PAIR + 1], flags_ref[3], flags_ref[2])
    total = returned[0][...].astype(F32) * marks[0]
    for side in range(1, 4):
        total += returned[side][...].astype(F32) * marks[side]
    back = mm(rim_picks[...], total.astype(BF)).astype(BF)
    return partial_ref[...] + mm_t(back, src_ref[...])


def backward_body(
    flags_ref,
    first_ref,
    second_ref,
    left_ref,
    right_ref,
    partial_ref,
    src_ref,
    rim_picks,
    msg_ref,
    slope_ref,
    picks_ref,
    grad_ref,
    grad_pre_ref,
    send0_ref,
    send1_ref,
    send2_ref,
    send3_ref,
):
    nodes = partial_ref.shape[0]
    returned = (first_ref, second_ref, left_ref, right_ref)
    grad = merged_grad(partial_ref, flags_ref, returned, src_ref, rim_picks)
    grad_ref[...] = grad
    back = mm_t(msg_ref[...], grad.astype(BF)).astype(BF)

    def step(start, at):
        grad_pre = mm(back, picks_ref[:nodes, at]) * slope_ref[:, at].astype(F32)
        grad_pre_ref[:, at] = grad_pre.astype(BF)

    chunks(picks_ref.shape[1], step)
    sums = mm_t(picks_ref[2 * nodes :, :], grad_pre_ref[...])
    put_sends(flags_ref, sums, (send0_ref, send1_ref, send2_ref, send3_ref))


def sums_body(picks_ref, grad_pre_ref, grad_ref, src_ref, dst_ref, own_ref, partial_ref):
    nodes = grad_ref.shape[0]
    own_ref[...] = mm_t(picks_ref[: 2 * nodes, :], grad_pre_ref[...]).astype(BF)
    partial_ref[...] = (
        grad_ref[...].astype(F32)
        + mm_t(own_ref[:nodes, :], dst_ref[...])
        + mm_t(own_ref[nodes:, :], src_ref[...])
    )


def out_body(picks_ref, act_edges_ref, state_ref, msg_ref, act_ref, out_ref):
    nodes = state_ref.shape[0]
    act_ref[...] = mm_t(picks_ref[:nodes, :], act_edges_ref[...]).astype(BF)
    out_ref[...] = (state_ref[...].astype(F32) + mm(act_ref[...], msg_ref[...])).astype(BF)


def put_halves(flags_ref, first, term, keep_ref, send_ref):
    half = term.shape[1] // 2
    odd = flags_ref[ODD_DOM] > 0.5
    low, high = term[:, :half].astype(BF), term[:, half:].astype(BF)
    keep_ref[first : first + term.shape[0], :] = jnp.where(odd, high, low)
    send_ref[first : first + term.shape[0], :] = jnp.where(odd, low, high)


def terms_body(
    flags_ref,
    first_ref,
    second_ref,
    left_ref,
    right_ref,
    send0_ref,
    send1_ref,
    send2_ref,
    send3_ref,
    state_ref,
    own_ref,
    act_ref,
    grad_ref,
    keep_ref,
    send_ref,
):
    nodes, width = state_ref.shape
    state = state_ref[...]
    src_term = t_mm(state, own_ref[nodes:, :])
    pairs = (
        (first_ref, send0_ref, flags_ref[PAIR]),
        (second_ref, send1_ref, flags_ref[PAIR + 1]),
        (left_ref, send2_ref, flags_ref[2]),
        (right_ref, send3_ref, flags_ref[3]),
    )
    for rim_ref, sums_ref, mark in pairs:
        src_term += t_mm(rim_ref[...], sums_ref[...]) * mark
    put_halves(flags_ref, 0, src_term, keep_ref, send_ref)
    put_halves(flags_ref, width, t_mm(state, own_ref[:nodes, :]), keep_ref, send_ref)
    put_halves(
        flags_ref, 2 * width, t_mm(act_ref[...], grad_ref[...].astype(BF)), keep_ref, send_ref
    )


def last_body(
    bucket,
    flags_ref,
    first_ref,
    second_ref,
    left_ref,
    right_ref,
    partial_ref,
    src_ref,
    rim_picks,
    packed_ref,
    enc_out_ref,
    pooled_ref,
    slope_ref,
    picks_ref,
    keep_ref,
    send_ref,
):
    fin = packed_ref.shape[2]
    peers_step = CHUNK // bucket
    returned = (first_ref, second_ref, left_ref, right_ref)
    grad = merged_grad(partial_ref, flags_ref, returned, src_ref, rim_picks).astype(BF)
    back = mm_t(enc_out_ref[...], grad).astype(BF)
    in_term = jnp.zeros((enc_out_ref.shape[0], fin), F32)
    for start in range(0, picks_ref.shape[1], CHUNK):
        at = pl.ds(start, CHUNK)
        first = start // bucket
        got = packed_ref[first : first + peers_step, :bucket, :].reshape(CHUNK, fin)
        grad_pre = mm(back, picks_ref[:, at]) * slope_ref[:, at].astype(F32)
        in_term += mm(grad_pre.astype(BF), got)
    put_halves(flags_ref, 0, in_term.T, keep_ref, send_ref)
    put_halves(flags_ref, fin, t_mm(pooled_ref[...], grad), keep_ref, send_ref)


def merge_body(*refs):
    out_ref = refs[-1]
    first = 0
    for keep_ref, got_ref in zip(refs[:-1:2], refs[1:-1:2]):
        rows = keep_ref.shape[0]
        total = keep_ref[...].astype(F32) + got_ref[...].astype(F32)
        out_ref[first : first + rows, :] = total.astype(BF)
        first += rows
    if first < out_ref.shape[0]:
        out_ref[first:, :] = jnp.zeros((out_ref.shape[0] - first, out_ref.shape[1]), BF)


def share_body(parts_ref, out_ref):
    count = parts_ref.shape[0]
    for odd in range(2):
        total = parts_ref[odd].astype(F32)
        for peer in range(odd + 2, count, 2):
            total += parts_ref[peer].astype(F32)
        for peer in range(odd, count, 2):
            out_ref[peer] = total.astype(BF)


def unpack_body(flags_ref, mine_ref, other_ref, *outs):
    odd = flags_ref[ODD_DOM] > 0.5
    half = mine_ref.shape[1]
    first = 0

    def put(ref, rows):
        nonlocal first
        mine = mine_ref[first : first + rows, :].astype(F32)
        other = other_ref[first : first + rows, :].astype(F32)
        ref[:, :half] = jnp.where(odd, other, mine)
        ref[:, half:] = jnp.where(odd, mine, other)
        first += rows

    enc_in_ref, enc_out_ref, *layer_refs = outs
    for layer in reversed(range(layer_refs[0].shape[0])):
        for ref in layer_refs:
            put(ref.at[layer], ref.shape[1])
    put(enc_in_ref, enc_in_ref.shape[0])
    put(enc_out_ref, enc_out_ref.shape[0])


def exchange(shard):
    return lax.all_to_all(shard, AXES, split_axis=0, concat_axis=0, tiled=True)


def turned(shard, axis, by):
    count = lax.axis_size(axis)
    return lax.ppermute(shard, axis, [(i, (i + by) % count) for i in range(count)])


def swapped(shard, axis, offset):
    count = lax.axis_size(axis)
    partner = list(range(count))
    for i in range(offset, count - 1, 2):
        partner[i], partner[i + 1] = i + 1, i
    return lax.ppermute(shard, axis, list(enumerate(partner)))


def from_neighbours(rim_rows):
    return (
        swapped(rim_rows, "grid", 0),
        swapped(rim_rows, "grid", 1),
        turned(rim_rows, "dom", 1),
        turned(rim_rows, "dom", -1),
    )


def to_neighbours(sends):
    return (
        swapped(sends[0], "grid", 0),
        swapped(sends[1], "grid", 1),
        turned(sends[2], "dom", -1),
        turned(sends[3], "dom", 1),
    )


def per_device(
    columns,
    column_live,
    col_weight,
    col_slot,
    node_static,
    boundary_idx,
    edge_src,
    edge_dst,
    edge_live,
    edge_weight,
    enc_in,
    enc_out,
    src_proj,
    dst_proj,
    msg_proj,
    node_cotangent,
):
    peers = lax.axis_size(AXES)
    cols, fin = columns.shape
    nodes, width = node_static.shape
    rim = boundary_idx.shape[0]
    edges = edge_src.shape[0]
    ext = 4 * rim
    bucket = cols // peers

    lanes = (cols // LANES, LANES)
    held = [pltpu.VMEM(lanes, jnp.int32), pltpu.VMEM(lanes, jnp.int32), pltpu.VMEM(lanes, F32)]
    (packed,) = call(
        pack_body,
        [((peers, bucket + 4, fin), BF)],
        held + [pltpu.SemaphoreType.DMA((4,))],
        "pack",
        space=pltpu.HBM,
    )(
        columns.reshape(peers, bucket, fin),
        col_slot.reshape(lanes),
        column_live.reshape(lanes),
        col_weight.reshape(lanes),
    )
    packed = exchange(packed)

    grid_at, grid_count = lax.axis_index("grid"), lax.axis_size("grid")
    dom_at, dom_count = lax.axis_index("dom"), lax.axis_size("dom")
    odd_grid, odd_dom = grid_at % 2, dom_at % 2
    up, down = grid_at > 0, grid_at < grid_count - 1
    flags = jnp.stack(
        [
            up,
            down,
            dom_at > 0,
            dom_at < dom_count - 1,
            jnp.where(odd_grid == 1, up, down),
            jnp.where(odd_grid == 1, down, up),
            odd_grid == 1,
            odd_dom == 1,
        ]
    ).astype(F32)
    edge_scale = edge_weight * edge_live.astype(F32)
    edge_rows = jnp.stack([edge_src.astype(F32), edge_dst.astype(F32), edge_scale])
    bound = boundary_idx.astype(F32)[None]
    enc_in_t = enc_in.T
    src_t = src_proj.transpose(0, 2, 1)
    dst_t = dst_proj.transpose(0, 2, 1)

    node_shape = ((nodes, width), BF)
    node_wide = ((nodes, width), F32)
    rim_shape = ((rim, width), BF)
    edge_shape = ((width, edges), BF)
    edge_wide = ((width, edges), F32)
    full = pltpu.VMEM((width, ext), BF)
    edge_buf = pltpu.VMEM((width, edges), BF)
    table_buf = pltpu.VMEM((width, 2 * nodes), BF)

    picks, rim_picks, rim_picks_t = call(
        picks_body,
        [((2 * nodes + ext, edges), BF), ((nodes, rim), BF), ((rim, nodes), BF)],
        [],
        "picks",
    )(edge_rows, bound)
    (back1,) = call(back_body, [edge_wide], [], "back")(msg_proj[1], node_cotangent, edge_rows, picks)
    packed, back1 = lax.optimization_barrier((packed, back1))

    at = (grid_at * dom_count + dom_at) % (LANES // bucket)
    extra = lax.dynamic_slice_in_dim(packed[:, bucket : bucket + 4], at * bucket, bucket, 2)
    extra = extra.astype(F32).transpose(1, 0, 2).reshape(4, cols)
    col_rows = jnp.stack([extra[0] * 256.0 + extra[1], extra[2] + extra[3]])

    pooled, col_slope, slot_picks, state0, rim0 = call(
        functools.partial(encode_body, bucket),
        [node_shape, ((width, cols), BF), ((nodes, cols), BF), node_shape, rim_shape],
        [pltpu.VMEM((width, cols), BF)],
        "encode",
    )(packed, col_rows, enc_in_t, enc_out, node_static, rim_picks_t)

    rims0 = from_neighbours(rim0)
    (pre0,) = call(own_body, [edge_wide], [table_buf], "own")(state0, src_t[0], dst_t[0], picks)
    slope0, act0, state1, rim1 = call(
        forward_body,
        [edge_shape, node_shape, node_shape, rim_shape],
        [full, edge_buf],
        "forward",
        True,
    )(flags, *rims0, pre0, edge_rows, picks, state0, src_t[0], msg_proj[0], rim_picks_t)

    rims1 = from_neighbours(rim1)
    (pre1,) = call(own_body, [edge_wide], [table_buf], "own")(state1, src_t[1], dst_t[1], picks)
    act_edges1, grad_pre1, *sends1 = call(
        turn_body, [edge_shape, edge_shape] + [rim_shape] * 4, [full], "turn", True
    )(flags, *rims1, pre1, back1, edge_rows, picks, src_t[1])

    returned1 = to_neighbours(sends1)
    own_shape = ((2 * nodes, width), BF)
    halves = [((3 * width, width // 2), BF)] * 2
    own1, partial1 = call(sums_body, [own_shape, node_wide], [], "sums")(
        picks, grad_pre1, node_cotangent, src_proj[1], dst_proj[1]
    )
    act1, node_out = call(out_body, [node_shape, node_shape], [], "out")(
        picks, act_edges1, state1, msg_proj[1]
    )
    keep1, send1 = call(terms_body, halves, [], "terms", True)(
        flags, *rims1, *sends1, state1, own1, act1, node_cotangent
    )
    partial1, keep1, send1 = lax.optimization_barrier((partial1, keep1, send1))
    grad1, grad_pre0, *sends0 = call(
        backward_body, [node_wide, edge_shape] + [rim_shape] * 4, [], "backward", True
    )(flags, *returned1, partial1, src_proj[1], rim_picks, msg_proj[0], slope0, picks)

    returned0 = to_neighbours(sends0)
    own0, partial0 = call(sums_body, [own_shape, node_wide], [], "sums")(
        picks, grad_pre0, grad1, src_proj[0], dst_proj[0]
    )
    keep0, send0 = call(terms_body, halves, [], "terms", True)(
        flags, *rims0, *sends0, state0, own0, act0, grad1
    )
    hidden = enc_out.shape[0]
    keep_enc, send_enc = call(
        functools.partial(last_body, bucket),
        [((fin + hidden, width // 2), BF)] * 2,
        [],
        "last",
        True,
    )(flags, *returned0, partial0, src_proj[0], rim_picks, packed, enc_out, pooled, col_slope, slot_picks)

    total_rows = 2 * 3 * width + fin + hidden
    share = -(-total_rows // (16 * peers)) * 16
    rows = peers * share
    (merged,) = call(merge_body, [((rows, width // 2), BF)], [], "merge")(
        keep1,
        swapped(send1, "dom", 0),
        keep0,
        swapped(send0, "dom", 0),
        keep_enc,
        swapped(send_enc, "dom", 0),
    )
    parts = exchange(merged.reshape(peers, share, width // 2))
    (spread,) = call(share_body, [((peers, share, width // 2), BF)], [], "share")(parts)
    mine = exchange(spread).reshape(rows, width // 2)
    layer_shape = ((2, width, width), F32)
    grads = call(
        unpack_body,
        [((fin, width), F32), ((hidden, width), F32), layer_shape, layer_shape, layer_shape],
        [],
        "unpack",
        True,
    )(flags, mine, swapped(mine, "dom", 0))
    return (node_out, *grads)


def solution(mesh):
    rows = P(AXES, None)
    flat = P(AXES)
    placed = (rows, flat, flat, flat, rows, flat, flat, flat, flat, flat, P(), P(), P(), P(), P(), rows)
    return jax.shard_map(
        per_device,
        mesh=mesh,
        in_specs=placed,
        out_specs=(rows, P(), P(), P(), P(), P()),
        check_vma=False,
    )
```

time: 134 us -> 134 us (level)
  local copies, waits for them, and re-layouts: 3.93 us -> 18.5 us
  Pallas kernels: 37.7 us -> 29.1 us
  waiting for transfers between devices: 22.6 us -> 16.4 us
    unnamed x35 -> x61, local copies, waits for them, and re-layouts: 3.56 us -> 17.1 us
    pallas_call x17 -> x18, Pallas kernels: 37.7 us -> 29.1 us  [run(): pl.pallas_call(body, out_shape=tuple((jax.ShapeDtypeStruct(shape, dtype)...]
    all_to_all x1, waiting for transfers between devices: 16 us -> 9.42 us  [exchange(): return lax.all_to_all(shard, AXES, split_axis=0, concat_axis=0, tiled=True)]
    ppermute x8, waiting for transfers between devices: 2.04 us -> 3.73 us  [turned(): lax.ppermute(shard, axis, [(i, (i + by) % count) for i in range(count)])]
  transfers between devices with their start and end apart: 21 -> 21, of which waited for: 5 -> 5; matrix products, arithmetic and copies ran while one was open for 0% -> 3% of each run, Pallas kernels for 13% -> 11%
where the time goes in v3:
time: 134 us; the launch traced here: 133 us
  blocking collectives  39.3 us (29%)
  Pallas kernels  29.1 us (22%)
  starting transfers between devices  28.6 us (21%)
  local copies, waits for them, and re-layouts  18.5 us (14%)
  waiting for transfers between devices  16.4 us (12%)
    all_to_all x2, blocking collectives, exchange(): return lax.all_to_all(shard, AXES, split_axis=0, concat_axis=0, tiled=True)  39.3 us
    pallas_call x18, Pallas kernels, run(): pl.pallas_call(body, out_shape=tuple((jax.ShapeDtypeStruct(shape, dtype)...  29.1 us
    unnamed x61, local copies, waits for them, and re-layouts  17.1 us
    ppermute x12, starting transfers between devices, swapped(): return lax.ppermute(shard, axis, list(enumerate(partner)))  12.4 us
    all_to_all x1, waiting for transfers between devices, exchange(): return lax.all_to_all(shard, AXES, split_axis=0, concat_axis=0, tiled=True)  9.42 us
    ppermute x8, starting transfers between devices, turned(): lax.ppermute(shard, axis, [(i, (i + by) % count) for i in range(count)])  8.88 us
    all_to_all x1, starting transfers between devices, exchange(): return lax.all_to_all(shard, AXES, split_axis=0, concat_axis=0, tiled=True)  7.33 us
    ppermute x8, waiting for transfers between devices, turned(): lax.ppermute(shard, axis, [(i, (i + by) % count) for i in range(count)])  3.73 us
  transfers between devices with their start and end apart: 21, of which 5 were waited for; matrix products, arithmetic and copies ran while one was open for 3% of the time, Pallas kernels for 11%

profile of v3, /device:TPU:0, one launch (start us, length us, event | category | flops | bytes accessed | tf_op | source)
XLA Modules:
  0.0 133.4 jit_solution(14165038821546830873)
XLA Ops:
  0.7 1.0 copy-done.9
  1.7 0.7 copy-done.14
  2.4 0.7 copy-done.15
  3.1 0.7 copy-done.16
  3.9 0.9 pack.1
  4.8 7.3 %all-to-all-start = ((bf16[32,68,128]{2,1,0:T(8,128)(2,1)}), bf16[32,68,128]{2,1,0:T(8,128)(2,1)S(1)}, u32[]{:S(2)}, u32[]{:S(2)}) async-start(bf16[32,68,128]{2,1,0:T(8,128)(2,1)} %pack.1), calls=%async_computation | async-start | bytes 1179648 | tf_op jit(solution)/shard_map/all_to_all | solution.py:438
  12.3 0.7 copy.22
  13.0 0.8 copy.23
  13.8 0.8 copy.24
  14.7 0.1 stack.56
  14.9 1.1 picks.1
  16.0 0.9 back.1.back_ref
  16.9 2.3 %copy-done = bf16[2048,2048]{1,0:T(8,128)(2,1)} copy-done((bf16[2048,2048]{1,0:T(8,128)(2,1)}, bf16[2048,2048]{1,0:T(8,128)(2,1)S(1)}, u32[]{:S(2)}) %copy-start) | copy-done | bytes 8388632
  19.3 0.1 copy-done.4
  19.4 0.1 copy-done.6
  19.5 9.4 %all-to-all-done.packed_ref = bf16[32,68,128]{2,1,0:T(8,128)(2,1)S(1)} async-done(((bf16[32,68,128]{2,1,0:T(8,128)(2,1)}), bf16[32,68,128]{2,1,0:T(8,128)(2,1)S(1)}, u32[]{:S(2)}, u32[]{:S(2)}) %all-to-all-start) | async-done | bytes 557088 | tf_op jit(solution)/shard_map/all_to_all | solution.py:438
  29.0 0.1 convert_bitcast_fusion
  29.0 0.1 fusion.1
  29.2 0.1 add.48
  29.3 0.1 add.50
  29.4 0.9 copy-done.7
  30.3 0.9 copy-done.10
  31.2 0.9 copy-done.12
  32.2 0.8 copy-done.13
  33.0 2.0 %encode.1 = (bf16[512,256]{1,0:T(8,128)(2,1)S(1)}, bf16[256,2048]{1,0:T(8,128)(2,1)S(1)}, bf16[512,2048]{1,0:T(8,128)(2,1)S(1)}, bf16[512,256]{1,0:T(8,128)(2,1)S(1)}, bf16[256,256]{1,0:T(8,128)(2,1)S(1)}) custom-call(bf16[32,68,128]{2,1,0:T(8,128)(2,1)S(1)} %all-to-all-done.packed_ref, f32[2,2048]{1,0:T(2,128)S(1)} %pad_maximum_fusion.1.rows_ref, ...), custom_call_target="tpu_custom_call" | custom-call | tf_op jit(solution)/shard_map/encode/pallas_call | solution.py:53
  35.0 1.4 %collective-permute-start = (bf16[256,256]{1,0:T(8,128)(2,1)S(1)}, bf16[256,256]{1,0:T(8,128)(2,1)S(1)}, u32[]{:S(2)}, u32[]{:S(2)}) collective-permute-start(bf16[256,256]{1,0:T(8,128)(2,1)S(1)} %get-tuple-element.55), channel_id=1, source_target_pairs={{0,8},{8,0},{16,24},{24,16},{1,9},{9,1},{17,25},{25,17},{2,10},{10... | collective-permute-start | bytes 393224 | tf_op jit(solution)/shard_map/ppermute | solution.py:451
  36.4 0.7 collective-permute-start.1
  37.1 0.1 collective-permute-start.2
  37.1 2.6 %collective-permute-start.3 = (bf16[256,256]{1,0:T(8,128)(2,1)S(1)}, bf16[256,256]{1,0:T(8,128)(2,1)S(1)}, u32[]{:S(2)}, u32[]{:S(2)}) collective-permute-start(bf16[256,256]{1,0:T(8,128)(2,1)S(1)} %get-tuple-element.55), channel_id=1, source_target_pairs={{0,7},{1,0},{2,1},{3,2},{4,3},{5,4},{6,5},{7,6},{8,15},{9,8},{10,9... | collective-permute-start | bytes 393224 | tf_op jit(solution)/shard_map/ppermute | solution.py:443
  39.8 1.0 slice_bitcast_fusion
  40.8 3.4 %copy-done.1 = bf16[2048,2048]{1,0:T(8,128)(2,1)S(1)} copy-done((bf16[2048,2048]{1,0:T(8,128)(2,1)S(1)}, bf16[2048,2048]{1,0:T(8,128)(2,1)}, u32[]{:S(2)}) %copy-start.1) | copy-done | bytes 8388632
  44.1 1.4 %own.2.own_pre_ref = f32[256,2048]{1,0:T(8,128)S(1)} custom-call(bf16[512,256]{1,0:T(8,128)(2,1)S(1)} %get-tuple-element.56.state_ref, bf16[256,256]{1,0:T(8,128)(2,1)S(1)} %get-tuple-element.107.src_t_ref, bf16[256,256]{1,0:T(8,128)(2,1)S(1)} %get-tuple-element.105.dst_t_ref, bf16[2048,2048]{1,0:T(8,128)(2,1)S(1)} %copy-done.1), custom_call_target="tpu_custom_call" | custom-call | tf_op jit(solution)/shard_map/own/pallas_call | solution.py:53
  45.6 1.9 %copy-done.2 = bf16[2048,2048]{1,0:T(8,128)(2,1)S(1)} copy-done((bf16[2048,2048]{1,0:T(8,128)(2,1)S(1)}, bf16[2048,2048]{1,0:T(8,128)(2,1)}, u32[]{:S(2)}) %copy-start.2) | copy-done | bytes 8388632
  47.6 3.4 %forward.1 = (bf16[256,2048]{1,0:T(8,128)(2,1)S(1)}, bf16[512,256]{1,0:T(8,128)(2,1)S(1)}, bf16[512,256]{1,0:T(8,128)(2,1)S(1)}, bf16[256,256]{1,0:T(8,128)(2,1)S(1)}) custom-call(f32[8]{0:T(128)S(1)} %convert_element_type.20.flags_ref, bf16[256,256]{1,0:T(8,128)(2,1)S(1)} %collective-permute-done.first_ref, ...), custom_call_target="tpu_custom_call" | custom-call | tf_op jit(solution)/shard_map/forward/pallas_call | solution.py:53
  51.0 2.1 %collective-permute-start.4 = (bf16[256,256]{1,0:T(8,128)(2,1)S(1)}, bf16[256,256]{1,0:T(8,128)(2,1)S(1)}, u32[]{:S(2)}, u32[]{:S(2)}) collective-permute-start(bf16[256,256]{1,0:T(8,128)(2,1)S(1)} %get-tuple-element.57), channel_id=1, source_target_pairs={{0,8},{8,0},{16,24},{24,16},{1,9},{9,1},{17,25},{25,17},{2,10},{10... | collective-permute-start | bytes 393224 | tf_op jit(solution)/shard_map/ppermute | solution.py:451
  53.1 0.7 collective-permute-start.5
  53.7 0.1 collective-permute-start.6
  53.8 2.6 %collective-permute-start.7 = (bf16[256,256]{1,0:T(8,128)(2,1)S(1)}, bf16[256,256]{1,0:T(8,128)(2,1)S(1)}, u32[]{:S(2)}, u32[]{:S(2)}) collective-permute-start(bf16[256,256]{1,0:T(8,128)(2,1)S(1)} %get-tuple-element.57), channel_id=1, source_target_pairs={{0,7},{1,0},{2,1},{3,2},{4,3},{5,4},{6,5},{7,6},{8,15},{9,8},{10,9... | collective-permute-start | bytes 393224 | tf_op jit(solution)/shard_map/ppermute | solution.py:443
  56.5 1.4 %own.3.own_pre_ref = f32[256,2048]{1,0:T(8,128)S(1)} custom-call(bf16[512,256]{1,0:T(8,128)(2,1)S(1)} %get-tuple-element.58.state_ref, bf16[256,256]{1,0:T(8,128)(2,1)S(1)} %get-tuple-element.106.src_t_ref, bf16[256,256]{1,0:T(8,128)(2,1)S(1)} %get-tuple-element.104.dst_t_ref, bf16[2048,2048]{1,0:T(8,128)(2,1)S(1)} %copy-done.2), custom_call_target="tpu_custom_call" | custom-call | tf_op jit(solution)/shard_map/own/pallas_call | solution.py:53
  57.9 1.7 %collective-permute-done.6.left_ref = bf16[256,256]{1,0:T(8,128)(2,1)S(1)} collective-permute-done((bf16[256,256]{1,0:T(8,128)(2,1)S(1)}, bf16[256,256]{1,0:T(8,128)(2,1)S(1)}, u32[]{:S(2)}, u32[]{:S(2)}) %collective-permute-start.6) | collective-permute-done | bytes 131104 | tf_op jit(solution)/shard_map/ppermute | solution.py:443
  59.6 3.8 %turn.1 = (bf16[256,2048]{1,0:T(8,128)(2,1)S(1)}, bf16[256,2048]{1,0:T(8,128)(2,1)S(1)}, bf16[256,256]{1,0:T(8,128)(2,1)S(1)}, bf16[256,256]{1,0:T(8,128)(2,1)S(...) custom-call(f32[8]{0:T(128)S(1)} %convert_element_type.20.flags_ref, ...), custom_call_target="tpu_custom_call" | custom-call | tf_op jit(solution)/shard_map/turn/pallas_call | solution.py:53
  63.4 0.7 collective-permute-start.10
  64.1 2.2 %collective-permute-start.11 = (bf16[256,256]{1,0:T(8,128)(2,1)S(1)}, bf16[256,256]{1,0:T(8,128)(2,1)S(1)}, u32[]{:S(2)}, u32[]{:S(2)}) collective-permute-start(bf16[256,256]{1,0:T(8,128)(2,1)S(1)} %get-tuple-element.66.send2_ref), channel_id=1, source_target_pairs={{0,7},{1,0},{2,1},{3,2},{4,3},{5,4},{6,5},{7,6},{8,15},{9,8},{10,9... | collective-permute-start | bytes 393224 | tf_op jit(solution)/shard_map/ppermute | solution.py:443
  66.3 4.4 %collective-permute-start.9 = (bf16[256,256]{1,0:T(8,128)(2,1)S(1)}, bf16[256,256]{1,0:T(8,128)(2,1)S(1)}, u32[]{:S(2)}, u32[]{:S(2)}) collective-permute-start(bf16[256,256]{1,0:T(8,128)(2,1)S(1)} %get-tuple-element.64.send0_ref), channel_id=1, source_target_pairs={{0,8},{8,0},{16,24},{24,16},{1,9},{9,1},{17,25},{25,17},{2,10},{10... | collective-permute-start | bytes 393224 | tf_op jit(solution)/shard_map/ppermute | solution.py:451
  70.7 1.6 %out.1 = (bf16[512,256]{1,0:T(8,128)(2,1)S(1)}, bf16[512,256]{1,0:T(8,128)(2,1)}) custom-call(bf16[2048,2048]{1,0:T(8,128)(2,1)S(1)} %copy-done.2, bf16[256,2048]{1,0:T(8,128)(2,1)S(1)} %get-tuple-element.60.act_edges_ref, bf16[512,256]{1,0:T(8,128)(2,1)S(1)} %get-tuple-element.58.state_ref, bf16[256,256]{1,0:T(8,128)(2,1)S(1)} %get-tuple-element.109.msg_ref), custom_call_target="tpu_custom_call" | custom-call | tf_op jit(solution)/shard_map/out/pallas_call | solution.py:53
  72.3 1.5 %sums.2 = (bf16[1024,256]{1,0:T(8,128)(2,1)S(1)}, f32[512,256]{1,0:T(8,128)S(1)}) custom-call(bf16[2048,2048]{1,0:T(8,128)(2,1)S(1)} %copy-done.2, bf16[256,2048]{1,0:T(8,128)(2,1)S(1)} %get-tuple-element.62.grad_pre_ref, bf16[512,256]{1,0:T(8,128)(2,1)S(1)} %copy-done.3, bf16[256,256]{1,0:T(8,128)(2,1)S(1)} %get-tuple-element.103.src_ref, ...), custom_call_target="tpu_custom_call" | custom-call | tf_op jit(solution)/shard_map/sums/pallas_call | solution.py:53
  73.9 1.1 terms.2
  75.1 2.9 %backward.1 = (f32[512,256]{1,0:T(8,128)S(1)}, bf16[256,2048]{1,0:T(8,128)(2,1)S(1)}, bf16[256,256]{1,0:T(8,128)(2,1)S(1)}, bf16[256,256]{1,0:T(8,128)(2,1)S(1)}...) custom-call(f32[8]{0:T(128)S(1)} %convert_element_type.20.flags_ref, ...), custom_call_target="tpu_custom_call" | custom-call | tf_op jit(solution)/shard_map/backward/pallas_call | solution.py:53
  77.9 1.2 collective-permute-start.14
  79.1 0.7 collective-permute-start.15
  79.7 1.3 %collective-permute-start.16 = (bf16[256,256]{1,0:T(8,128)(2,1)S(1)}, bf16[256,256]{1,0:T(8,128)(2,1)S(1)}, u32[]{:S(2)}, u32[]{:S(2)}) collective-permute-start(bf16[256,256]{1,0:T(8,128)(2,1)S(1)} %get-tuple-element.79.send2_ref), channel_id=1, source_target_pairs={{0,7},{1,0},{2,1},{3,2},{4,3},{5,4},{6,5},{7,6},{8,15},{9,8},{10,9... | collective-permute-start | bytes 393224 | tf_op jit(solution)/shard_map/ppermute | solution.py:443
  81.1 1.5 %sums.3 = (bf16[1024,256]{1,0:T(8,128)(2,1)S(1)}, f32[512,256]{1,0:T(8,128)S(1)}) custom-call(bf16[2048,2048]{1,0:T(8,128)(2,1)S(1)} %copy-done.2, bf16[256,2048]{1,0:T(8,128)(2,1)S(1)} %get-tuple-element.81.grad_pre_ref, f32[512,256]{1,0:T(8,128)S(1)} %get-tuple-element.82.grad_ref, bf16[256,256]{1,0:T(8,128)(2,1)S(1)} %get-tuple-element.102.src_ref, ...), custom_call_target="tpu_custom_call" | custom-call | tf_op jit(solution)/shard_map/sums/pallas_call | solution.py:53
  82.7 1.1 terms.3
  83.8 0.6 collective-permute-start.13
  84.4 2.0 %collective-permute-done.17.right_ref = bf16[256,256]{1,0:T(8,128)(2,1)S(1)} collective-permute-done((bf16[256,256]{1,0:T(8,128)(2,1)S(1)}, bf16[256,256]{1,0:T(8,128)(2,1)S(1)}, u32[]{:S(2)}, u32[]{:S(2)}) %collective-permute-start.17) | collective-permute-done | bytes 131104 | tf_op jit(solution)/shard_map/ppermute | solution.py:443
  86.4 2.3 %last.1 = (bf16[384,128]{1,0:T(8,128)(2,1)S(1)}, bf16[384,128]{1,0:T(8,128)(2,1)S(1)}) custom-call(f32[8]{0:T(128)S(1)} %convert_element_type.20.flags_ref, bf16[256,256]{1,0:T(8,128)(2,1)S(1)} %collective-permute-done.14.first_ref, bf16[256,256]{1,0:T(8,128)(2,1)S(1)} %collective-permute-done.15.second_ref, ...), custom_call_target="tpu_custom_call" | custom-call | tf_op jit(solution)/shard_map/last/pallas_call | solution.py:53
  88.7 0.1 collective-permute-start.18
  88.8 1.3 collective-permute-done.18.refs_5_
  90.1 0.1 merge.1
  90.2 20.9 %all_to_all.15.parts_ref = bf16[32,64,128]{2,1,0:T(8,128)(2,1)S(1)} all-to-all(bf16[32,64,128]{2,1,0:T(8,128)(2,1)S(1)} %bitcast.43), channel_id=1, replica_groups=mesh['grid'=4,'dom'=8] {'grid','dom'}, dimensions={0} | all-to-all | bytes 1048576 | tf_op jit(solution)/shard_map/all_to_all | solution.py:438
  111.2 0.1 share.1
  111.3 18.4 %all_to_all.16 = bf16[32,64,128]{2,1,0:T(8,128)(2,1)S(1)} all-to-all(bf16[32,64,128]{2,1,0:T(8,128)(2,1)S(1)} %share.1), channel_id=1, replica_groups=mesh['grid'=4,'dom'=8] {'grid','dom'}, dimensions={0} | all-to-all | bytes 1048576 | tf_op jit(solution)/shard_map/all_to_all | solution.py:438
  129.7 1.9 %collective-permute-done.19.other_ref = bf16[2048,128]{1,0:T(8,128)(2,1)S(1)} collective-permute-done((bf16[2048,128]{1,0:T(8,128)(2,1)S(1)}, bf16[2048,128]{1,0:T(8,128)(2,1)S(1)}, u32[]{:S(2)}, u32[]{:S(2)}) %collective-permute-start.19) | collective-permute-done | bytes 524320 | tf_op jit(solution)/shard_map/ppermute | solution.py:451
  131.6 1.9 %unpack.1 = (f32[128,256]{1,0:T(8,128)}, f32[256,256]{1,0:T(8,128)}, f32[2,256,256]{2,1,0:T(8,128)}, f32[2,256,256]{2,1,0:T(8,128)}, f32[2,256,256]{2,1,0:T(8,128)}) custom-call(f32[8]{0:T(128)S(1)} %convert_element_type.20.flags_ref, bf16[2048,128]{1,0:T(8,128)(2,1)S(1)} %bitcast.45, bf16[2048,128]{1,0:T(8,128)(2,1)S(1)} %collective-permute-done.19.other_ref), custom_call_target="tpu_custom_call" | custom-call | tf_op jit(solution)/shard_map/unpack/pallas_call | solution.py:53
  (77 shorter events, 0.3 us)
Async XLA Ops:
  0.6 11.6 %copy-start.28 = (s32[256]{0:T(256)S(1)}, s32[256]{0:T(256)}, u32[]{:S(2)}) copy-start(s32[256]{0:T(256)} %param.21) | copy-start | bytes 3076
  0.6 1.0 copy-start.9
  1.7 0.7 copy-start.14
  2.4 0.7 copy-start.15
  3.1 0.7 copy-start.16
  3.8 8.4 %copy-start.26 = (s32[2048]{0:T(1024)S(1)}, s32[2048]{0:T(1024)}, u32[]{:S(2)}) copy-start(s32[2048]{0:T(1024)} %param.22) | copy-start | bytes 24580
  3.8 8.4 %copy-start.27 = (s32[2048]{0:T(1024)S(1)}, s32[2048]{0:T(1024)}, u32[]{:S(2)}) copy-start(s32[2048]{0:T(1024)} %param.23) | copy-start | bytes 24580
  3.8 8.5 %copy-start.23 = (bf16[128,256]{1,0:T(8,128)(2,1)S(1)}, bf16[128,256]{1,0:T(8,128)(2,1)}, u32[]{:S(2)}) copy-start(bf16[128,256]{1,0:T(8,128)(2,1)} %param.26) | copy-start | bytes 196612
  3.8 9.2 %copy-start.17 = (bf16[2,256,256]{2,1,0:T(8,128)(2,1)S(1)}, bf16[2,256,256]{2,1,0:T(8,128)(2,1)}, u32[]{:S(2)}) copy-start(bf16[2,256,256]{2,1,0:T(8,128)(2,1)} %param.28) | copy-start | bytes 786436
  3.8 10.0 %copy-start.19 = (bf16[2,256,256]{2,1,0:T(8,128)(2,1)S(1)}, bf16[2,256,256]{2,1,0:T(8,128)(2,1)}, u32[]{:S(2)}) copy-start(bf16[2,256,256]{2,1,0:T(8,128)(2,1)} %param.29) | copy-start | bytes 786436
  3.8 11.0 %copy-start.24 = (f32[2048]{0:T(1024)S(1)}, f32[2048]{0:T(1024)}, u32[]{:S(2)}) copy-start(f32[2048]{0:T(1024)} %param.25) | copy-start | bytes 24580
  3.8 11.0 %copy-start.25 = (s32[2048]{0:T(1024)S(1)}, s32[2048]{0:T(1024)}, u32[]{:S(2)}) copy-start(s32[2048]{0:T(1024)} %param.24) | copy-start | bytes 24580
  3.8 12.1 %copy-start.22 = (bf16[2,256,256]{2,1,0:T(8,128)(2,1)S(1)}, bf16[2,256,256]{2,1,0:T(8,128)(2,1)}, u32[]{:S(2)}) copy-start(bf16[2,256,256]{2,1,0:T(8,128)(2,1)} %param.30) | copy-start | bytes 786436
  3.8 12.2 %copy-start.3 = (bf16[512,256]{1,0:T(8,128)(2,1)S(1)}, bf16[512,256]{1,0:T(8,128)(2,1)}, u32[]{:S(2)}) copy-start(bf16[512,256]{1,0:T(8,128)(2,1)} %grad_ref.5) | copy-start | bytes 786436
  4.8 24.1 %all-to-all-start = ((bf16[32,68,128]{2,1,0:T(8,128)(2,1)}), bf16[32,68,128]{2,1,0:T(8,128)(2,1)S(1)}, u32[]{:S(2)}, u32[]{:S(2)}) async-start(bf16[32,68,128]{2,1,0:T(8,128)(2,1)} %pack.1), calls=%async_computation | async-start | bytes 1179648 | tf_op jit(solution)/shard_map/all_to_all | solution.py:438
  15.9 3.3 %copy-start = (bf16[2048,2048]{1,0:T(8,128)(2,1)}, bf16[2048,2048]{1,0:T(8,128)(2,1)S(1)}, u32[]{:S(2)}) copy-start(bf16[2048,2048]{1,0:T(8,128)(2,1)S(1)} %get-tuple-element.52.picks_ref) | copy-start | bytes 25165828
  16.0 3.5 %copy-start.4 = (bf16[512,256]{1,0:T(8,128)(2,1)}, bf16[512,256]{1,0:T(8,128)(2,1)S(1)}, u32[]{:S(2)}) copy-start(bf16[512,256]{1,0:T(8,128)(2,1)S(1)} %get-tuple-element.75.rim_picks) | copy-start | bytes 786436
  16.0 3.5 %copy-start.6 = (bf16[256,512]{1,0:T(8,128)(2,1)}, bf16[256,512]{1,0:T(8,128)(2,1)S(1)}, u32[]{:S(2)}) copy-start(bf16[256,512]{1,0:T(8,128)(2,1)S(1)} %get-tuple-element.54.rim_picks_t) | copy-start | bytes 786436
  16.0 3.5 %copy-start.21 = (bf16[2,256,256]{1,2,0:T(8,128)(2,1)S(1)}, bf16[2,256,256]{1,2,0:T(8,128)(2,1)}, u32[]{:S(2)}) copy-start(bf16[2,256,256]{1,2,0:T(8,128)(2,1)} %copy.23) | copy-start | bytes 786436
  29.4 1.0 copy-start.7
  30.3 0.9 copy-start.10
  31.2 0.9 copy-start.12
  32.2 0.8 copy-start.13
  35.0 10.6 %collective-permute-start = (bf16[256,256]{1,0:T(8,128)(2,1)S(1)}, bf16[256,256]{1,0:T(8,128)(2,1)S(1)}, u32[]{:S(2)}, u32[]{:S(2)}) collective-permute-start(bf16[256,256]{1,0:T(8,128)(2,1)S(1)} %get-tuple-element.55), channel_id=1, source_target_pairs={{0,8},{8,0},{16,24},{24,16},{1,9},{9,1},{17,25},{25,17},{2,10},{10... | collective-permute-start | bytes 393224 | tf_op jit(solution)/shard_map/ppermute | solution.py:451
  36.4 9.2 %collective-permute-start.1 = (bf16[256,256]{1,0:T(8,128)(2,1)S(1)}, bf16[256,256]{1,0:T(8,128)(2,1)S(1)}, u32[]{:S(2)}, u32[]{:S(2)}) collective-permute-start(bf16[256,256]{1,0:T(8,128)(2,1)S(1)} %get-tuple-element.55), channel_id=1, source_target_pairs={{0,0},{8,16},{16,8},{24,24},{1,1},{9,17},{17,9},{25,25},{2,2},{10,... | collective-permute-start | bytes 393224 | tf_op jit(solution)/shard_map/ppermute | solution.py:451
  37.1 8.5 %collective-permute-start.2 = (bf16[256,256]{1,0:T(8,128)(2,1)S(1)}, bf16[256,256]{1,0:T(8,128)(2,1)S(1)}, u32[]{:S(2)}, u32[]{:S(2)}) collective-permute-start(bf16[256,256]{1,0:T(8,128)(2,1)S(1)} %get-tuple-element.55), channel_id=1, source_target_pairs={{0,1},{1,2},{2,3},{3,4},{4,5},{5,6},{6,7},{7,0},{8,9},{9,10},{10,1... | collective-permute-start | bytes 393224 | tf_op jit(solution)/shard_map/ppermute | solution.py:443
  37.1 8.5 %collective-permute-start.3 = (bf16[256,256]{1,0:T(8,128)(2,1)S(1)}, bf16[256,256]{1,0:T(8,128)(2,1)S(1)}, u32[]{:S(2)}, u32[]{:S(2)}) collective-permute-start(bf16[256,256]{1,0:T(8,128)(2,1)S(1)} %get-tuple-element.55), channel_id=1, source_target_pairs={{0,7},{1,0},{2,1},{3,2},{4,3},{5,4},{6,5},{7,6},{8,15},{9,8},{10,9... | collective-permute-start | bytes 393224 | tf_op jit(solution)/shard_map/ppermute | solution.py:443
  40.8 3.4 %copy-start.1 = (bf16[2048,2048]{1,0:T(8,128)(2,1)S(1)}, bf16[2048,2048]{1,0:T(8,128)(2,1)}, u32[]{:S(2)}) copy-start(bf16[2048,2048]{1,0:T(8,128)(2,1)} %copy-done) | copy-start | bytes 25165828
  44.1 3.4 %copy-start.2 = (bf16[2048,2048]{1,0:T(8,128)(2,1)S(1)}, bf16[2048,2048]{1,0:T(8,128)(2,1)}, u32[]{:S(2)}) copy-start(bf16[2048,2048]{1,0:T(8,128)(2,1)} %copy-done) | copy-start | bytes 25165828
  44.1 3.4 %copy-start.8 = (bf16[256,512]{1,0:T(8,128)(2,1)S(1)}, bf16[256,512]{1,0:T(8,128)(2,1)}, u32[]{:S(2)}) copy-start(bf16[256,512]{1,0:T(8,128)(2,1)} %copy-done.6) | copy-start | bytes 786436
  47.6 8.9 %copy-start.18 = (bf16[2,256,256]{2,1,0:T(8,128)(2,1)S(1)}, bf16[2,256,256]{2,1,0:T(8,128)(2,1)}, u32[]{:S(2)}) copy-start(bf16[2,256,256]{2,1,0:T(8,128)(2,1)} %param.28) | copy-start | bytes 786436
  51.0 7.0 %collective-permute-start.4 = (bf16[256,256]{1,0:T(8,128)(2,1)S(1)}, bf16[256,256]{1,0:T(8,128)(2,1)S(1)}, u32[]{:S(2)}, u32[]{:S(2)}) collective-permute-start(bf16[256,256]{1,0:T(8,128)(2,1)S(1)} %get-tuple-element.57), channel_id=1, source_target_pairs={{0,8},{8,0},{16,24},{24,16},{1,9},{9,1},{17,25},{25,17},{2,10},{10... | collective-permute-start | bytes 393224 | tf_op jit(solution)/shard_map/ppermute | solution.py:451
  53.1 4.8 %collective-permute-start.5 = (bf16[256,256]{1,0:T(8,128)(2,1)S(1)}, bf16[256,256]{1,0:T(8,128)(2,1)S(1)}, u32[]{:S(2)}, u32[]{:S(2)}) collective-permute-start(bf16[256,256]{1,0:T(8,128)(2,1)S(1)} %get-tuple-element.57), channel_id=1, source_target_pairs={{0,0},{8,16},{16,8},{24,24},{1,1},{9,17},{17,9},{25,25},{2,2},{10,... | collective-permute-start | bytes 393224 | tf_op jit(solution)/shard_map/ppermute | solution.py:451
  53.7 5.9 %collective-permute-start.6 = (bf16[256,256]{1,0:T(8,128)(2,1)S(1)}, bf16[256,256]{1,0:T(8,128)(2,1)S(1)}, u32[]{:S(2)}, u32[]{:S(2)}) collective-permute-start(bf16[256,256]{1,0:T(8,128)(2,1)S(1)} %get-tuple-element.57), channel_id=1, source_target_pairs={{0,1},{1,2},{2,3},{3,4},{4,5},{5,6},{6,7},{7,0},{8,9},{9,10},{10,1... | collective-permute-start | bytes 393224 | tf_op jit(solution)/shard_map/ppermute | solution.py:443
  53.8 5.8 %collective-permute-start.7 = (bf16[256,256]{1,0:T(8,128)(2,1)S(1)}, bf16[256,256]{1,0:T(8,128)(2,1)S(1)}, u32[]{:S(2)}, u32[]{:S(2)}) collective-permute-start(bf16[256,256]{1,0:T(8,128)(2,1)S(1)} %get-tuple-element.57), channel_id=1, source_target_pairs={{0,7},{1,0},{2,1},{3,2},{4,3},{5,4},{6,5},{7,6},{8,15},{9,8},{10,9... | collective-permute-start | bytes 393224 | tf_op jit(solution)/shard_map/ppermute | solution.py:443
  57.9 12.8 %copy-start.20 = (bf16[2,256,256]{2,1,0:T(8,128)(2,1)S(1)}, bf16[2,256,256]{2,1,0:T(8,128)(2,1)}, u32[]{:S(2)}) copy-start(bf16[2,256,256]{2,1,0:T(8,128)(2,1)} %param.29) | copy-start | bytes 786436
  63.4 11.6 %collective-permute-start.10 = (bf16[256,256]{1,0:T(8,128)(2,1)S(1)}, bf16[256,256]{1,0:T(8,128)(2,1)S(1)}, u32[]{:S(2)}, u32[]{:S(2)}) collective-permute-start(bf16[256,256]{1,0:T(8,128)(2,1)S(1)} %get-tuple-element.65.send1_ref), channel_id=1, source_target_pairs={{0,0},{8,16},{16,8},{24,24},{1,1},{9,17},{17,9},{25,25},{2,2},{10,... | collective-permute-start | bytes 393224 | tf_op jit(solution)/shard_map/ppermute | solution.py:451
  64.1 10.9 %collective-permute-start.11 = (bf16[256,256]{1,0:T(8,128)(2,1)S(1)}, bf16[256,256]{1,0:T(8,128)(2,1)S(1)}, u32[]{:S(2)}, u32[]{:S(2)}) collective-permute-start(bf16[256,256]{1,0:T(8,128)(2,1)S(1)} %get-tuple-element.66.send2_ref), channel_id=1, source_target_pairs={{0,7},{1,0},{2,1},{3,2},{4,3},{5,4},{6,5},{7,6},{8,15},{9,8},{10,9... | collective-permute-start | bytes 393224 | tf_op jit(solution)/shard_map/ppermute | solution.py:443
  66.3 8.8 %collective-permute-start.12 = (bf16[256,256]{1,0:T(8,128)(2,1)S(1)}, bf16[256,256]{1,0:T(8,128)(2,1)S(1)}, u32[]{:S(2)}, u32[]{:S(2)}) collective-permute-start(bf16[256,256]{1,0:T(8,128)(2,1)S(1)} %get-tuple-element.67.send3_ref), channel_id=1, source_target_pairs={{0,1},{1,2},{2,3},{3,4},{4,5},{5,6},{6,7},{7,0},{8,9},{9,10},{10,1... | collective-permute-start | bytes 393224 | tf_op jit(solution)/shard_map/ppermute | solution.py:443
  66.3 8.8 %collective-permute-start.9 = (bf16[256,256]{1,0:T(8,128)(2,1)S(1)}, bf16[256,256]{1,0:T(8,128)(2,1)S(1)}, u32[]{:S(2)}, u32[]{:S(2)}) collective-permute-start(bf16[256,256]{1,0:T(8,128)(2,1)S(1)} %get-tuple-element.64.send0_ref), channel_id=1, source_target_pairs={{0,8},{8,0},{16,24},{24,16},{1,9},{9,1},{17,25},{25,17},{2,10},{10... | collective-permute-start | bytes 393224 | tf_op jit(solution)/shard_map/ppermute | solution.py:451
  73.9 1.2 copy-start.5
  77.9 5.9 %collective-permute-start.14 = (bf16[256,256]{1,0:T(8,128)(2,1)S(1)}, bf16[256,256]{1,0:T(8,128)(2,1)S(1)}, u32[]{:S(2)}, u32[]{:S(2)}) collective-permute-start(bf16[256,256]{1,0:T(8,128)(2,1)S(1)} %get-tuple-element.77.send0_ref), channel_id=1, source_target_pairs={{0,8},{8,0},{16,24},{24,16},{1,9},{9,1},{17,25},{25,17},{2,10},{10... | collective-permute-start | bytes 393224 | tf_op jit(solution)/shard_map/ppermute | solution.py:451
  79.1 5.3 %collective-permute-start.15 = (bf16[256,256]{1,0:T(8,128)(2,1)S(1)}, bf16[256,256]{1,0:T(8,128)(2,1)S(1)}, u32[]{:S(2)}, u32[]{:S(2)}) collective-permute-start(bf16[256,256]{1,0:T(8,128)(2,1)S(1)} %get-tuple-element.78.send1_ref), channel_id=1, source_target_pairs={{0,0},{8,16},{16,8},{24,24},{1,1},{9,17},{17,9},{25,25},{2,2},{10,... | collective-permute-start | bytes 393224 | tf_op jit(solution)/shard_map/ppermute | solution.py:451
  79.7 4.6 %collective-permute-start.16 = (bf16[256,256]{1,0:T(8,128)(2,1)S(1)}, bf16[256,256]{1,0:T(8,128)(2,1)S(1)}, u32[]{:S(2)}, u32[]{:S(2)}) collective-permute-start(bf16[256,256]{1,0:T(8,128)(2,1)S(1)} %get-tuple-element.79.send2_ref), channel_id=1, source_target_pairs={{0,7},{1,0},{2,1},{3,2},{4,3},{5,4},{6,5},{7,6},{8,15},{9,8},{10,9... | collective-permute-start | bytes 393224 | tf_op jit(solution)/shard_map/ppermute | solution.py:443
  81.1 5.3 %collective-permute-start.17 = (bf16[256,256]{1,0:T(8,128)(2,1)S(1)}, bf16[256,256]{1,0:T(8,128)(2,1)S(1)}, u32[]{:S(2)}, u32[]{:S(2)}) collective-permute-start(bf16[256,256]{1,0:T(8,128)(2,1)S(1)} %get-tuple-element.80.send3_ref), channel_id=1, source_target_pairs={{0,1},{1,2},{2,3},{3,4},{4,5},{5,6},{6,7},{7,0},{8,9},{9,10},{10,1... | collective-permute-start | bytes 393224 | tf_op jit(solution)/shard_map/ppermute | solution.py:443
  81.1 7.7 %collective-permute-start.8 = (bf16[768,128]{1,0:T(8,128)(2,1)S(1)}, bf16[768,128]{1,0:T(8,128)(2,1)S(1)}, u32[]{:S(2)}, u32[]{:S(2)}) collective-permute-start(bf16[768,128]{1,0:T(8,128)(2,1)S(1)} %get-tuple-element.73), channel_id=1, source_target_pairs={{0,1},{1,0},{2,3},{3,2},{4,5},{5,4},{6,7},{7,6},{8,9},{9,8},{10,11... | collective-permute-start | bytes 589832 | tf_op jit(solution)/shard_map/ppermute | solution.py:451
  82.6 3.7 %copy-start.11 = (bf16[256,256]{1,0:T(8,128)(2,1)S(1)}, bf16[256,256]{1,0:T(8,128)(2,1)}, u32[]{:S(2)}) copy-start(bf16[256,256]{1,0:T(8,128)(2,1)} %enc_out_ref.3) | copy-start | bytes 393220
  83.8 5.0 %collective-permute-start.13 = (bf16[768,128]{1,0:T(8,128)(2,1)S(1)}, bf16[768,128]{1,0:T(8,128)(2,1)S(1)}, u32[]{:S(2)}, u32[]{:S(2)}) collective-permute-start(bf16[768,128]{1,0:T(8,128)(2,1)S(1)} %get-tuple-element.86), channel_id=1, source_target_pairs={{0,1},{1,0},{2,3},{3,2},{4,5},{5,4},{6,7},{7,6},{8,9},{9,8},{10,11... | collective-permute-start | bytes 589832 | tf_op jit(solution)/shard_map/ppermute | solution.py:451
  88.7 1.4 %collective-permute-start.18 = (bf16[384,128]{1,0:T(8,128)(2,1)S(1)}, bf16[384,128]{1,0:T(8,128)(2,1)S(1)}, u32[]{:S(2)}, u32[]{:S(2)}) collective-permute-start(bf16[384,128]{1,0:T(8,128)(2,1)S(1)} %get-tuple-element.92), channel_id=1, source_target_pairs={{0,1},{1,0},{2,3},{3,2},{4,5},{5,4},{6,7},{7,6},{8,9},{9,8},{10,11... | collective-permute-start | bytes 294920 | tf_op jit(solution)/shard_map/ppermute | solution.py:451
  129.6 1.9 %collective-permute-start.19 = (bf16[2048,128]{1,0:T(8,128)(2,1)S(1)}, bf16[2048,128]{1,0:T(8,128)(2,1)S(1)}, u32[]{:S(2)}, u32[]{:S(2)}) collective-permute-start(bf16[2048,128]{1,0:T(8,128)(2,1)S(1)} %bitcast.44), channel_id=1, source_target_pairs={{0,1},{1,0},{2,3},{3,2},{4,5},{5,4},{6,7},{7,6},{8,9},{9,8},{10,11... | collective-permute-start | bytes 1572872 | tf_op jit(solution)/shard_map/ppermute | solution.py:451

commit v4 on v3

--- a/solution.py
+++ b/solution.py
@@ -44,16 +44,21 @@
     return 0.5 * jnp.tanh(0.5 * values) + 0.5
 
 
-def call(body, outs, scratch, name, flagged=False, space=pltpu.VMEM):
+def call(body, outs, scratch, name, flagged=False, far=()):
     vmem = pl.BlockSpec(memory_space=pltpu.VMEM)
-    operand = pl.BlockSpec(memory_space=space)
-    first = pl.BlockSpec(memory_space=pltpu.SMEM) if flagged else operand
 
     def run(*args):
+        specs = [vmem] * len(args)
+        if flagged:
+            specs[0] = pl.BlockSpec(memory_space=pltpu.SMEM)
+        args = list(args)
+        for at in far:
+            specs[at] = pl.BlockSpec(memory_space=pltpu.HBM)
+            args[at] = pltpu.with_memory_space_constraint(args[at], pltpu.HBM)
         return pl.pallas_call(
             body,
             out_shape=tuple(jax.ShapeDtypeStruct(shape, dtype) for shape, dtype in outs),
-            in_specs=[first] + [operand] * (len(args) - 1),
+            in_specs=specs,
             out_specs=tuple(vmem for _ in outs),
             scratch_shapes=scratch,
             compiler_params=pltpu.CompilerParams(vmem_limit_bytes=GRANT),
@@ -95,7 +100,7 @@
     copies[0].wait()
 
 
-PAIR, ODD_GRID, ODD_DOM = 4, 6, 7
+PAIR, ODD_GRID, ODD_DOM, PLACE = 4, 6, 7, 8
 
 
 def picks_body(rows_ref, bound_ref, picks_ref, rim_picks, rim_picks_t):
@@ -122,23 +127,58 @@
     return [rows * flags_ref[side].astype(BF) for side, rows in enumerate(ordered)]
 
 
+def put_col_rows(flags_ref, packed_ref, bucket, rows_ref):
+    peers = packed_ref.shape[0]
+    per_row = LANES // bucket
+    place = flags_ref[PLACE].astype(jnp.int32)
+    lane = lax.broadcasted_iota(jnp.int32, (4, LANES), 1)
+    for row in range(peers // per_row):
+        out = jnp.zeros((4, LANES), F32)
+        for j in range(per_row):
+            part = packed_ref[row * per_row + j, bucket : bucket + 4, :].astype(F32)
+            shift = lax.rem((j - place + per_row) * bucket, LANES)
+            part = pltpu.roll(part, shift, 1)
+            here = (lane >= j * bucket) & (lane < (j + 1) * bucket)
+            out = jnp.where(here, part, out)
+        at = pl.ds(row * LANES, LANES)
+        rows_ref[0:1, at] = out[0:1] * 256.0 + out[1:2]
+        rows_ref[1:2, at] = out[2:3] + out[3:4]
+
+
 def encode_body(
     bucket,
+    flags_ref,
     packed_ref,
-    rows_ref,
-    enc_in_t_ref,
-    enc_out_ref,
-    static_ref,
-    rim_picks_t,
+    enc_in_t_far,
+    enc_out_far,
+    static_far,
+    bound_far,
     pooled_ref,
     slope_ref,
     picks_ref,
     state_ref,
     rim_ref,
     act_ref,
+    rows_ref,
+    enc_in_t_ref,
+    enc_out_ref,
+    static_ref,
+    bound_ref,
+    rim_picks,
+    sems,
 ):
     nodes = static_ref.shape[0]
     peers_step = CHUNK // bucket
+    copies = [
+        pltpu.make_async_copy(enc_in_t_far, enc_in_t_ref, sems.at[0]),
+        pltpu.make_async_copy(enc_out_far, enc_out_ref, sems.at[1]),
+        pltpu.make_async_copy(static_far, static_ref, sems.at[2]),
+        pltpu.make_async_copy(bound_far, bound_ref, sems.at[3]),
+    ]
+    for copy in copies:
+        copy.start()
+    put_col_rows(flags_ref, packed_ref, bucket, rows_ref)
+    copies[0].wait()
 
     def step(start, at):
         first = start // bucket
@@ -152,21 +192,25 @@
 
     chunks(rows_ref.shape[1], step)
     pooled_ref[...] = mm_t(picks_ref[...], act_ref[...]).astype(BF)
+    for copy in copies[1:]:
+        copy.wait()
+    put_picks(rim_picks, 0, bound_ref[0:1, :], nodes)
     state = static_ref[...].astype(F32) + mm(pooled_ref[...], enc_out_ref[...])
-    put_state(state, state_ref, rim_ref, rim_picks_t)
-
-
-def own_body(state_ref, src_t_ref, dst_t_ref, picks_ref, out_ref, table_ref):
+    state_ref[...] = state.astype(BF)
+    rim_ref[...] = t_mm(rim_picks[...], state_ref[...]).astype(BF)
+
+
+def own_body(layer, state_ref, src_t_ref, dst_t_ref, picks_ref, out_ref, table_ref):
     nodes = state_ref.shape[0]
     held = state_ref[...]
-    table_ref[:, :nodes] = mm_t(dst_t_ref[...], held).astype(BF)
-    table_ref[:, nodes:] = mm_t(src_t_ref[...], held).astype(BF)
+    table_ref[:, :nodes] = mm_t(dst_t_ref[layer], held).astype(BF)
+    table_ref[:, nodes:] = mm_t(src_t_ref[layer], held).astype(BF)
     out_ref[...] = mm(table_ref[...], picks_ref[: 2 * nodes, :])
 
 
-def back_body(msg_ref, grad_ref, rows_ref, picks_ref, out_ref):
+def back_body(layer, msg_ref, grad_ref, rows_ref, picks_ref, out_ref):
     nodes = grad_ref.shape[0]
-    back = mm_t(msg_ref[...], grad_ref[...]).astype(BF)
+    back = mm_t(msg_ref[layer], grad_ref[...]).astype(BF)
     out_ref[...] = mm(back, picks_ref[:nodes, :]) * rows_ref[2:3, :]
 
 
@@ -177,6 +221,7 @@
 
 
 def forward_body(
+    layer,
     flags_ref,
     first_ref,
     second_ref,
@@ -197,7 +242,7 @@
     act_ref,
 ):
     nodes = state_ref.shape[0]
-    fill_rims(full_ref, flags_ref, (first_ref, second_ref, left_ref, right_ref), src_t_ref)
+    fill_rims(full_ref, flags_ref, (first_ref, second_ref, left_ref, right_ref), src_t_ref.at[layer])
 
     def step(start, at):
         pre = own_pre_ref[:, at] + mm(full_ref[...], picks_ref[2 * nodes :, at])
@@ -208,7 +253,7 @@
 
     chunks(rows_ref.shape[1], step)
     node_act_ref[...] = mm_t(picks_ref[:nodes, :], act_ref[...]).astype(BF)
-    state = state_ref[...].astype(F32) + mm(node_act_ref[...], msg_ref[...])
+    state = state_ref[...].astype(F32) + mm(node_act_ref[...], msg_ref[layer])
     put_state(state, next_state_ref, rim_ref, rim_picks_t)
 
 
@@ -223,6 +268,7 @@
 
 
 def turn_body(
+    layer,
     flags_ref,
     first_ref,
     second_ref,
@@ -242,7 +288,7 @@
     full_ref,
 ):
     first = picks_ref.shape[0] - full_ref.shape[1]
-    fill_rims(full_ref, flags_ref, (first_ref, second_ref, left_ref, right_ref), src_t_ref)
+    fill_rims(full_ref, flags_ref, (first_ref, second_ref, left_ref, right_ref), src_t_ref.at[layer])
 
     def step(start, at):
         pre = own_pre_ref[:, at] + mm(full_ref[...], picks_ref[first:, at])
@@ -265,6 +311,7 @@
 
 
 def backward_body(
+    layer,
     flags_ref,
     first_ref,
     second_ref,
@@ -285,9 +332,9 @@
 ):
     nodes = partial_ref.shape[0]
     returned = (first_ref, second_ref, left_ref, right_ref)
-    grad = merged_grad(partial_ref, flags_ref, returned, src_ref, rim_picks)
+    grad = merged_grad(partial_ref, flags_ref, returned, src_ref.at[layer], rim_picks)
     grad_ref[...] = grad
-    back = mm_t(msg_ref[...], grad.astype(BF)).astype(BF)
+    back = mm_t(msg_ref[layer - 1], grad.astype(BF)).astype(BF)
 
     def step(start, at):
         grad_pre = mm(back, picks_ref[:nodes, at]) * slope_ref[:, at].astype(F32)
@@ -298,20 +345,20 @@
     put_sends(flags_ref, sums, (send0_ref, send1_ref, send2_ref, send3_ref))
 
 
-def sums_body(picks_ref, grad_pre_ref, grad_ref, src_ref, dst_ref, own_ref, partial_ref):
+def sums_body(layer, picks_ref, grad_pre_ref, grad_ref, src_ref, dst_ref, own_ref, partial_ref):
     nodes = grad_ref.shape[0]
     own_ref[...] = mm_t(picks_ref[: 2 * nodes, :], grad_pre_ref[...]).astype(BF)
     partial_ref[...] = (
         grad_ref[...].astype(F32)
-        + mm_t(own_ref[:nodes, :], dst_ref[...])
-        + mm_t(own_ref[nodes:, :], src_ref[...])
-    )
-
-
-def out_body(picks_ref, act_edges_ref, state_ref, msg_ref, act_ref, out_ref):
+        + mm_t(own_ref[:nodes, :], dst_ref[layer])
+        + mm_t(own_ref[nodes:, :], src_ref[layer])
+    )
+
+
+def out_body(layer, picks_ref, act_edges_ref, state_ref, msg_ref, act_ref, out_ref):
     nodes = state_ref.shape[0]
     act_ref[...] = mm_t(picks_ref[:nodes, :], act_edges_ref[...]).astype(BF)
-    out_ref[...] = (state_ref[...].astype(F32) + mm(act_ref[...], msg_ref[...])).astype(BF)
+    out_ref[...] = (state_ref[...].astype(F32) + mm(act_ref[...], msg_ref[layer])).astype(BF)
 
 
 def put_halves(flags_ref, first, term, keep_ref, send_ref):
@@ -378,7 +425,7 @@
     fin = packed_ref.shape[2]
     peers_step = CHUNK // bucket
     returned = (first_ref, second_ref, left_ref, right_ref)
-    grad = merged_grad(partial_ref, flags_ref, returned, src_ref, rim_picks).astype(BF)
+    grad = merged_grad(partial_ref, flags_ref, returned, src_ref.at[0], rim_picks).astype(BF)
     back = mm_t(enc_out_ref[...], grad).astype(BF)
     in_term = jnp.zeros((enc_out_ref.shape[0], fin), F32)
     for start in range(0, picks_ref.shape[1], CHUNK):
@@ -467,6 +514,10 @@
         turned(sends[2], "dom", -1),
         turned(sends[3], "dom", 1),
     )
+
+
+def floats(scalars):
+    return jnp.stack([scalar.astype(F32) for scalar in scalars])
 
 
 def per_device(
@@ -502,7 +553,7 @@
         [((peers, bucket + 4, fin), BF)],
         held + [pltpu.SemaphoreType.DMA((4,))],
         "pack",
-        space=pltpu.HBM,
+        far=range(4),
     )(
         columns.reshape(peers, bucket, fin),
         col_slot.reshape(lanes),
@@ -515,7 +566,7 @@
     dom_at, dom_count = lax.axis_index("dom"), lax.axis_size("dom")
     odd_grid, odd_dom = grid_at % 2, dom_at % 2
     up, down = grid_at > 0, grid_at < grid_count - 1
-    flags = jnp.stack(
+    flags = floats(
         [
             up,
             down,
@@ -525,8 +576,9 @@
             jnp.where(odd_grid == 1, down, up),
             odd_grid == 1,
             odd_dom == 1,
+            (grid_at * dom_count + dom_at) % (LANES // bucket),
         ]
-    ).astype(F32)
+    )
     edge_scale = edge_weight * edge_live.astype(F32)
     edge_rows = jnp.stack([edge_src.astype(F32), edge_dst.astype(F32), edge_scale])
     bound = boundary_idx.astype(F32)[None]
@@ -543,63 +595,83 @@
     edge_buf = pltpu.VMEM((width, edges), BF)
     table_buf = pltpu.VMEM((width, 2 * nodes), BF)
 
+    flags, edge_rows, bound, enc_in_t, src_t, dst_t = lax.optimization_barrier(
+        (flags, edge_rows, bound, enc_in_t, src_t, dst_t)
+    )
+
+    pooled, col_slope, slot_picks, state0, rim0 = call(
+        functools.partial(encode_body, bucket),
+        [node_shape, ((width, cols), BF), ((nodes, cols), BF), node_shape, rim_shape],
+        [
+            edge_buf,
+            pltpu.VMEM((2, cols), F32),
+            pltpu.VMEM((width, fin), BF),
+            pltpu.VMEM(enc_out.shape, BF),
+            pltpu.VMEM((nodes, width), BF),
+            pltpu.VMEM((1, rim), F32),
+            pltpu.VMEM((nodes, rim), BF),
+            pltpu.SemaphoreType.DMA((4,)),
+        ],
+        "encode",
+        True,
+        far=range(2, 6),
+    )(flags, packed, enc_in_t, enc_out, node_static, bound)
+
+    state0, edge_rows, bound = lax.optimization_barrier((state0, edge_rows, bound))
     picks, rim_picks, rim_picks_t = call(
         picks_body,
         [((2 * nodes + ext, edges), BF), ((nodes, rim), BF), ((rim, nodes), BF)],
         [],
         "picks",
     )(edge_rows, bound)
-    (back1,) = call(back_body, [edge_wide], [], "back")(msg_proj[1], node_cotangent, edge_rows, picks)
-    packed, back1 = lax.optimization_barrier((packed, back1))
-
-    at = (grid_at * dom_count + dom_at) % (LANES // bucket)
-    extra = lax.dynamic_slice_in_dim(packed[:, bucket : bucket + 4], at * bucket, bucket, 2)
-    extra = extra.astype(F32).transpose(1, 0, 2).reshape(4, cols)
-    col_rows = jnp.stack([extra[0] * 256.0 + extra[1], extra[2] + extra[3]])
-
-    pooled, col_slope, slot_picks, state0, rim0 = call(
-        functools.partial(encode_body, bucket),
-        [node_shape, ((width, cols), BF), ((nodes, cols), BF), node_shape, rim_shape],
-        [pltpu.VMEM((width, cols), BF)],
-        "encode",
-    )(packed, col_rows, enc_in_t, enc_out, node_static, rim_picks_t)
 
     rims0 = from_neighbours(rim0)
-    (pre0,) = call(own_body, [edge_wide], [table_buf], "own")(state0, src_t[0], dst_t[0], picks)
+    (pre0,) = call(functools.partial(own_body, 0), [edge_wide], [table_buf], "own")(
+        state0, src_t, dst_t, picks
+    )
     slope0, act0, state1, rim1 = call(
-        forward_body,
+        functools.partial(forward_body, 0),
         [edge_shape, node_shape, node_shape, rim_shape],
         [full, edge_buf],
         "forward",
         True,
-    )(flags, *rims0, pre0, edge_rows, picks, state0, src_t[0], msg_proj[0], rim_picks_t)
+    )(flags, *rims0, pre0, edge_rows, picks, state0, src_t, msg_proj, rim_picks_t)
 
     rims1 = from_neighbours(rim1)
-    (pre1,) = call(own_body, [edge_wide], [table_buf], "own")(state1, src_t[1], dst_t[1], picks)
+    (back1,) = call(functools.partial(back_body, 1), [edge_wide], [], "back")(
+        msg_proj, node_cotangent, edge_rows, picks
+    )
+    (pre1,) = call(functools.partial(own_body, 1), [edge_wide], [table_buf], "own")(
+        state1, src_t, dst_t, picks
+    )
     act_edges1, grad_pre1, *sends1 = call(
-        turn_body, [edge_shape, edge_shape] + [rim_shape] * 4, [full], "turn", True
-    )(flags, *rims1, pre1, back1, edge_rows, picks, src_t[1])
+        functools.partial(turn_body, 1), [edge_shape, edge_shape] + [rim_shape] * 4, [full], "turn", True
+    )(flags, *rims1, pre1, back1, edge_rows, picks, src_t)
 
     returned1 = to_neighbours(sends1)
     own_shape = ((2 * nodes, width), BF)
     halves = [((3 * width, width // 2), BF)] * 2
-    own1, partial1 = call(sums_body, [own_shape, node_wide], [], "sums")(
-        picks, grad_pre1, node_cotangent, src_proj[1], dst_proj[1]
-    )
-    act1, node_out = call(out_body, [node_shape, node_shape], [], "out")(
-        picks, act_edges1, state1, msg_proj[1]
+    own1, partial1 = call(functools.partial(sums_body, 1), [own_shape, node_wide], [], "sums")(
+        picks, grad_pre1, node_cotangent, src_proj, dst_proj
+    )
+    act1, node_out = call(functools.partial(out_body, 1), [node_shape, node_shape], [], "out")(
+        picks, act_edges1, state1, msg_proj
     )
     keep1, send1 = call(terms_body, halves, [], "terms", True)(
         flags, *rims1, *sends1, state1, own1, act1, node_cotangent
     )
     partial1, keep1, send1 = lax.optimization_barrier((partial1, keep1, send1))
     grad1, grad_pre0, *sends0 = call(
-        backward_body, [node_wide, edge_shape] + [rim_shape] * 4, [], "backward", True
-    )(flags, *returned1, partial1, src_proj[1], rim_picks, msg_proj[0], slope0, picks)
+        functools.partial(backward_body, 1),
+        [node_wide, edge_shape] + [rim_shape] * 4,
+        [],
+        "backward",
+        True,
+    )(flags, *returned1, partial1, src_proj, rim_picks, msg_proj, slope0, picks)
 
     returned0 = to_neighbours(sends0)
-    own0, partial0 = call(sums_body, [own_shape, node_wide], [], "sums")(
-        picks, grad_pre0, grad1, src_proj[0], dst_proj[0]
+    own0, partial0 = call(functools.partial(sums_body, 0), [own_shape, node_wide], [], "sums")(
+        picks, grad_pre0, grad1, src_proj, dst_proj
     )
     keep0, send0 = call(terms_body, halves, [], "terms", True)(
         flags, *rims0, *sends0, state0, own0, act0, grad1
@@ -611,7 +683,7 @@
         [],
         "last",
         True,
-    )(flags, *returned0, partial0, src_proj[0], rim_picks, packed, enc_out, pooled, col_slope, slot_picks)
+    )(flags, *returned0, partial0, src_proj, rim_picks, packed, enc_out, pooled, col_slope, slot_picks)
 
     total_rows = 2 * 3 * width + fin + hidden
     share = -(-total_rows // (16 * peers)) * 16

time: 134 us -> 123 us (0.918)
  local copies, waits for them, and re-layouts: 18.5 us -> 1.14 us
  waiting for transfers between devices: 16.4 us -> 23.3 us
  Pallas kernels: 29.1 us -> 31.8 us
  starting transfers between devices: 28.6 us -> 26.4 us
    unnamed x61 -> x27, local copies, waits for them, and re-layouts: 17.1 us -> 1.05 us
    all_to_all x1, waiting for transfers between devices: 9.42 us -> 15 us  [exchange(): return lax.all_to_all(shard, AXES, split_axis=0, concat_axis=0, tiled=True)]
    ppermute x8, starting transfers between devices: 8.88 us -> 4.83 us  [turned(): lax.ppermute(shard, axis, [(i, (i + by) % count) for i in range(count)])]
    pallas_call x18, Pallas kernels: 29.1 us -> 31.8 us  [run(): pl.pallas_call(body, out_shape=tuple((jax.ShapeDtypeStruct(shape, dtype)...]
    ppermute x12, waiting for transfers between devices: 3.2 us -> 5.49 us  [swapped(): return lax.ppermute(shard, axis, list(enumerate(partner)))]
    ppermute x12, starting transfers between devices: 12.4 us -> 14.2 us  [swapped(): return lax.ppermute(shard, axis, list(enumerate(partner)))]
  transfers between devices with their start and end apart: 21 -> 21, of which waited for: 5 -> 8; matrix products, arithmetic and copies ran while one was open for 3% -> 1% of each run, Pallas kernels for 11% -> 11%
where the time goes in v4:
time: 123 us
  blocking collectives  38.8 us (32%)
  Pallas kernels  31.8 us (26%)
  starting transfers between devices  26.4 us (21%)
  waiting for transfers between devices  23.3 us (19%)
    all_to_all x2, blocking collectives, exchange(): return lax.all_to_all(shard, AXES, split_axis=0, concat_axis=0, tiled=True)  38.8 us
    pallas_call x18, Pallas kernels, run(): pl.pallas_call(body, out_shape=tuple((jax.ShapeDtypeStruct(shape, dtype)...  31.8 us
    all_to_all x1, waiting for transfers between devices, exchange(): return lax.all_to_all(shard, AXES, split_axis=0, concat_axis=0, tiled=True)  15 us
    ppermute x12, starting transfers between devices, swapped(): return lax.ppermute(shard, axis, list(enumerate(partner)))  14.2 us
    all_to_all x1, starting transfers between devices, exchange(): return lax.all_to_all(shard, AXES, split_axis=0, concat_axis=0, tiled=True)  7.33 us
    ppermute x12, waiting for transfers between devices, swapped(): return lax.ppermute(shard, axis, list(enumerate(partner)))  5.49 us
    ppermute x8, starting transfers between devices, turned(): lax.ppermute(shard, axis, [(i, (i + by) % count) for i in range(count)])  4.83 us
    ppermute x8, waiting for transfers between devices, turned(): lax.ppermute(shard, axis, [(i, (i + by) % count) for i in range(count)])  2.87 us
  transfers between devices with their start and end apart: 21, of which 8 were waited for; matrix products, arithmetic and copies ran while one was open for 1% of the time, Pallas kernels for 11%

profile of v4, /device:TPU:0, one launch (start us, length us, event | category | flops | bytes accessed | tf_op | source)
XLA Modules:
  0.0 123.1 jit_solution(16731764870864809608)
XLA Ops:
  0.7 2.0 %pack.1 = bf16[32,68,128]{2,1,0:T(8,128)(2,1)} custom-call(bf16[32,64,128]{2,1,0:T(8,128)(2,1)} %bitcast.33, s32[16,128]{1,0:T(8,128)} %bitcast.38, s32[16,128]{1,0:T(8,128)} %bitcast.39, f32[16,128]{1,0:T(8,128)} %bitcast.40), custom_call_target="tpu_custom_call" | custom-call | tf_op jit(solution)/shard_map/pack/pallas_call | solution.py:58
  2.7 7.3 %all-to-all-start = ((bf16[32,68,128]{2,1,0:T(8,128)(2,1)}), bf16[32,68,128]{2,1,0:T(8,128)(2,1)S(1)}, u32[]{:S(2)}, u32[]{:S(2)}) async-start(bf16[32,68,128]{2,1,0:T(8,128)(2,1)} %pack.1), calls=%async_computation | async-start | bytes 1179648 | tf_op jit(solution)/shard_map/all_to_all | solution.py:485
  10.1 0.6 convert_element_type.27
  10.7 0.7 copy.22
  11.4 0.1 copy.24
  11.6 0.1 copy.23
  11.7 0.1 stack.83.flags_ref
  11.9 15.0 %all-to-all-done.packed_ref = bf16[32,68,128]{2,1,0:T(8,128)(2,1)S(1)} async-done(((bf16[32,68,128]{2,1,0:T(8,128)(2,1)}), bf16[32,68,128]{2,1,0:T(8,128)(2,1)S(1)}, u32[]{:S(2)}, u32[]{:S(2)}) %all-to-all-start) | async-done | bytes 557088 | tf_op jit(solution)/shard_map/all_to_all | solution.py:485
  26.8 3.6 %encode.1 = (bf16[512,256]{1,0:T(8,128)(2,1)S(1)}, bf16[256,2048]{1,0:T(8,128)(2,1)S(1)}, bf16[512,2048]{1,0:T(8,128)(2,1)S(1)}, bf16[512,256]{1,0:T(8,128)(2,1)S(1)}, bf16[256,256]{1,0:T(8,128)(2,1)S(1)}) custom-call(f32[9]{0:T(128)S(1)} %stack.83.flags_ref, bf16[32,68,128]{2,1,0:T(8,128)(2,1)S(1)} %all-to-all-done.packed_ref, bf16[256,128]{1,0:T(8,128)(2,1)} %bitcast.34, ...), custom_call_target="tpu_custom_call" | custom-call | tf_op jit(solution)/shard_map/encode/pallas_call | solution.py:58
  30.4 1.2 collective-permute-start.3
  31.6 0.0 collective-permute-start.2
  31.6 0.7 collective-permute-start.1
  32.3 2.3 %collective-permute-start = (bf16[256,256]{1,0:T(8,128)(2,1)S(1)}, bf16[256,256]{1,0:T(8,128)(2,1)S(1)}, u32[]{:S(2)}, u32[]{:S(2)}) collective-permute-start(bf16[256,256]{1,0:T(8,128)(2,1)S(1)} %get-tuple-element.67), channel_id=1, source_target_pairs={{0,8},{8,0},{16,24},{24,16},{1,9},{9,1},{17,25},{25,17},{2,10},{10... | collective-permute-start | bytes 393224 | tf_op jit(solution)/shard_map/ppermute | solution.py:498
  34.6 1.1 picks.1
  35.7 0.0 copy-start.1
  35.7 1.4 %own.2.own_pre_ref = f32[256,2048]{1,0:T(8,128)S(1)} custom-call(bf16[512,256]{1,0:T(8,128)(2,1)S(1)} %get-tuple-element.68.state_ref, bf16[2,256,256]{2,1,0:T(8,128)(2,1)S(1)} %bitcast.22, bf16[2,256,256]{2,1,0:T(8,128)(2,1)S(1)} %bitcast.26, bf16[2048,2048]{1,0:T(8,128)(2,1)S(1)} %get-tuple-element.66.picks_ref), custom_call_target="tpu_custom_call" | custom-call | tf_op jit(solution)/shard_map/own/pallas_call | solution.py:58
  37.1 0.0 collective-permute-done.3.right_ref
  37.1 0.0 collective-permute-done.2.left_ref
  37.1 0.0 collective-permute-done.1.second_ref
  37.1 1.1 collective-permute-done.first_ref
  38.2 3.4 %forward.1 = (bf16[256,2048]{1,0:T(8,128)(2,1)S(1)}, bf16[512,256]{1,0:T(8,128)(2,1)S(1)}, bf16[512,256]{1,0:T(8,128)(2,1)S(1)}, bf16[256,256]{1,0:T(8,128)(2,1)S(1)}) custom-call(f32[9]{0:T(128)S(1)} %stack.83.flags_ref, bf16[256,256]{1,0:T(8,128)(2,1)S(1)} %collective-permute-done.first_ref, bf16[256,256]{1,0:T(8,128)(2,1)S(1)} %collective-permute-done.1.second_ref, ...), custom_call_target="tpu_custom_call" | custom-call | tf_op jit(solution)/shard_map/forward/pallas_call | solution.py:58
  41.6 1.3 %collective-permute-start.7 = (bf16[256,256]{1,0:T(8,128)(2,1)S(1)}, bf16[256,256]{1,0:T(8,128)(2,1)S(1)}, u32[]{:S(2)}, u32[]{:S(2)}) collective-permute-start(bf16[256,256]{1,0:T(8,128)(2,1)S(1)} %get-tuple-element.72), channel_id=1, source_target_pairs={{0,7},{1,0},{2,1},{3,2},{4,3},{5,4},{6,5},{7,6},{8,15},{9,8},{10,9... | collective-permute-start | bytes 393224 | tf_op jit(solution)/shard_map/ppermute | solution.py:490
  43.0 0.0 collective-permute-start.6
  43.0 0.8 collective-permute-start.5
  43.8 4.8 %collective-permute-start.4 = (bf16[256,256]{1,0:T(8,128)(2,1)S(1)}, bf16[256,256]{1,0:T(8,128)(2,1)S(1)}, u32[]{:S(2)}, u32[]{:S(2)}) collective-permute-start(bf16[256,256]{1,0:T(8,128)(2,1)S(1)} %get-tuple-element.72), channel_id=1, source_target_pairs={{0,8},{8,0},{16,24},{24,16},{1,9},{9,1},{17,25},{25,17},{2,10},{10... | collective-permute-start | bytes 393224 | tf_op jit(solution)/shard_map/ppermute | solution.py:498
  48.6 0.9 back.1.back_ref
  49.5 1.4 %own.3.own_pre_ref = f32[256,2048]{1,0:T(8,128)S(1)} custom-call(bf16[512,256]{1,0:T(8,128)(2,1)S(1)} %get-tuple-element.73.state_ref, bf16[2,256,256]{2,1,0:T(8,128)(2,1)S(1)} %bitcast.24, bf16[2,256,256]{2,1,0:T(8,128)(2,1)S(1)} %bitcast.27, bf16[2048,2048]{1,0:T(8,128)(2,1)S(1)} %get-tuple-element.66.picks_ref), custom_call_target="tpu_custom_call" | custom-call | tf_op jit(solution)/shard_map/own/pallas_call | solution.py:58
  50.9 0.0 collective-permute-done.5.second_ref
  50.9 1.2 collective-permute-done.4.first_ref
  52.2 3.8 %turn.1 = (bf16[256,2048]{1,0:T(8,128)(2,1)S(1)}, bf16[256,2048]{1,0:T(8,128)(2,1)S(1)}, bf16[256,256]{1,0:T(8,128)(2,1)S(1)}, bf16[256,256]{1,0:T(8,128)(2,1)S(...) custom-call(f32[9]{0:T(128)S(1)} %stack.83.flags_ref, ...), custom_call_target="tpu_custom_call" | custom-call | tf_op jit(solution)/shard_map/turn/pallas_call | solution.py:58
  56.0 1.8 %collective-permute-start.9 = (bf16[256,256]{1,0:T(8,128)(2,1)S(1)}, bf16[256,256]{1,0:T(8,128)(2,1)S(1)}, u32[]{:S(2)}, u32[]{:S(2)}) collective-permute-start(bf16[256,256]{1,0:T(8,128)(2,1)S(1)} %get-tuple-element.78.send0_ref), channel_id=1, source_target_pairs={{0,8},{8,0},{16,24},{24,16},{1,9},{9,1},{17,25},{25,17},{2,10},{10... | collective-permute-start | bytes 393224 | tf_op jit(solution)/shard_map/ppermute | solution.py:498
  57.8 0.7 collective-permute-start.10
  58.5 0.8 collective-permute-start.11
  59.3 1.6 %out.1 = (bf16[512,256]{1,0:T(8,128)(2,1)S(1)}, bf16[512,256]{1,0:T(8,128)(2,1)}) custom-call(bf16[2048,2048]{1,0:T(8,128)(2,1)S(1)} %get-tuple-element.66.picks_ref, bf16[256,2048]{1,0:T(8,128)(2,1)S(1)} %get-tuple-element.74.act_edges_ref, bf16[512,256]{1,0:T(8,128)(2,1)S(1)} %get-tuple-element.73.state_ref, bf16[2,256,256]{2,1,0:T(8,128)(2,1)S(1)} %copy-done.1), custom_call_target="tpu_custom_call" | custom-call | tf_op jit(solution)/shard_map/out/pallas_call | solution.py:58
  60.9 1.5 %sums.2 = (bf16[1024,256]{1,0:T(8,128)(2,1)S(1)}, f32[512,256]{1,0:T(8,128)S(1)}) custom-call(bf16[2048,2048]{1,0:T(8,128)(2,1)S(1)} %get-tuple-element.66.picks_ref, bf16[256,2048]{1,0:T(8,128)(2,1)S(1)} %get-tuple-element.76.grad_pre_ref, bf16[512,256]{1,0:T(8,128)(2,1)S(1)} %copy-done.2, bf16[2,256,256]{2,1,0:T(8,128)(2,1)S(1)} %copy-done, ...), custom_call_target="tpu_custom_call" | custom-call | tf_op jit(solution)/shard_map/sums/pallas_call | solution.py:58
  62.5 1.1 terms.2
  63.6 0.0 collective-permute-done.9.first_ref
  63.6 1.0 collective-permute-done.12.right_ref
  64.6 2.9 %backward.1 = (f32[512,256]{1,0:T(8,128)S(1)}, bf16[256,2048]{1,0:T(8,128)(2,1)S(1)}, bf16[256,256]{1,0:T(8,128)(2,1)S(1)}, bf16[256,256]{1,0:T(8,128)(2,1)S(1)}...) custom-call(f32[9]{0:T(128)S(1)} %stack.83.flags_ref, ...), custom_call_target="tpu_custom_call" | custom-call | tf_op jit(solution)/shard_map/backward/pallas_call | solution.py:58
  67.5 1.8 %collective-permute-start.14 = (bf16[256,256]{1,0:T(8,128)(2,1)S(1)}, bf16[256,256]{1,0:T(8,128)(2,1)S(1)}, u32[]{:S(2)}, u32[]{:S(2)}) collective-permute-start(bf16[256,256]{1,0:T(8,128)(2,1)S(1)} %get-tuple-element.91.send0_ref), channel_id=1, source_target_pairs={{0,8},{8,0},{16,24},{24,16},{1,9},{9,1},{17,25},{25,17},{2,10},{10... | collective-permute-start | bytes 393224 | tf_op jit(solution)/shard_map/ppermute | solution.py:498
  69.2 0.7 collective-permute-start.15
  69.9 1.5 %collective-permute-start.16 = (bf16[256,256]{1,0:T(8,128)(2,1)S(1)}, bf16[256,256]{1,0:T(8,128)(2,1)S(1)}, u32[]{:S(2)}, u32[]{:S(2)}) collective-permute-start(bf16[256,256]{1,0:T(8,128)(2,1)S(1)} %get-tuple-element.93.send2_ref), channel_id=1, source_target_pairs={{0,7},{1,0},{2,1},{3,2},{4,3},{5,4},{6,5},{7,6},{8,15},{9,8},{10,9... | collective-permute-start | bytes 393224 | tf_op jit(solution)/shard_map/ppermute | solution.py:490
  71.3 0.0 collective-permute-start.17
  71.3 0.6 collective-permute-start.8
  72.0 1.6 %sums.3 = (bf16[1024,256]{1,0:T(8,128)(2,1)S(1)}, f32[512,256]{1,0:T(8,128)S(1)}) custom-call(bf16[2048,2048]{1,0:T(8,128)(2,1)S(1)} %get-tuple-element.66.picks_ref, bf16[256,2048]{1,0:T(8,128)(2,1)S(1)} %get-tuple-element.95.grad_pre_ref, f32[512,256]{1,0:T(8,128)S(1)} %get-tuple-element.96.grad_ref, bf16[2,256,256]{2,1,0:T(8,128)(2,1)S(1)} %copy-done, ...), custom_call_target="tpu_custom_call" | custom-call | tf_op jit(solution)/shard_map/sums/pallas_call | solution.py:58
  73.5 0.0 copy-start.4
  73.5 1.1 terms.3
  74.6 0.0 collective-permute-done.14.first_ref
  74.7 0.1 collective-permute-start.13
  74.7 0.0 collective-permute-done.15.second_ref
  74.7 0.4 collective-permute-done.16.left_ref
  75.2 1.5 %collective-permute-done.17.right_ref = bf16[256,256]{1,0:T(8,128)(2,1)S(1)} collective-permute-done((bf16[256,256]{1,0:T(8,128)(2,1)S(1)}, bf16[256,256]{1,0:T(8,128)(2,1)S(1)}, u32[]{:S(2)}, u32[]{:S(2)}) %collective-permute-start.17) | collective-permute-done | bytes 131104 | tf_op jit(solution)/shard_map/ppermute | solution.py:490
  76.6 2.3 %last.1 = (bf16[384,128]{1,0:T(8,128)(2,1)S(1)}, bf16[384,128]{1,0:T(8,128)(2,1)S(1)}) custom-call(f32[9]{0:T(128)S(1)} %stack.83.flags_ref, bf16[256,256]{1,0:T(8,128)(2,1)S(1)} %collective-permute-done.14.first_ref, bf16[256,256]{1,0:T(8,128)(2,1)S(1)} %collective-permute-done.15.second_ref, bf16[256,256]{1,0:T(8,128)(2,1)S(1)} %collective-permute-done.16.left_ref, ...), custom_call_target="tpu_custom_call" | custom-call | tf_op jit(solution)/shard_map/last/pallas_call | solution.py:58
  79.0 0.1 collective-permute-start.18
  79.1 0.0 collective-permute-done.8.refs_1_
  79.1 0.0 collective-permute-done.13.refs_3_
  79.1 1.3 %collective-permute-done.18.refs_5_ = bf16[384,128]{1,0:T(8,128)(2,1)S(1)} collective-permute-done((bf16[384,128]{1,0:T(8,128)(2,1)S(1)}, bf16[384,128]{1,0:T(8,128)(2,1)S(1)}, u32[]{:S(2)}, u32[]{:S(2)}) %collective-permute-start.18) | collective-permute-done | bytes 98336 | tf_op jit(solution)/shard_map/ppermute | solution.py:498
  80.4 0.1 merge.1
  80.5 20.4 %all_to_all.15.parts_ref = bf16[32,64,128]{2,1,0:T(8,128)(2,1)S(1)} all-to-all(bf16[32,64,128]{2,1,0:T(8,128)(2,1)S(1)} %bitcast.28), channel_id=1, replica_groups=mesh['grid'=4,'dom'=8] {'grid','dom'}, dimensions={0} | all-to-all | bytes 1048576 | tf_op jit(solution)/shard_map/all_to_all | solution.py:485
  100.9 0.1 share.1
  100.9 18.4 %all_to_all.16 = bf16[32,64,128]{2,1,0:T(8,128)(2,1)S(1)} all-to-all(bf16[32,64,128]{2,1,0:T(8,128)(2,1)S(1)} %share.1), channel_id=1, replica_groups=mesh['grid'=4,'dom'=8] {'grid','dom'}, dimensions={0} | all-to-all | bytes 1048576 | tf_op jit(solution)/shard_map/all_to_all | solution.py:485
  119.3 0.0 collective-permute-start.19
  119.3 1.9 %collective-permute-done.19.other_ref = bf16[2048,128]{1,0:T(8,128)(2,1)S(1)} collective-permute-done((bf16[2048,128]{1,0:T(8,128)(2,1)S(1)}, bf16[2048,128]{1,0:T(8,128)(2,1)S(1)}, u32[]{:S(2)}, u32[]{:S(2)}) %collective-permute-start.19) | collective-permute-done | bytes 524320 | tf_op jit(solution)/shard_map/ppermute | solution.py:498
  121.3 1.8 %unpack.1 = (f32[128,256]{1,0:T(8,128)}, f32[256,256]{1,0:T(8,128)}, f32[2,256,256]{2,1,0:T(8,128)}, f32[2,256,256]{2,1,0:T(8,128)}, f32[2,256,256]{2,1,0:T(8,128)}) custom-call(f32[9]{0:T(128)S(1)} %stack.83.flags_ref, bf16[2048,128]{1,0:T(8,128)(2,1)S(1)} %bitcast.30, bf16[2048,128]{1,0:T(8,128)(2,1)S(1)} %collective-permute-done.19.other_ref), custom_call_target="tpu_custom_call" | custom-call | tf_op jit(solution)/shard_map/unpack/pallas_call | solution.py:58
  (31 shorter events, 0.1 us)
Async XLA Ops:
  0.6 9.4 %copy-start.11 = (s32[256]{0:T(256)S(1)}, s32[256]{0:T(256)}, u32[]{:S(2)}) copy-start(s32[256]{0:T(256)} %param.21) | copy-start | bytes 3076
  0.6 10.0 %copy-start.9 = (s32[2048]{0:T(1024)S(1)}, s32[2048]{0:T(1024)}, u32[]{:S(2)}) copy-start(s32[2048]{0:T(1024)} %param.22) | copy-start | bytes 24580
  0.7 10.0 %copy-start.10 = (s32[2048]{0:T(1024)S(1)}, s32[2048]{0:T(1024)}, u32[]{:S(2)}) copy-start(s32[2048]{0:T(1024)} %param.23) | copy-start | bytes 24580
  0.7 10.0 %copy-start.6 = (bf16[128,256]{1,0:T(8,128)(2,1)S(1)}, bf16[128,256]{1,0:T(8,128)(2,1)}, u32[]{:S(2)}) copy-start(bf16[128,256]{1,0:T(8,128)(2,1)} %param.26) | copy-start | bytes 196612
  0.7 10.7 %copy-start.3 = (bf16[2,256,256]{2,1,0:T(8,128)(2,1)S(1)}, bf16[2,256,256]{2,1,0:T(8,128)(2,1)}, u32[]{:S(2)}) copy-start(bf16[2,256,256]{2,1,0:T(8,128)(2,1)} %dst_ref.3) | copy-start | bytes 786436
  0.7 10.9 %copy-start = (bf16[2,256,256]{2,1,0:T(8,128)(2,1)S(1)}, bf16[2,256,256]{2,1,0:T(8,128)(2,1)}, u32[]{:S(2)}) copy-start(bf16[2,256,256]{2,1,0:T(8,128)(2,1)} %src_ref.7) | copy-start | bytes 786436
  0.7 11.1 %copy-start.7 = (f32[2048]{0:T(1024)S(1)}, f32[2048]{0:T(1024)}, u32[]{:S(2)}) copy-start(f32[2048]{0:T(1024)} %param.25) | copy-start | bytes 24580
  0.7 11.1 %copy-start.8 = (s32[2048]{0:T(1024)S(1)}, s32[2048]{0:T(1024)}, u32[]{:S(2)}) copy-start(s32[2048]{0:T(1024)} %param.24) | copy-start | bytes 24580
  2.7 24.1 %all-to-all-start = ((bf16[32,68,128]{2,1,0:T(8,128)(2,1)}), bf16[32,68,128]{2,1,0:T(8,128)(2,1)S(1)}, u32[]{:S(2)}, u32[]{:S(2)}) async-start(bf16[32,68,128]{2,1,0:T(8,128)(2,1)} %pack.1), calls=%async_computation | async-start | bytes 1179648 | tf_op jit(solution)/shard_map/all_to_all | solution.py:485
  10.7 23.9 %copy-start.5 = (f32[256]{0:T(256)S(1)}, f32[256]{0:T(256)}, u32[]{:S(2)}) copy-start(f32[256]{0:T(256)} %convert_element_type.27) | copy-start | bytes 3076
  30.4 6.7 %collective-permute-start.3 = (bf16[256,256]{1,0:T(8,128)(2,1)S(1)}, bf16[256,256]{1,0:T(8,128)(2,1)S(1)}, u32[]{:S(2)}, u32[]{:S(2)}) collective-permute-start(bf16[256,256]{1,0:T(8,128)(2,1)S(1)} %get-tuple-element.67), channel_id=1, source_target_pairs={{0,7},{1,0},{2,1},{3,2},{4,3},{5,4},{6,5},{7,6},{8,15},{9,8},{10,9... | collective-permute-start | bytes 393224 | tf_op jit(solution)/shard_map/ppermute | solution.py:490
  31.6 5.5 %collective-permute-start.2 = (bf16[256,256]{1,0:T(8,128)(2,1)S(1)}, bf16[256,256]{1,0:T(8,128)(2,1)S(1)}, u32[]{:S(2)}, u32[]{:S(2)}) collective-permute-start(bf16[256,256]{1,0:T(8,128)(2,1)S(1)} %get-tuple-element.67), channel_id=1, source_target_pairs={{0,1},{1,2},{2,3},{3,4},{4,5},{5,6},{6,7},{7,0},{8,9},{9,10},{10,1... | collective-permute-start | bytes 393224 | tf_op jit(solution)/shard_map/ppermute | solution.py:490
  31.6 5.5 %collective-permute-start.1 = (bf16[256,256]{1,0:T(8,128)(2,1)S(1)}, bf16[256,256]{1,0:T(8,128)(2,1)S(1)}, u32[]{:S(2)}, u32[]{:S(2)}) collective-permute-start(bf16[256,256]{1,0:T(8,128)(2,1)S(1)} %get-tuple-element.67), channel_id=1, source_target_pairs={{0,0},{8,16},{16,8},{24,24},{1,1},{9,17},{17,9},{25,25},{2,2},{10,... | collective-permute-start | bytes 393224 | tf_op jit(solution)/shard_map/ppermute | solution.py:498
  32.3 5.9 %collective-permute-start = (bf16[256,256]{1,0:T(8,128)(2,1)S(1)}, bf16[256,256]{1,0:T(8,128)(2,1)S(1)}, u32[]{:S(2)}, u32[]{:S(2)}) collective-permute-start(bf16[256,256]{1,0:T(8,128)(2,1)S(1)} %get-tuple-element.67), channel_id=1, source_target_pairs={{0,8},{8,0},{16,24},{24,16},{1,9},{9,1},{17,25},{25,17},{2,10},{10... | collective-permute-start | bytes 393224 | tf_op jit(solution)/shard_map/ppermute | solution.py:498
  35.7 2.6 %copy-start.1 = (bf16[2,256,256]{2,1,0:T(8,128)(2,1)S(1)}, bf16[2,256,256]{2,1,0:T(8,128)(2,1)}, u32[]{:S(2)}) copy-start(bf16[2,256,256]{2,1,0:T(8,128)(2,1)} %msg_ref.7) | copy-start | bytes 786436
  38.2 10.4 %copy-start.2 = (bf16[512,256]{1,0:T(8,128)(2,1)S(1)}, bf16[512,256]{1,0:T(8,128)(2,1)}, u32[]{:S(2)}) copy-start(bf16[512,256]{1,0:T(8,128)(2,1)} %grad_ref.5) | copy-start | bytes 786436
  41.6 9.3 %collective-permute-start.7 = (bf16[256,256]{1,0:T(8,128)(2,1)S(1)}, bf16[256,256]{1,0:T(8,128)(2,1)S(1)}, u32[]{:S(2)}, u32[]{:S(2)}) collective-permute-start(bf16[256,256]{1,0:T(8,128)(2,1)S(1)} %get-tuple-element.72), channel_id=1, source_target_pairs={{0,7},{1,0},{2,1},{3,2},{4,3},{5,4},{6,5},{7,6},{8,15},{9,8},{10,9... | collective-permute-start | bytes 393224 | tf_op jit(solution)/shard_map/ppermute | solution.py:490
  43.0 8.0 %collective-permute-start.6 = (bf16[256,256]{1,0:T(8,128)(2,1)S(1)}, bf16[256,256]{1,0:T(8,128)(2,1)S(1)}, u32[]{:S(2)}, u32[]{:S(2)}) collective-permute-start(bf16[256,256]{1,0:T(8,128)(2,1)S(1)} %get-tuple-element.72), channel_id=1, source_target_pairs={{0,1},{1,2},{2,3},{3,4},{4,5},{5,6},{6,7},{7,0},{8,9},{9,10},{10,1... | collective-permute-start | bytes 393224 | tf_op jit(solution)/shard_map/ppermute | solution.py:490
  43.0 8.0 %collective-permute-start.5 = (bf16[256,256]{1,0:T(8,128)(2,1)S(1)}, bf16[256,256]{1,0:T(8,128)(2,1)S(1)}, u32[]{:S(2)}, u32[]{:S(2)}) collective-permute-start(bf16[256,256]{1,0:T(8,128)(2,1)S(1)} %get-tuple-element.72), channel_id=1, source_target_pairs={{0,0},{8,16},{16,8},{24,24},{1,1},{9,17},{17,9},{25,25},{2,2},{10,... | collective-permute-start | bytes 393224 | tf_op jit(solution)/shard_map/ppermute | solution.py:498
  43.8 8.4 %collective-permute-start.4 = (bf16[256,256]{1,0:T(8,128)(2,1)S(1)}, bf16[256,256]{1,0:T(8,128)(2,1)S(1)}, u32[]{:S(2)}, u32[]{:S(2)}) collective-permute-start(bf16[256,256]{1,0:T(8,128)(2,1)S(1)} %get-tuple-element.72), channel_id=1, source_target_pairs={{0,8},{8,0},{16,24},{24,16},{1,9},{9,1},{17,25},{25,17},{2,10},{10... | collective-permute-start | bytes 393224 | tf_op jit(solution)/shard_map/ppermute | solution.py:498
  56.0 7.6 %collective-permute-start.9 = (bf16[256,256]{1,0:T(8,128)(2,1)S(1)}, bf16[256,256]{1,0:T(8,128)(2,1)S(1)}, u32[]{:S(2)}, u32[]{:S(2)}) collective-permute-start(bf16[256,256]{1,0:T(8,128)(2,1)S(1)} %get-tuple-element.78.send0_ref), channel_id=1, source_target_pairs={{0,8},{8,0},{16,24},{24,16},{1,9},{9,1},{17,25},{25,17},{2,10},{10... | collective-permute-start | bytes 393224 | tf_op jit(solution)/shard_map/ppermute | solution.py:498
  57.8 5.8 %collective-permute-start.10 = (bf16[256,256]{1,0:T(8,128)(2,1)S(1)}, bf16[256,256]{1,0:T(8,128)(2,1)S(1)}, u32[]{:S(2)}, u32[]{:S(2)}) collective-permute-start(bf16[256,256]{1,0:T(8,128)(2,1)S(1)} %get-tuple-element.79.send1_ref), channel_id=1, source_target_pairs={{0,0},{8,16},{16,8},{24,24},{1,1},{9,17},{17,9},{25,25},{2,2},{10,... | collective-permute-start | bytes 393224 | tf_op jit(solution)/shard_map/ppermute | solution.py:498
  58.5 5.1 %collective-permute-start.11 = (bf16[256,256]{1,0:T(8,128)(2,1)S(1)}, bf16[256,256]{1,0:T(8,128)(2,1)S(1)}, u32[]{:S(2)}, u32[]{:S(2)}) collective-permute-start(bf16[256,256]{1,0:T(8,128)(2,1)S(1)} %get-tuple-element.80.send2_ref), channel_id=1, source_target_pairs={{0,7},{1,0},{2,1},{3,2},{4,3},{5,4},{6,5},{7,6},{8,15},{9,8},{10,9... | collective-permute-start | bytes 393224 | tf_op jit(solution)/shard_map/ppermute | solution.py:490
  59.3 5.3 %collective-permute-start.12 = (bf16[256,256]{1,0:T(8,128)(2,1)S(1)}, bf16[256,256]{1,0:T(8,128)(2,1)S(1)}, u32[]{:S(2)}, u32[]{:S(2)}) collective-permute-start(bf16[256,256]{1,0:T(8,128)(2,1)S(1)} %get-tuple-element.81.send3_ref), channel_id=1, source_target_pairs={{0,1},{1,2},{2,3},{3,4},{4,5},{5,6},{6,7},{7,0},{8,9},{9,10},{10,1... | collective-permute-start | bytes 393224 | tf_op jit(solution)/shard_map/ppermute | solution.py:490
  67.5 7.2 %collective-permute-start.14 = (bf16[256,256]{1,0:T(8,128)(2,1)S(1)}, bf16[256,256]{1,0:T(8,128)(2,1)S(1)}, u32[]{:S(2)}, u32[]{:S(2)}) collective-permute-start(bf16[256,256]{1,0:T(8,128)(2,1)S(1)} %get-tuple-element.91.send0_ref), channel_id=1, source_target_pairs={{0,8},{8,0},{16,24},{24,16},{1,9},{9,1},{17,25},{25,17},{2,10},{10... | collective-permute-start | bytes 393224 | tf_op jit(solution)/shard_map/ppermute | solution.py:498
  69.2 5.5 %collective-permute-start.15 = (bf16[256,256]{1,0:T(8,128)(2,1)S(1)}, bf16[256,256]{1,0:T(8,128)(2,1)S(1)}, u32[]{:S(2)}, u32[]{:S(2)}) collective-permute-start(bf16[256,256]{1,0:T(8,128)(2,1)S(1)} %get-tuple-element.92.send1_ref), channel_id=1, source_target_pairs={{0,0},{8,16},{16,8},{24,24},{1,1},{9,17},{17,9},{25,25},{2,2},{10,... | collective-permute-start | bytes 393224 | tf_op jit(solution)/shard_map/ppermute | solution.py:498
  69.9 5.3 %collective-permute-start.16 = (bf16[256,256]{1,0:T(8,128)(2,1)S(1)}, bf16[256,256]{1,0:T(8,128)(2,1)S(1)}, u32[]{:S(2)}, u32[]{:S(2)}) collective-permute-start(bf16[256,256]{1,0:T(8,128)(2,1)S(1)} %get-tuple-element.93.send2_ref), channel_id=1, source_target_pairs={{0,7},{1,0},{2,1},{3,2},{4,3},{5,4},{6,5},{7,6},{8,15},{9,8},{10,9... | collective-permute-start | bytes 393224 | tf_op jit(solution)/shard_map/ppermute | solution.py:490
  71.3 5.3 %collective-permute-start.17 = (bf16[256,256]{1,0:T(8,128)(2,1)S(1)}, bf16[256,256]{1,0:T(8,128)(2,1)S(1)}, u32[]{:S(2)}, u32[]{:S(2)}) collective-permute-start(bf16[256,256]{1,0:T(8,128)(2,1)S(1)} %get-tuple-element.94.send3_ref), channel_id=1, source_target_pairs={{0,1},{1,2},{2,3},{3,4},{4,5},{5,6},{6,7},{7,0},{8,9},{9,10},{10,1... | collective-permute-start | bytes 393224 | tf_op jit(solution)/shard_map/ppermute | solution.py:490
  71.3 7.7 %collective-permute-start.8 = (bf16[768,128]{1,0:T(8,128)(2,1)S(1)}, bf16[768,128]{1,0:T(8,128)(2,1)S(1)}, u32[]{:S(2)}, u32[]{:S(2)}) collective-permute-start(bf16[768,128]{1,0:T(8,128)(2,1)S(1)} %get-tuple-element.87), channel_id=1, source_target_pairs={{0,1},{1,0},{2,3},{3,2},{4,5},{5,4},{6,7},{7,6},{8,9},{9,8},{10,11... | collective-permute-start | bytes 589832 | tf_op jit(solution)/shard_map/ppermute | solution.py:498
  73.5 3.1 %copy-start.4 = (bf16[256,256]{1,0:T(8,128)(2,1)S(1)}, bf16[256,256]{1,0:T(8,128)(2,1)}, u32[]{:S(2)}) copy-start(bf16[256,256]{1,0:T(8,128)(2,1)} %enc_out_ref.1) | copy-start | bytes 393220
  74.7 4.4 %collective-permute-start.13 = (bf16[768,128]{1,0:T(8,128)(2,1)S(1)}, bf16[768,128]{1,0:T(8,128)(2,1)S(1)}, u32[]{:S(2)}, u32[]{:S(2)}) collective-permute-start(bf16[768,128]{1,0:T(8,128)(2,1)S(1)} %get-tuple-element.100), channel_id=1, source_target_pairs={{0,1},{1,0},{2,3},{3,2},{4,5},{5,4},{6,7},{7,6},{8,9},{9,8},{10,11... | collective-permute-start | bytes 589832 | tf_op jit(solution)/shard_map/ppermute | solution.py:498
  79.0 1.4 %collective-permute-start.18 = (bf16[384,128]{1,0:T(8,128)(2,1)S(1)}, bf16[384,128]{1,0:T(8,128)(2,1)S(1)}, u32[]{:S(2)}, u32[]{:S(2)}) collective-permute-start(bf16[384,128]{1,0:T(8,128)(2,1)S(1)} %get-tuple-element.106), channel_id=1, source_target_pairs={{0,1},{1,0},{2,3},{3,2},{4,5},{5,4},{6,7},{7,6},{8,9},{9,8},{10,11... | collective-permute-start | bytes 294920 | tf_op jit(solution)/shard_map/ppermute | solution.py:498
  119.3 1.9 %collective-permute-start.19 = (bf16[2048,128]{1,0:T(8,128)(2,1)S(1)}, bf16[2048,128]{1,0:T(8,128)(2,1)S(1)}, u32[]{:S(2)}, u32[]{:S(2)}) collective-permute-start(bf16[2048,128]{1,0:T(8,128)(2,1)S(1)} %bitcast.29), channel_id=1, source_target_pairs={{0,1},{1,0},{2,3},{3,2},{4,5},{5,4},{6,7},{7,6},{8,9},{9,8},{10,11... | collective-permute-start | bytes 1572872 | tf_op jit(solution)/shard_map/ppermute | solution.py:498

commit v5 on v4

--- a/solution.py
+++ b/solution.py
@@ -73,7 +73,9 @@
         body(start, pl.ds(start, CHUNK))
 
 
-def pack_body(cols_ref, slot_ref, live_ref, weight_ref, out_ref, slot_buf, live_buf, weight_buf, sems):
+def pack_body(
+    where_ref, cols_ref, slot_ref, live_ref, weight_ref, out_ref, slot_buf, live_buf, weight_buf, sems
+):
     peers, bucket, _ = cols_ref.shape
     per_row = LANES // bucket
     copies = [
@@ -82,37 +84,83 @@
         pltpu.make_async_copy(live_ref, live_buf, sems.at[2]),
         pltpu.make_async_copy(weight_ref, weight_buf, sems.at[3]),
     ]
-    for copy in copies:
+    for copy in copies[1:] + copies[:1]:
         copy.start()
     for copy in copies[1:]:
         copy.wait()
     slot = slot_buf[...].astype(F32)
     high = jnp.floor(slot * (1.0 / 256.0))
-    low = slot - 256.0 * high
     scale = weight_buf[...] * live_buf[...].astype(F32)
-    scale_high = scale.astype(BF)
-    scale_low = (scale - scale_high.astype(F32)).astype(BF)
-    fields = [high.astype(BF), low.astype(BF), scale_high, scale_low]
-    for peer in range(peers):
-        row = peer // per_row
-        extra = jnp.concatenate([field[row : row + 1, :] for field in fields], 0)
-        out_ref[peer, bucket : bucket + 4, :] = extra
+    scale_high = scale.astype(BF).astype(F32)
+    fields = [high, slot - 256.0 * high, scale_high, scale - scale_high]
+    place = where_ref[PLACE]
+    lane = lax.broadcasted_iota(jnp.int32, fields[0].shape, 1)
+    here = (lane >= place * bucket) & (lane < (place + 1) * bucket)
+    for j in range(per_row):
+        shift = lax.rem((place - j + per_row) * bucket, LANES)
+        moved = [jnp.where(here, pltpu.roll(field, shift, 1), 0.0).astype(BF) for field in fields]
+        for row in range(peers // per_row):
+            extra = jnp.concatenate([field[row : row + 1, :] for field in moved], 0)
+            out_ref[row * per_row + j, bucket : bucket + 4, :] = extra
     copies[0].wait()
 
 
-PAIR, ODD_GRID, ODD_DOM, PLACE = 4, 6, 7, 8
-
-
-def picks_body(rows_ref, bound_ref, picks_ref, rim_picks, rim_picks_t):
+GRID_AT, DOM_AT, GRID_COUNT, DOM_COUNT, PLACE = range(5)
+
+
+def mark(condition):
+    return jnp.where(condition, jnp.float32(1.0), jnp.float32(0.0))
+
+
+def is_odd(place):
+    return lax.rem(place, 2) == 1
+
+
+def side_marks(where_ref):
+    grid_at, dom_at = where_ref[GRID_AT], where_ref[DOM_AT]
+    return (
+        mark(grid_at > 0),
+        mark(grid_at < where_ref[GRID_COUNT] - 1),
+        mark(dom_at > 0),
+        mark(dom_at < where_ref[DOM_COUNT] - 1),
+    )
+
+
+def pair_marks(where_ref):
+    up, down, _, _ = side_marks(where_ref)
+    odd = is_odd(where_ref[GRID_AT])
+    return jnp.where(odd, up, down), jnp.where(odd, down, up)
+
+
+def picks_body(
+    src_ref,
+    dst_ref,
+    live_ref,
+    weight_ref,
+    bound_ref,
+    src_proj_ref,
+    dst_proj_ref,
+    picks_ref,
+    rim_picks,
+    rim_picks_t,
+    scale_ref,
+    src_t_ref,
+    dst_t_ref,
+):
     nodes = rim_picks.shape[0]
     ext = picks_ref.shape[0] - 2 * nodes
-    for start in range(0, rows_ref.shape[1], CHUNK):
-        at = pl.ds(start, CHUNK)
-        block = picks_ref.at[:, at]
-        put_picks(block, 0, rows_ref[1:2, at], nodes)
-        put_picks(block, nodes, rows_ref[0:1, at], nodes + ext)
-    put_picks(rim_picks, 0, bound_ref[0:1, :], nodes)
-    rim_picks_t[...] = rim_picks[...].astype(F32).T.astype(BF)
+    src = long_row(src_ref[...].astype(F32))
+    dst = long_row(dst_ref[...].astype(F32))
+    scale_ref[...] = long_row(weight_ref[...] * live_ref[...].astype(F32))
+    for start in range(0, picks_ref.shape[1], CHUNK):
+        block = picks_ref.at[:, pl.ds(start, CHUNK)]
+        put_picks(block, 0, dst[:, start : start + CHUNK], nodes)
+        put_picks(block, nodes, src[:, start : start + CHUNK], nodes + ext)
+    put_picks(rim_picks, 0, long_row(bound_ref[...].astype(F32)), nodes)
+    rim_picks_t[...] = turned_over(rim_picks[...])
+    for layer in range(src_t_ref.shape[0]):
+        src_t_ref[layer] = turned_over(src_proj_ref[layer])
+        dst_t_ref[layer] = turned_over(dst_proj_ref[layer])
 
 
 def put_state(state, state_ref, rim_ref, rim_picks_t):
@@ -120,36 +168,38 @@
     rim_ref[...] = mm(rim_picks_t[...], state_ref[...]).astype(BF)
 
 
-def in_order(flags_ref, rims):
+def in_order(where_ref, rims):
     first, second, left, right = (ref[...] for ref in rims)
-    odd = flags_ref[ODD_GRID] > 0.5
+    odd = is_odd(where_ref[GRID_AT])
     ordered = (jnp.where(odd, first, second), jnp.where(odd, second, first), left, right)
-    return [rows * flags_ref[side].astype(BF) for side, rows in enumerate(ordered)]
-
-
-def put_col_rows(flags_ref, packed_ref, bucket, rows_ref):
+    return [rows * side.astype(BF) for rows, side in zip(ordered, side_marks(where_ref))]
+
+
+def put_col_rows(packed_ref, bucket, rows_ref):
     peers = packed_ref.shape[0]
     per_row = LANES // bucket
-    place = flags_ref[PLACE].astype(jnp.int32)
-    lane = lax.broadcasted_iota(jnp.int32, (4, LANES), 1)
     for row in range(peers // per_row):
-        out = jnp.zeros((4, LANES), F32)
-        for j in range(per_row):
-            part = packed_ref[row * per_row + j, bucket : bucket + 4, :].astype(F32)
-            shift = lax.rem((j - place + per_row) * bucket, LANES)
-            part = pltpu.roll(part, shift, 1)
-            here = (lane >= j * bucket) & (lane < (j + 1) * bucket)
-            out = jnp.where(here, part, out)
+        parts = [
+            packed_ref[row * per_row + j, bucket : bucket + 4, :].astype(F32) for j in range(per_row)
+        ]
+        total = sum(parts[1:], parts[0])
         at = pl.ds(row * LANES, LANES)
-        rows_ref[0:1, at] = out[0:1] * 256.0 + out[1:2]
-        rows_ref[1:2, at] = out[2:3] + out[3:4]
+        rows_ref[0:1, at] = total[0:1] * 256.0 + total[1:2]
+        rows_ref[1:2, at] = total[2:3] + total[3:4]
+
+
+def long_row(rows):
+    return jnp.concatenate([rows[i : i + 1, :] for i in range(rows.shape[0])], 1)
+
+
+def turned_over(rows):
+    return rows.astype(F32).T.astype(BF)
 
 
 def encode_body(
     bucket,
-    flags_ref,
     packed_ref,
-    enc_in_t_far,
+    enc_in_far,
     enc_out_far,
     static_far,
     bound_far,
@@ -160,7 +210,7 @@
     rim_ref,
     act_ref,
     rows_ref,
-    enc_in_t_ref,
+    enc_in_ref,
     enc_out_ref,
     static_ref,
     bound_ref,
@@ -170,20 +220,21 @@
     nodes = static_ref.shape[0]
     peers_step = CHUNK // bucket
     copies = [
-        pltpu.make_async_copy(enc_in_t_far, enc_in_t_ref, sems.at[0]),
+        pltpu.make_async_copy(enc_in_far, enc_in_ref, sems.at[0]),
         pltpu.make_async_copy(enc_out_far, enc_out_ref, sems.at[1]),
         pltpu.make_async_copy(static_far, static_ref, sems.at[2]),
         pltpu.make_async_copy(bound_far, bound_ref, sems.at[3]),
     ]
     for copy in copies:
         copy.start()
-    put_col_rows(flags_ref, packed_ref, bucket, rows_ref)
+    put_col_rows(packed_ref, bucket, rows_ref)
     copies[0].wait()
+    enc_in_t = turned_over(enc_in_ref[...])
 
     def step(start, at):
         first = start // bucket
         got = packed_ref[first : first + peers_step, :bucket, :].reshape(CHUNK, packed_ref.shape[2])
-        pre = mm_t(enc_in_t_ref[...], got)
+        pre = mm_t(enc_in_t, got)
         scale = rows_ref[1:2, at]
         sig = sigmoid(pre)
         act_ref[:, at] = (pre * sig * scale).astype(BF)
@@ -194,7 +245,7 @@
     pooled_ref[...] = mm_t(picks_ref[...], act_ref[...]).astype(BF)
     for copy in copies[1:]:
         copy.wait()
-    put_picks(rim_picks, 0, bound_ref[0:1, :], nodes)
+    put_picks(rim_picks, 0, long_row(bound_ref[...].astype(F32)), nodes)
     state = static_ref[...].astype(F32) + mm(pooled_ref[...], enc_out_ref[...])
     state_ref[...] = state.astype(BF)
     rim_ref[...] = t_mm(rim_picks[...], state_ref[...]).astype(BF)
@@ -208,27 +259,27 @@
     out_ref[...] = mm(table_ref[...], picks_ref[: 2 * nodes, :])
 
 
-def back_body(layer, msg_ref, grad_ref, rows_ref, picks_ref, out_ref):
+def back_body(layer, msg_ref, grad_ref, scale_ref, picks_ref, out_ref):
     nodes = grad_ref.shape[0]
     back = mm_t(msg_ref[layer], grad_ref[...]).astype(BF)
-    out_ref[...] = mm(back, picks_ref[:nodes, :]) * rows_ref[2:3, :]
-
-
-def fill_rims(full_ref, flags_ref, rims, src_t_ref):
+    out_ref[...] = mm(back, picks_ref[:nodes, :]) * scale_ref[...]
+
+
+def fill_rims(full_ref, where_ref, rims, src_t_ref):
     rim = rims[0].shape[0]
-    for side, rim_rows in enumerate(in_order(flags_ref, rims)):
+    for side, rim_rows in enumerate(in_order(where_ref, rims)):
         full_ref[:, side * rim : (side + 1) * rim] = mm_t(src_t_ref[...], rim_rows).astype(BF)
 
 
 def forward_body(
     layer,
-    flags_ref,
+    where_ref,
     first_ref,
     second_ref,
     left_ref,
     right_ref,
     own_pre_ref,
-    rows_ref,
+    scale_ref,
     picks_ref,
     state_ref,
     src_t_ref,
@@ -242,25 +293,25 @@
     act_ref,
 ):
     nodes = state_ref.shape[0]
-    fill_rims(full_ref, flags_ref, (first_ref, second_ref, left_ref, right_ref), src_t_ref.at[layer])
+    fill_rims(full_ref, where_ref, (first_ref, second_ref, left_ref, right_ref), src_t_ref.at[layer])
 
     def step(start, at):
         pre = own_pre_ref[:, at] + mm(full_ref[...], picks_ref[2 * nodes :, at])
-        scale = rows_ref[2:3, at]
+        scale = scale_ref[:, at]
         sig = sigmoid(pre)
         act_ref[:, at] = (pre * sig * scale).astype(BF)
         slope_ref[:, at] = (sig * (1.0 + pre * (1.0 - sig)) * scale).astype(BF)
 
-    chunks(rows_ref.shape[1], step)
+    chunks(scale_ref.shape[1], step)
     node_act_ref[...] = mm_t(picks_ref[:nodes, :], act_ref[...]).astype(BF)
     state = state_ref[...].astype(F32) + mm(node_act_ref[...], msg_ref[layer])
     put_state(state, next_state_ref, rim_ref, rim_picks_t)
 
 
-def put_sends(flags_ref, sums, sends):
+def put_sends(where_ref, sums, sends):
     rim = sums.shape[0] // 4
     up, down, left, right = (sums[side * rim : (side + 1) * rim, :].astype(BF) for side in range(4))
-    odd = flags_ref[ODD_GRID] > 0.5
+    odd = is_odd(where_ref[GRID_AT])
     sends[0][...] = jnp.where(odd, up, down)
     sends[1][...] = jnp.where(odd, down, up)
     sends[2][...] = left
@@ -269,14 +320,14 @@
 
 def turn_body(
     layer,
-    flags_ref,
+    where_ref,
     first_ref,
     second_ref,
     left_ref,
     right_ref,
     own_pre_ref,
     back_ref,
-    rows_ref,
+    scale_ref,
     picks_ref,
     src_t_ref,
     act_ref,
@@ -288,21 +339,22 @@
     full_ref,
 ):
     first = picks_ref.shape[0] - full_ref.shape[1]
-    fill_rims(full_ref, flags_ref, (first_ref, second_ref, left_ref, right_ref), src_t_ref.at[layer])
+    fill_rims(full_ref, where_ref, (first_ref, second_ref, left_ref, right_ref), src_t_ref.at[layer])
 
     def step(start, at):
         pre = own_pre_ref[:, at] + mm(full_ref[...], picks_ref[first:, at])
         sig = sigmoid(pre)
-        act_ref[:, at] = (pre * sig * rows_ref[2:3, at]).astype(BF)
+        act_ref[:, at] = (pre * sig * scale_ref[:, at]).astype(BF)
         grad_pre_ref[:, at] = (back_ref[:, at] * (sig * (1.0 + pre * (1.0 - sig)))).astype(BF)
 
-    chunks(rows_ref.shape[1], step)
+    chunks(scale_ref.shape[1], step)
     sums = mm_t(picks_ref[first:, :], grad_pre_ref[...])
-    put_sends(flags_ref, sums, (send0_ref, send1_ref, send2_ref, send3_ref))
-
-
-def merged_grad(partial_ref, flags_ref, returned, src_ref, rim_picks):
-    marks = (flags_ref[PAIR], flags_ref[PAIR + 1], flags_ref[3], flags_ref[2])
+    put_sends(where_ref, sums, (send0_ref, send1_ref, send2_ref, send3_ref))
+
+
+def merged_grad(partial_ref, where_ref, returned, src_ref, rim_picks):
+    sides = side_marks(where_ref)
+    marks = (*pair_marks(where_ref), sides[3], sides[2])
     total = returned[0][...].astype(F32) * marks[0]
     for side in range(1, 4):
         total += returned[side][...].astype(F32) * marks[side]
@@ -312,7 +364,7 @@
 
 def backward_body(
     layer,
-    flags_ref,
+    where_ref,
     first_ref,
     second_ref,
     left_ref,
@@ -332,7 +384,7 @@
 ):
     nodes = partial_ref.shape[0]
     returned = (first_ref, second_ref, left_ref, right_ref)
-    grad = merged_grad(partial_ref, flags_ref, returned, src_ref.at[layer], rim_picks)
+    grad = merged_grad(partial_ref, where_ref, returned, src_ref.at[layer], rim_picks)
     grad_ref[...] = grad
     back = mm_t(msg_ref[layer - 1], grad.astype(BF)).astype(BF)
 
@@ -342,7 +394,7 @@
 
     chunks(picks_ref.shape[1], step)
     sums = mm_t(picks_ref[2 * nodes :, :], grad_pre_ref[...])
-    put_sends(flags_ref, sums, (send0_ref, send1_ref, send2_ref, send3_ref))
+    put_sends(where_ref, sums, (send0_ref, send1_ref, send2_ref, send3_ref))
 
 
 def sums_body(layer, picks_ref, grad_pre_ref, grad_ref, src_ref, dst_ref, own_ref, partial_ref):
@@ -361,16 +413,16 @@
     out_ref[...] = (state_ref[...].astype(F32) + mm(act_ref[...], msg_ref[layer])).astype(BF)
 
 
-def put_halves(flags_ref, first, term, keep_ref, send_ref):
+def put_halves(where_ref, first, term, keep_ref, send_ref):
     half = term.shape[1] // 2
-    odd = flags_ref[ODD_DOM] > 0.5
+    odd = is_odd(where_ref[DOM_AT])
     low, high = term[:, :half].astype(BF), term[:, half:].astype(BF)
     keep_ref[first : first + term.shape[0], :] = jnp.where(odd, high, low)
     send_ref[first : first + term.shape[0], :] = jnp.where(odd, low, high)
 
 
 def terms_body(
-    flags_ref,
+    where_ref,
     first_ref,
     second_ref,
     left_ref,
@@ -389,24 +441,21 @@
     nodes, width = state_ref.shape
     state = state_ref[...]
     src_term = t_mm(state, own_ref[nodes:, :])
-    pairs = (
-        (first_ref, send0_ref, flags_ref[PAIR]),
-        (second_ref, send1_ref, flags_ref[PAIR + 1]),
-        (left_ref, send2_ref, flags_ref[2]),
-        (right_ref, send3_ref, flags_ref[3]),
-    )
-    for rim_ref, sums_ref, mark in pairs:
-        src_term += t_mm(rim_ref[...], sums_ref[...]) * mark
-    put_halves(flags_ref, 0, src_term, keep_ref, send_ref)
-    put_halves(flags_ref, width, t_mm(state, own_ref[:nodes, :]), keep_ref, send_ref)
+    marks = (*pair_marks(where_ref), *side_marks(where_ref)[2:])
+    rims = (first_ref, second_ref, left_ref, right_ref)
+    sends = (send0_ref, send1_ref, send2_ref, send3_ref)
+    for rim_ref, sums_ref, present in zip(rims, sends, marks):
+        src_term += t_mm(rim_ref[...], sums_ref[...]) * present
+    put_halves(where_ref, 0, src_term, keep_ref, send_ref)
+    put_halves(where_ref, width, t_mm(state, own_ref[:nodes, :]), keep_ref, send_ref)
     put_halves(
-        flags_ref, 2 * width, t_mm(act_ref[...], grad_ref[...].astype(BF)), keep_ref, send_ref
+        where_ref, 2 * width, t_mm(act_ref[...], grad_ref[...].astype(BF)), keep_ref, send_ref
     )
 
 
 def last_body(
     bucket,
-    flags_ref,
+    where_ref,
     first_ref,
     second_ref,
     left_ref,
@@ -425,7 +474,7 @@
     fin = packed_ref.shape[2]
     peers_step = CHUNK // bucket
     returned = (first_ref, second_ref, left_ref, right_ref)
-    grad = merged_grad(partial_ref, flags_ref, returned, src_ref.at[0], rim_picks).astype(BF)
+    grad = merged_grad(partial_ref, where_ref, returned, src_ref.at[0], rim_picks).astype(BF)
     back = mm_t(enc_out_ref[...], grad).astype(BF)
     in_term = jnp.zeros((enc_out_ref.shape[0], fin), F32)
     for start in range(0, picks_ref.shape[1], CHUNK):
@@ -434,8 +483,8 @@
         got = packed_ref[first : first + peers_step, :bucket, :].reshape(CHUNK, fin)
         grad_pre = mm(back, picks_ref[:, at]) * slope_ref[:, at].astype(F32)
         in_term += mm(grad_pre.astype(BF), got)
-    put_halves(flags_ref, 0, in_term.T, keep_ref, send_ref)
-    put_halves(flags_ref, fin, t_mm(pooled_ref[...], grad), keep_ref, send_ref)
+    put_halves(where_ref, 0, in_term.T, keep_ref, send_ref)
+    put_halves(where_ref, fin, t_mm(pooled_ref[...], grad), keep_ref, send_ref)
 
 
 def merge_body(*refs):
@@ -460,8 +509,8 @@
             out_ref[peer] = total.astype(BF)
 
 
-def unpack_body(flags_ref, mine_ref, other_ref, *outs):
-    odd = flags_ref[ODD_DOM] > 0.5
+def unpack_body(where_ref, mine_ref, other_ref, *outs):
+    odd = is_odd(where_ref[DOM_AT])
     half = mine_ref.shape[1]
     first = 0
 
@@ -514,10 +563,6 @@
         turned(sends[2], "dom", -1),
         turned(sends[3], "dom", 1),
     )
-
-
-def floats(scalars):
-    return jnp.stack([scalar.astype(F32) for scalar in scalars])
 
 
 def per_device(
@@ -546,6 +591,11 @@
     ext = 4 * rim
     bucket = cols // peers
 
+    grid_at, grid_count = lax.axis_index("grid"), lax.axis_size("grid")
+    dom_at, dom_count = lax.axis_index("dom"), lax.axis_size("dom")
+    place = (grid_at * dom_count + dom_at) % (LANES // bucket)
+    where = jnp.stack([grid_at, dom_at, jnp.int32(grid_count), jnp.int32(dom_count), place])
+
     lanes = (cols // LANES, LANES)
     held = [pltpu.VMEM(lanes, jnp.int32), pltpu.VMEM(lanes, jnp.int32), pltpu.VMEM(lanes, F32)]
     (packed,) = call(
@@ -553,38 +603,16 @@
         [((peers, bucket + 4, fin), BF)],
         held + [pltpu.SemaphoreType.DMA((4,))],
         "pack",
-        far=range(4),
+        True,
+        far=range(1, 5),
     )(
+        where,
         columns.reshape(peers, bucket, fin),
         col_slot.reshape(lanes),
         column_live.reshape(lanes),
         col_weight.reshape(lanes),
     )
     packed = exchange(packed)
-
-    grid_at, grid_count = lax.axis_index("grid"), lax.axis_size("grid")
-    dom_at, dom_count = lax.axis_index("dom"), lax.axis_size("dom")
-    odd_grid, odd_dom = grid_at % 2, dom_at % 2
-    up, down = grid_at > 0, grid_at < grid_count - 1
-    flags = floats(
-        [
-            up,
-            down,
-            dom_at > 0,
-            dom_at < dom_count - 1,
-            jnp.where(odd_grid == 1, up, down),
-            jnp.where(odd_grid == 1, down, up),
-            odd_grid == 1,
-            odd_dom == 1,
-            (grid_at * dom_count + dom_at) % (LANES // bucket),
-        ]
-    )
-    edge_scale = edge_weight * edge_live.astype(F32)
-    edge_rows = jnp.stack([edge_src.astype(F32), edge_dst.astype(F32), edge_scale])
-    bound = boundary_idx.astype(F32)[None]
-    enc_in_t = enc_in.T
-    src_t = src_proj.transpose(0, 2, 1)
-    dst_t = dst_proj.transpose(0, 2, 1)
 
     node_shape = ((nodes, width), BF)
     node_wide = ((nodes, width), F32)
@@ -595,35 +623,48 @@
     edge_buf = pltpu.VMEM((width, edges), BF)
     table_buf = pltpu.VMEM((width, 2 * nodes), BF)
 
-    flags, edge_rows, bound, enc_in_t, src_t, dst_t = lax.optimization_barrier(
-        (flags, edge_rows, bound, enc_in_t, src_t, dst_t)
-    )
-
+    bound = boundary_idx.reshape(rim // LANES, LANES)
     pooled, col_slope, slot_picks, state0, rim0 = call(
         functools.partial(encode_body, bucket),
         [node_shape, ((width, cols), BF), ((nodes, cols), BF), node_shape, rim_shape],
         [
             edge_buf,
             pltpu.VMEM((2, cols), F32),
-            pltpu.VMEM((width, fin), BF),
+            pltpu.VMEM(enc_in.shape, BF),
             pltpu.VMEM(enc_out.shape, BF),
             pltpu.VMEM((nodes, width), BF),
-            pltpu.VMEM((1, rim), F32),
+            pltpu.VMEM(bound.shape, jnp.int32),
             pltpu.VMEM((nodes, rim), BF),
             pltpu.SemaphoreType.DMA((4,)),
         ],
         "encode",
-        True,
-        far=range(2, 6),
-    )(flags, packed, enc_in_t, enc_out, node_static, bound)
-
-    state0, edge_rows, bound = lax.optimization_barrier((state0, edge_rows, bound))
-    picks, rim_picks, rim_picks_t = call(
+        far=range(1, 5),
+    )(packed, enc_in, enc_out, node_static, bound)
+
+    edge_lanes = (edges // LANES, LANES)
+    state0, edge_dst = lax.optimization_barrier((state0, edge_dst))
+    layered = (src_proj.shape, BF)
+    picks, rim_picks, rim_picks_t, edge_scale, src_t, dst_t = call(
         picks_body,
-        [((2 * nodes + ext, edges), BF), ((nodes, rim), BF), ((rim, nodes), BF)],
+        [
+            ((2 * nodes + ext, edges), BF),
+            ((nodes, rim), BF),
+            ((rim, nodes), BF),
+            ((1, edges), F32),
+            layered,
+            layered,
+        ],
         [],
         "picks",
-    )(edge_rows, bound)
+    )(
+        edge_src.reshape(edge_lanes),
+        edge_dst.reshape(edge_lanes),
+        edge_live.reshape(edge_lanes),
+        edge_weight.reshape(edge_lanes),
+        bound,
+        src_proj,
+        dst_proj,
+    )
 
     rims0 = from_neighbours(rim0)
     (pre0,) = call(functools.partial(own_body, 0), [edge_wide], [table_buf], "own")(
@@ -635,18 +676,18 @@
         [full, edge_buf],
         "forward",
         True,
-    )(flags, *rims0, pre0, edge_rows, picks, state0, src_t, msg_proj, rim_picks_t)
+    )(where, *rims0, pre0, edge_scale, picks, state0, src_t, msg_proj, rim_picks_t)
 
     rims1 = from_neighbours(rim1)
     (back1,) = call(functools.partial(back_body, 1), [edge_wide], [], "back")(
-        msg_proj, node_cotangent, edge_rows, picks
+        msg_proj, node_cotangent, edge_scale, picks
     )
     (pre1,) = call(functools.partial(own_body, 1), [edge_wide], [table_buf], "own")(
         state1, src_t, dst_t, picks
     )
     act_edges1, grad_pre1, *sends1 = call(
         functools.partial(turn_body, 1), [edge_shape, edge_shape] + [rim_shape] * 4, [full], "turn", True
-    )(flags, *rims1, pre1, back1, edge_rows, picks, src_t)
+    )(where, *rims1, pre1, back1, edge_scale, picks, src_t)
 
     returned1 = to_neighbours(sends1)
     own_shape = ((2 * nodes, width), BF)
@@ -658,7 +699,7 @@
         picks, act_edges1, state1, msg_proj
     )
     keep1, send1 = call(terms_body, halves, [], "terms", True)(
-        flags, *rims1, *sends1, state1, own1, act1, node_cotangent
+        where, *rims1, *sends1, state1, own1, act1, node_cotangent
     )
     partial1, keep1, send1 = lax.optimization_barrier((partial1, keep1, send1))
     grad1, grad_pre0, *sends0 = call(
@@ -667,14 +708,14 @@
         [],
         "backward",
         True,
-    )(flags, *returned1, partial1, src_proj, rim_picks, msg_proj, slope0, picks)
+    )(where, *returned1, partial1, src_proj, rim_picks, msg_proj, slope0, picks)
 
     returned0 = to_neighbours(sends0)
     own0, partial0 = call(functools.partial(sums_body, 0), [own_shape, node_wide], [], "sums")(
         picks, grad_pre0, grad1, src_proj, dst_proj
     )
     keep0, send0 = call(terms_body, halves, [], "terms", True)(
-        flags, *rims0, *sends0, state0, own0, act0, grad1
+        where, *rims0, *sends0, state0, own0, act0, grad1
     )
     hidden = enc_out.shape[0]
     keep_enc, send_enc = call(
@@ -683,7 +724,7 @@
         [],
         "last",
         True,
-    )(flags, *returned0, partial0, src_proj, rim_picks, packed, enc_out, pooled, col_slope, slot_picks)
+    )(where, *returned0, partial0, src_proj, rim_picks, packed, enc_out, pooled, col_slope, slot_picks)
 
     total_rows = 2 * 3 * width + fin + hidden
     share = -(-total_rows // (16 * peers)) * 16
@@ -706,7 +747,7 @@
         [],
         "unpack",
         True,
-    )(flags, mine, swapped(mine, "dom", 0))
+    )(where, mine, swapped(mine, "dom", 0))
     return (node_out, *grads)
 
 

time: 123 us -> 123 us (level)
  blocking collectives: 38.8 us -> 62.7 us
  waiting for transfers between devices: 23.3 us -> 8.2 us
  starting transfers between devices: 26.4 us -> 19.1 us
    all_to_all x2 -> x3, blocking collectives: 38.8 us -> 62.7 us  [exchange(): return lax.all_to_all(shard, AXES, split_axis=0, concat_axis=0, tiled=True)]
    all_to_all x1 -> x0, waiting for transfers between devices: 15 us -> none  [exchange(): return lax.all_to_all(shard, AXES, split_axis=0, concat_axis=0, tiled=True)]
    all_to_all x1 -> x0, starting transfers between devices: 7.33 us -> none  [exchange(): return lax.all_to_all(shard, AXES, split_axis=0, concat_axis=0, tiled=True)]
  transfers between devices with their start and end apart: 21 -> 20, of which waited for: 8 -> 7; matrix products, arithmetic and copies ran while one was open for 1% -> 0% of each run, Pallas kernels for 11% -> 12%
where the time goes in v5:
time: 123 us; the launch traced here: 122 us
  blocking collectives  62.7 us (51%)
  Pallas kernels  31.2 us (25%)
  starting transfers between devices  19.1 us (16%)
  waiting for transfers between devices  8.2 us (7%)
    all_to_all x3, blocking collectives, exchange(): return lax.all_to_all(shard, AXES, split_axis=0, concat_axis=0, tiled=True)  62.7 us
    pallas_call x18, Pallas kernels, run(): pl.pallas_call(body, out_shape=tuple((jax.ShapeDtypeStruct(shape, dtype)...  31.2 us
    ppermute x12, starting transfers between devices, swapped(): return lax.ppermute(shard, axis, list(enumerate(partner)))  14.2 us
    ppermute x12, waiting for transfers between devices, swapped(): return lax.ppermute(shard, axis, list(enumerate(partner)))  5.34 us
    ppermute x8, starting transfers between devices, turned(): lax.ppermute(shard, axis, [(i, (i + by) % count) for i in range(count)])  4.83 us
    ppermute x8, waiting for transfers between devices, turned(): lax.ppermute(shard, axis, [(i, (i + by) % count) for i in range(count)])  2.85 us
  transfers between devices with their start and end apart: 20, of which 7 were waited for; matrix products, arithmetic and copies ran while one was open for 0% of the time, Pallas kernels for 12%

profile of v5, /device:TPU:0, one launch (start us, length us, event | category | flops | bytes accessed | tf_op | source)
XLA Modules:
  0.0 122.3 jit_solution(14084926735142159130)
XLA Ops:
  0.6 0.0 copy-start.9
  0.7 0.1 stack.15.where_ref
  0.8 1.7 %pack.1 = bf16[32,68,128]{2,1,0:T(8,128)(2,1)S(1)} custom-call(s32[5]{0:T(128)S(1)} %stack.15.where_ref, bf16[32,64,128]{2,1,0:T(8,128)(2,1)} %bitcast.23, s32[16,128]{1,0:T(8,128)} %bitcast.24, s32[16,128]{1,0:T(8,128)} %bitcast.25, f32[16,128]{1,0:T(8,128)} %bitcast.26), custom_call_target="tpu_custom_call" | custom-call | tf_op jit(solution)/shard_map/pack/pallas_call | solution.py:58
  2.5 23.9 %all_to_all.15.packed_ref = bf16[32,68,128]{2,1,0:T(8,128)(2,1)S(1)} all-to-all(bf16[32,68,128]{2,1,0:T(8,128)(2,1)S(1)} %pack.1), channel_id=1, replica_groups=mesh['grid'=4,'dom'=8] {'grid','dom'}, dimensions={0} | all-to-all | bytes 1114112 | tf_op jit(solution)/shard_map/all_to_all | solution.py:534
  26.4 3.1 %encode.1 = (bf16[512,256]{1,0:T(8,128)(2,1)S(1)}, bf16[256,2048]{1,0:T(8,128)(2,1)S(1)}, bf16[512,2048]{1,0:T(8,128)(2,1)S(1)}, bf16[512,256]{1,0:T(8,128)(2,1)S(1)}, bf16[256,256]{1,0:T(8,128)(2,1)S(1)}) custom-call(bf16[32,68,128]{2,1,0:T(8,128)(2,1)S(1)} %all_to_all.15.packed_ref, bf16[128,256]{1,0:T(8,128)(2,1)} %enc_in_far.1, ...), custom_call_target="tpu_custom_call" | custom-call | tf_op jit(solution)/shard_map/encode/pallas_call | solution.py:58
  29.5 1.2 collective-permute-start.3
  30.8 0.0 collective-permute-start.2
  30.8 0.7 collective-permute-start.1
  31.4 2.3 %collective-permute-start = (bf16[256,256]{1,0:T(8,128)(2,1)S(1)}, bf16[256,256]{1,0:T(8,128)(2,1)S(1)}, u32[]{:S(2)}, u32[]{:S(2)}) collective-permute-start(bf16[256,256]{1,0:T(8,128)(2,1)S(1)} %get-tuple-element.58), channel_id=1, source_target_pairs={{0,8},{8,0},{16,24},{24,16},{1,9},{9,1},{17,25},{25,17},{2,10},{10... | collective-permute-start | bytes 393224 | tf_op jit(solution)/shard_map/ppermute | solution.py:547
  33.8 1.2 picks.1
  35.0 0.0 copy-start.1
  35.0 1.4 %own.2.own_pre_ref = f32[256,2048]{1,0:T(8,128)S(1)} custom-call(bf16[512,256]{1,0:T(8,128)(2,1)S(1)} %get-tuple-element.59.state_ref, bf16[2,256,256]{2,1,0:T(8,128)(2,1)S(1)} %get-tuple-element.60.src_t_ref, bf16[2,256,256]{2,1,0:T(8,128)(2,1)S(1)} %get-tuple-element.61.dst_t_ref, bf16[2048,2048]{1,0:T(8,128)(2,1)S(1)} %get-tuple-element.57.picks_ref), custom_call_target="tpu_custom_call" | custom-call | tf_op jit(solution)/shard_map/own/pallas_call | solution.py:58
  36.4 0.0 collective-permute-done.3.right_ref
  36.4 0.0 collective-permute-done.2.left_ref
  36.4 0.0 collective-permute-done.1.second_ref
  36.4 0.9 collective-permute-done.first_ref
  37.4 3.4 %forward.1 = (bf16[256,2048]{1,0:T(8,128)(2,1)S(1)}, bf16[512,256]{1,0:T(8,128)(2,1)S(1)}, bf16[512,256]{1,0:T(8,128)(2,1)S(1)}, bf16[256,256]{1,0:T(8,128)(2,1)S(1)}) custom-call(s32[5]{0:T(128)S(1)} %stack.15.where_ref, bf16[256,256]{1,0:T(8,128)(2,1)S(1)} %collective-permute-done.first_ref, bf16[256,256]{1,0:T(8,128)(2,1)S(1)} %collective-permute-done.1.second_ref, ...), custom_call_target="tpu_custom_call" | custom-call | tf_op jit(solution)/shard_map/forward/pallas_call | solution.py:58
  40.8 1.3 %collective-permute-start.7 = (bf16[256,256]{1,0:T(8,128)(2,1)S(1)}, bf16[256,256]{1,0:T(8,128)(2,1)S(1)}, u32[]{:S(2)}, u32[]{:S(2)}) collective-permute-start(bf16[256,256]{1,0:T(8,128)(2,1)S(1)} %get-tuple-element.64), channel_id=1, source_target_pairs={{0,7},{1,0},{2,1},{3,2},{4,3},{5,4},{6,5},{7,6},{8,15},{9,8},{10,9... | collective-permute-start | bytes 393224 | tf_op jit(solution)/shard_map/ppermute | solution.py:539
  42.1 0.0 collective-permute-start.6
  42.1 0.8 collective-permute-start.5
  43.0 4.8 %collective-permute-start.4 = (bf16[256,256]{1,0:T(8,128)(2,1)S(1)}, bf16[256,256]{1,0:T(8,128)(2,1)S(1)}, u32[]{:S(2)}, u32[]{:S(2)}) collective-permute-start(bf16[256,256]{1,0:T(8,128)(2,1)S(1)} %get-tuple-element.64), channel_id=1, source_target_pairs={{0,8},{8,0},{16,24},{24,16},{1,9},{9,1},{17,25},{25,17},{2,10},{10... | collective-permute-start | bytes 393224 | tf_op jit(solution)/shard_map/ppermute | solution.py:547
  47.8 0.9 back.1.back_ref
  48.6 1.4 %own.3.own_pre_ref = f32[256,2048]{1,0:T(8,128)S(1)} custom-call(bf16[512,256]{1,0:T(8,128)(2,1)S(1)} %get-tuple-element.65.state_ref, bf16[2,256,256]{2,1,0:T(8,128)(2,1)S(1)} %get-tuple-element.60.src_t_ref, bf16[2,256,256]{2,1,0:T(8,128)(2,1)S(1)} %get-tuple-element.61.dst_t_ref, bf16[2048,2048]{1,0:T(8,128)(2,1)S(1)} %get-tuple-element.57.picks_ref), custom_call_target="tpu_custom_call" | custom-call | tf_op jit(solution)/shard_map/own/pallas_call | solution.py:58
  50.1 0.0 collective-permute-done.7.right_ref
  50.1 0.0 collective-permute-done.6.left_ref
  50.1 0.0 collective-permute-done.5.second_ref
  50.1 1.2 collective-permute-done.4.first_ref
  51.3 3.8 %turn.1 = (bf16[256,2048]{1,0:T(8,128)(2,1)S(1)}, bf16[256,2048]{1,0:T(8,128)(2,1)S(1)}, bf16[256,256]{1,0:T(8,128)(2,1)S(1)}, bf16[256,256]{1,0:T(8,128)(2,1)S(...) custom-call(s32[5]{0:T(128)S(1)} %stack.15.where_ref, ...), custom_call_target="tpu_custom_call" | custom-call | tf_op jit(solution)/shard_map/turn/pallas_call | solution.py:58
  55.1 1.8 %collective-permute-start.9 = (bf16[256,256]{1,0:T(8,128)(2,1)S(1)}, bf16[256,256]{1,0:T(8,128)(2,1)S(1)}, u32[]{:S(2)}, u32[]{:S(2)}) collective-permute-start(bf16[256,256]{1,0:T(8,128)(2,1)S(1)} %get-tuple-element.70.send0_ref), channel_id=1, source_target_pairs={{0,8},{8,0},{16,24},{24,16},{1,9},{9,1},{17,25},{25,17},{2,10},{10... | collective-permute-start | bytes 393224 | tf_op jit(solution)/shard_map/ppermute | solution.py:547
  56.9 0.7 collective-permute-start.10
  57.6 0.8 collective-permute-start.11
  58.5 0.0 collective-permute-start.12
  58.5 1.6 %out.1 = (bf16[512,256]{1,0:T(8,128)(2,1)S(1)}, bf16[512,256]{1,0:T(8,128)(2,1)}) custom-call(bf16[2048,2048]{1,0:T(8,128)(2,1)S(1)} %get-tuple-element.57.picks_ref, bf16[256,2048]{1,0:T(8,128)(2,1)S(1)} %get-tuple-element.66.act_edges_ref, bf16[512,256]{1,0:T(8,128)(2,1)S(1)} %get-tuple-element.65.state_ref, bf16[2,256,256]{2,1,0:T(8,128)(2,1)S(1)} %copy-done.1), custom_call_target="tpu_custom_call" | custom-call | tf_op jit(solution)/shard_map/out/pallas_call | solution.py:58
  60.1 1.5 %sums.2 = (bf16[1024,256]{1,0:T(8,128)(2,1)S(1)}, f32[512,256]{1,0:T(8,128)S(1)}) custom-call(bf16[2048,2048]{1,0:T(8,128)(2,1)S(1)} %get-tuple-element.57.picks_ref, bf16[256,2048]{1,0:T(8,128)(2,1)S(1)} %get-tuple-element.68.grad_pre_ref, bf16[512,256]{1,0:T(8,128)(2,1)S(1)} %copy-done.2, bf16[2,256,256]{2,1,0:T(8,128)(2,1)S(1)} %copy-done, ...), custom_call_target="tpu_custom_call" | custom-call | tf_op jit(solution)/shard_map/sums/pallas_call | solution.py:58
  61.6 1.1 terms.2
  62.8 0.0 collective-permute-done.9.first_ref
  62.8 0.0 collective-permute-done.10.second_ref
  62.8 0.0 collective-permute-done.11.left_ref
  62.8 0.9 collective-permute-done.12.right_ref
  63.7 2.9 %backward.1 = (f32[512,256]{1,0:T(8,128)S(1)}, bf16[256,2048]{1,0:T(8,128)(2,1)S(1)}, bf16[256,256]{1,0:T(8,128)(2,1)S(1)}, bf16[256,256]{1,0:T(8,128)(2,1)S(1)}...) custom-call(s32[5]{0:T(128)S(1)} %stack.15.where_ref, ...), custom_call_target="tpu_custom_call" | custom-call | tf_op jit(solution)/shard_map/backward/pallas_call | solution.py:58
  66.6 1.8 %collective-permute-start.14 = (bf16[256,256]{1,0:T(8,128)(2,1)S(1)}, bf16[256,256]{1,0:T(8,128)(2,1)S(1)}, u32[]{:S(2)}, u32[]{:S(2)}) collective-permute-start(bf16[256,256]{1,0:T(8,128)(2,1)S(1)} %get-tuple-element.83.send0_ref), channel_id=1, source_target_pairs={{0,8},{8,0},{16,24},{24,16},{1,9},{9,1},{17,25},{25,17},{2,10},{10... | collective-permute-start | bytes 393224 | tf_op jit(solution)/shard_map/ppermute | solution.py:547
  68.4 0.7 collective-permute-start.15
  69.1 1.5 %collective-permute-start.16 = (bf16[256,256]{1,0:T(8,128)(2,1)S(1)}, bf16[256,256]{1,0:T(8,128)(2,1)S(1)}, u32[]{:S(2)}, u32[]{:S(2)}) collective-permute-start(bf16[256,256]{1,0:T(8,128)(2,1)S(1)} %get-tuple-element.85.send2_ref), channel_id=1, source_target_pairs={{0,7},{1,0},{2,1},{3,2},{4,3},{5,4},{6,5},{7,6},{8,15},{9,8},{10,9... | collective-permute-start | bytes 393224 | tf_op jit(solution)/shard_map/ppermute | solution.py:539
  70.5 0.0 collective-permute-start.17
  70.5 0.6 collective-permute-start.8
  71.1 1.5 %sums.3 = (bf16[1024,256]{1,0:T(8,128)(2,1)S(1)}, f32[512,256]{1,0:T(8,128)S(1)}) custom-call(bf16[2048,2048]{1,0:T(8,128)(2,1)S(1)} %get-tuple-element.57.picks_ref, bf16[256,2048]{1,0:T(8,128)(2,1)S(1)} %get-tuple-element.87.grad_pre_ref, f32[512,256]{1,0:T(8,128)S(1)} %get-tuple-element.88.grad_ref, bf16[2,256,256]{2,1,0:T(8,128)(2,1)S(1)} %copy-done, ...), custom_call_target="tpu_custom_call" | custom-call | tf_op jit(solution)/shard_map/sums/pallas_call | solution.py:58
  72.7 0.0 copy-start.4
  72.7 1.1 terms.3
  73.8 0.0 collective-permute-done.14.first_ref
  73.8 0.1 collective-permute-start.13
  73.9 0.0 collective-permute-done.15.second_ref
  73.9 0.4 collective-permute-done.16.left_ref
  74.4 1.5 %collective-permute-done.17.right_ref = bf16[256,256]{1,0:T(8,128)(2,1)S(1)} collective-permute-done((bf16[256,256]{1,0:T(8,128)(2,1)S(1)}, bf16[256,256]{1,0:T(8,128)(2,1)S(1)}, u32[]{:S(2)}, u32[]{:S(2)}) %collective-permute-start.17) | collective-permute-done | bytes 131104 | tf_op jit(solution)/shard_map/ppermute | solution.py:539
  75.8 2.3 %last.1 = (bf16[384,128]{1,0:T(8,128)(2,1)S(1)}, bf16[384,128]{1,0:T(8,128)(2,1)S(1)}) custom-call(s32[5]{0:T(128)S(1)} %stack.15.where_ref, bf16[256,256]{1,0:T(8,128)(2,1)S(1)} %collective-permute-done.14.first_ref, bf16[256,256]{1,0:T(8,128)(2,1)S(1)} %collective-permute-done.15.second_ref, bf16[256,256]{1,0:T(8,128)(2,1)S(1)} %collective-permute-done.16.left_ref, ...), custom_call_target="tpu_custom_call" | custom-call | tf_op jit(solution)/shard_map/last/pallas_call | solution.py:58
  78.2 0.1 collective-permute-start.18
  78.3 0.0 collective-permute-done.13.refs_3_
  78.3 1.3 %collective-permute-done.18.refs_5_ = bf16[384,128]{1,0:T(8,128)(2,1)S(1)} collective-permute-done((bf16[384,128]{1,0:T(8,128)(2,1)S(1)}, bf16[384,128]{1,0:T(8,128)(2,1)S(1)}, u32[]{:S(2)}, u32[]{:S(2)}) %collective-permute-start.18) | collective-permute-done | bytes 98336 | tf_op jit(solution)/shard_map/ppermute | solution.py:547
  79.5 0.1 merge.1
  79.7 20.4 %all_to_all.16.parts_ref = bf16[32,64,128]{2,1,0:T(8,128)(2,1)S(1)} all-to-all(bf16[32,64,128]{2,1,0:T(8,128)(2,1)S(1)} %bitcast.14), channel_id=1, replica_groups=mesh['grid'=4,'dom'=8] {'grid','dom'}, dimensions={0} | all-to-all | bytes 1048576 | tf_op jit(solution)/shard_map/all_to_all | solution.py:534
  100.1 0.1 share.1
  100.2 18.4 %all_to_all.17 = bf16[32,64,128]{2,1,0:T(8,128)(2,1)S(1)} all-to-all(bf16[32,64,128]{2,1,0:T(8,128)(2,1)S(1)} %share.1), channel_id=1, replica_groups=mesh['grid'=4,'dom'=8] {'grid','dom'}, dimensions={0} | all-to-all | bytes 1048576 | tf_op jit(solution)/shard_map/all_to_all | solution.py:534
  118.6 0.0 collective-permute-start.19
  118.6 1.9 %collective-permute-done.19.other_ref = bf16[2048,128]{1,0:T(8,128)(2,1)S(1)} collective-permute-done((bf16[2048,128]{1,0:T(8,128)(2,1)S(1)}, bf16[2048,128]{1,0:T(8,128)(2,1)S(1)}, u32[]{:S(2)}, u32[]{:S(2)}) %collective-permute-start.19) | collective-permute-done | bytes 524320 | tf_op jit(solution)/shard_map/ppermute | solution.py:547
  120.5 1.9 %unpack.1 = (f32[128,256]{1,0:T(8,128)}, f32[256,256]{1,0:T(8,128)}, f32[2,256,256]{2,1,0:T(8,128)}, f32[2,256,256]{2,1,0:T(8,128)}, f32[2,256,256]{2,1,0:T(8,128)}) custom-call(s32[5]{0:T(128)S(1)} %stack.15.where_ref, bf16[2048,128]{1,0:T(8,128)(2,1)S(1)} %bitcast.16, bf16[2048,128]{1,0:T(8,128)(2,1)S(1)} %collective-permute-done.19.other_ref), custom_call_target="tpu_custom_call" | custom-call | tf_op jit(solution)/shard_map/unpack/pallas_call | solution.py:58
  (18 shorter events, 0.0 us)
Async XLA Ops:
  0.6 33.1 %copy-start.9 = (s32[256]{0:T(256)S(1)}, s32[256]{0:T(256)}, u32[]{:S(2)}) copy-start(s32[256]{0:T(256)} %param.21) | copy-start | bytes 3076
  0.6 33.1 %copy-start.6 = (s32[2048]{0:T(1024)S(1)}, s32[2048]{0:T(1024)}, u32[]{:S(2)}) copy-start(s32[2048]{0:T(1024)} %param.23) | copy-start | bytes 24580
  0.7 33.1 %copy-start = (bf16[2,256,256]{2,1,0:T(8,128)(2,1)S(1)}, bf16[2,256,256]{2,1,0:T(8,128)(2,1)}, u32[]{:S(2)}) copy-start(bf16[2,256,256]{2,1,0:T(8,128)(2,1)} %src_ref.7) | copy-start | bytes 786436
  0.7 33.1 %copy-start.3 = (bf16[2,256,256]{2,1,0:T(8,128)(2,1)S(1)}, bf16[2,256,256]{2,1,0:T(8,128)(2,1)}, u32[]{:S(2)}) copy-start(bf16[2,256,256]{2,1,0:T(8,128)(2,1)} %dst_ref.3) | copy-start | bytes 786436
  0.7 33.1 %copy-start.8 = (f32[2048]{0:T(1024)S(1)}, f32[2048]{0:T(1024)}, u32[]{:S(2)}) copy-start(f32[2048]{0:T(1024)} %param.25) | copy-start | bytes 24580
  0.7 33.1 %copy-start.7 = (s32[2048]{0:T(1024)S(1)}, s32[2048]{0:T(1024)}, u32[]{:S(2)}) copy-start(s32[2048]{0:T(1024)} %param.24) | copy-start | bytes 24580
  0.7 33.1 %copy-start.5 = (s32[2048]{0:T(1024)S(1)}, s32[2048]{0:T(1024)}, u32[]{:S(2)}) copy-start(s32[2048]{0:T(1024)} %param.22) | copy-start | bytes 24580
  29.5 6.9 %collective-permute-start.3 = (bf16[256,256]{1,0:T(8,128)(2,1)S(1)}, bf16[256,256]{1,0:T(8,128)(2,1)S(1)}, u32[]{:S(2)}, u32[]{:S(2)}) collective-permute-start(bf16[256,256]{1,0:T(8,128)(2,1)S(1)} %get-tuple-element.58), channel_id=1, source_target_pairs={{0,7},{1,0},{2,1},{3,2},{4,3},{5,4},{6,5},{7,6},{8,15},{9,8},{10,9... | collective-permute-start | bytes 393224 | tf_op jit(solution)/shard_map/ppermute | solution.py:539
  30.8 5.7 %collective-permute-start.2 = (bf16[256,256]{1,0:T(8,128)(2,1)S(1)}, bf16[256,256]{1,0:T(8,128)(2,1)S(1)}, u32[]{:S(2)}, u32[]{:S(2)}) collective-permute-start(bf16[256,256]{1,0:T(8,128)(2,1)S(1)} %get-tuple-element.58), channel_id=1, source_target_pairs={{0,1},{1,2},{2,3},{3,4},{4,5},{5,6},{6,7},{7,0},{8,9},{9,10},{10,1... | collective-permute-start | bytes 393224 | tf_op jit(solution)/shard_map/ppermute | solution.py:539
  30.8 5.7 %collective-permute-start.1 = (bf16[256,256]{1,0:T(8,128)(2,1)S(1)}, bf16[256,256]{1,0:T(8,128)(2,1)S(1)}, u32[]{:S(2)}, u32[]{:S(2)}) collective-permute-start(bf16[256,256]{1,0:T(8,128)(2,1)S(1)} %get-tuple-element.58), channel_id=1, source_target_pairs={{0,0},{8,16},{16,8},{24,24},{1,1},{9,17},{17,9},{25,25},{2,2},{10,... | collective-permute-start | bytes 393224 | tf_op jit(solution)/shard_map/ppermute | solution.py:547
  31.4 5.9 %collective-permute-start = (bf16[256,256]{1,0:T(8,128)(2,1)S(1)}, bf16[256,256]{1,0:T(8,128)(2,1)S(1)}, u32[]{:S(2)}, u32[]{:S(2)}) collective-permute-start(bf16[256,256]{1,0:T(8,128)(2,1)S(1)} %get-tuple-element.58), channel_id=1, source_target_pairs={{0,8},{8,0},{16,24},{24,16},{1,9},{9,1},{17,25},{25,17},{2,10},{10... | collective-permute-start | bytes 393224 | tf_op jit(solution)/shard_map/ppermute | solution.py:547
  35.0 2.4 %copy-start.1 = (bf16[2,256,256]{2,1,0:T(8,128)(2,1)S(1)}, bf16[2,256,256]{2,1,0:T(8,128)(2,1)}, u32[]{:S(2)}) copy-start(bf16[2,256,256]{2,1,0:T(8,128)(2,1)} %msg_ref.7) | copy-start | bytes 786436
  37.4 10.4 %copy-start.2 = (bf16[512,256]{1,0:T(8,128)(2,1)S(1)}, bf16[512,256]{1,0:T(8,128)(2,1)}, u32[]{:S(2)}) copy-start(bf16[512,256]{1,0:T(8,128)(2,1)} %grad_ref.5) | copy-start | bytes 786436
  40.8 9.3 %collective-permute-start.7 = (bf16[256,256]{1,0:T(8,128)(2,1)S(1)}, bf16[256,256]{1,0:T(8,128)(2,1)S(1)}, u32[]{:S(2)}, u32[]{:S(2)}) collective-permute-start(bf16[256,256]{1,0:T(8,128)(2,1)S(1)} %get-tuple-element.64), channel_id=1, source_target_pairs={{0,7},{1,0},{2,1},{3,2},{4,3},{5,4},{6,5},{7,6},{8,15},{9,8},{10,9... | collective-permute-start | bytes 393224 | tf_op jit(solution)/shard_map/ppermute | solution.py:539
  42.1 8.0 %collective-permute-start.6 = (bf16[256,256]{1,0:T(8,128)(2,1)S(1)}, bf16[256,256]{1,0:T(8,128)(2,1)S(1)}, u32[]{:S(2)}, u32[]{:S(2)}) collective-permute-start(bf16[256,256]{1,0:T(8,128)(2,1)S(1)} %get-tuple-element.64), channel_id=1, source_target_pairs={{0,1},{1,2},{2,3},{3,4},{4,5},{5,6},{6,7},{7,0},{8,9},{9,10},{10,1... | collective-permute-start | bytes 393224 | tf_op jit(solution)/shard_map/ppermute | solution.py:539
  42.1 8.0 %collective-permute-start.5 = (bf16[256,256]{1,0:T(8,128)(2,1)S(1)}, bf16[256,256]{1,0:T(8,128)(2,1)S(1)}, u32[]{:S(2)}, u32[]{:S(2)}) collective-permute-start(bf16[256,256]{1,0:T(8,128)(2,1)S(1)} %get-tuple-element.64), channel_id=1, source_target_pairs={{0,0},{8,16},{16,8},{24,24},{1,1},{9,17},{17,9},{25,25},{2,2},{10,... | collective-permute-start | bytes 393224 | tf_op jit(solution)/shard_map/ppermute | solution.py:547
  43.0 8.4 %collective-permute-start.4 = (bf16[256,256]{1,0:T(8,128)(2,1)S(1)}, bf16[256,256]{1,0:T(8,128)(2,1)S(1)}, u32[]{:S(2)}, u32[]{:S(2)}) collective-permute-start(bf16[256,256]{1,0:T(8,128)(2,1)S(1)} %get-tuple-element.64), channel_id=1, source_target_pairs={{0,8},{8,0},{16,24},{24,16},{1,9},{9,1},{17,25},{25,17},{2,10},{10... | collective-permute-start | bytes 393224 | tf_op jit(solution)/shard_map/ppermute | solution.py:547
  55.1 7.6 %collective-permute-start.9 = (bf16[256,256]{1,0:T(8,128)(2,1)S(1)}, bf16[256,256]{1,0:T(8,128)(2,1)S(1)}, u32[]{:S(2)}, u32[]{:S(2)}) collective-permute-start(bf16[256,256]{1,0:T(8,128)(2,1)S(1)} %get-tuple-element.70.send0_ref), channel_id=1, source_target_pairs={{0,8},{8,0},{16,24},{24,16},{1,9},{9,1},{17,25},{25,17},{2,10},{10... | collective-permute-start | bytes 393224 | tf_op jit(solution)/shard_map/ppermute | solution.py:547
  56.9 5.8 %collective-permute-start.10 = (bf16[256,256]{1,0:T(8,128)(2,1)S(1)}, bf16[256,256]{1,0:T(8,128)(2,1)S(1)}, u32[]{:S(2)}, u32[]{:S(2)}) collective-permute-start(bf16[256,256]{1,0:T(8,128)(2,1)S(1)} %get-tuple-element.71.send1_ref), channel_id=1, source_target_pairs={{0,0},{8,16},{16,8},{24,24},{1,1},{9,17},{17,9},{25,25},{2,2},{10,... | collective-permute-start | bytes 393224 | tf_op jit(solution)/shard_map/ppermute | solution.py:547
  57.6 5.2 %collective-permute-start.11 = (bf16[256,256]{1,0:T(8,128)(2,1)S(1)}, bf16[256,256]{1,0:T(8,128)(2,1)S(1)}, u32[]{:S(2)}, u32[]{:S(2)}) collective-permute-start(bf16[256,256]{1,0:T(8,128)(2,1)S(1)} %get-tuple-element.72.send2_ref), channel_id=1, source_target_pairs={{0,7},{1,0},{2,1},{3,2},{4,3},{5,4},{6,5},{7,6},{8,15},{9,8},{10,9... | collective-permute-start | bytes 393224 | tf_op jit(solution)/shard_map/ppermute | solution.py:539
  58.5 5.3 %collective-permute-start.12 = (bf16[256,256]{1,0:T(8,128)(2,1)S(1)}, bf16[256,256]{1,0:T(8,128)(2,1)S(1)}, u32[]{:S(2)}, u32[]{:S(2)}) collective-permute-start(bf16[256,256]{1,0:T(8,128)(2,1)S(1)} %get-tuple-element.73.send3_ref), channel_id=1, source_target_pairs={{0,1},{1,2},{2,3},{3,4},{4,5},{5,6},{6,7},{7,0},{8,9},{9,10},{10,1... | collective-permute-start | bytes 393224 | tf_op jit(solution)/shard_map/ppermute | solution.py:539
  66.6 7.2 %collective-permute-start.14 = (bf16[256,256]{1,0:T(8,128)(2,1)S(1)}, bf16[256,256]{1,0:T(8,128)(2,1)S(1)}, u32[]{:S(2)}, u32[]{:S(2)}) collective-permute-start(bf16[256,256]{1,0:T(8,128)(2,1)S(1)} %get-tuple-element.83.send0_ref), channel_id=1, source_target_pairs={{0,8},{8,0},{16,24},{24,16},{1,9},{9,1},{17,25},{25,17},{2,10},{10... | collective-permute-start | bytes 393224 | tf_op jit(solution)/shard_map/ppermute | solution.py:547
  68.4 5.5 %collective-permute-start.15 = (bf16[256,256]{1,0:T(8,128)(2,1)S(1)}, bf16[256,256]{1,0:T(8,128)(2,1)S(1)}, u32[]{:S(2)}, u32[]{:S(2)}) collective-permute-start(bf16[256,256]{1,0:T(8,128)(2,1)S(1)} %get-tuple-element.84.send1_ref), channel_id=1, source_target_pairs={{0,0},{8,16},{16,8},{24,24},{1,1},{9,17},{17,9},{25,25},{2,2},{10,... | collective-permute-start | bytes 393224 | tf_op jit(solution)/shard_map/ppermute | solution.py:547
  69.1 5.3 %collective-permute-start.16 = (bf16[256,256]{1,0:T(8,128)(2,1)S(1)}, bf16[256,256]{1,0:T(8,128)(2,1)S(1)}, u32[]{:S(2)}, u32[]{:S(2)}) collective-permute-start(bf16[256,256]{1,0:T(8,128)(2,1)S(1)} %get-tuple-element.85.send2_ref), channel_id=1, source_target_pairs={{0,7},{1,0},{2,1},{3,2},{4,3},{5,4},{6,5},{7,6},{8,15},{9,8},{10,9... | collective-permute-start | bytes 393224 | tf_op jit(solution)/shard_map/ppermute | solution.py:539
  70.5 5.3 %collective-permute-start.17 = (bf16[256,256]{1,0:T(8,128)(2,1)S(1)}, bf16[256,256]{1,0:T(8,128)(2,1)S(1)}, u32[]{:S(2)}, u32[]{:S(2)}) collective-permute-start(bf16[256,256]{1,0:T(8,128)(2,1)S(1)} %get-tuple-element.86.send3_ref), channel_id=1, source_target_pairs={{0,1},{1,2},{2,3},{3,4},{4,5},{5,6},{6,7},{7,0},{8,9},{9,10},{10,1... | collective-permute-start | bytes 393224 | tf_op jit(solution)/shard_map/ppermute | solution.py:539
  70.5 7.7 %collective-permute-start.8 = (bf16[768,128]{1,0:T(8,128)(2,1)S(1)}, bf16[768,128]{1,0:T(8,128)(2,1)S(1)}, u32[]{:S(2)}, u32[]{:S(2)}) collective-permute-start(bf16[768,128]{1,0:T(8,128)(2,1)S(1)} %get-tuple-element.79), channel_id=1, source_target_pairs={{0,1},{1,0},{2,3},{3,2},{4,5},{5,4},{6,7},{7,6},{8,9},{9,8},{10,11... | collective-permute-start | bytes 589832 | tf_op jit(solution)/shard_map/ppermute | solution.py:547
  72.7 3.1 %copy-start.4 = (bf16[256,256]{1,0:T(8,128)(2,1)S(1)}, bf16[256,256]{1,0:T(8,128)(2,1)}, u32[]{:S(2)}) copy-start(bf16[256,256]{1,0:T(8,128)(2,1)} %enc_out_ref.1) | copy-start | bytes 393220
  73.8 4.4 %collective-permute-start.13 = (bf16[768,128]{1,0:T(8,128)(2,1)S(1)}, bf16[768,128]{1,0:T(8,128)(2,1)S(1)}, u32[]{:S(2)}, u32[]{:S(2)}) collective-permute-start(bf16[768,128]{1,0:T(8,128)(2,1)S(1)} %get-tuple-element.92), channel_id=1, source_target_pairs={{0,1},{1,0},{2,3},{3,2},{4,5},{5,4},{6,7},{7,6},{8,9},{9,8},{10,11... | collective-permute-start | bytes 589832 | tf_op jit(solution)/shard_map/ppermute | solution.py:547
  78.2 1.4 %collective-permute-start.18 = (bf16[384,128]{1,0:T(8,128)(2,1)S(1)}, bf16[384,128]{1,0:T(8,128)(2,1)S(1)}, u32[]{:S(2)}, u32[]{:S(2)}) collective-permute-start(bf16[384,128]{1,0:T(8,128)(2,1)S(1)} %get-tuple-element.98), channel_id=1, source_target_pairs={{0,1},{1,0},{2,3},{3,2},{4,5},{5,4},{6,7},{7,6},{8,9},{9,8},{10,11... | collective-permute-start | bytes 294920 | tf_op jit(solution)/shard_map/ppermute | solution.py:547
  118.6 1.9 %collective-permute-start.19 = (bf16[2048,128]{1,0:T(8,128)(2,1)S(1)}, bf16[2048,128]{1,0:T(8,128)(2,1)S(1)}, u32[]{:S(2)}, u32[]{:S(2)}) collective-permute-start(bf16[2048,128]{1,0:T(8,128)(2,1)S(1)} %bitcast.15), channel_id=1, source_target_pairs={{0,1},{1,0},{2,3},{3,2},{4,5},{5,4},{6,7},{7,6},{8,9},{9,8},{10,11... | collective-permute-start | bytes 1572872 | tf_op jit(solution)/shard_map/ppermute | solution.py:547

commit v6 on v5

--- a/solution.py
+++ b/solution.py
@@ -147,15 +147,17 @@
     src_t_ref,
     dst_t_ref,
 ):
-    nodes = rim_picks.shape[0]
-    ext = picks_ref.shape[0] - 2 * nodes
+    nodes, rim = rim_picks.shape
     src = long_row(src_ref[...].astype(F32))
     dst = long_row(dst_ref[...].astype(F32))
     scale_ref[...] = long_row(weight_ref[...] * live_ref[...].astype(F32))
     for start in range(0, picks_ref.shape[1], CHUNK):
         block = picks_ref.at[:, pl.ds(start, CHUNK)]
-        put_picks(block, 0, dst[:, start : start + CHUNK], nodes)
-        put_picks(block, nodes, src[:, start : start + CHUNK], nodes + ext)
+        here = src[:, start : start + CHUNK]
+        put_picks(block, 0, here - float(nodes), 2 * rim)
+        put_picks(block, 2 * rim, dst[:, start : start + CHUNK], nodes)
+        put_picks(block, 2 * rim + nodes, here, nodes)
+        put_picks(block, 2 * rim + 2 * nodes, here - float(nodes + 2 * rim), 2 * rim)
     put_picks(rim_picks, 0, long_row(bound_ref[...].astype(F32)), nodes)
     rim_picks_t[...] = turned_over(rim_picks[...])
     for layer in range(src_t_ref.shape[0]):
@@ -168,11 +170,19 @@
     rim_ref[...] = mm(rim_picks_t[...], state_ref[...]).astype(BF)
 
 
-def in_order(where_ref, rims):
-    first, second, left, right = (ref[...] for ref in rims)
+def grid_rims(where_ref, first_ref, second_ref):
     odd = is_odd(where_ref[GRID_AT])
-    ordered = (jnp.where(odd, first, second), jnp.where(odd, second, first), left, right)
-    return [rows * side.astype(BF) for rows, side in zip(ordered, side_marks(where_ref))]
+    up, down, _, _ = side_marks(where_ref)
+    first, second = first_ref[...], second_ref[...]
+    return (
+        jnp.where(odd, first, second) * up.astype(BF),
+        jnp.where(odd, second, first) * down.astype(BF),
+    )
+
+
+def dom_rims(where_ref, left_ref, right_ref):
+    _, _, left, right = side_marks(where_ref)
+    return left_ref[...] * left.astype(BF), right_ref[...] * right.astype(BF)
 
 
 def put_col_rows(packed_ref, bucket, rows_ref):
@@ -199,10 +209,10 @@
 def encode_body(
     bucket,
     packed_ref,
-    enc_in_far,
-    enc_out_far,
-    static_far,
-    bound_far,
+    enc_in_ref,
+    enc_out_ref,
+    static_ref,
+    bound_ref,
     pooled_ref,
     slope_ref,
     picks_ref,
@@ -210,25 +220,11 @@
     rim_ref,
     act_ref,
     rows_ref,
-    enc_in_ref,
-    enc_out_ref,
-    static_ref,
-    bound_ref,
     rim_picks,
-    sems,
 ):
     nodes = static_ref.shape[0]
     peers_step = CHUNK // bucket
-    copies = [
-        pltpu.make_async_copy(enc_in_far, enc_in_ref, sems.at[0]),
-        pltpu.make_async_copy(enc_out_far, enc_out_ref, sems.at[1]),
-        pltpu.make_async_copy(static_far, static_ref, sems.at[2]),
-        pltpu.make_async_copy(bound_far, bound_ref, sems.at[3]),
-    ]
-    for copy in copies:
-        copy.start()
     put_col_rows(packed_ref, bucket, rows_ref)
-    copies[0].wait()
     enc_in_t = turned_over(enc_in_ref[...])
 
     def step(start, at):
@@ -243,31 +239,39 @@
 
     chunks(rows_ref.shape[1], step)
     pooled_ref[...] = mm_t(picks_ref[...], act_ref[...]).astype(BF)
-    for copy in copies[1:]:
-        copy.wait()
     put_picks(rim_picks, 0, long_row(bound_ref[...].astype(F32)), nodes)
     state = static_ref[...].astype(F32) + mm(pooled_ref[...], enc_out_ref[...])
     state_ref[...] = state.astype(BF)
     rim_ref[...] = t_mm(rim_picks[...], state_ref[...]).astype(BF)
 
 
-def own_body(layer, state_ref, src_t_ref, dst_t_ref, picks_ref, out_ref, table_ref):
+def own_body(
+    layer, where_ref, left_ref, right_ref, state_ref, src_t_ref, dst_t_ref, picks_ref, out_ref, table_ref
+):
     nodes = state_ref.shape[0]
+    rim = left_ref.shape[0]
     held = state_ref[...]
     table_ref[:, :nodes] = mm_t(dst_t_ref[layer], held).astype(BF)
-    table_ref[:, nodes:] = mm_t(src_t_ref[layer], held).astype(BF)
-    out_ref[...] = mm(table_ref[...], picks_ref[: 2 * nodes, :])
+    table_ref[:, nodes : 2 * nodes] = mm_t(src_t_ref[layer], held).astype(BF)
+    for side, rim_rows in enumerate(dom_rims(where_ref, left_ref, right_ref)):
+        start = 2 * nodes + side * rim
+        table_ref[:, start : start + rim] = mm_t(src_t_ref[layer], rim_rows).astype(BF)
+    out_ref[...] = mm(table_ref[...], picks_ref[2 * rim :, :])
+
+
+def by_target(picks_ref, nodes):
+    return pl.ds((picks_ref.shape[0] - 2 * nodes) // 2, nodes)
 
 
 def back_body(layer, msg_ref, grad_ref, scale_ref, picks_ref, out_ref):
     nodes = grad_ref.shape[0]
     back = mm_t(msg_ref[layer], grad_ref[...]).astype(BF)
-    out_ref[...] = mm(back, picks_ref[:nodes, :]) * scale_ref[...]
-
-
-def fill_rims(full_ref, where_ref, rims, src_t_ref):
+    out_ref[...] = mm(back, picks_ref[by_target(picks_ref, nodes), :]) * scale_ref[...]
+
+
+def fill_rims(full_ref, rims, src_t_ref):
     rim = rims[0].shape[0]
-    for side, rim_rows in enumerate(in_order(where_ref, rims)):
+    for side, rim_rows in enumerate(rims):
         full_ref[:, side * rim : (side + 1) * rim] = mm_t(src_t_ref[...], rim_rows).astype(BF)
 
 
@@ -276,8 +280,6 @@
     where_ref,
     first_ref,
     second_ref,
-    left_ref,
-    right_ref,
     own_pre_ref,
     scale_ref,
     picks_ref,
@@ -293,29 +295,36 @@
     act_ref,
 ):
     nodes = state_ref.shape[0]
-    fill_rims(full_ref, where_ref, (first_ref, second_ref, left_ref, right_ref), src_t_ref.at[layer])
+    rims = grid_rims(where_ref, first_ref, second_ref)
+    fill_rims(full_ref, rims, src_t_ref.at[layer])
+    sides = pl.ds(0, full_ref.shape[1])
 
     def step(start, at):
-        pre = own_pre_ref[:, at] + mm(full_ref[...], picks_ref[2 * nodes :, at])
+        pre = own_pre_ref[:, at] + mm(full_ref[...], picks_ref[sides, at])
         scale = scale_ref[:, at]
         sig = sigmoid(pre)
         act_ref[:, at] = (pre * sig * scale).astype(BF)
         slope_ref[:, at] = (sig * (1.0 + pre * (1.0 - sig)) * scale).astype(BF)
 
     chunks(scale_ref.shape[1], step)
-    node_act_ref[...] = mm_t(picks_ref[:nodes, :], act_ref[...]).astype(BF)
+    node_act_ref[...] = mm_t(picks_ref[by_target(picks_ref, nodes), :], act_ref[...]).astype(BF)
     state = state_ref[...].astype(F32) + mm(node_act_ref[...], msg_ref[layer])
     put_state(state, next_state_ref, rim_ref, rim_picks_t)
 
 
-def put_sends(where_ref, sums, sends):
-    rim = sums.shape[0] // 4
-    up, down, left, right = (sums[side * rim : (side + 1) * rim, :].astype(BF) for side in range(4))
+def put_grid_sends(where_ref, sums, first_ref, second_ref):
+    rim = sums.shape[0] // 2
+    up, down = sums[:rim, :].astype(BF), sums[rim:, :].astype(BF)
     odd = is_odd(where_ref[GRID_AT])
-    sends[0][...] = jnp.where(odd, up, down)
-    sends[1][...] = jnp.where(odd, down, up)
-    sends[2][...] = left
-    sends[3][...] = right
+    first_ref[...] = jnp.where(odd, up, down)
+    second_ref[...] = jnp.where(odd, down, up)
+
+
+def dom_sums_body(picks_ref, grad_pre_ref, left_ref, right_ref):
+    rim = left_ref.shape[0]
+    first = picks_ref.shape[0] - 2 * rim
+    left_ref[...] = mm_t(picks_ref[first : first + rim, :], grad_pre_ref[...]).astype(BF)
+    right_ref[...] = mm_t(picks_ref[first + rim :, :], grad_pre_ref[...]).astype(BF)
 
 
 def turn_body(
@@ -323,8 +332,6 @@
     where_ref,
     first_ref,
     second_ref,
-    left_ref,
-    right_ref,
     own_pre_ref,
     back_ref,
     scale_ref,
@@ -334,22 +341,22 @@
     grad_pre_ref,
     send0_ref,
     send1_ref,
-    send2_ref,
-    send3_ref,
     full_ref,
 ):
-    first = picks_ref.shape[0] - full_ref.shape[1]
-    fill_rims(full_ref, where_ref, (first_ref, second_ref, left_ref, right_ref), src_t_ref.at[layer])
+    rim = first_ref.shape[0]
+    rims = grid_rims(where_ref, first_ref, second_ref)
+    fill_rims(full_ref, rims, src_t_ref.at[layer])
+    sides = pl.ds(0, 2 * rim)
 
     def step(start, at):
-        pre = own_pre_ref[:, at] + mm(full_ref[...], picks_ref[first:, at])
+        pre = own_pre_ref[:, at] + mm(full_ref[...], picks_ref[sides, at])
         sig = sigmoid(pre)
         act_ref[:, at] = (pre * sig * scale_ref[:, at]).astype(BF)
         grad_pre_ref[:, at] = (back_ref[:, at] * (sig * (1.0 + pre * (1.0 - sig)))).astype(BF)
 
     chunks(scale_ref.shape[1], step)
-    sums = mm_t(picks_ref[first:, :], grad_pre_ref[...])
-    put_sends(where_ref, sums, (send0_ref, send1_ref, send2_ref, send3_ref))
+    sums = mm_t(picks_ref[sides, :], grad_pre_ref[...])
+    put_grid_sends(where_ref, sums, send0_ref, send1_ref)
 
 
 def merged_grad(partial_ref, where_ref, returned, src_ref, rim_picks):
@@ -379,8 +386,6 @@
     grad_pre_ref,
     send0_ref,
     send1_ref,
-    send2_ref,
-    send3_ref,
 ):
     nodes = partial_ref.shape[0]
     returned = (first_ref, second_ref, left_ref, right_ref)
@@ -389,17 +394,19 @@
     back = mm_t(msg_ref[layer - 1], grad.astype(BF)).astype(BF)
 
     def step(start, at):
-        grad_pre = mm(back, picks_ref[:nodes, at]) * slope_ref[:, at].astype(F32)
+        grad_pre = mm(back, picks_ref[by_target(picks_ref, nodes), at]) * slope_ref[:, at].astype(F32)
         grad_pre_ref[:, at] = grad_pre.astype(BF)
 
     chunks(picks_ref.shape[1], step)
-    sums = mm_t(picks_ref[2 * nodes :, :], grad_pre_ref[...])
-    put_sends(where_ref, sums, (send0_ref, send1_ref, send2_ref, send3_ref))
+    sides = pl.ds(0, 2 * first_ref.shape[0])
+    sums = mm_t(picks_ref[sides, :], grad_pre_ref[...])
+    put_grid_sends(where_ref, sums, send0_ref, send1_ref)
 
 
 def sums_body(layer, picks_ref, grad_pre_ref, grad_ref, src_ref, dst_ref, own_ref, partial_ref):
     nodes = grad_ref.shape[0]
-    own_ref[...] = mm_t(picks_ref[: 2 * nodes, :], grad_pre_ref[...]).astype(BF)
+    first = by_target(picks_ref, nodes).start
+    own_ref[...] = mm_t(picks_ref[first : first + 2 * nodes, :], grad_pre_ref[...]).astype(BF)
     partial_ref[...] = (
         grad_ref[...].astype(F32)
         + mm_t(own_ref[:nodes, :], dst_ref[layer])
@@ -409,7 +416,7 @@
 
 def out_body(layer, picks_ref, act_edges_ref, state_ref, msg_ref, act_ref, out_ref):
     nodes = state_ref.shape[0]
-    act_ref[...] = mm_t(picks_ref[:nodes, :], act_edges_ref[...]).astype(BF)
+    act_ref[...] = mm_t(picks_ref[by_target(picks_ref, nodes), :], act_edges_ref[...]).astype(BF)
     out_ref[...] = (state_ref[...].astype(F32) + mm(act_ref[...], msg_ref[layer])).astype(BF)
 
 
@@ -421,36 +428,22 @@
     send_ref[first : first + term.shape[0], :] = jnp.where(odd, low, high)
 
 
-def terms_body(
-    where_ref,
-    first_ref,
-    second_ref,
-    left_ref,
-    right_ref,
-    send0_ref,
-    send1_ref,
-    send2_ref,
-    send3_ref,
-    state_ref,
-    own_ref,
-    act_ref,
-    grad_ref,
-    keep_ref,
-    send_ref,
-):
-    nodes, width = state_ref.shape
-    state = state_ref[...]
-    src_term = t_mm(state, own_ref[nodes:, :])
+def terms_body(where_ref, *refs):
+    keep_ref, send_ref = refs[-2:]
     marks = (*pair_marks(where_ref), *side_marks(where_ref)[2:])
-    rims = (first_ref, second_ref, left_ref, right_ref)
-    sends = (send0_ref, send1_ref, send2_ref, send3_ref)
-    for rim_ref, sums_ref, present in zip(rims, sends, marks):
-        src_term += t_mm(rim_ref[...], sums_ref[...]) * present
-    put_halves(where_ref, 0, src_term, keep_ref, send_ref)
-    put_halves(where_ref, width, t_mm(state, own_ref[:nodes, :]), keep_ref, send_ref)
-    put_halves(
-        where_ref, 2 * width, t_mm(act_ref[...], grad_ref[...].astype(BF)), keep_ref, send_ref
-    )
+    for layer in range(len(refs) // 12):
+        held = refs[12 * layer : 12 * layer + 12]
+        rims, sends, (state_ref, own_ref, act_ref, grad_ref) = held[:4], held[4:8], held[8:]
+        nodes, width = state_ref.shape
+        first = 3 * width * layer
+        state = state_ref[...]
+        src_term = t_mm(state, own_ref[nodes:, :])
+        for rim_ref, sums_ref, present in zip(rims, sends, marks):
+            src_term += t_mm(rim_ref[...], sums_ref[...]) * present
+        put_halves(where_ref, first, src_term, keep_ref, send_ref)
+        put_halves(where_ref, first + width, t_mm(state, own_ref[:nodes, :]), keep_ref, send_ref)
+        msg_term = t_mm(act_ref[...], grad_ref[...].astype(BF))
+        put_halves(where_ref, first + 2 * width, msg_term, keep_ref, send_ref)
 
 
 def last_body(
@@ -619,9 +612,9 @@
     rim_shape = ((rim, width), BF)
     edge_shape = ((width, edges), BF)
     edge_wide = ((width, edges), F32)
-    full = pltpu.VMEM((width, ext), BF)
+    full = pltpu.VMEM((width, 2 * rim), BF)
     edge_buf = pltpu.VMEM((width, edges), BF)
-    table_buf = pltpu.VMEM((width, 2 * nodes), BF)
+    table_buf = pltpu.VMEM((width, 2 * nodes + 2 * rim), BF)
 
     bound = boundary_idx.reshape(rim // LANES, LANES)
     pooled, col_slope, slot_picks, state0, rim0 = call(
@@ -630,15 +623,9 @@
         [
             edge_buf,
             pltpu.VMEM((2, cols), F32),
-            pltpu.VMEM(enc_in.shape, BF),
-            pltpu.VMEM(enc_out.shape, BF),
-            pltpu.VMEM((nodes, width), BF),
-            pltpu.VMEM(bound.shape, jnp.int32),
             pltpu.VMEM((nodes, rim), BF),
-            pltpu.SemaphoreType.DMA((4,)),
         ],
         "encode",
-        far=range(1, 5),
     )(packed, enc_in, enc_out, node_static, bound)
 
     edge_lanes = (edges // LANES, LANES)
@@ -667,8 +654,8 @@
     )
 
     rims0 = from_neighbours(rim0)
-    (pre0,) = call(functools.partial(own_body, 0), [edge_wide], [table_buf], "own")(
-        state0, src_t, dst_t, picks
+    (pre0,) = call(functools.partial(own_body, 0), [edge_wide], [table_buf], "own", True)(
+        where, *rims0[2:], state0, src_t, dst_t, picks
     )
     slope0, act0, state1, rim1 = call(
         functools.partial(forward_body, 0),
@@ -676,47 +663,48 @@
         [full, edge_buf],
         "forward",
         True,
-    )(where, *rims0, pre0, edge_scale, picks, state0, src_t, msg_proj, rim_picks_t)
+    )(where, *rims0[:2], pre0, edge_scale, picks, state0, src_t, msg_proj, rim_picks_t)
 
     rims1 = from_neighbours(rim1)
     (back1,) = call(functools.partial(back_body, 1), [edge_wide], [], "back")(
         msg_proj, node_cotangent, edge_scale, picks
     )
-    (pre1,) = call(functools.partial(own_body, 1), [edge_wide], [table_buf], "own")(
-        state1, src_t, dst_t, picks
+    (pre1,) = call(functools.partial(own_body, 1), [edge_wide], [table_buf], "own", True)(
+        where, *rims1[2:], state1, src_t, dst_t, picks
     )
     act_edges1, grad_pre1, *sends1 = call(
-        functools.partial(turn_body, 1), [edge_shape, edge_shape] + [rim_shape] * 4, [full], "turn", True
-    )(where, *rims1, pre1, back1, edge_scale, picks, src_t)
-
+        functools.partial(turn_body, 1), [edge_shape, edge_shape] + [rim_shape] * 2, [full], "turn", True
+    )(where, *rims1[:2], pre1, back1, edge_scale, picks, src_t)
+
+    sends1 += call(dom_sums_body, [rim_shape] * 2, [], "sides")(picks, grad_pre1)
     returned1 = to_neighbours(sends1)
     own_shape = ((2 * nodes, width), BF)
-    halves = [((3 * width, width // 2), BF)] * 2
     own1, partial1 = call(functools.partial(sums_body, 1), [own_shape, node_wide], [], "sums")(
         picks, grad_pre1, node_cotangent, src_proj, dst_proj
     )
     act1, node_out = call(functools.partial(out_body, 1), [node_shape, node_shape], [], "out")(
         picks, act_edges1, state1, msg_proj
     )
-    keep1, send1 = call(terms_body, halves, [], "terms", True)(
-        where, *rims1, *sends1, state1, own1, act1, node_cotangent
-    )
-    partial1, keep1, send1 = lax.optimization_barrier((partial1, keep1, send1))
+    partial1, act1 = lax.optimization_barrier((partial1, act1))
     grad1, grad_pre0, *sends0 = call(
         functools.partial(backward_body, 1),
-        [node_wide, edge_shape] + [rim_shape] * 4,
+        [node_wide, edge_shape] + [rim_shape] * 2,
         [],
         "backward",
         True,
     )(where, *returned1, partial1, src_proj, rim_picks, msg_proj, slope0, picks)
 
+    sends0 += call(dom_sums_body, [rim_shape] * 2, [], "sides")(picks, grad_pre0)
     returned0 = to_neighbours(sends0)
     own0, partial0 = call(functools.partial(sums_body, 0), [own_shape, node_wide], [], "sums")(
         picks, grad_pre0, grad1, src_proj, dst_proj
     )
-    keep0, send0 = call(terms_body, halves, [], "terms", True)(
-        where, *rims0, *sends0, state0, own0, act0, grad1
-    )
+    keep, send = call(terms_body, [((2 * 3 * width, width // 2), BF)] * 2, [], "terms", True)(
+        where,
+        *(*rims1, *sends1, state1, own1, act1, node_cotangent),
+        *(*rims0, *sends0, state0, own0, act0, grad1),
+    )
+    send, *returned0 = lax.optimization_barrier((send, *returned0))
     hidden = enc_out.shape[0]
     keep_enc, send_enc = call(
         functools.partial(last_body, bucket),
@@ -730,10 +718,8 @@
     share = -(-total_rows // (16 * peers)) * 16
     rows = peers * share
     (merged,) = call(merge_body, [((rows, width // 2), BF)], [], "merge")(
-        keep1,
-        swapped(send1, "dom", 0),
-        keep0,
-        swapped(send0, "dom", 0),
+        keep,
+        swapped(send, "dom", 0),
         keep_enc,
         swapped(send_enc, "dom", 0),
     )

time: 123 us -> 121 us (0.984)
  starting transfers between devices: 19.1 us -> 17.8 us
    ppermute x8, waiting for transfers between devices: 2.85 us -> 5.73 us  [turned(): lax.ppermute(shard, axis, [(i, (i + by) % count) for i in range(count)])]
    ppermute x12 -> x11, waiting for transfers between devices: 5.34 us -> 2.88 us  [swapped(): return lax.ppermute(shard, axis, list(enumerate(partner)))]
    ppermute x12 -> x11, starting transfers between devices: 14.2 us -> 13.3 us  [swapped(): return lax.ppermute(shard, axis, list(enumerate(partner)))]
    pallas_call x18 -> x19, Pallas kernels: 31.2 us -> 31 us  [run(): pl.pallas_call(body, out_shape=tuple((jax.ShapeDtypeStruct(shape, dtype)...]
  transfers between devices with their start and end apart: 20 -> 19, of which waited for: 7 -> 7; matrix products, arithmetic and copies ran while one was open for 0% -> 0% of each run, Pallas kernels for 12% -> 14%
where the time goes in v6:
time: 121 us; the launch traced here: 120 us
  blocking collectives  61.8 us (51%)
  Pallas kernels  31 us (26%)
  starting transfers between devices  17.8 us (15%)
  waiting for transfers between devices  8.6 us (7%)
    all_to_all x3, blocking collectives, exchange(): return lax.all_to_all(shard, AXES, split_axis=0, concat_axis=0, tiled=True)  61.8 us
    pallas_call x19, Pallas kernels, run(): pl.pallas_call(body, out_shape=tuple((jax.ShapeDtypeStruct(shape, dtype)...  31 us
    ppermute x11, starting transfers between devices, swapped(): return lax.ppermute(shard, axis, list(enumerate(partner)))  13.3 us
    ppermute x8, waiting for transfers between devices, turned(): lax.ppermute(shard, axis, [(i, (i + by) % count) for i in range(count)])  5.73 us
    ppermute x8, starting transfers between devices, turned(): lax.ppermute(shard, axis, [(i, (i + by) % count) for i in range(count)])  4.54 us
    ppermute x11, waiting for transfers between devices, swapped(): return lax.ppermute(shard, axis, list(enumerate(partner)))  2.88 us
  transfers between devices with their start and end apart: 19, of which 7 were waited for; matrix products, arithmetic and copies ran while one was open for 0% of the time, Pallas kernels for 14%

profile of v6, /device:TPU:0, one launch (start us, length us, event | category | flops | bytes accessed | tf_op | source)
XLA Modules:
  0.0 120.4 jit_solution(7505238808465850666)
XLA Ops:
  0.7 0.1 stack.15.where_ref
  0.8 1.7 %pack.1 = bf16[32,68,128]{2,1,0:T(8,128)(2,1)S(1)} custom-call(s32[5]{0:T(128)S(1)} %stack.15.where_ref, bf16[32,64,128]{2,1,0:T(8,128)(2,1)} %bitcast.23, s32[16,128]{1,0:T(8,128)} %bitcast.24, s32[16,128]{1,0:T(8,128)} %bitcast.25, f32[16,128]{1,0:T(8,128)} %bitcast.26), custom_call_target="tpu_custom_call" | custom-call | tf_op jit(solution)/shard_map/pack/pallas_call | solution.py:58
  2.5 23.9 %all_to_all.15.packed_ref = bf16[32,68,128]{2,1,0:T(8,128)(2,1)S(1)} all-to-all(bf16[32,68,128]{2,1,0:T(8,128)(2,1)S(1)} %pack.1), channel_id=1, replica_groups=mesh['grid'=4,'dom'=8] {'grid','dom'}, dimensions={0} | all-to-all | bytes 1114112 | tf_op jit(solution)/shard_map/all_to_all | solution.py:527
  26.5 0.0 copy-done.5
  26.5 2.1 %encode.1 = (bf16[512,256]{1,0:T(8,128)(2,1)S(1)}, bf16[256,2048]{1,0:T(8,128)(2,1)S(1)}, bf16[512,2048]{1,0:T(8,128)(2,1)S(1)}, bf16[512,256]{1,0:T(8,128)(2,1)S(1)}, bf16[256,256]{1,0:T(8,128)(2,1)S(1)}) custom-call(bf16[32,68,128]{2,1,0:T(8,128)(2,1)S(1)} %all_to_all.15.packed_ref, bf16[128,256]{1,0:T(8,128)(2,1)S(1)} %copy-done.6, ...), custom_call_target="tpu_custom_call" | custom-call | tf_op jit(solution)/shard_map/encode/pallas_call | solution.py:58
  28.5 1.2 %collective-permute-start.3 = (bf16[256,256]{1,0:T(8,128)(2,1)S(1)}, bf16[256,256]{1,0:T(8,128)(2,1)S(1)}, u32[]{:S(2)}, u32[]{:S(2)}) collective-permute-start(bf16[256,256]{1,0:T(8,128)(2,1)S(1)} %get-tuple-element.60), channel_id=1, source_target_pairs={{0,7},{1,0},{2,1},{3,2},{4,3},{5,4},{6,5},{7,6},{8,15},{9,8},{10,9... | collective-permute-start | bytes 393224 | tf_op jit(solution)/shard_map/ppermute | solution.py:532
  29.8 0.0 collective-permute-start.2
  29.8 0.7 collective-permute-start.1
  30.4 2.3 %collective-permute-start = (bf16[256,256]{1,0:T(8,128)(2,1)S(1)}, bf16[256,256]{1,0:T(8,128)(2,1)S(1)}, u32[]{:S(2)}, u32[]{:S(2)}) collective-permute-start(bf16[256,256]{1,0:T(8,128)(2,1)S(1)} %get-tuple-element.60), channel_id=1, source_target_pairs={{0,8},{8,0},{16,24},{24,16},{1,9},{9,1},{17,25},{25,17},{2,10},{10... | collective-permute-start | bytes 393224 | tf_op jit(solution)/shard_map/ppermute | solution.py:540
  32.7 0.0 copy-done
  32.8 1.2 picks.1
  33.9 0.0 collective-permute-done.3.right_ref.refs_15_
  33.9 1.1 collective-permute-done.2.left_ref.refs_14_
  35.1 2.6 %own.2.own_pre_ref = f32[256,2048]{1,0:T(8,128)S(1)} custom-call(s32[5]{0:T(128)S(1)} %stack.15.where_ref, bf16[256,256]{1,0:T(8,128)(2,1)S(1)} %collective-permute-done.2.left_ref.refs_14_, bf16[256,256]{1,0:T(8,128)(2,1)S(1)} %collective-permute-done.3.right_ref.refs_15_, bf16[512,256]{1,0:T(8,128)(2,1)S(1)} %get-tuple-element.61.state_ref.refs_20_, ...), custom_call_target="tpu_custom_call" | custom-call | tf_op jit(solution)/shard_map/own/pallas_call | solution.py:58
  37.6 0.0 collective-permute-done.1.second_ref.refs_13_
  37.7 0.0 collective-permute-done.first_ref.refs_12_
  37.7 0.0 copy-start.2
  37.7 2.9 %forward.1 = (bf16[256,2048]{1,0:T(8,128)(2,1)S(1)}, bf16[512,256]{1,0:T(8,128)(2,1)S(1)}, bf16[512,256]{1,0:T(8,128)(2,1)S(1)}, bf16[256,256]{1,0:T(8,128)(2,1)S(1)}) custom-call(s32[5]{0:T(128)S(1)} %stack.15.where_ref, bf16[256,256]{1,0:T(8,128)(2,1)S(1)} %collective-permute-done.first_ref.refs_12_, ...), custom_call_target="tpu_custom_call" | custom-call | tf_op jit(solution)/shard_map/forward/pallas_call | solution.py:58
  40.6 1.3 %collective-permute-start.7 = (bf16[256,256]{1,0:T(8,128)(2,1)S(1)}, bf16[256,256]{1,0:T(8,128)(2,1)S(1)}, u32[]{:S(2)}, u32[]{:S(2)}) collective-permute-start(bf16[256,256]{1,0:T(8,128)(2,1)S(1)} %get-tuple-element.66), channel_id=1, source_target_pairs={{0,7},{1,0},{2,1},{3,2},{4,3},{5,4},{6,5},{7,6},{8,15},{9,8},{10,9... | collective-permute-start | bytes 393224 | tf_op jit(solution)/shard_map/ppermute | solution.py:532
  42.0 0.0 collective-permute-start.6
  42.0 0.7 collective-permute-start.5
  42.6 3.4 %collective-permute-start.4 = (bf16[256,256]{1,0:T(8,128)(2,1)S(1)}, bf16[256,256]{1,0:T(8,128)(2,1)S(1)}, u32[]{:S(2)}, u32[]{:S(2)}) collective-permute-start(bf16[256,256]{1,0:T(8,128)(2,1)S(1)} %get-tuple-element.66), channel_id=1, source_target_pairs={{0,8},{8,0},{16,24},{24,16},{1,9},{9,1},{17,25},{25,17},{2,10},{10... | collective-permute-start | bytes 393224 | tf_op jit(solution)/shard_map/ppermute | solution.py:540
  46.1 0.9 back.1.back_ref
  47.0 0.0 collective-permute-done.7.right_ref.refs_3_
  47.0 0.3 collective-permute-done.6.left_ref.refs_2_
  47.3 2.6 %own.3.own_pre_ref = f32[256,2048]{1,0:T(8,128)S(1)} custom-call(s32[5]{0:T(128)S(1)} %stack.15.where_ref, bf16[256,256]{1,0:T(8,128)(2,1)S(1)} %collective-permute-done.6.left_ref.refs_2_, bf16[256,256]{1,0:T(8,128)(2,1)S(1)} %collective-permute-done.7.right_ref.refs_3_, bf16[512,256]{1,0:T(8,128)(2,1)S(1)} %get-tuple-element.67.state_ref.refs_8_, ...), custom_call_target="tpu_custom_call" | custom-call | tf_op jit(solution)/shard_map/own/pallas_call | solution.py:58
  49.9 0.0 collective-permute-done.5.second_ref.refs_1_
  49.9 0.0 collective-permute-done.4.first_ref.refs_0_
  49.9 2.7 %turn.1 = (bf16[256,2048]{1,0:T(8,128)(2,1)S(1)}, bf16[256,2048]{1,0:T(8,128)(2,1)S(1)}, bf16[256,256]{1,0:T(8,128)(2,1)S(1)}, bf16[256,256]{1,0:T(8,128)(2,1)S(1)}) custom-call(s32[5]{0:T(128)S(1)} %stack.15.where_ref, bf16[256,256]{1,0:T(8,128)(2,1)S(1)} %collective-permute-done.4.first_ref.refs_0_, ...), custom_call_target="tpu_custom_call" | custom-call | tf_op jit(solution)/shard_map/turn/pallas_call | solution.py:58
  52.6 1.6 %collective-permute-start.8 = (bf16[256,256]{1,0:T(8,128)(2,1)S(1)}, bf16[256,256]{1,0:T(8,128)(2,1)S(1)}, u32[]{:S(2)}, u32[]{:S(2)}) collective-permute-start(bf16[256,256]{1,0:T(8,128)(2,1)S(1)} %get-tuple-element.70.refs_4_), channel_id=1, source_target_pairs={{0,8},{8,0},{16,24},{24,16},{1,9},{9,1},{17,25},{25,17},{2,10},{10... | collective-permute-start | bytes 393224 | tf_op jit(solution)/shard_map/ppermute | solution.py:540
  54.1 0.8 collective-permute-start.9
  55.0 0.7 sides.2
  55.7 0.8 collective-permute-start.10
  56.5 0.0 collective-permute-start.11
  56.5 1.5 %sums.2 = (bf16[1024,256]{1,0:T(8,128)(2,1)S(1)}, f32[512,256]{1,0:T(8,128)S(1)}) custom-call(bf16[2048,2048]{1,0:T(8,128)(2,1)S(1)} %get-tuple-element.59.picks_ref, bf16[256,2048]{1,0:T(8,128)(2,1)S(1)} %get-tuple-element.72.grad_pre_ref, bf16[512,256]{1,0:T(8,128)(2,1)S(1)} %copy-done.2, bf16[2,256,256]{2,1,0:T(8,128)(2,1)S(1)} %copy-done, ...), custom_call_target="tpu_custom_call" | custom-call | tf_op jit(solution)/shard_map/sums/pallas_call | solution.py:58
  58.1 1.6 %out.1 = (bf16[512,256]{1,0:T(8,128)(2,1)S(1)}, bf16[512,256]{1,0:T(8,128)(2,1)}) custom-call(bf16[2048,2048]{1,0:T(8,128)(2,1)S(1)} %get-tuple-element.59.picks_ref, bf16[256,2048]{1,0:T(8,128)(2,1)S(1)} %get-tuple-element.68.act_edges_ref, bf16[512,256]{1,0:T(8,128)(2,1)S(1)} %get-tuple-element.67.state_ref.refs_8_, bf16[2,256,256]{2,1,0:T(8,128)(2,1)S(1)} %copy-done.1), custom_call_target="tpu_custom_call" | custom-call | tf_op jit(solution)/shard_map/out/pallas_call | solution.py:58
  59.7 0.0 collective-permute-done.8.first_ref
  59.7 0.0 collective-permute-done.9.second_ref
  59.7 0.0 collective-permute-done.10.left_ref
  59.7 2.1 %collective-permute-done.11.right_ref = bf16[256,256]{1,0:T(8,128)(2,1)S(1)} collective-permute-done((bf16[256,256]{1,0:T(8,128)(2,1)S(1)}, bf16[256,256]{1,0:T(8,128)(2,1)S(1)}, u32[]{:S(2)}, u32[]{:S(2)}) %collective-permute-start.11) | collective-permute-done | bytes 131104 | tf_op jit(solution)/shard_map/ppermute | solution.py:532
  61.8 2.3 %backward.1 = (f32[512,256]{1,0:T(8,128)S(1)}, bf16[256,2048]{1,0:T(8,128)(2,1)S(1)}, bf16[256,256]{1,0:T(8,128)(2,1)S(1)}, bf16[256,256]{1,0:T(8,128)(2,1)S(1)}) custom-call(s32[5]{0:T(128)S(1)} %stack.15.where_ref, bf16[256,256]{1,0:T(8,128)(2,1)S(1)} %collective-permute-done.8.first_ref, bf16[256,256]{1,0:T(8,128)(2,1)S(1)} %collective-permute-done.9.second_ref, ...), custom_call_target="tpu_custom_call" | custom-call | tf_op jit(solution)/shard_map/backward/pallas_call | solution.py:58
  64.2 2.6 %collective-permute-start.12 = (bf16[256,256]{1,0:T(8,128)(2,1)S(1)}, bf16[256,256]{1,0:T(8,128)(2,1)S(1)}, u32[]{:S(2)}, u32[]{:S(2)}) collective-permute-start(bf16[256,256]{1,0:T(8,128)(2,1)S(1)} %get-tuple-element.82.refs_16_), channel_id=1, source_target_pairs={{0,8},{8,0},{16,24},{24,16},{1,9},{9,1},{17,25},{25,17},{2,10},{10... | collective-permute-start | bytes 393224 | tf_op jit(solution)/shard_map/ppermute | solution.py:540
  66.8 0.7 collective-permute-start.13
  67.4 0.8 sides.3
  68.2 1.2 collective-permute-start.14
  69.4 0.0 collective-permute-start.15
  69.4 1.5 %sums.3 = (bf16[1024,256]{1,0:T(8,128)(2,1)S(1)}, f32[512,256]{1,0:T(8,128)S(1)}) custom-call(bf16[2048,2048]{1,0:T(8,128)(2,1)S(1)} %get-tuple-element.59.picks_ref, bf16[256,2048]{1,0:T(8,128)(2,1)S(1)} %get-tuple-element.84.grad_pre_ref, f32[512,256]{1,0:T(8,128)S(1)} %get-tuple-element.87.grad_ref.refs_23_, bf16[2,256,256]{2,1,0:T(8,128)(2,1)S(1)} %copy-done, ...), custom_call_target="tpu_custom_call" | custom-call | tf_op jit(solution)/shard_map/sums/pallas_call | solution.py:58
  70.9 1.5 %terms.1 = (bf16[1536,128]{1,0:T(8,128)(2,1)S(1)}, bf16[1536,128]{1,0:T(8,128)(2,1)S(1)}) custom-call(s32[5]{0:T(128)S(1)} %stack.15.where_ref, bf16[256,256]{1,0:T(8,128)(2,1)S(1)} %collective-permute-done.4.first_ref.refs_0_, bf16[256,256]{1,0:T(8,128)(2,1)S(1)} %collective-permute-done.5.second_ref.refs_1_, ...), custom_call_target="tpu_custom_call" | custom-call | tf_op jit(solution)/shard_map/terms/pallas_call | solution.py:58
  72.4 0.0 collective-permute-done.12.first_ref
  72.4 0.0 collective-permute-done.13.second_ref
  72.4 0.3 collective-permute-done.14.left_ref
  72.7 2.0 %collective-permute-done.15.right_ref = bf16[256,256]{1,0:T(8,128)(2,1)S(1)} collective-permute-done((bf16[256,256]{1,0:T(8,128)(2,1)S(1)}, bf16[256,256]{1,0:T(8,128)(2,1)S(1)}, u32[]{:S(2)}, u32[]{:S(2)}) %collective-permute-start.15) | collective-permute-done | bytes 131104 | tf_op jit(solution)/shard_map/ppermute | solution.py:532
  74.7 0.0 collective-permute-start.16
  74.7 2.4 %last.1 = (bf16[384,128]{1,0:T(8,128)(2,1)S(1)}, bf16[384,128]{1,0:T(8,128)(2,1)S(1)}) custom-call(s32[5]{0:T(128)S(1)} %stack.15.where_ref, bf16[256,256]{1,0:T(8,128)(2,1)S(1)} %collective-permute-done.12.first_ref, bf16[256,256]{1,0:T(8,128)(2,1)S(1)} %collective-permute-done.13.second_ref, bf16[256,256]{1,0:T(8,128)(2,1)S(1)} %collective-permute-done.14.left_ref, ...), custom_call_target="tpu_custom_call" | custom-call | tf_op jit(solution)/shard_map/last/pallas_call | solution.py:58
  77.0 0.6 collective-permute-start.17
  77.6 0.9 collective-permute-done.17.refs_3_
  78.6 0.0 collective-permute-done.16.refs_1_
  78.6 0.1 merge.1
  78.7 19.4 %all_to_all.16.parts_ref = bf16[32,64,128]{2,1,0:T(8,128)(2,1)S(1)} all-to-all(bf16[32,64,128]{2,1,0:T(8,128)(2,1)S(1)} %bitcast.14), channel_id=1, replica_groups=mesh['grid'=4,'dom'=8] {'grid','dom'}, dimensions={0} | all-to-all | bytes 1048576 | tf_op jit(solution)/shard_map/all_to_all | solution.py:527
  98.1 0.1 share.1
  98.2 18.4 %all_to_all.17 = bf16[32,64,128]{2,1,0:T(8,128)(2,1)S(1)} all-to-all(bf16[32,64,128]{2,1,0:T(8,128)(2,1)S(1)} %share.1), channel_id=1, replica_groups=mesh['grid'=4,'dom'=8] {'grid','dom'}, dimensions={0} | all-to-all | bytes 1048576 | tf_op jit(solution)/shard_map/all_to_all | solution.py:527
  116.6 0.0 collective-permute-start.18
  116.6 1.9 %collective-permute-done.18.other_ref = bf16[2048,128]{1,0:T(8,128)(2,1)S(1)} collective-permute-done((bf16[2048,128]{1,0:T(8,128)(2,1)S(1)}, bf16[2048,128]{1,0:T(8,128)(2,1)S(1)}, u32[]{:S(2)}, u32[]{:S(2)}) %collective-permute-start.18) | collective-permute-done | bytes 524320 | tf_op jit(solution)/shard_map/ppermute | solution.py:540
  118.5 1.9 %unpack.1 = (f32[128,256]{1,0:T(8,128)}, f32[256,256]{1,0:T(8,128)}, f32[2,256,256]{2,1,0:T(8,128)}, f32[2,256,256]{2,1,0:T(8,128)}, f32[2,256,256]{2,1,0:T(8,128)}) custom-call(s32[5]{0:T(128)S(1)} %stack.15.where_ref, bf16[2048,128]{1,0:T(8,128)(2,1)S(1)} %bitcast.16, bf16[2048,128]{1,0:T(8,128)(2,1)S(1)} %collective-permute-done.18.other_ref), custom_call_target="tpu_custom_call" | custom-call | tf_op jit(solution)/shard_map/unpack/pallas_call | solution.py:58
  (21 shorter events, 0.0 us)
Async XLA Ops:
  0.6 25.8 %copy-start.4 = (bf16[256,256]{1,0:T(8,128)(2,1)S(1)}, bf16[256,256]{1,0:T(8,128)(2,1)}, u32[]{:S(2)}) copy-start(bf16[256,256]{1,0:T(8,128)(2,1)} %enc_out_ref.3) | copy-start | bytes 393220
  0.6 25.8 %copy-start.6 = (bf16[128,256]{1,0:T(8,128)(2,1)S(1)}, bf16[128,256]{1,0:T(8,128)(2,1)}, u32[]{:S(2)}) copy-start(bf16[128,256]{1,0:T(8,128)(2,1)} %enc_in_ref.1) | copy-start | bytes 196612
  0.7 25.8 %copy-start.11 = (s32[256]{0:T(256)S(1)}, s32[256]{0:T(256)}, u32[]{:S(2)}) copy-start(s32[256]{0:T(256)} %param.21) | copy-start | bytes 3076
  0.7 25.8 %copy-start.5 = (bf16[512,256]{1,0:T(8,128)(2,1)S(1)}, bf16[512,256]{1,0:T(8,128)(2,1)}, u32[]{:S(2)}) copy-start(bf16[512,256]{1,0:T(8,128)(2,1)} %static_ref.1) | copy-start | bytes 786436
  0.7 32.0 %copy-start.8 = (s32[2048]{0:T(1024)S(1)}, s32[2048]{0:T(1024)}, u32[]{:S(2)}) copy-start(s32[2048]{0:T(1024)} %param.23) | copy-start | bytes 24580
  0.7 32.0 %copy-start = (bf16[2,256,256]{2,1,0:T(8,128)(2,1)S(1)}, bf16[2,256,256]{2,1,0:T(8,128)(2,1)}, u32[]{:S(2)}) copy-start(bf16[2,256,256]{2,1,0:T(8,128)(2,1)} %src_ref.7) | copy-start | bytes 786436
  0.7 32.0 %copy-start.3 = (bf16[2,256,256]{2,1,0:T(8,128)(2,1)S(1)}, bf16[2,256,256]{2,1,0:T(8,128)(2,1)}, u32[]{:S(2)}) copy-start(bf16[2,256,256]{2,1,0:T(8,128)(2,1)} %dst_ref.3) | copy-start | bytes 786436
  0.7 32.0 %copy-start.10 = (f32[2048]{0:T(1024)S(1)}, f32[2048]{0:T(1024)}, u32[]{:S(2)}) copy-start(f32[2048]{0:T(1024)} %param.25) | copy-start | bytes 24580
  0.7 32.0 %copy-start.9 = (s32[2048]{0:T(1024)S(1)}, s32[2048]{0:T(1024)}, u32[]{:S(2)}) copy-start(s32[2048]{0:T(1024)} %param.24) | copy-start | bytes 24580
  0.7 32.0 %copy-start.7 = (s32[2048]{0:T(1024)S(1)}, s32[2048]{0:T(1024)}, u32[]{:S(2)}) copy-start(s32[2048]{0:T(1024)} %param.22) | copy-start | bytes 24580
  28.5 5.4 %collective-permute-start.3 = (bf16[256,256]{1,0:T(8,128)(2,1)S(1)}, bf16[256,256]{1,0:T(8,128)(2,1)S(1)}, u32[]{:S(2)}, u32[]{:S(2)}) collective-permute-start(bf16[256,256]{1,0:T(8,128)(2,1)S(1)} %get-tuple-element.60), channel_id=1, source_target_pairs={{0,7},{1,0},{2,1},{3,2},{4,3},{5,4},{6,5},{7,6},{8,15},{9,8},{10,9... | collective-permute-start | bytes 393224 | tf_op jit(solution)/shard_map/ppermute | solution.py:532
  29.8 5.3 %collective-permute-start.2 = (bf16[256,256]{1,0:T(8,128)(2,1)S(1)}, bf16[256,256]{1,0:T(8,128)(2,1)S(1)}, u32[]{:S(2)}, u32[]{:S(2)}) collective-permute-start(bf16[256,256]{1,0:T(8,128)(2,1)S(1)} %get-tuple-element.60), channel_id=1, source_target_pairs={{0,1},{1,2},{2,3},{3,4},{4,5},{5,6},{6,7},{7,0},{8,9},{9,10},{10,1... | collective-permute-start | bytes 393224 | tf_op jit(solution)/shard_map/ppermute | solution.py:532
  29.8 7.9 %collective-permute-start.1 = (bf16[256,256]{1,0:T(8,128)(2,1)S(1)}, bf16[256,256]{1,0:T(8,128)(2,1)S(1)}, u32[]{:S(2)}, u32[]{:S(2)}) collective-permute-start(bf16[256,256]{1,0:T(8,128)(2,1)S(1)} %get-tuple-element.60), channel_id=1, source_target_pairs={{0,0},{8,16},{16,8},{24,24},{1,1},{9,17},{17,9},{25,25},{2,2},{10,... | collective-permute-start | bytes 393224 | tf_op jit(solution)/shard_map/ppermute | solution.py:540
  30.4 7.2 %collective-permute-start = (bf16[256,256]{1,0:T(8,128)(2,1)S(1)}, bf16[256,256]{1,0:T(8,128)(2,1)S(1)}, u32[]{:S(2)}, u32[]{:S(2)}) collective-permute-start(bf16[256,256]{1,0:T(8,128)(2,1)S(1)} %get-tuple-element.60), channel_id=1, source_target_pairs={{0,8},{8,0},{16,24},{24,16},{1,9},{9,1},{17,25},{25,17},{2,10},{10... | collective-permute-start | bytes 393224 | tf_op jit(solution)/shard_map/ppermute | solution.py:540
  35.0 2.6 %copy-start.1 = (bf16[2,256,256]{2,1,0:T(8,128)(2,1)S(1)}, bf16[2,256,256]{2,1,0:T(8,128)(2,1)}, u32[]{:S(2)}) copy-start(bf16[2,256,256]{2,1,0:T(8,128)(2,1)} %msg_ref.7) | copy-start | bytes 786436
  37.7 8.4 %copy-start.2 = (bf16[512,256]{1,0:T(8,128)(2,1)S(1)}, bf16[512,256]{1,0:T(8,128)(2,1)}, u32[]{:S(2)}) copy-start(bf16[512,256]{1,0:T(8,128)(2,1)} %refs_11_.1) | copy-start | bytes 786436
  40.6 6.3 %collective-permute-start.7 = (bf16[256,256]{1,0:T(8,128)(2,1)S(1)}, bf16[256,256]{1,0:T(8,128)(2,1)S(1)}, u32[]{:S(2)}, u32[]{:S(2)}) collective-permute-start(bf16[256,256]{1,0:T(8,128)(2,1)S(1)} %get-tuple-element.66), channel_id=1, source_target_pairs={{0,7},{1,0},{2,1},{3,2},{4,3},{5,4},{6,5},{7,6},{8,15},{9,8},{10,9... | collective-permute-start | bytes 393224 | tf_op jit(solution)/shard_map/ppermute | solution.py:532
  42.0 5.3 %collective-permute-start.6 = (bf16[256,256]{1,0:T(8,128)(2,1)S(1)}, bf16[256,256]{1,0:T(8,128)(2,1)S(1)}, u32[]{:S(2)}, u32[]{:S(2)}) collective-permute-start(bf16[256,256]{1,0:T(8,128)(2,1)S(1)} %get-tuple-element.66), channel_id=1, source_target_pairs={{0,1},{1,2},{2,3},{3,4},{4,5},{5,6},{6,7},{7,0},{8,9},{9,10},{10,1... | collective-permute-start | bytes 393224 | tf_op jit(solution)/shard_map/ppermute | solution.py:532
  42.0 7.9 %collective-permute-start.5 = (bf16[256,256]{1,0:T(8,128)(2,1)S(1)}, bf16[256,256]{1,0:T(8,128)(2,1)S(1)}, u32[]{:S(2)}, u32[]{:S(2)}) collective-permute-start(bf16[256,256]{1,0:T(8,128)(2,1)S(1)} %get-tuple-element.66), channel_id=1, source_target_pairs={{0,0},{8,16},{16,8},{24,24},{1,1},{9,17},{17,9},{25,25},{2,2},{10,... | collective-permute-start | bytes 393224 | tf_op jit(solution)/shard_map/ppermute | solution.py:540
  42.6 7.2 %collective-permute-start.4 = (bf16[256,256]{1,0:T(8,128)(2,1)S(1)}, bf16[256,256]{1,0:T(8,128)(2,1)S(1)}, u32[]{:S(2)}, u32[]{:S(2)}) collective-permute-start(bf16[256,256]{1,0:T(8,128)(2,1)S(1)} %get-tuple-element.66), channel_id=1, source_target_pairs={{0,8},{8,0},{16,24},{24,16},{1,9},{9,1},{17,25},{25,17},{2,10},{10... | collective-permute-start | bytes 393224 | tf_op jit(solution)/shard_map/ppermute | solution.py:540
  52.6 7.2 %collective-permute-start.8 = (bf16[256,256]{1,0:T(8,128)(2,1)S(1)}, bf16[256,256]{1,0:T(8,128)(2,1)S(1)}, u32[]{:S(2)}, u32[]{:S(2)}) collective-permute-start(bf16[256,256]{1,0:T(8,128)(2,1)S(1)} %get-tuple-element.70.refs_4_), channel_id=1, source_target_pairs={{0,8},{8,0},{16,24},{24,16},{1,9},{9,1},{17,25},{25,17},{2,10},{10... | collective-permute-start | bytes 393224 | tf_op jit(solution)/shard_map/ppermute | solution.py:540
  54.1 5.6 %collective-permute-start.9 = (bf16[256,256]{1,0:T(8,128)(2,1)S(1)}, bf16[256,256]{1,0:T(8,128)(2,1)S(1)}, u32[]{:S(2)}, u32[]{:S(2)}) collective-permute-start(bf16[256,256]{1,0:T(8,128)(2,1)S(1)} %get-tuple-element.71.refs_5_), channel_id=1, source_target_pairs={{0,0},{8,16},{16,8},{24,24},{1,1},{9,17},{17,9},{25,25},{2,2},{10,... | collective-permute-start | bytes 393224 | tf_op jit(solution)/shard_map/ppermute | solution.py:540
  55.7 4.0 %collective-permute-start.10 = (bf16[256,256]{1,0:T(8,128)(2,1)S(1)}, bf16[256,256]{1,0:T(8,128)(2,1)S(1)}, u32[]{:S(2)}, u32[]{:S(2)}) collective-permute-start(bf16[256,256]{1,0:T(8,128)(2,1)S(1)} %get-tuple-element.73.refs_6_), channel_id=1, source_target_pairs={{0,7},{1,0},{2,1},{3,2},{4,3},{5,4},{6,5},{7,6},{8,15},{9,8},{10,9... | collective-permute-start | bytes 393224 | tf_op jit(solution)/shard_map/ppermute | solution.py:532
  56.5 5.3 %collective-permute-start.11 = (bf16[256,256]{1,0:T(8,128)(2,1)S(1)}, bf16[256,256]{1,0:T(8,128)(2,1)S(1)}, u32[]{:S(2)}, u32[]{:S(2)}) collective-permute-start(bf16[256,256]{1,0:T(8,128)(2,1)S(1)} %get-tuple-element.74.refs_7_), channel_id=1, source_target_pairs={{0,1},{1,2},{2,3},{3,4},{4,5},{5,6},{6,7},{7,0},{8,9},{9,10},{10,1... | collective-permute-start | bytes 393224 | tf_op jit(solution)/shard_map/ppermute | solution.py:532
  64.2 8.2 %collective-permute-start.12 = (bf16[256,256]{1,0:T(8,128)(2,1)S(1)}, bf16[256,256]{1,0:T(8,128)(2,1)S(1)}, u32[]{:S(2)}, u32[]{:S(2)}) collective-permute-start(bf16[256,256]{1,0:T(8,128)(2,1)S(1)} %get-tuple-element.82.refs_16_), channel_id=1, source_target_pairs={{0,8},{8,0},{16,24},{24,16},{1,9},{9,1},{17,25},{25,17},{2,10},{10... | collective-permute-start | bytes 393224 | tf_op jit(solution)/shard_map/ppermute | solution.py:540
  66.8 5.6 %collective-permute-start.13 = (bf16[256,256]{1,0:T(8,128)(2,1)S(1)}, bf16[256,256]{1,0:T(8,128)(2,1)S(1)}, u32[]{:S(2)}, u32[]{:S(2)}) collective-permute-start(bf16[256,256]{1,0:T(8,128)(2,1)S(1)} %get-tuple-element.83.refs_17_), channel_id=1, source_target_pairs={{0,0},{8,16},{16,8},{24,24},{1,1},{9,17},{17,9},{25,25},{2,2},{10,... | collective-permute-start | bytes 393224 | tf_op jit(solution)/shard_map/ppermute | solution.py:540
  68.2 4.5 %collective-permute-start.14 = (bf16[256,256]{1,0:T(8,128)(2,1)S(1)}, bf16[256,256]{1,0:T(8,128)(2,1)S(1)}, u32[]{:S(2)}, u32[]{:S(2)}) collective-permute-start(bf16[256,256]{1,0:T(8,128)(2,1)S(1)} %get-tuple-element.85.refs_18_), channel_id=1, source_target_pairs={{0,7},{1,0},{2,1},{3,2},{4,3},{5,4},{6,5},{7,6},{8,15},{9,8},{10,9... | collective-permute-start | bytes 393224 | tf_op jit(solution)/shard_map/ppermute | solution.py:532
  69.4 5.3 %collective-permute-start.15 = (bf16[256,256]{1,0:T(8,128)(2,1)S(1)}, bf16[256,256]{1,0:T(8,128)(2,1)S(1)}, u32[]{:S(2)}, u32[]{:S(2)}) collective-permute-start(bf16[256,256]{1,0:T(8,128)(2,1)S(1)} %get-tuple-element.86.refs_19_), channel_id=1, source_target_pairs={{0,1},{1,2},{2,3},{3,4},{4,5},{5,6},{6,7},{7,0},{8,9},{9,10},{10,1... | collective-permute-start | bytes 393224 | tf_op jit(solution)/shard_map/ppermute | solution.py:532
  74.7 3.9 %collective-permute-start.16 = (bf16[1536,128]{1,0:T(8,128)(2,1)S(1)}, bf16[1536,128]{1,0:T(8,128)(2,1)S(1)}, u32[]{:S(2)}, u32[]{:S(2)}) collective-permute-start(bf16[1536,128]{1,0:T(8,128)(2,1)S(1)} %get-tuple-element.92), channel_id=1, source_target_pairs={{0,1},{1,0},{2,3},{3,2},{4,5},{5,4},{6,7},{7,6},{8,9},{9,8},{10,11... | collective-permute-start | bytes 1179656 | tf_op jit(solution)/shard_map/ppermute | solution.py:540
  77.0 1.5 %collective-permute-start.17 = (bf16[384,128]{1,0:T(8,128)(2,1)S(1)}, bf16[384,128]{1,0:T(8,128)(2,1)S(1)}, u32[]{:S(2)}, u32[]{:S(2)}) collective-permute-start(bf16[384,128]{1,0:T(8,128)(2,1)S(1)} %get-tuple-element.102), channel_id=1, source_target_pairs={{0,1},{1,0},{2,3},{3,2},{4,5},{5,4},{6,7},{7,6},{8,9},{9,8},{10,11... | collective-permute-start | bytes 294920 | tf_op jit(solution)/shard_map/ppermute | solution.py:540
  116.6 1.9 %collective-permute-start.18 = (bf16[2048,128]{1,0:T(8,128)(2,1)S(1)}, bf16[2048,128]{1,0:T(8,128)(2,1)S(1)}, u32[]{:S(2)}, u32[]{:S(2)}) collective-permute-start(bf16[2048,128]{1,0:T(8,128)(2,1)S(1)} %bitcast.15), channel_id=1, source_target_pairs={{0,1},{1,0},{2,3},{3,2},{4,5},{5,4},{6,7},{7,6},{8,9},{9,8},{10,11... | collective-permute-start | bytes 1572872 | tf_op jit(solution)/shard_map/ppermute | solution.py:540

commit v7 on v6

--- a/solution.py
+++ b/solution.py
@@ -233,8 +233,9 @@
         pre = mm_t(enc_in_t, got)
         scale = rows_ref[1:2, at]
         sig = sigmoid(pre)
-        act_ref[:, at] = (pre * sig * scale).astype(BF)
-        slope_ref[:, at] = (sig * (1.0 + pre * (1.0 - sig)) * scale).astype(BF)
+        act = pre * sig
+        act_ref[:, at] = (act * scale).astype(BF)
+        slope_ref[:, at] = (sig + act * (1.0 - sig)) * scale
         put_picks(picks_ref.at[:, at], 0, rows_ref[0:1, at], nodes)
 
     chunks(rows_ref.shape[1], step)
@@ -303,8 +304,9 @@
         pre = own_pre_ref[:, at] + mm(full_ref[...], picks_ref[sides, at])
         scale = scale_ref[:, at]
         sig = sigmoid(pre)
-        act_ref[:, at] = (pre * sig * scale).astype(BF)
-        slope_ref[:, at] = (sig * (1.0 + pre * (1.0 - sig)) * scale).astype(BF)
+        act = pre * sig
+        act_ref[:, at] = (act * scale).astype(BF)
+        slope_ref[:, at] = (sig + act * (1.0 - sig)) * scale
 
     chunks(scale_ref.shape[1], step)
     node_act_ref[...] = mm_t(picks_ref[by_target(picks_ref, nodes), :], act_ref[...]).astype(BF)
@@ -312,12 +314,12 @@
     put_state(state, next_state_ref, rim_ref, rim_picks_t)
 
 
-def put_grid_sends(where_ref, sums, first_ref, second_ref):
-    rim = sums.shape[0] // 2
-    up, down = sums[:rim, :].astype(BF), sums[rim:, :].astype(BF)
-    odd = is_odd(where_ref[GRID_AT])
-    first_ref[...] = jnp.where(odd, up, down)
-    second_ref[...] = jnp.where(odd, down, up)
+def put_sums(odd, picks_ref, start, grad_pre_ref, first_ref, second_ref):
+    rim = first_ref.shape[0]
+    first = pl.multiple_of(start + jnp.where(odd, 0, rim), rim)
+    second = pl.multiple_of(start + jnp.where(odd, rim, 0), rim)
+    first_ref[...] = mm_t(picks_ref[pl.ds(first, rim), :], grad_pre_ref[...]).astype(BF)
+    second_ref[...] = mm_t(picks_ref[pl.ds(second, rim), :], grad_pre_ref[...]).astype(BF)
 
 
 def dom_sums_body(picks_ref, grad_pre_ref, left_ref, right_ref):
@@ -351,12 +353,12 @@
     def step(start, at):
         pre = own_pre_ref[:, at] + mm(full_ref[...], picks_ref[sides, at])
         sig = sigmoid(pre)
-        act_ref[:, at] = (pre * sig * scale_ref[:, at]).astype(BF)
-        grad_pre_ref[:, at] = (back_ref[:, at] * (sig * (1.0 + pre * (1.0 - sig)))).astype(BF)
+        act = pre * sig
+        act_ref[:, at] = (act * scale_ref[:, at]).astype(BF)
+        grad_pre_ref[:, at] = (back_ref[:, at] * (sig + act * (1.0 - sig))).astype(BF)
 
     chunks(scale_ref.shape[1], step)
-    sums = mm_t(picks_ref[sides, :], grad_pre_ref[...])
-    put_grid_sends(where_ref, sums, send0_ref, send1_ref)
+    put_sums(is_odd(where_ref[GRID_AT]), picks_ref, 0, grad_pre_ref, send0_ref, send1_ref)
 
 
 def merged_grad(partial_ref, where_ref, returned, src_ref, rim_picks):
@@ -394,13 +396,11 @@
     back = mm_t(msg_ref[layer - 1], grad.astype(BF)).astype(BF)
 
     def step(start, at):
-        grad_pre = mm(back, picks_ref[by_target(picks_ref, nodes), at]) * slope_ref[:, at].astype(F32)
+        grad_pre = mm(back, picks_ref[by_target(picks_ref, nodes), at]) * slope_ref[:, at]
         grad_pre_ref[:, at] = grad_pre.astype(BF)
 
     chunks(picks_ref.shape[1], step)
-    sides = pl.ds(0, 2 * first_ref.shape[0])
-    sums = mm_t(picks_ref[sides, :], grad_pre_ref[...])
-    put_grid_sends(where_ref, sums, send0_ref, send1_ref)
+    put_sums(is_odd(where_ref[GRID_AT]), picks_ref, 0, grad_pre_ref, send0_ref, send1_ref)
 
 
 def sums_body(layer, picks_ref, grad_pre_ref, grad_ref, src_ref, dst_ref, own_ref, partial_ref):
@@ -423,9 +423,9 @@
 def put_halves(where_ref, first, term, keep_ref, send_ref):
     half = term.shape[1] // 2
     odd = is_odd(where_ref[DOM_AT])
-    low, high = term[:, :half].astype(BF), term[:, half:].astype(BF)
+    low, high = term[:, :half], term[:, half:]
     keep_ref[first : first + term.shape[0], :] = jnp.where(odd, high, low)
-    send_ref[first : first + term.shape[0], :] = jnp.where(odd, low, high)
+    send_ref[first : first + term.shape[0], :] = jnp.where(odd, low, high).astype(BF)
 
 
 def terms_body(where_ref, *refs):
@@ -474,7 +474,7 @@
         at = pl.ds(start, CHUNK)
         first = start // bucket
         got = packed_ref[first : first + peers_step, :bucket, :].reshape(CHUNK, fin)
-        grad_pre = mm(back, picks_ref[:, at]) * slope_ref[:, at].astype(F32)
+        grad_pre = mm(back, picks_ref[:, at]) * slope_ref[:, at]
         in_term += mm(grad_pre.astype(BF), got)
     put_halves(where_ref, 0, in_term.T, keep_ref, send_ref)
     put_halves(where_ref, fin, t_mm(pooled_ref[...], grad), keep_ref, send_ref)
@@ -485,7 +485,7 @@
     first = 0
     for keep_ref, got_ref in zip(refs[:-1:2], refs[1:-1:2]):
         rows = keep_ref.shape[0]
-        total = keep_ref[...].astype(F32) + got_ref[...].astype(F32)
+        total = keep_ref[...] + got_ref[...].astype(F32)
         out_ref[first : first + rows, :] = total.astype(BF)
         first += rows
     if first < out_ref.shape[0]:
@@ -619,7 +619,7 @@
     bound = boundary_idx.reshape(rim // LANES, LANES)
     pooled, col_slope, slot_picks, state0, rim0 = call(
         functools.partial(encode_body, bucket),
-        [node_shape, ((width, cols), BF), ((nodes, cols), BF), node_shape, rim_shape],
+        [node_shape, ((width, cols), F32), ((nodes, cols), BF), node_shape, rim_shape],
         [
             edge_buf,
             pltpu.VMEM((2, cols), F32),
@@ -659,7 +659,7 @@
     )
     slope0, act0, state1, rim1 = call(
         functools.partial(forward_body, 0),
-        [edge_shape, node_shape, node_shape, rim_shape],
+        [edge_wide, node_shape, node_shape, rim_shape],
         [full, edge_buf],
         "forward",
         True,
@@ -699,7 +699,13 @@
     own0, partial0 = call(functools.partial(sums_body, 0), [own_shape, node_wide], [], "sums")(
         picks, grad_pre0, grad1, src_proj, dst_proj
     )
-    keep, send = call(terms_body, [((2 * 3 * width, width // 2), BF)] * 2, [], "terms", True)(
+    keep, send = call(
+        terms_body,
+        [((2 * 3 * width, width // 2), dtype) for dtype in (F32, BF)],
+        [],
+        "terms",
+        True,
+    )(
         where,
         *(*rims1, *sends1, state1, own1, act1, node_cotangent),
         *(*rims0, *sends0, state0, own0, act0, grad1),
@@ -708,7 +714,7 @@
     hidden = enc_out.shape[0]
     keep_enc, send_enc = call(
         functools.partial(last_body, bucket),
-        [((fin + hidden, width // 2), BF)] * 2,
+        [((fin + hidden, width // 2), dtype) for dtype in (F32, BF)],
         [],
         "last",
         True,

time: 121 us -> 120 us (level)
  no operation moved by 1% of the time
where the time goes in v7:
time: 120 us
  blocking collectives  61.8 us (52%)
  Pallas kernels  30.8 us (26%)
  starting transfers between devices  17.8 us (15%)
  waiting for transfers between devices  8.62 us (7%)
    all_to_all x3, blocking collectives, exchange(): return lax.all_to_all(shard, AXES, split_axis=0, concat_axis=0, tiled=True)  61.8 us
    pallas_call x19, Pallas kernels, run(): pl.pallas_call(body, out_shape=tuple((jax.ShapeDtypeStruct(shape, dtype)...  30.8 us
    ppermute x11, starting transfers between devices, swapped(): return lax.ppermute(shard, axis, list(enumerate(partner)))  13.1 us
    ppermute x8, waiting for transfers between devices, turned(): lax.ppermute(shard, axis, [(i, (i + by) % count) for i in range(count)])  5.74 us
    ppermute x8, starting transfers between devices, turned(): lax.ppermute(shard, axis, [(i, (i + by) % count) for i in range(count)])  4.73 us
    ppermute x11, waiting for transfers between devices, swapped(): return lax.ppermute(shard, axis, list(enumerate(partner)))  2.88 us
  transfers between devices with their start and end apart: 19, of which 7 were waited for; matrix products, arithmetic and copies ran while one was open for 0% of the time, Pallas kernels for 14%

profile of v7, /device:TPU:0, one launch (start us, length us, event | category | flops | bytes accessed | tf_op | source)
XLA Modules:
  0.0 120.1 jit_solution(17060318582213515010)
XLA Ops:
  0.7 0.1 stack.15.where_ref
  0.8 1.7 %pack.1 = bf16[32,68,128]{2,1,0:T(8,128)(2,1)S(1)} custom-call(s32[5]{0:T(128)S(1)} %stack.15.where_ref, bf16[32,64,128]{2,1,0:T(8,128)(2,1)} %bitcast.23, s32[16,128]{1,0:T(8,128)} %bitcast.24, s32[16,128]{1,0:T(8,128)} %bitcast.25, f32[16,128]{1,0:T(8,128)} %bitcast.26), custom_call_target="tpu_custom_call" | custom-call | tf_op jit(solution)/shard_map/pack/pallas_call | solution.py:58
  2.5 23.9 %all_to_all.15.packed_ref = bf16[32,68,128]{2,1,0:T(8,128)(2,1)S(1)} all-to-all(bf16[32,68,128]{2,1,0:T(8,128)(2,1)S(1)} %pack.1), channel_id=1, replica_groups=mesh['grid'=4,'dom'=8] {'grid','dom'}, dimensions={0} | all-to-all | bytes 1114112 | tf_op jit(solution)/shard_map/all_to_all | solution.py:527
  26.5 0.0 copy-done.5
  26.5 2.0 %encode.1 = (bf16[512,256]{1,0:T(8,128)(2,1)S(1)}, f32[256,2048]{1,0:T(8,128)S(1)}, bf16[512,2048]{1,0:T(8,128)(2,1)S(1)}, bf16[512,256]{1,0:T(8,128)(2,1)S(1)}, bf16[256,256]{1,0:T(8,128)(2,1)S(1)}) custom-call(bf16[32,68,128]{2,1,0:T(8,128)(2,1)S(1)} %all_to_all.15.packed_ref, bf16[128,256]{1,0:T(8,128)(2,1)S(1)} %copy-done.6, ...), custom_call_target="tpu_custom_call" | custom-call | tf_op jit(solution)/shard_map/encode/pallas_call | solution.py:58
  28.4 1.2 %collective-permute-start.3 = (bf16[256,256]{1,0:T(8,128)(2,1)S(1)}, bf16[256,256]{1,0:T(8,128)(2,1)S(1)}, u32[]{:S(2)}, u32[]{:S(2)}) collective-permute-start(bf16[256,256]{1,0:T(8,128)(2,1)S(1)} %get-tuple-element.60), channel_id=1, source_target_pairs={{0,7},{1,0},{2,1},{3,2},{4,3},{5,4},{6,5},{7,6},{8,15},{9,8},{10,9... | collective-permute-start | bytes 393224 | tf_op jit(solution)/shard_map/ppermute | solution.py:532
  29.7 0.0 collective-permute-start.2
  29.7 0.7 collective-permute-start.1
  30.3 2.3 %collective-permute-start = (bf16[256,256]{1,0:T(8,128)(2,1)S(1)}, bf16[256,256]{1,0:T(8,128)(2,1)S(1)}, u32[]{:S(2)}, u32[]{:S(2)}) collective-permute-start(bf16[256,256]{1,0:T(8,128)(2,1)S(1)} %get-tuple-element.60), channel_id=1, source_target_pairs={{0,8},{8,0},{16,24},{24,16},{1,9},{9,1},{17,25},{25,17},{2,10},{10... | collective-permute-start | bytes 393224 | tf_op jit(solution)/shard_map/ppermute | solution.py:540
  32.6 0.0 copy-done
  32.6 1.2 picks.1
  33.8 0.0 collective-permute-done.3.right_ref.refs_15_
  33.8 1.1 collective-permute-done.2.left_ref.refs_14_
  35.0 2.6 %own.2.own_pre_ref = f32[256,2048]{1,0:T(8,128)S(1)} custom-call(s32[5]{0:T(128)S(1)} %stack.15.where_ref, bf16[256,256]{1,0:T(8,128)(2,1)S(1)} %collective-permute-done.2.left_ref.refs_14_, bf16[256,256]{1,0:T(8,128)(2,1)S(1)} %collective-permute-done.3.right_ref.refs_15_, bf16[512,256]{1,0:T(8,128)(2,1)S(1)} %get-tuple-element.61.state_ref.refs_20_, ...), custom_call_target="tpu_custom_call" | custom-call | tf_op jit(solution)/shard_map/own/pallas_call | solution.py:58
  37.5 0.0 collective-permute-done.1.second_ref.refs_13_
  37.6 0.0 collective-permute-done.first_ref.refs_12_
  37.6 0.0 copy-start.2
  37.6 2.8 %forward.1 = (f32[256,2048]{1,0:T(8,128)S(1)}, bf16[512,256]{1,0:T(8,128)(2,1)S(1)}, bf16[512,256]{1,0:T(8,128)(2,1)S(1)}, bf16[256,256]{1,0:T(8,128)(2,1)S(1)}) custom-call(s32[5]{0:T(128)S(1)} %stack.15.where_ref, bf16[256,256]{1,0:T(8,128)(2,1)S(1)} %collective-permute-done.first_ref.refs_12_, ...), custom_call_target="tpu_custom_call" | custom-call | tf_op jit(solution)/shard_map/forward/pallas_call | solution.py:58
  40.4 1.3 %collective-permute-start.7 = (bf16[256,256]{1,0:T(8,128)(2,1)S(1)}, bf16[256,256]{1,0:T(8,128)(2,1)S(1)}, u32[]{:S(2)}, u32[]{:S(2)}) collective-permute-start(bf16[256,256]{1,0:T(8,128)(2,1)S(1)} %get-tuple-element.66), channel_id=1, source_target_pairs={{0,7},{1,0},{2,1},{3,2},{4,3},{5,4},{6,5},{7,6},{8,15},{9,8},{10,9... | collective-permute-start | bytes 393224 | tf_op jit(solution)/shard_map/ppermute | solution.py:532
  41.8 0.0 collective-permute-start.6
  41.8 0.7 collective-permute-start.5
  42.4 3.4 %collective-permute-start.4 = (bf16[256,256]{1,0:T(8,128)(2,1)S(1)}, bf16[256,256]{1,0:T(8,128)(2,1)S(1)}, u32[]{:S(2)}, u32[]{:S(2)}) collective-permute-start(bf16[256,256]{1,0:T(8,128)(2,1)S(1)} %get-tuple-element.66), channel_id=1, source_target_pairs={{0,8},{8,0},{16,24},{24,16},{1,9},{9,1},{17,25},{25,17},{2,10},{10... | collective-permute-start | bytes 393224 | tf_op jit(solution)/shard_map/ppermute | solution.py:540
  45.9 0.9 back.1.back_ref
  46.8 0.0 collective-permute-done.7.right_ref.refs_3_
  46.8 0.3 collective-permute-done.6.left_ref.refs_2_
  47.1 2.6 %own.3.own_pre_ref = f32[256,2048]{1,0:T(8,128)S(1)} custom-call(s32[5]{0:T(128)S(1)} %stack.15.where_ref, bf16[256,256]{1,0:T(8,128)(2,1)S(1)} %collective-permute-done.6.left_ref.refs_2_, bf16[256,256]{1,0:T(8,128)(2,1)S(1)} %collective-permute-done.7.right_ref.refs_3_, bf16[512,256]{1,0:T(8,128)(2,1)S(1)} %get-tuple-element.67.state_ref.refs_8_, ...), custom_call_target="tpu_custom_call" | custom-call | tf_op jit(solution)/shard_map/own/pallas_call | solution.py:58
  49.7 0.0 collective-permute-done.5.second_ref.refs_1_
  49.7 0.0 collective-permute-done.4.first_ref.refs_0_
  49.7 2.6 %turn.1 = (bf16[256,2048]{1,0:T(8,128)(2,1)S(1)}, bf16[256,2048]{1,0:T(8,128)(2,1)S(1)}, bf16[256,256]{1,0:T(8,128)(2,1)S(1)}, bf16[256,256]{1,0:T(8,128)(2,1)S(1)}) custom-call(s32[5]{0:T(128)S(1)} %stack.15.where_ref, bf16[256,256]{1,0:T(8,128)(2,1)S(1)} %collective-permute-done.4.first_ref.refs_0_, ...), custom_call_target="tpu_custom_call" | custom-call | tf_op jit(solution)/shard_map/turn/pallas_call | solution.py:58
  52.3 1.6 %collective-permute-start.8 = (bf16[256,256]{1,0:T(8,128)(2,1)S(1)}, bf16[256,256]{1,0:T(8,128)(2,1)S(1)}, u32[]{:S(2)}, u32[]{:S(2)}) collective-permute-start(bf16[256,256]{1,0:T(8,128)(2,1)S(1)} %get-tuple-element.70.refs_4_), channel_id=1, source_target_pairs={{0,8},{8,0},{16,24},{24,16},{1,9},{9,1},{17,25},{25,17},{2,10},{10... | collective-permute-start | bytes 393224 | tf_op jit(solution)/shard_map/ppermute | solution.py:540
  53.9 0.7 collective-permute-start.9
  54.6 0.8 sides.2
  55.3 1.0 collective-permute-start.10
  56.3 0.0 collective-permute-start.11
  56.3 1.5 %sums.2 = (bf16[1024,256]{1,0:T(8,128)(2,1)S(1)}, f32[512,256]{1,0:T(8,128)S(1)}) custom-call(bf16[2048,2048]{1,0:T(8,128)(2,1)S(1)} %get-tuple-element.59.picks_ref, bf16[256,2048]{1,0:T(8,128)(2,1)S(1)} %get-tuple-element.72.grad_pre_ref, bf16[512,256]{1,0:T(8,128)(2,1)S(1)} %copy-done.2, bf16[2,256,256]{2,1,0:T(8,128)(2,1)S(1)} %copy-done, ...), custom_call_target="tpu_custom_call" | custom-call | tf_op jit(solution)/shard_map/sums/pallas_call | solution.py:58
  57.9 1.6 %out.1 = (bf16[512,256]{1,0:T(8,128)(2,1)S(1)}, bf16[512,256]{1,0:T(8,128)(2,1)}) custom-call(bf16[2048,2048]{1,0:T(8,128)(2,1)S(1)} %get-tuple-element.59.picks_ref, bf16[256,2048]{1,0:T(8,128)(2,1)S(1)} %get-tuple-element.68.act_edges_ref, bf16[512,256]{1,0:T(8,128)(2,1)S(1)} %get-tuple-element.67.state_ref.refs_8_, bf16[2,256,256]{2,1,0:T(8,128)(2,1)S(1)} %copy-done.1), custom_call_target="tpu_custom_call" | custom-call | tf_op jit(solution)/shard_map/out/pallas_call | solution.py:58
  59.5 0.0 collective-permute-done.8.first_ref
  59.5 0.0 collective-permute-done.9.second_ref
  59.5 0.0 collective-permute-done.10.left_ref
  59.5 2.1 %collective-permute-done.11.right_ref = bf16[256,256]{1,0:T(8,128)(2,1)S(1)} collective-permute-done((bf16[256,256]{1,0:T(8,128)(2,1)S(1)}, bf16[256,256]{1,0:T(8,128)(2,1)S(1)}, u32[]{:S(2)}, u32[]{:S(2)}) %collective-permute-start.11) | collective-permute-done | bytes 131104 | tf_op jit(solution)/shard_map/ppermute | solution.py:532
  61.6 2.3 %backward.1 = (f32[512,256]{1,0:T(8,128)S(1)}, bf16[256,2048]{1,0:T(8,128)(2,1)S(1)}, bf16[256,256]{1,0:T(8,128)(2,1)S(1)}, bf16[256,256]{1,0:T(8,128)(2,1)S(1)}) custom-call(s32[5]{0:T(128)S(1)} %stack.15.where_ref, bf16[256,256]{1,0:T(8,128)(2,1)S(1)} %collective-permute-done.8.first_ref, bf16[256,256]{1,0:T(8,128)(2,1)S(1)} %collective-permute-done.9.second_ref, ...), custom_call_target="tpu_custom_call" | custom-call | tf_op jit(solution)/shard_map/backward/pallas_call | solution.py:58
  63.9 2.6 %collective-permute-start.12 = (bf16[256,256]{1,0:T(8,128)(2,1)S(1)}, bf16[256,256]{1,0:T(8,128)(2,1)S(1)}, u32[]{:S(2)}, u32[]{:S(2)}) collective-permute-start(bf16[256,256]{1,0:T(8,128)(2,1)S(1)} %get-tuple-element.82.refs_16_), channel_id=1, source_target_pairs={{0,8},{8,0},{16,24},{24,16},{1,9},{9,1},{17,25},{25,17},{2,10},{10... | collective-permute-start | bytes 393224 | tf_op jit(solution)/shard_map/ppermute | solution.py:540
  66.5 0.7 collective-permute-start.13
  67.2 0.7 sides.3
  67.9 1.2 collective-permute-start.14
  69.1 0.0 collective-permute-start.15
  69.1 1.5 %sums.3 = (bf16[1024,256]{1,0:T(8,128)(2,1)S(1)}, f32[512,256]{1,0:T(8,128)S(1)}) custom-call(bf16[2048,2048]{1,0:T(8,128)(2,1)S(1)} %get-tuple-element.59.picks_ref, bf16[256,2048]{1,0:T(8,128)(2,1)S(1)} %get-tuple-element.84.grad_pre_ref, f32[512,256]{1,0:T(8,128)S(1)} %get-tuple-element.87.grad_ref.refs_23_, bf16[2,256,256]{2,1,0:T(8,128)(2,1)S(1)} %copy-done, ...), custom_call_target="tpu_custom_call" | custom-call | tf_op jit(solution)/shard_map/sums/pallas_call | solution.py:58
  70.7 1.5 %terms.1 = (f32[1536,128]{1,0:T(8,128)S(1)}, bf16[1536,128]{1,0:T(8,128)(2,1)S(1)}) custom-call(s32[5]{0:T(128)S(1)} %stack.15.where_ref, bf16[256,256]{1,0:T(8,128)(2,1)S(1)} %collective-permute-done.4.first_ref.refs_0_, bf16[256,256]{1,0:T(8,128)(2,1)S(1)} %collective-permute-done.5.second_ref.refs_1_, ...), custom_call_target="tpu_custom_call" | custom-call | tf_op jit(solution)/shard_map/terms/pallas_call | solution.py:58
  72.1 0.0 collective-permute-done.12.first_ref
  72.2 0.0 collective-permute-done.13.second_ref
  72.2 0.3 collective-permute-done.14.left_ref
  72.5 1.9 %collective-permute-done.15.right_ref = bf16[256,256]{1,0:T(8,128)(2,1)S(1)} collective-permute-done((bf16[256,256]{1,0:T(8,128)(2,1)S(1)}, bf16[256,256]{1,0:T(8,128)(2,1)S(1)}, u32[]{:S(2)}, u32[]{:S(2)}) %collective-permute-start.15) | collective-permute-done | bytes 131104 | tf_op jit(solution)/shard_map/ppermute | solution.py:532
  74.4 0.0 collective-permute-start.16
  74.4 2.3 %last.1 = (f32[384,128]{1,0:T(8,128)S(1)}, bf16[384,128]{1,0:T(8,128)(2,1)S(1)}) custom-call(s32[5]{0:T(128)S(1)} %stack.15.where_ref, bf16[256,256]{1,0:T(8,128)(2,1)S(1)} %collective-permute-done.12.first_ref, bf16[256,256]{1,0:T(8,128)(2,1)S(1)} %collective-permute-done.13.second_ref, bf16[256,256]{1,0:T(8,128)(2,1)S(1)} %collective-permute-done.14.left_ref, ...), custom_call_target="tpu_custom_call" | custom-call | tf_op jit(solution)/shard_map/last/pallas_call | solution.py:58
  76.8 0.6 collective-permute-start.17
  77.4 0.9 collective-permute-done.17.refs_3_
  78.3 0.0 collective-permute-done.16.refs_1_
  78.3 0.1 merge.1
  78.4 19.5 %all_to_all.16.parts_ref = bf16[32,64,128]{2,1,0:T(8,128)(2,1)S(1)} all-to-all(bf16[32,64,128]{2,1,0:T(8,128)(2,1)S(1)} %bitcast.16), channel_id=1, replica_groups=mesh['grid'=4,'dom'=8] {'grid','dom'}, dimensions={0} | all-to-all | bytes 1048576 | tf_op jit(solution)/shard_map/all_to_all | solution.py:527
  97.9 0.1 share.1
  98.0 18.4 %all_to_all.17 = bf16[32,64,128]{2,1,0:T(8,128)(2,1)S(1)} all-to-all(bf16[32,64,128]{2,1,0:T(8,128)(2,1)S(1)} %share.1), channel_id=1, replica_groups=mesh['grid'=4,'dom'=8] {'grid','dom'}, dimensions={0} | all-to-all | bytes 1048576 | tf_op jit(solution)/shard_map/all_to_all | solution.py:527
  116.4 0.0 collective-permute-start.18
  116.4 1.9 %collective-permute-done.18.other_ref = bf16[2048,128]{1,0:T(8,128)(2,1)S(1)} collective-permute-done((bf16[2048,128]{1,0:T(8,128)(2,1)S(1)}, bf16[2048,128]{1,0:T(8,128)(2,1)S(1)}, u32[]{:S(2)}, u32[]{:S(2)}) %collective-permute-start.18) | collective-permute-done | bytes 524320 | tf_op jit(solution)/shard_map/ppermute | solution.py:540
  118.3 1.9 %unpack.1 = (f32[128,256]{1,0:T(8,128)}, f32[256,256]{1,0:T(8,128)}, f32[2,256,256]{2,1,0:T(8,128)}, f32[2,256,256]{2,1,0:T(8,128)}, f32[2,256,256]{2,1,0:T(8,128)}) custom-call(s32[5]{0:T(128)S(1)} %stack.15.where_ref, bf16[2048,128]{1,0:T(8,128)(2,1)S(1)} %bitcast.15, bf16[2048,128]{1,0:T(8,128)(2,1)S(1)} %collective-permute-done.18.other_ref), custom_call_target="tpu_custom_call" | custom-call | tf_op jit(solution)/shard_map/unpack/pallas_call | solution.py:58
  (21 shorter events, 0.0 us)
Async XLA Ops:
  0.6 25.8 %copy-start.4 = (bf16[256,256]{1,0:T(8,128)(2,1)S(1)}, bf16[256,256]{1,0:T(8,128)(2,1)}, u32[]{:S(2)}) copy-start(bf16[256,256]{1,0:T(8,128)(2,1)} %enc_out_ref.3) | copy-start | bytes 393220
  0.6 25.8 %copy-start.6 = (bf16[128,256]{1,0:T(8,128)(2,1)S(1)}, bf16[128,256]{1,0:T(8,128)(2,1)}, u32[]{:S(2)}) copy-start(bf16[128,256]{1,0:T(8,128)(2,1)} %enc_in_ref.1) | copy-start | bytes 196612
  0.7 25.8 %copy-start.11 = (s32[256]{0:T(256)S(1)}, s32[256]{0:T(256)}, u32[]{:S(2)}) copy-start(s32[256]{0:T(256)} %param.21) | copy-start | bytes 3076
  0.7 25.8 %copy-start.5 = (bf16[512,256]{1,0:T(8,128)(2,1)S(1)}, bf16[512,256]{1,0:T(8,128)(2,1)}, u32[]{:S(2)}) copy-start(bf16[512,256]{1,0:T(8,128)(2,1)} %static_ref.1) | copy-start | bytes 786436
  0.7 31.9 %copy-start.8 = (s32[2048]{0:T(1024)S(1)}, s32[2048]{0:T(1024)}, u32[]{:S(2)}) copy-start(s32[2048]{0:T(1024)} %param.23) | copy-start | bytes 24580
  0.7 31.9 %copy-start = (bf16[2,256,256]{2,1,0:T(8,128)(2,1)S(1)}, bf16[2,256,256]{2,1,0:T(8,128)(2,1)}, u32[]{:S(2)}) copy-start(bf16[2,256,256]{2,1,0:T(8,128)(2,1)} %src_ref.7) | copy-start | bytes 786436
  0.7 31.9 %copy-start.3 = (bf16[2,256,256]{2,1,0:T(8,128)(2,1)S(1)}, bf16[2,256,256]{2,1,0:T(8,128)(2,1)}, u32[]{:S(2)}) copy-start(bf16[2,256,256]{2,1,0:T(8,128)(2,1)} %dst_ref.3) | copy-start | bytes 786436
  0.7 31.9 %copy-start.10 = (f32[2048]{0:T(1024)S(1)}, f32[2048]{0:T(1024)}, u32[]{:S(2)}) copy-start(f32[2048]{0:T(1024)} %param.25) | copy-start | bytes 24580
  0.7 31.9 %copy-start.9 = (s32[2048]{0:T(1024)S(1)}, s32[2048]{0:T(1024)}, u32[]{:S(2)}) copy-start(s32[2048]{0:T(1024)} %param.24) | copy-start | bytes 24580
  0.7 31.9 %copy-start.7 = (s32[2048]{0:T(1024)S(1)}, s32[2048]{0:T(1024)}, u32[]{:S(2)}) copy-start(s32[2048]{0:T(1024)} %param.22) | copy-start | bytes 24580
  28.4 5.4 %collective-permute-start.3 = (bf16[256,256]{1,0:T(8,128)(2,1)S(1)}, bf16[256,256]{1,0:T(8,128)(2,1)S(1)}, u32[]{:S(2)}, u32[]{:S(2)}) collective-permute-start(bf16[256,256]{1,0:T(8,128)(2,1)S(1)} %get-tuple-element.60), channel_id=1, source_target_pairs={{0,7},{1,0},{2,1},{3,2},{4,3},{5,4},{6,5},{7,6},{8,15},{9,8},{10,9... | collective-permute-start | bytes 393224 | tf_op jit(solution)/shard_map/ppermute | solution.py:532
  29.7 5.3 %collective-permute-start.2 = (bf16[256,256]{1,0:T(8,128)(2,1)S(1)}, bf16[256,256]{1,0:T(8,128)(2,1)S(1)}, u32[]{:S(2)}, u32[]{:S(2)}) collective-permute-start(bf16[256,256]{1,0:T(8,128)(2,1)S(1)} %get-tuple-element.60), channel_id=1, source_target_pairs={{0,1},{1,2},{2,3},{3,4},{4,5},{5,6},{6,7},{7,0},{8,9},{9,10},{10,1... | collective-permute-start | bytes 393224 | tf_op jit(solution)/shard_map/ppermute | solution.py:532
  29.7 7.9 %collective-permute-start.1 = (bf16[256,256]{1,0:T(8,128)(2,1)S(1)}, bf16[256,256]{1,0:T(8,128)(2,1)S(1)}, u32[]{:S(2)}, u32[]{:S(2)}) collective-permute-start(bf16[256,256]{1,0:T(8,128)(2,1)S(1)} %get-tuple-element.60), channel_id=1, source_target_pairs={{0,0},{8,16},{16,8},{24,24},{1,1},{9,17},{17,9},{25,25},{2,2},{10,... | collective-permute-start | bytes 393224 | tf_op jit(solution)/shard_map/ppermute | solution.py:540
  30.3 7.2 %collective-permute-start = (bf16[256,256]{1,0:T(8,128)(2,1)S(1)}, bf16[256,256]{1,0:T(8,128)(2,1)S(1)}, u32[]{:S(2)}, u32[]{:S(2)}) collective-permute-start(bf16[256,256]{1,0:T(8,128)(2,1)S(1)} %get-tuple-element.60), channel_id=1, source_target_pairs={{0,8},{8,0},{16,24},{24,16},{1,9},{9,1},{17,25},{25,17},{2,10},{10... | collective-permute-start | bytes 393224 | tf_op jit(solution)/shard_map/ppermute | solution.py:540
  34.9 2.6 %copy-start.1 = (bf16[2,256,256]{2,1,0:T(8,128)(2,1)S(1)}, bf16[2,256,256]{2,1,0:T(8,128)(2,1)}, u32[]{:S(2)}) copy-start(bf16[2,256,256]{2,1,0:T(8,128)(2,1)} %msg_ref.7) | copy-start | bytes 786436
  37.6 8.3 %copy-start.2 = (bf16[512,256]{1,0:T(8,128)(2,1)S(1)}, bf16[512,256]{1,0:T(8,128)(2,1)}, u32[]{:S(2)}) copy-start(bf16[512,256]{1,0:T(8,128)(2,1)} %refs_11_.1) | copy-start | bytes 786436
  40.4 6.3 %collective-permute-start.7 = (bf16[256,256]{1,0:T(8,128)(2,1)S(1)}, bf16[256,256]{1,0:T(8,128)(2,1)S(1)}, u32[]{:S(2)}, u32[]{:S(2)}) collective-permute-start(bf16[256,256]{1,0:T(8,128)(2,1)S(1)} %get-tuple-element.66), channel_id=1, source_target_pairs={{0,7},{1,0},{2,1},{3,2},{4,3},{5,4},{6,5},{7,6},{8,15},{9,8},{10,9... | collective-permute-start | bytes 393224 | tf_op jit(solution)/shard_map/ppermute | solution.py:532
  41.8 5.3 %collective-permute-start.6 = (bf16[256,256]{1,0:T(8,128)(2,1)S(1)}, bf16[256,256]{1,0:T(8,128)(2,1)S(1)}, u32[]{:S(2)}, u32[]{:S(2)}) collective-permute-start(bf16[256,256]{1,0:T(8,128)(2,1)S(1)} %get-tuple-element.66), channel_id=1, source_target_pairs={{0,1},{1,2},{2,3},{3,4},{4,5},{5,6},{6,7},{7,0},{8,9},{9,10},{10,1... | collective-permute-start | bytes 393224 | tf_op jit(solution)/shard_map/ppermute | solution.py:532
  41.8 7.9 %collective-permute-start.5 = (bf16[256,256]{1,0:T(8,128)(2,1)S(1)}, bf16[256,256]{1,0:T(8,128)(2,1)S(1)}, u32[]{:S(2)}, u32[]{:S(2)}) collective-permute-start(bf16[256,256]{1,0:T(8,128)(2,1)S(1)} %get-tuple-element.66), channel_id=1, source_target_pairs={{0,0},{8,16},{16,8},{24,24},{1,1},{9,17},{17,9},{25,25},{2,2},{10,... | collective-permute-start | bytes 393224 | tf_op jit(solution)/shard_map/ppermute | solution.py:540
  42.4 7.2 %collective-permute-start.4 = (bf16[256,256]{1,0:T(8,128)(2,1)S(1)}, bf16[256,256]{1,0:T(8,128)(2,1)S(1)}, u32[]{:S(2)}, u32[]{:S(2)}) collective-permute-start(bf16[256,256]{1,0:T(8,128)(2,1)S(1)} %get-tuple-element.66), channel_id=1, source_target_pairs={{0,8},{8,0},{16,24},{24,16},{1,9},{9,1},{17,25},{25,17},{2,10},{10... | collective-permute-start | bytes 393224 | tf_op jit(solution)/shard_map/ppermute | solution.py:540
  52.3 7.2 %collective-permute-start.8 = (bf16[256,256]{1,0:T(8,128)(2,1)S(1)}, bf16[256,256]{1,0:T(8,128)(2,1)S(1)}, u32[]{:S(2)}, u32[]{:S(2)}) collective-permute-start(bf16[256,256]{1,0:T(8,128)(2,1)S(1)} %get-tuple-element.70.refs_4_), channel_id=1, source_target_pairs={{0,8},{8,0},{16,24},{24,16},{1,9},{9,1},{17,25},{25,17},{2,10},{10... | collective-permute-start | bytes 393224 | tf_op jit(solution)/shard_map/ppermute | solution.py:540
  53.9 5.6 %collective-permute-start.9 = (bf16[256,256]{1,0:T(8,128)(2,1)S(1)}, bf16[256,256]{1,0:T(8,128)(2,1)S(1)}, u32[]{:S(2)}, u32[]{:S(2)}) collective-permute-start(bf16[256,256]{1,0:T(8,128)(2,1)S(1)} %get-tuple-element.71.refs_5_), channel_id=1, source_target_pairs={{0,0},{8,16},{16,8},{24,24},{1,1},{9,17},{17,9},{25,25},{2,2},{10,... | collective-permute-start | bytes 393224 | tf_op jit(solution)/shard_map/ppermute | solution.py:540
  55.3 4.2 %collective-permute-start.10 = (bf16[256,256]{1,0:T(8,128)(2,1)S(1)}, bf16[256,256]{1,0:T(8,128)(2,1)S(1)}, u32[]{:S(2)}, u32[]{:S(2)}) collective-permute-start(bf16[256,256]{1,0:T(8,128)(2,1)S(1)} %get-tuple-element.73.refs_6_), channel_id=1, source_target_pairs={{0,7},{1,0},{2,1},{3,2},{4,3},{5,4},{6,5},{7,6},{8,15},{9,8},{10,9... | collective-permute-start | bytes 393224 | tf_op jit(solution)/shard_map/ppermute | solution.py:532
  56.3 5.3 %collective-permute-start.11 = (bf16[256,256]{1,0:T(8,128)(2,1)S(1)}, bf16[256,256]{1,0:T(8,128)(2,1)S(1)}, u32[]{:S(2)}, u32[]{:S(2)}) collective-permute-start(bf16[256,256]{1,0:T(8,128)(2,1)S(1)} %get-tuple-element.74.refs_7_), channel_id=1, source_target_pairs={{0,1},{1,2},{2,3},{3,4},{4,5},{5,6},{6,7},{7,0},{8,9},{9,10},{10,1... | collective-permute-start | bytes 393224 | tf_op jit(solution)/shard_map/ppermute | solution.py:532
  63.9 8.2 %collective-permute-start.12 = (bf16[256,256]{1,0:T(8,128)(2,1)S(1)}, bf16[256,256]{1,0:T(8,128)(2,1)S(1)}, u32[]{:S(2)}, u32[]{:S(2)}) collective-permute-start(bf16[256,256]{1,0:T(8,128)(2,1)S(1)} %get-tuple-element.82.refs_16_), channel_id=1, source_target_pairs={{0,8},{8,0},{16,24},{24,16},{1,9},{9,1},{17,25},{25,17},{2,10},{10... | collective-permute-start | bytes 393224 | tf_op jit(solution)/shard_map/ppermute | solution.py:540
  66.5 5.6 %collective-permute-start.13 = (bf16[256,256]{1,0:T(8,128)(2,1)S(1)}, bf16[256,256]{1,0:T(8,128)(2,1)S(1)}, u32[]{:S(2)}, u32[]{:S(2)}) collective-permute-start(bf16[256,256]{1,0:T(8,128)(2,1)S(1)} %get-tuple-element.83.refs_17_), channel_id=1, source_target_pairs={{0,0},{8,16},{16,8},{24,24},{1,1},{9,17},{17,9},{25,25},{2,2},{10,... | collective-permute-start | bytes 393224 | tf_op jit(solution)/shard_map/ppermute | solution.py:540
  67.9 4.5 %collective-permute-start.14 = (bf16[256,256]{1,0:T(8,128)(2,1)S(1)}, bf16[256,256]{1,0:T(8,128)(2,1)S(1)}, u32[]{:S(2)}, u32[]{:S(2)}) collective-permute-start(bf16[256,256]{1,0:T(8,128)(2,1)S(1)} %get-tuple-element.85.refs_18_), channel_id=1, source_target_pairs={{0,7},{1,0},{2,1},{3,2},{4,3},{5,4},{6,5},{7,6},{8,15},{9,8},{10,9... | collective-permute-start | bytes 393224 | tf_op jit(solution)/shard_map/ppermute | solution.py:532
  69.1 5.3 %collective-permute-start.15 = (bf16[256,256]{1,0:T(8,128)(2,1)S(1)}, bf16[256,256]{1,0:T(8,128)(2,1)S(1)}, u32[]{:S(2)}, u32[]{:S(2)}) collective-permute-start(bf16[256,256]{1,0:T(8,128)(2,1)S(1)} %get-tuple-element.86.refs_19_), channel_id=1, source_target_pairs={{0,1},{1,2},{2,3},{3,4},{4,5},{5,6},{6,7},{7,0},{8,9},{9,10},{10,1... | collective-permute-start | bytes 393224 | tf_op jit(solution)/shard_map/ppermute | solution.py:532
  74.4 3.9 %collective-permute-start.16 = (bf16[1536,128]{1,0:T(8,128)(2,1)S(1)}, bf16[1536,128]{1,0:T(8,128)(2,1)S(1)}, u32[]{:S(2)}, u32[]{:S(2)}) collective-permute-start(bf16[1536,128]{1,0:T(8,128)(2,1)S(1)} %get-tuple-element.92), channel_id=1, source_target_pairs={{0,1},{1,0},{2,3},{3,2},{4,5},{5,4},{6,7},{7,6},{8,9},{9,8},{10,11... | collective-permute-start | bytes 1179656 | tf_op jit(solution)/shard_map/ppermute | solution.py:540
  76.8 1.5 %collective-permute-start.17 = (bf16[384,128]{1,0:T(8,128)(2,1)S(1)}, bf16[384,128]{1,0:T(8,128)(2,1)S(1)}, u32[]{:S(2)}, u32[]{:S(2)}) collective-permute-start(bf16[384,128]{1,0:T(8,128)(2,1)S(1)} %get-tuple-element.102), channel_id=1, source_target_pairs={{0,1},{1,0},{2,3},{3,2},{4,5},{5,4},{6,7},{7,6},{8,9},{9,8},{10,11... | collective-permute-start | bytes 294920 | tf_op jit(solution)/shard_map/ppermute | solution.py:540
  116.4 1.9 %collective-permute-start.18 = (bf16[2048,128]{1,0:T(8,128)(2,1)S(1)}, bf16[2048,128]{1,0:T(8,128)(2,1)S(1)}, u32[]{:S(2)}, u32[]{:S(2)}) collective-permute-start(bf16[2048,128]{1,0:T(8,128)(2,1)S(1)} %bitcast.14), channel_id=1, source_target_pairs={{0,1},{1,0},{2,3},{3,2},{4,5},{5,4},{6,7},{7,6},{8,9},{9,8},{10,11... | collective-permute-start | bytes 1572872 | tf_op jit(solution)/shard_map/ppermute | solution.py:540

commit v8 on v7

--- a/solution.py
+++ b/solution.py
@@ -12,7 +12,7 @@
 F32 = jnp.float32
 LANES = 128
 TILE = 256
-CHUNK = 512
+CHUNK = 1024
 GRANT = 20 << 20
 
 
@@ -368,7 +368,7 @@
     for side in range(1, 4):
         total += returned[side][...].astype(F32) * marks[side]
     back = mm(rim_picks[...], total.astype(BF)).astype(BF)
-    return partial_ref[...] + mm_t(back, src_ref[...])
+    return partial_ref[...] + mm_t(back, src_ref[...]), back
 
 
 def backward_body(
@@ -385,13 +385,15 @@
     slope_ref,
     picks_ref,
     grad_ref,
+    back_src_ref,
     grad_pre_ref,
     send0_ref,
     send1_ref,
 ):
     nodes = partial_ref.shape[0]
     returned = (first_ref, second_ref, left_ref, right_ref)
-    grad = merged_grad(partial_ref, where_ref, returned, src_ref.at[layer], rim_picks)
+    grad, back_src = merged_grad(partial_ref, where_ref, returned, src_ref.at[layer], rim_picks)
+    back_src_ref[...] = back_src
     grad_ref[...] = grad
     back = mm_t(msg_ref[layer - 1], grad.astype(BF)).astype(BF)
 
@@ -431,13 +433,17 @@
 def terms_body(where_ref, *refs):
     keep_ref, send_ref = refs[-2:]
     marks = (*pair_marks(where_ref), *side_marks(where_ref)[2:])
-    for layer in range(len(refs) // 12):
-        held = refs[12 * layer : 12 * layer + 12]
-        rims, sends, (state_ref, own_ref, act_ref, grad_ref) = held[:4], held[4:8], held[8:]
+    later, first_layer = refs[:5], refs[5:-2]
+    for layer, held in enumerate((later, first_layer)):
+        rims, sends = (held[:4], held[4:8]) if layer else ((), ())
+        state_ref, own_ref, act_ref, grad_ref = held[-4:]
         nodes, width = state_ref.shape
         first = 3 * width * layer
         state = state_ref[...]
-        src_term = t_mm(state, own_ref[nodes:, :])
+        own_src = own_ref[nodes:, :]
+        if not layer:
+            own_src = (own_src.astype(F32) + held[0][...].astype(F32)).astype(BF)
+        src_term = t_mm(state, own_src)
         for rim_ref, sums_ref, present in zip(rims, sends, marks):
             src_term += t_mm(rim_ref[...], sums_ref[...]) * present
         put_halves(where_ref, first, src_term, keep_ref, send_ref)
@@ -467,7 +473,8 @@
     fin = packed_ref.shape[2]
     peers_step = CHUNK // bucket
     returned = (first_ref, second_ref, left_ref, right_ref)
-    grad = merged_grad(partial_ref, where_ref, returned, src_ref.at[0], rim_picks).astype(BF)
+    grad, _ = merged_grad(partial_ref, where_ref, returned, src_ref.at[0], rim_picks)
+    grad = grad.astype(BF)
     back = mm_t(enc_out_ref[...], grad).astype(BF)
     in_term = jnp.zeros((enc_out_ref.shape[0], fin), F32)
     for start in range(0, picks_ref.shape[1], CHUNK):
@@ -686,9 +693,9 @@
         picks, act_edges1, state1, msg_proj
     )
     partial1, act1 = lax.optimization_barrier((partial1, act1))
-    grad1, grad_pre0, *sends0 = call(
+    grad1, back_src1, grad_pre0, *sends0 = call(
         functools.partial(backward_body, 1),
-        [node_wide, edge_shape] + [rim_shape] * 2,
+        [node_wide, node_shape, edge_shape] + [rim_shape] * 2,
         [],
         "backward",
         True,
@@ -707,7 +714,7 @@
         True,
     )(
         where,
-        *(*rims1, *sends1, state1, own1, act1, node_cotangent),
+        *(back_src1, state1, own1, act1, node_cotangent),
         *(*rims0, *sends0, state0, own0, act0, grad1),
     )
     send, *returned0 = lax.optimization_barrier((send, *returned0))

time: 120 us -> 120 us (level)
  no operation moved by 1% of the time
where the time goes in v8:
time: 120 us
  blocking collectives  61.8 us (52%)
  Pallas kernels  30.5 us (25%)
  starting transfers between devices  17.8 us (15%)
  waiting for transfers between devices  8.78 us (7%)
    all_to_all x3, blocking collectives, exchange(): return lax.all_to_all(shard, AXES, split_axis=0, concat_axis=0, tiled=True)  61.8 us
    pallas_call x19, Pallas kernels, run(): pl.pallas_call(body, out_shape=tuple((jax.ShapeDtypeStruct(shape, dtype)...  30.5 us
    ppermute x11, starting transfers between devices, swapped(): return lax.ppermute(shard, axis, list(enumerate(partner)))  13.1 us
    ppermute x8, waiting for transfers between devices, turned(): lax.ppermute(shard, axis, [(i, (i + by) % count) for i in range(count)])  5.91 us
    ppermute x8, starting transfers between devices, turned(): lax.ppermute(shard, axis, [(i, (i + by) % count) for i in range(count)])  4.74 us
    ppermute x11, waiting for transfers between devices, swapped(): return lax.ppermute(shard, axis, list(enumerate(partner)))  2.88 us
  transfers between devices with their start and end apart: 19, of which 7 were waited for; matrix products, arithmetic and copies ran while one was open for 0% of the time, Pallas kernels for 14%

profile of v8, /device:TPU:0, one launch (start us, length us, event | category | flops | bytes accessed | tf_op | source)
XLA Modules:
  0.0 120.0 jit_solution(4326712804911553152)
XLA Ops:
  0.7 0.1 stack.15.where_ref
  0.8 1.7 %pack.1 = bf16[32,68,128]{2,1,0:T(8,128)(2,1)S(1)} custom-call(s32[5]{0:T(128)S(1)} %stack.15.where_ref, bf16[32,64,128]{2,1,0:T(8,128)(2,1)} %bitcast.23, s32[16,128]{1,0:T(8,128)} %bitcast.24, s32[16,128]{1,0:T(8,128)} %bitcast.25, f32[16,128]{1,0:T(8,128)} %bitcast.26), custom_call_target="tpu_custom_call" | custom-call | tf_op jit(solution)/shard_map/pack/pallas_call | solution.py:58
  2.5 23.9 %all_to_all.15.packed_ref = bf16[32,68,128]{2,1,0:T(8,128)(2,1)S(1)} all-to-all(bf16[32,68,128]{2,1,0:T(8,128)(2,1)S(1)} %pack.1), channel_id=1, replica_groups=mesh['grid'=4,'dom'=8] {'grid','dom'}, dimensions={0} | all-to-all | bytes 1114112 | tf_op jit(solution)/shard_map/all_to_all | solution.py:534
  26.5 0.0 copy-done.5
  26.5 2.0 %encode.1 = (bf16[512,256]{1,0:T(8,128)(2,1)S(1)}, f32[256,2048]{1,0:T(8,128)S(1)}, bf16[512,2048]{1,0:T(8,128)(2,1)S(1)}, bf16[512,256]{1,0:T(8,128)(2,1)S(1)}, bf16[256,256]{1,0:T(8,128)(2,1)S(1)}) custom-call(bf16[32,68,128]{2,1,0:T(8,128)(2,1)S(1)} %all_to_all.15.packed_ref, bf16[128,256]{1,0:T(8,128)(2,1)S(1)} %copy-done.6, ...), custom_call_target="tpu_custom_call" | custom-call | tf_op jit(solution)/shard_map/encode/pallas_call | solution.py:58
  28.5 1.2 %collective-permute-start.3 = (bf16[256,256]{1,0:T(8,128)(2,1)S(1)}, bf16[256,256]{1,0:T(8,128)(2,1)S(1)}, u32[]{:S(2)}, u32[]{:S(2)}) collective-permute-start(bf16[256,256]{1,0:T(8,128)(2,1)S(1)} %get-tuple-element.61), channel_id=1, source_target_pairs={{0,7},{1,0},{2,1},{3,2},{4,3},{5,4},{6,5},{7,6},{8,15},{9,8},{10,9... | collective-permute-start | bytes 393224 | tf_op jit(solution)/shard_map/ppermute | solution.py:539
  29.7 0.0 collective-permute-start.2
  29.7 0.7 collective-permute-start.1
  30.4 2.3 %collective-permute-start = (bf16[256,256]{1,0:T(8,128)(2,1)S(1)}, bf16[256,256]{1,0:T(8,128)(2,1)S(1)}, u32[]{:S(2)}, u32[]{:S(2)}) collective-permute-start(bf16[256,256]{1,0:T(8,128)(2,1)S(1)} %get-tuple-element.61), channel_id=1, source_target_pairs={{0,8},{8,0},{16,24},{24,16},{1,9},{9,1},{17,25},{25,17},{2,10},{10... | collective-permute-start | bytes 393224 | tf_op jit(solution)/shard_map/ppermute | solution.py:547
  32.7 1.2 picks.1
  33.9 0.0 collective-permute-done.3.right_ref.refs_8_
  33.9 1.1 collective-permute-done.2.left_ref.refs_7_
  35.0 2.6 %own.2.own_pre_ref = f32[256,2048]{1,0:T(8,128)S(1)} custom-call(s32[5]{0:T(128)S(1)} %stack.15.where_ref, bf16[256,256]{1,0:T(8,128)(2,1)S(1)} %collective-permute-done.2.left_ref.refs_7_, bf16[256,256]{1,0:T(8,128)(2,1)S(1)} %collective-permute-done.3.right_ref.refs_8_, bf16[512,256]{1,0:T(8,128)(2,1)S(1)} %get-tuple-element.62.state_ref.refs_13_, ...), custom_call_target="tpu_custom_call" | custom-call | tf_op jit(solution)/shard_map/own/pallas_call | solution.py:58
  37.6 0.0 collective-permute-done.1.second_ref.refs_6_
  37.6 0.0 collective-permute-done.first_ref.refs_5_
  37.6 0.0 copy-done.1
  37.6 0.0 copy-start.2
  37.6 2.8 %forward.1 = (f32[256,2048]{1,0:T(8,128)S(1)}, bf16[512,256]{1,0:T(8,128)(2,1)S(1)}, bf16[512,256]{1,0:T(8,128)(2,1)S(1)}, bf16[256,256]{1,0:T(8,128)(2,1)S(1)}) custom-call(s32[5]{0:T(128)S(1)} %stack.15.where_ref, bf16[256,256]{1,0:T(8,128)(2,1)S(1)} %collective-permute-done.first_ref.refs_5_, ...), custom_call_target="tpu_custom_call" | custom-call | tf_op jit(solution)/shard_map/forward/pallas_call | solution.py:58
  40.5 1.3 %collective-permute-start.7 = (bf16[256,256]{1,0:T(8,128)(2,1)S(1)}, bf16[256,256]{1,0:T(8,128)(2,1)S(1)}, u32[]{:S(2)}, u32[]{:S(2)}) collective-permute-start(bf16[256,256]{1,0:T(8,128)(2,1)S(1)} %get-tuple-element.67), channel_id=1, source_target_pairs={{0,7},{1,0},{2,1},{3,2},{4,3},{5,4},{6,5},{7,6},{8,15},{9,8},{10,9... | collective-permute-start | bytes 393224 | tf_op jit(solution)/shard_map/ppermute | solution.py:539
  41.8 0.0 collective-permute-start.6
  41.8 0.7 collective-permute-start.5
  42.5 3.4 %collective-permute-start.4 = (bf16[256,256]{1,0:T(8,128)(2,1)S(1)}, bf16[256,256]{1,0:T(8,128)(2,1)S(1)}, u32[]{:S(2)}, u32[]{:S(2)}) collective-permute-start(bf16[256,256]{1,0:T(8,128)(2,1)S(1)} %get-tuple-element.67), channel_id=1, source_target_pairs={{0,8},{8,0},{16,24},{24,16},{1,9},{9,1},{17,25},{25,17},{2,10},{10... | collective-permute-start | bytes 393224 | tf_op jit(solution)/shard_map/ppermute | solution.py:547
  45.9 0.9 back.1.back_ref
  46.8 0.0 collective-permute-done.7.right_ref
  46.8 0.3 collective-permute-done.6.left_ref
  47.1 2.6 %own.3.own_pre_ref = f32[256,2048]{1,0:T(8,128)S(1)} custom-call(s32[5]{0:T(128)S(1)} %stack.15.where_ref, bf16[256,256]{1,0:T(8,128)(2,1)S(1)} %collective-permute-done.6.left_ref, bf16[256,256]{1,0:T(8,128)(2,1)S(1)} %collective-permute-done.7.right_ref, bf16[512,256]{1,0:T(8,128)(2,1)S(1)} %get-tuple-element.68.state_ref.refs_1_, ...), custom_call_target="tpu_custom_call" | custom-call | tf_op jit(solution)/shard_map/own/pallas_call | solution.py:58
  49.7 0.0 collective-permute-done.5.second_ref
  49.7 0.0 collective-permute-done.4.first_ref
  49.7 2.6 %turn.1 = (bf16[256,2048]{1,0:T(8,128)(2,1)S(1)}, bf16[256,2048]{1,0:T(8,128)(2,1)S(1)}, bf16[256,256]{1,0:T(8,128)(2,1)S(1)}, bf16[256,256]{1,0:T(8,128)(2,1)S(1)}) custom-call(s32[5]{0:T(128)S(1)} %stack.15.where_ref, bf16[256,256]{1,0:T(8,128)(2,1)S(1)} %collective-permute-done.4.first_ref, bf16[256,256]{1,0:T(8,128)(2,1)S(1)} %collective-permute-done.5.second_ref, ...), custom_call_target="tpu_custom_call" | custom-call | tf_op jit(solution)/shard_map/turn/pallas_call | solution.py:58
  52.4 1.6 %collective-permute-start.8 = (bf16[256,256]{1,0:T(8,128)(2,1)S(1)}, bf16[256,256]{1,0:T(8,128)(2,1)S(1)}, u32[]{:S(2)}, u32[]{:S(2)}) collective-permute-start(bf16[256,256]{1,0:T(8,128)(2,1)S(1)} %get-tuple-element.71), channel_id=1, source_target_pairs={{0,8},{8,0},{16,24},{24,16},{1,9},{9,1},{17,25},{25,17},{2,10},{10... | collective-permute-start | bytes 393224 | tf_op jit(solution)/shard_map/ppermute | solution.py:547
  53.9 0.7 collective-permute-start.9
  54.6 0.8 sides.2
  55.4 1.0 collective-permute-start.10
  56.4 0.0 collective-permute-start.11
  56.4 1.5 %sums.2 = (bf16[1024,256]{1,0:T(8,128)(2,1)S(1)}, f32[512,256]{1,0:T(8,128)S(1)}) custom-call(bf16[2048,2048]{1,0:T(8,128)(2,1)S(1)} %get-tuple-element.60.picks_ref, bf16[256,2048]{1,0:T(8,128)(2,1)S(1)} %get-tuple-element.73.grad_pre_ref, bf16[512,256]{1,0:T(8,128)(2,1)S(1)} %copy-done.2, bf16[2,256,256]{2,1,0:T(8,128)(2,1)S(1)} %copy-done, ...), custom_call_target="tpu_custom_call" | custom-call | tf_op jit(solution)/shard_map/sums/pallas_call | solution.py:58
  57.9 1.6 %out.1 = (bf16[512,256]{1,0:T(8,128)(2,1)S(1)}, bf16[512,256]{1,0:T(8,128)(2,1)}) custom-call(bf16[2048,2048]{1,0:T(8,128)(2,1)S(1)} %get-tuple-element.60.picks_ref, bf16[256,2048]{1,0:T(8,128)(2,1)S(1)} %get-tuple-element.69.act_edges_ref, bf16[512,256]{1,0:T(8,128)(2,1)S(1)} %get-tuple-element.68.state_ref.refs_1_, bf16[2,256,256]{2,1,0:T(8,128)(2,1)S(1)} %copy-done.1), custom_call_target="tpu_custom_call" | custom-call | tf_op jit(solution)/shard_map/out/pallas_call | solution.py:58
  59.5 0.0 collective-permute-done.8.first_ref
  59.6 0.0 collective-permute-done.9.second_ref
  59.6 0.0 collective-permute-done.10.left_ref
  59.6 2.1 %collective-permute-done.11.right_ref = bf16[256,256]{1,0:T(8,128)(2,1)S(1)} collective-permute-done((bf16[256,256]{1,0:T(8,128)(2,1)S(1)}, bf16[256,256]{1,0:T(8,128)(2,1)S(1)}, u32[]{:S(2)}, u32[]{:S(2)}) %collective-permute-start.11) | collective-permute-done | bytes 131104 | tf_op jit(solution)/shard_map/ppermute | solution.py:539
  61.7 2.3 %backward.1 = (f32[512,256]{1,0:T(8,128)S(1)}, bf16[512,256]{1,0:T(8,128)(2,1)S(1)}, bf16[256,2048]{1,0:T(8,128)(2,1)S(1)}, bf16[256,256]{1,0:T(8,128)(2,1)S(1)}, bf16[256,256]{1,0:T(8,128)(2,1)S(1)}) custom-call(s32[5]{0:T(128)S(1)} %stack.15.where_ref, bf16[256,256]{1,0:T(8,128)(2,1)S(1)} %collective-permute-done.8.first_ref, ...), custom_call_target="tpu_custom_call" | custom-call | tf_op jit(solution)/shard_map/backward/pallas_call | solution.py:58
  64.0 2.6 %collective-permute-start.12 = (bf16[256,256]{1,0:T(8,128)(2,1)S(1)}, bf16[256,256]{1,0:T(8,128)(2,1)S(1)}, u32[]{:S(2)}, u32[]{:S(2)}) collective-permute-start(bf16[256,256]{1,0:T(8,128)(2,1)S(1)} %get-tuple-element.84.refs_9_), channel_id=1, source_target_pairs={{0,8},{8,0},{16,24},{24,16},{1,9},{9,1},{17,25},{25,17},{2,10},{10... | collective-permute-start | bytes 393224 | tf_op jit(solution)/shard_map/ppermute | solution.py:547
  66.6 0.7 collective-permute-start.13
  67.2 0.7 sides.3
  68.0 1.2 collective-permute-start.14
  69.2 0.0 collective-permute-start.15
  69.2 1.5 %sums.3 = (bf16[1024,256]{1,0:T(8,128)(2,1)S(1)}, f32[512,256]{1,0:T(8,128)S(1)}) custom-call(bf16[2048,2048]{1,0:T(8,128)(2,1)S(1)} %get-tuple-element.60.picks_ref, bf16[256,2048]{1,0:T(8,128)(2,1)S(1)} %get-tuple-element.86.grad_pre_ref, f32[512,256]{1,0:T(8,128)S(1)} %get-tuple-element.89.grad_ref.refs_16_, bf16[2,256,256]{2,1,0:T(8,128)(2,1)S(1)} %copy-done, ...), custom_call_target="tpu_custom_call" | custom-call | tf_op jit(solution)/shard_map/sums/pallas_call | solution.py:58
  70.7 1.3 %terms.1 = (f32[1536,128]{1,0:T(8,128)S(1)}, bf16[1536,128]{1,0:T(8,128)(2,1)S(1)}) custom-call(s32[5]{0:T(128)S(1)} %stack.15.where_ref, bf16[512,256]{1,0:T(8,128)(2,1)S(1)} %get-tuple-element.81.refs_0_, bf16[512,256]{1,0:T(8,128)(2,1)S(1)} %get-tuple-element.68.state_ref.refs_1_, bf16[1024,256]{1,0:T(8,128)(2,1)S(1)} %get-tuple-element.82.refs_2_, ...), custom_call_target="tpu_custom_call" | custom-call | tf_op jit(solution)/shard_map/terms/pallas_call | solution.py:58
  72.0 0.0 collective-permute-done.12.first_ref
  72.0 0.0 collective-permute-done.13.second_ref
  72.0 0.5 collective-permute-done.14.left_ref
  72.5 2.0 %collective-permute-done.15.right_ref = bf16[256,256]{1,0:T(8,128)(2,1)S(1)} collective-permute-done((bf16[256,256]{1,0:T(8,128)(2,1)S(1)}, bf16[256,256]{1,0:T(8,128)(2,1)S(1)}, u32[]{:S(2)}, u32[]{:S(2)}) %collective-permute-start.15) | collective-permute-done | bytes 131104 | tf_op jit(solution)/shard_map/ppermute | solution.py:539
  74.5 0.0 collective-permute-start.16
  74.5 2.2 %last.1 = (f32[384,128]{1,0:T(8,128)S(1)}, bf16[384,128]{1,0:T(8,128)(2,1)S(1)}) custom-call(s32[5]{0:T(128)S(1)} %stack.15.where_ref, bf16[256,256]{1,0:T(8,128)(2,1)S(1)} %collective-permute-done.12.first_ref, bf16[256,256]{1,0:T(8,128)(2,1)S(1)} %collective-permute-done.13.second_ref, bf16[256,256]{1,0:T(8,128)(2,1)S(1)} %collective-permute-done.14.left_ref, ...), custom_call_target="tpu_custom_call" | custom-call | tf_op jit(solution)/shard_map/last/pallas_call | solution.py:58
  76.7 0.6 collective-permute-start.17
  77.2 0.9 collective-permute-done.17.refs_3_
  78.2 0.0 collective-permute-done.16.refs_1_
  78.2 0.1 merge.1
  78.3 19.5 %all_to_all.16.parts_ref = bf16[32,64,128]{2,1,0:T(8,128)(2,1)S(1)} all-to-all(bf16[32,64,128]{2,1,0:T(8,128)(2,1)S(1)} %bitcast.16), channel_id=1, replica_groups=mesh['grid'=4,'dom'=8] {'grid','dom'}, dimensions={0} | all-to-all | bytes 1048576 | tf_op jit(solution)/shard_map/all_to_all | solution.py:534
  97.8 0.1 share.1
  97.9 18.4 %all_to_all.17 = bf16[32,64,128]{2,1,0:T(8,128)(2,1)S(1)} all-to-all(bf16[32,64,128]{2,1,0:T(8,128)(2,1)S(1)} %share.1), channel_id=1, replica_groups=mesh['grid'=4,'dom'=8] {'grid','dom'}, dimensions={0} | all-to-all | bytes 1048576 | tf_op jit(solution)/shard_map/all_to_all | solution.py:534
  116.3 0.0 collective-permute-start.18
  116.3 1.9 %collective-permute-done.18.other_ref = bf16[2048,128]{1,0:T(8,128)(2,1)S(1)} collective-permute-done((bf16[2048,128]{1,0:T(8,128)(2,1)S(1)}, bf16[2048,128]{1,0:T(8,128)(2,1)S(1)}, u32[]{:S(2)}, u32[]{:S(2)}) %collective-permute-start.18) | collective-permute-done | bytes 524320 | tf_op jit(solution)/shard_map/ppermute | solution.py:547
  118.2 1.9 %unpack.1 = (f32[128,256]{1,0:T(8,128)}, f32[256,256]{1,0:T(8,128)}, f32[2,256,256]{2,1,0:T(8,128)}, f32[2,256,256]{2,1,0:T(8,128)}, f32[2,256,256]{2,1,0:T(8,128)}) custom-call(s32[5]{0:T(128)S(1)} %stack.15.where_ref, bf16[2048,128]{1,0:T(8,128)(2,1)S(1)} %bitcast.15, bf16[2048,128]{1,0:T(8,128)(2,1)S(1)} %collective-permute-done.18.other_ref), custom_call_target="tpu_custom_call" | custom-call | tf_op jit(solution)/shard_map/unpack/pallas_call | solution.py:58
  (21 shorter events, 0.0 us)
Async XLA Ops:
  0.6 25.8 %copy-start.4 = (bf16[256,256]{1,0:T(8,128)(2,1)S(1)}, bf16[256,256]{1,0:T(8,128)(2,1)}, u32[]{:S(2)}) copy-start(bf16[256,256]{1,0:T(8,128)(2,1)} %enc_out_ref.3) | copy-start | bytes 393220
  0.6 25.8 %copy-start.6 = (bf16[128,256]{1,0:T(8,128)(2,1)S(1)}, bf16[128,256]{1,0:T(8,128)(2,1)}, u32[]{:S(2)}) copy-start(bf16[128,256]{1,0:T(8,128)(2,1)} %enc_in_ref.1) | copy-start | bytes 196612
  0.7 25.8 %copy-start.11 = (s32[256]{0:T(256)S(1)}, s32[256]{0:T(256)}, u32[]{:S(2)}) copy-start(s32[256]{0:T(256)} %param.21) | copy-start | bytes 3076
  0.7 25.8 %copy-start.5 = (bf16[512,256]{1,0:T(8,128)(2,1)S(1)}, bf16[512,256]{1,0:T(8,128)(2,1)}, u32[]{:S(2)}) copy-start(bf16[512,256]{1,0:T(8,128)(2,1)} %static_ref.1) | copy-start | bytes 786436
  0.7 32.0 %copy-start.8 = (s32[2048]{0:T(1024)S(1)}, s32[2048]{0:T(1024)}, u32[]{:S(2)}) copy-start(s32[2048]{0:T(1024)} %param.23) | copy-start | bytes 24580
  0.7 32.0 %copy-start = (bf16[2,256,256]{2,1,0:T(8,128)(2,1)S(1)}, bf16[2,256,256]{2,1,0:T(8,128)(2,1)}, u32[]{:S(2)}) copy-start(bf16[2,256,256]{2,1,0:T(8,128)(2,1)} %src_ref.7) | copy-start | bytes 786436
  0.7 32.0 %copy-start.3 = (bf16[2,256,256]{2,1,0:T(8,128)(2,1)S(1)}, bf16[2,256,256]{2,1,0:T(8,128)(2,1)}, u32[]{:S(2)}) copy-start(bf16[2,256,256]{2,1,0:T(8,128)(2,1)} %dst_ref.3) | copy-start | bytes 786436
  0.7 32.0 %copy-start.10 = (f32[2048]{0:T(1024)S(1)}, f32[2048]{0:T(1024)}, u32[]{:S(2)}) copy-start(f32[2048]{0:T(1024)} %param.25) | copy-start | bytes 24580
  0.7 32.0 %copy-start.9 = (s32[2048]{0:T(1024)S(1)}, s32[2048]{0:T(1024)}, u32[]{:S(2)}) copy-start(s32[2048]{0:T(1024)} %param.24) | copy-start | bytes 24580
  0.7 32.0 %copy-start.7 = (s32[2048]{0:T(1024)S(1)}, s32[2048]{0:T(1024)}, u32[]{:S(2)}) copy-start(s32[2048]{0:T(1024)} %param.22) | copy-start | bytes 24580
  28.5 5.4 %collective-permute-start.3 = (bf16[256,256]{1,0:T(8,128)(2,1)S(1)}, bf16[256,256]{1,0:T(8,128)(2,1)S(1)}, u32[]{:S(2)}, u32[]{:S(2)}) collective-permute-start(bf16[256,256]{1,0:T(8,128)(2,1)S(1)} %get-tuple-element.61), channel_id=1, source_target_pairs={{0,7},{1,0},{2,1},{3,2},{4,3},{5,4},{6,5},{7,6},{8,15},{9,8},{10,9... | collective-permute-start | bytes 393224 | tf_op jit(solution)/shard_map/ppermute | solution.py:539
  29.7 5.3 %collective-permute-start.2 = (bf16[256,256]{1,0:T(8,128)(2,1)S(1)}, bf16[256,256]{1,0:T(8,128)(2,1)S(1)}, u32[]{:S(2)}, u32[]{:S(2)}) collective-permute-start(bf16[256,256]{1,0:T(8,128)(2,1)S(1)} %get-tuple-element.61), channel_id=1, source_target_pairs={{0,1},{1,2},{2,3},{3,4},{4,5},{5,6},{6,7},{7,0},{8,9},{9,10},{10,1... | collective-permute-start | bytes 393224 | tf_op jit(solution)/shard_map/ppermute | solution.py:539
  29.7 7.9 %collective-permute-start.1 = (bf16[256,256]{1,0:T(8,128)(2,1)S(1)}, bf16[256,256]{1,0:T(8,128)(2,1)S(1)}, u32[]{:S(2)}, u32[]{:S(2)}) collective-permute-start(bf16[256,256]{1,0:T(8,128)(2,1)S(1)} %get-tuple-element.61), channel_id=1, source_target_pairs={{0,0},{8,16},{16,8},{24,24},{1,1},{9,17},{17,9},{25,25},{2,2},{10,... | collective-permute-start | bytes 393224 | tf_op jit(solution)/shard_map/ppermute | solution.py:547
  30.4 7.2 %collective-permute-start = (bf16[256,256]{1,0:T(8,128)(2,1)S(1)}, bf16[256,256]{1,0:T(8,128)(2,1)S(1)}, u32[]{:S(2)}, u32[]{:S(2)}) collective-permute-start(bf16[256,256]{1,0:T(8,128)(2,1)S(1)} %get-tuple-element.61), channel_id=1, source_target_pairs={{0,8},{8,0},{16,24},{24,16},{1,9},{9,1},{17,25},{25,17},{2,10},{10... | collective-permute-start | bytes 393224 | tf_op jit(solution)/shard_map/ppermute | solution.py:547
  35.0 2.6 %copy-start.1 = (bf16[2,256,256]{2,1,0:T(8,128)(2,1)S(1)}, bf16[2,256,256]{2,1,0:T(8,128)(2,1)}, u32[]{:S(2)}) copy-start(bf16[2,256,256]{2,1,0:T(8,128)(2,1)} %msg_ref.7) | copy-start | bytes 786436
  37.6 8.3 %copy-start.2 = (bf16[512,256]{1,0:T(8,128)(2,1)S(1)}, bf16[512,256]{1,0:T(8,128)(2,1)}, u32[]{:S(2)}) copy-start(bf16[512,256]{1,0:T(8,128)(2,1)} %refs_4_.1) | copy-start | bytes 786436
  40.5 6.3 %collective-permute-start.7 = (bf16[256,256]{1,0:T(8,128)(2,1)S(1)}, bf16[256,256]{1,0:T(8,128)(2,1)S(1)}, u32[]{:S(2)}, u32[]{:S(2)}) collective-permute-start(bf16[256,256]{1,0:T(8,128)(2,1)S(1)} %get-tuple-element.67), channel_id=1, source_target_pairs={{0,7},{1,0},{2,1},{3,2},{4,3},{5,4},{6,5},{7,6},{8,15},{9,8},{10,9... | collective-permute-start | bytes 393224 | tf_op jit(solution)/shard_map/ppermute | solution.py:539
  41.8 5.3 %collective-permute-start.6 = (bf16[256,256]{1,0:T(8,128)(2,1)S(1)}, bf16[256,256]{1,0:T(8,128)(2,1)S(1)}, u32[]{:S(2)}, u32[]{:S(2)}) collective-permute-start(bf16[256,256]{1,0:T(8,128)(2,1)S(1)} %get-tuple-element.67), channel_id=1, source_target_pairs={{0,1},{1,2},{2,3},{3,4},{4,5},{5,6},{6,7},{7,0},{8,9},{9,10},{10,1... | collective-permute-start | bytes 393224 | tf_op jit(solution)/shard_map/ppermute | solution.py:539
  41.8 7.9 %collective-permute-start.5 = (bf16[256,256]{1,0:T(8,128)(2,1)S(1)}, bf16[256,256]{1,0:T(8,128)(2,1)S(1)}, u32[]{:S(2)}, u32[]{:S(2)}) collective-permute-start(bf16[256,256]{1,0:T(8,128)(2,1)S(1)} %get-tuple-element.67), channel_id=1, source_target_pairs={{0,0},{8,16},{16,8},{24,24},{1,1},{9,17},{17,9},{25,25},{2,2},{10,... | collective-permute-start | bytes 393224 | tf_op jit(solution)/shard_map/ppermute | solution.py:547
  42.5 7.2 %collective-permute-start.4 = (bf16[256,256]{1,0:T(8,128)(2,1)S(1)}, bf16[256,256]{1,0:T(8,128)(2,1)S(1)}, u32[]{:S(2)}, u32[]{:S(2)}) collective-permute-start(bf16[256,256]{1,0:T(8,128)(2,1)S(1)} %get-tuple-element.67), channel_id=1, source_target_pairs={{0,8},{8,0},{16,24},{24,16},{1,9},{9,1},{17,25},{25,17},{2,10},{10... | collective-permute-start | bytes 393224 | tf_op jit(solution)/shard_map/ppermute | solution.py:547
  52.4 7.2 %collective-permute-start.8 = (bf16[256,256]{1,0:T(8,128)(2,1)S(1)}, bf16[256,256]{1,0:T(8,128)(2,1)S(1)}, u32[]{:S(2)}, u32[]{:S(2)}) collective-permute-start(bf16[256,256]{1,0:T(8,128)(2,1)S(1)} %get-tuple-element.71), channel_id=1, source_target_pairs={{0,8},{8,0},{16,24},{24,16},{1,9},{9,1},{17,25},{25,17},{2,10},{10... | collective-permute-start | bytes 393224 | tf_op jit(solution)/shard_map/ppermute | solution.py:547
  53.9 5.6 %collective-permute-start.9 = (bf16[256,256]{1,0:T(8,128)(2,1)S(1)}, bf16[256,256]{1,0:T(8,128)(2,1)S(1)}, u32[]{:S(2)}, u32[]{:S(2)}) collective-permute-start(bf16[256,256]{1,0:T(8,128)(2,1)S(1)} %get-tuple-element.72), channel_id=1, source_target_pairs={{0,0},{8,16},{16,8},{24,24},{1,1},{9,17},{17,9},{25,25},{2,2},{10,... | collective-permute-start | bytes 393224 | tf_op jit(solution)/shard_map/ppermute | solution.py:547
  55.4 4.2 %collective-permute-start.10 = (bf16[256,256]{1,0:T(8,128)(2,1)S(1)}, bf16[256,256]{1,0:T(8,128)(2,1)S(1)}, u32[]{:S(2)}, u32[]{:S(2)}) collective-permute-start(bf16[256,256]{1,0:T(8,128)(2,1)S(1)} %get-tuple-element.74), channel_id=1, source_target_pairs={{0,7},{1,0},{2,1},{3,2},{4,3},{5,4},{6,5},{7,6},{8,15},{9,8},{10,9... | collective-permute-start | bytes 393224 | tf_op jit(solution)/shard_map/ppermute | solution.py:539
  56.4 5.3 %collective-permute-start.11 = (bf16[256,256]{1,0:T(8,128)(2,1)S(1)}, bf16[256,256]{1,0:T(8,128)(2,1)S(1)}, u32[]{:S(2)}, u32[]{:S(2)}) collective-permute-start(bf16[256,256]{1,0:T(8,128)(2,1)S(1)} %get-tuple-element.75), channel_id=1, source_target_pairs={{0,1},{1,2},{2,3},{3,4},{4,5},{5,6},{6,7},{7,0},{8,9},{9,10},{10,1... | collective-permute-start | bytes 393224 | tf_op jit(solution)/shard_map/ppermute | solution.py:539
  64.0 8.0 %collective-permute-start.12 = (bf16[256,256]{1,0:T(8,128)(2,1)S(1)}, bf16[256,256]{1,0:T(8,128)(2,1)S(1)}, u32[]{:S(2)}, u32[]{:S(2)}) collective-permute-start(bf16[256,256]{1,0:T(8,128)(2,1)S(1)} %get-tuple-element.84.refs_9_), channel_id=1, source_target_pairs={{0,8},{8,0},{16,24},{24,16},{1,9},{9,1},{17,25},{25,17},{2,10},{10... | collective-permute-start | bytes 393224 | tf_op jit(solution)/shard_map/ppermute | solution.py:547
  66.6 5.5 %collective-permute-start.13 = (bf16[256,256]{1,0:T(8,128)(2,1)S(1)}, bf16[256,256]{1,0:T(8,128)(2,1)S(1)}, u32[]{:S(2)}, u32[]{:S(2)}) collective-permute-start(bf16[256,256]{1,0:T(8,128)(2,1)S(1)} %get-tuple-element.85.refs_10_), channel_id=1, source_target_pairs={{0,0},{8,16},{16,8},{24,24},{1,1},{9,17},{17,9},{25,25},{2,2},{10,... | collective-permute-start | bytes 393224 | tf_op jit(solution)/shard_map/ppermute | solution.py:547
  68.0 4.5 %collective-permute-start.14 = (bf16[256,256]{1,0:T(8,128)(2,1)S(1)}, bf16[256,256]{1,0:T(8,128)(2,1)S(1)}, u32[]{:S(2)}, u32[]{:S(2)}) collective-permute-start(bf16[256,256]{1,0:T(8,128)(2,1)S(1)} %get-tuple-element.87.refs_11_), channel_id=1, source_target_pairs={{0,7},{1,0},{2,1},{3,2},{4,3},{5,4},{6,5},{7,6},{8,15},{9,8},{10,9... | collective-permute-start | bytes 393224 | tf_op jit(solution)/shard_map/ppermute | solution.py:539
  69.2 5.3 %collective-permute-start.15 = (bf16[256,256]{1,0:T(8,128)(2,1)S(1)}, bf16[256,256]{1,0:T(8,128)(2,1)S(1)}, u32[]{:S(2)}, u32[]{:S(2)}) collective-permute-start(bf16[256,256]{1,0:T(8,128)(2,1)S(1)} %get-tuple-element.88.refs_12_), channel_id=1, source_target_pairs={{0,1},{1,2},{2,3},{3,4},{4,5},{5,6},{6,7},{7,0},{8,9},{9,10},{10,1... | collective-permute-start | bytes 393224 | tf_op jit(solution)/shard_map/ppermute | solution.py:539
  74.5 3.7 %collective-permute-start.16 = (bf16[1536,128]{1,0:T(8,128)(2,1)S(1)}, bf16[1536,128]{1,0:T(8,128)(2,1)S(1)}, u32[]{:S(2)}, u32[]{:S(2)}) collective-permute-start(bf16[1536,128]{1,0:T(8,128)(2,1)S(1)} %get-tuple-element.94), channel_id=1, source_target_pairs={{0,1},{1,0},{2,3},{3,2},{4,5},{5,4},{6,7},{7,6},{8,9},{9,8},{10,11... | collective-permute-start | bytes 1179656 | tf_op jit(solution)/shard_map/ppermute | solution.py:547
  76.7 1.5 %collective-permute-start.17 = (bf16[384,128]{1,0:T(8,128)(2,1)S(1)}, bf16[384,128]{1,0:T(8,128)(2,1)S(1)}, u32[]{:S(2)}, u32[]{:S(2)}) collective-permute-start(bf16[384,128]{1,0:T(8,128)(2,1)S(1)} %get-tuple-element.104), channel_id=1, source_target_pairs={{0,1},{1,0},{2,3},{3,2},{4,5},{5,4},{6,7},{7,6},{8,9},{9,8},{10,11... | collective-permute-start | bytes 294920 | tf_op jit(solution)/shard_map/ppermute | solution.py:547
  116.3 1.9 %collective-permute-start.18 = (bf16[2048,128]{1,0:T(8,128)(2,1)S(1)}, bf16[2048,128]{1,0:T(8,128)(2,1)S(1)}, u32[]{:S(2)}, u32[]{:S(2)}) collective-permute-start(bf16[2048,128]{1,0:T(8,128)(2,1)S(1)} %bitcast.14), channel_id=1, source_target_pairs={{0,1},{1,0},{2,3},{3,2},{4,5},{5,4},{6,7},{7,6},{8,9},{9,8},{10,11... | collective-permute-start | bytes 1572872 | tf_op jit(solution)/shard_map/ppermute | solution.py:547
